TPU v7x, 256 devices: a whole 4x4x8 slice. The times are simulated.
256 devices in a mesh: aux: 4 (over x_hi, core), row: 64 (over z, x_lo, y).
Axes of the slice: x: 4 (x_hi: 2, x_lo: 2; x = x_hi * 2 + x_lo), y: 4, z: 8, core: 2. Of those that a mesh axis runs over, the one named last changes fastest.
Arguments:
- integrals: bfloat16 [4, 8192, 8192], P('aux', 'row'), may hold values from -6 to 6
- orbitals: bfloat16 [8192, 768], P('row'), may hold values from -0.0011901855 to 0.0011901855
Outputs:
- exchange_matrix: float32 [8192, 8192], P('row', 'aux')
All inputs are finite; a program needn't handle non-finite values.
Results may differ from a plain program's by a relative error of at most 0.0033.
Values may be sent and summed in bfloat16 or wider, within the bound.
No kernel may reach another device: no remote copies, remote signals or barrier semaphores. Data moves between devices by JAX's collectives and lax.ppermute only.
A program may use at most 128 MiB of HBM per device.

v0:
```python
import jax
import jax.numpy as jnp
from jax import lax
from jax.experimental import pallas as pl
from jax.experimental.pallas import tpu as pltpu
from jax.sharding import Mesh
from jax.sharding import PartitionSpec as P

AXES = ("x_hi", "core", "z", "x_lo", "y")
SIZES = (2, 2, 8, 2, 4)
NZ, NX, NY = 8, 2, 4
ROWS = 128
N = 8192
OCC = 768
COLS = OCC // 2
WIDTH = 128
F32 = jnp.float32
BF16 = jnp.bfloat16


def ring_pairs(size, step):
    pairs = []
    for core in range(2):
        sign = 1 - 2 * core
        for i in range(size):
            pairs.append((core * size + i, core * size + (i + sign * step) % size))
    return pairs


def ring_send(x, axis, step):
    size = SIZES[AXES.index(axis)]
    return lax.ppermute(x, ("core", axis), ring_pairs(size, step))


def x_send(x):
    pairs = []
    for core in range(2):
        for i in range(4):
            j = (i + 1 - 2 * core) % 4
            src = ((i // 2) * 2 + core) * 2 + i % 2
            dst = ((j // 2) * 2 + core) * 2 + j % 2
            pairs.append((src, dst))
    return lax.ppermute(x, ("x_hi", "core", "x_lo"), pairs)


def swap(x, axes, flips):
    sizes = [SIZES[AXES.index(a)] for a in axes]
    total = 1
    for s in sizes:
        total *= s
    mask = 0
    for f in flips:
        mask = mask * 2 + f
    return lax.ppermute(x, axes, [(i, i ^ mask) for i in range(total)])


RING = {"z": (0, -1, 1, -2, 2, -3, 3, -4), "y": (0, -1, 1, -2), "x": (0, 1)}


def ring_gather(x, axis):
    if axis == "x":
        return [x, x_send(x)]
    size = SIZES[AXES.index(axis)]
    fwd, bwd, out = x, x, [x]
    for k in range(1, size // 2 + 1):
        fwd = ring_send(fwd, axis, 1)
        out.append(fwd)
        if 2 * k < size:
            bwd = ring_send(bwd, axis, -1)
            out.append(bwd)
    return out


def gathered_by_exchange(x, axes):
    size = 1
    for axis in axes:
        size *= SIZES[AXES.index(axis)]
    return lax.all_to_all(jnp.broadcast_to(x, (size, *x.shape)), axes, 0, 0, tiled=True)


def dot(lhs, rhs):
    return jnp.dot(lhs, rhs, preferred_element_type=F32)


def half_kernel(own_ref, sib_ref, *refs):
    by_z, by_y, by_x, out = refs[:8], refs[8:12], refs[12:14], refs[14]
    sign = 1 - 2 * lax.axis_index("core")
    z, x, y = lax.axis_index("z"), lax.axis_index("x_lo"), lax.axis_index("y")

    def strided(ref, x, y):
        start = (x * NY + y) * ROWS
        cols = [pl.multiple_of(k * NX * NY * ROWS + start, ROWS) for k in range(NZ)]
        return jnp.concatenate([ref[:, pl.ds(c, ROWS)] for c in cols], axis=1)

    depth = NZ * ROWS
    for p, ref in enumerate((own_ref, sib_ref)):
        total = jnp.zeros((ROWS, WIDTH), F32)
        for k, off in enumerate(RING["z"]):
            at = (z + sign * off) % NZ
            lhs = ref[:, pl.ds(pl.multiple_of(at * NX * NY * ROWS, ROWS), NX * NY * ROWS)]
            total += dot(lhs, by_z[k][...])
        out[:, (3 * p) * WIDTH : (3 * p + 1) * WIDTH] = total.astype(BF16)
        total = jnp.zeros((ROWS, WIDTH), F32)
        for k, off in enumerate(RING["y"]):
            for dx in range(NX):
                lhs = strided(ref, (x + dx) % NX, (y + sign * off) % NY)
                total += dot(lhs, by_y[k][dx * depth : (dx + 1) * depth])
        out[:, (3 * p + 1) * WIDTH : (3 * p + 2) * WIDTH] = total.astype(BF16)
        total = jnp.zeros((ROWS, WIDTH), F32)
        for dx in range(NX):
            for k, off in enumerate(RING["y"]):
                lhs = strided(ref, (x + dx) % NX, (y + sign * off) % NY)
                total += dot(lhs, by_x[dx][k * depth : (k + 1) * depth])
        out[:, (3 * p + 2) * WIDTH : (3 * p + 3) * WIDTH] = total.astype(BF16)


def half_blocks(own, sib, by_z, by_y, by_x):
    return pl.pallas_call(
        half_kernel,
        out_shape=jax.ShapeDtypeStruct((ROWS, OCC), BF16),
        compiler_params=pltpu.CompilerParams(vmem_limit_bytes=48 << 20),
    )(own, sib, *by_z, *by_y, *by_x)


def tile_kernel(*refs):
    z_blocks, xy_blocks = refs[:8], refs[8:16]
    send_ref, keep_ref, z_buf, xy_buf, sems = refs[16:]
    core = lax.axis_index("core")
    sign = 1 - 2 * core
    z = lax.axis_index("z")
    copies = []
    for k, off in enumerate(RING["z"]):
        slot = (z + sign * off) % NZ
        copies.append(pltpu.make_async_copy(z_blocks[k], z_buf.at[slot], sems.at[k]))
    for k in range(8):
        copies.append(pltpu.make_async_copy(xy_blocks[k], xy_buf.at[k], sems.at[8 + k]))
    for c in copies:
        c.start()
    for c in copies:
        c.wait()
    for out, low in ((send_ref, 1 - core), (keep_ref, core)):
        for high in range(2):
            rhs = z_buf[pl.ds(4 * high + 2 * low, 2)].reshape(2 * ROWS, OCC)
            for k in range(0, 8, 4):
                prod = lax.dot_general(
                    xy_buf[k : k + 4].reshape(4 * ROWS, OCC),
                    rhs,
                    (((1,), (1,)), ((), ())),
                    preferred_element_type=F32,
                )
                out[high, k : k + 4] = prod.astype(out.dtype).reshape(4, ROWS, 2 * ROWS)


def tile_product(z_blocks, xy_blocks):
    anyspace = pl.BlockSpec(memory_space=pl.ANY)
    shape = (2, 8, ROWS, 2 * ROWS)
    return pl.pallas_call(
        tile_kernel,
        in_specs=[anyspace] * 16,
        out_shape=[jax.ShapeDtypeStruct(shape, BF16), jax.ShapeDtypeStruct(shape, F32)],
        scratch_shapes=[
            pltpu.VMEM((8, ROWS, OCC), BF16),
            pltpu.VMEM((8, ROWS, OCC), BF16),
            pltpu.SemaphoreType.DMA((16,)),
        ],
        compiler_params=pltpu.CompilerParams(vmem_limit_bytes=48 << 20),
    )(*z_blocks, *xy_blocks)


Y_STEPS = (0, 1, 2, 3)


def final_kernel(own_ref, *refs):
    recv, out = refs[:-1], refs[-1]
    x_lo, y = lax.axis_index("x_lo"), lax.axis_index("y")
    for k, step in enumerate(Y_STEPS):
        src_y = (y - step) % NY
        for dx in range(2):
            src_x = (x_lo + dx) % NX
            for zl in range(2):
                start = pl.multiple_of(((zl * NX + src_x) * NY + src_y) * ROWS, ROWS)
                piece = slice(zl * ROWS, (zl + 1) * ROWS)
                val = own_ref[dx, :, piece] if k == 0 else recv[k - 1][dx, :, piece].astype(F32)
                out[:, pl.ds(start, ROWS)] = val


def assemble(own, received):
    return pl.pallas_call(
        final_kernel, out_shape=jax.ShapeDtypeStruct((ROWS, 16 * ROWS), F32)
    )(own, *received)


def body(integrals, orbitals):
    own = integrals[0]
    sib = swap(own, ("core",), (1,))
    core = lax.axis_index("core")
    mine = lax.dynamic_slice(orbitals, (0, core * COLS), (ROWS, COLS))
    lines = gathered_by_exchange(mine[:, WIDTH:], ("z",)).reshape(NZ * ROWS, 2 * WIDTH)
    plane = gathered_by_exchange(mine[:, :WIDTH], ("x_lo", "y")).reshape(NX * NY * ROWS, WIDTH)
    by_z = ring_gather(plane, "z")
    by_y = ring_gather(jnp.concatenate(ring_gather(lines[:, :WIDTH], "x"), axis=0), "y")
    by_x = ring_gather(jnp.concatenate(ring_gather(lines[:, WIDTH:], "y"), axis=0), "x")
    half = half_blocks(own, sib, by_z, by_y, by_x)

    z_blocks = ring_gather(half, "z")
    pair = jnp.stack([half, swap(half, ("x_lo",), (1,))])
    lines = [pair] + [lax.ppermute(pair, "y", [(i, (i - s) % NY) for i in range(NY)]) for s in (1, 2, 3)]
    xy_blocks = [lines[s][dx] for dx in range(2) for s in range(4)]

    send, keep = tile_product(z_blocks, xy_blocks)
    total = keep + swap(send, ("core",), (1,)).astype(F32)
    total = total.reshape(2, 2, 4, ROWS, 2 * ROWS)
    a_hi = lax.axis_index("x_hi")
    near = lax.dynamic_index_in_dim(total, a_hi, 0, keepdims=False)
    far = lax.dynamic_index_in_dim(total, 1 - a_hi, 0, keepdims=False).astype(BF16)
    x_axes = ("x_hi", "x_lo")
    from_far = swap(far[0], x_axes, (1, 0))
    from_diag = swap(far[1], x_axes, (1, 1))
    from_near = swap(near[1].astype(BF16), x_axes, (0, 1))
    sums = jnp.stack([near[0] + from_far.astype(F32), from_near.astype(F32) + from_diag.astype(F32)])
    outgoing = sums[:, 1:].astype(BF16)
    received = [
        lax.ppermute(outgoing[:, s - 1], "y", [(i, (i + s) % NY) for i in range(NY)]) for s in (1, 2, 3)
    ]
    return assemble(sums[:, 0], received)


def solution(mesh):
    split = Mesh(mesh.devices.reshape(SIZES), AXES)
    row = ("z", "x_lo", "y")
    aux = ("x_hi", "core")
    return jax.shard_map(
        body,
        mesh=split,
        in_specs=(P(aux, row, None), P(row, None)),
        out_specs=P(row, aux),
        check_vma=False,
    )
```

profile of v0, /device:TPU:1, one launch (start us, length us, event | category | flops | bytes accessed | tf_op | source)
XLA Modules:
  0.0 162.6 jit_solution(14262421375362279486)
XLA Ops:
  1.8 9.0 %all-to-all-start.1 = ((bf16[8,128,256]{2,1,0:T(8,128)(2,1)}), bf16[8,128,256]{2,1,0:T(8,128)(2,1)S(1)}, u32[]{:S(2)}, u32[]{:S(2)}) async-start(bf16[8,128,256]{2,1,0:T(8,128)(2,1)} %broadcast_in_dim.7), calls=%async_computation.1 | async-start | bytes 1048576 | tf_op jit(solution)/shard_map/all_to_all | solution.py:78
  11.7 17.0 %all-to-all-done.1 = bf16[8,128,256]{2,1,0:T(8,128)(2,1)S(1)} async-done(((bf16[8,128,256]{2,1,0:T(8,128)(2,1)}), bf16[8,128,256]{2,1,0:T(8,128)(2,1)S(1)}, u32[]{:S(2)}, u32[]{:S(2)}) %all-to-all-start.1) | async-done | bytes 524320 | tf_op jit(solution)/shard_map/all_to_all | solution.py:78
  29.5 5.1 %all-to-all-start = ((bf16[8,128,128]{2,1,0:T(8,128)(2,1)}), bf16[8,128,128]{2,1,0:T(8,128)(2,1)S(1)}, u32[]{:S(2)}, u32[]{:S(2)}) async-start(bf16[8,128,128]{2,1,0:T(8,128)(2,1)} %broadcast_in_dim.6), calls=%async_computation | async-start | bytes 524288 | tf_op jit(solution)/shard_map/all_to_all | solution.py:78
  35.3 2.7 %collective-permute-start.12 = (bf16[1024,128]{1,0:T(8,128)(2,1)}, bf16[1024,128]{1,0:T(8,128)(2,1)S(1)}, u32[]{:S(2)}, u32[]{:S(2)}) collective-permute-start(bf16[1024,128]{1,0:T(8,128)(2,1)} %get-tuple-element.14), channel_id=1, source_target_pairs={{0,1},{1,2},{2,3},{3,0},{64,67},{65,64},{66,65},{67,66},{4,5},{5,6... | collective-permute-start | bytes 786440 | tf_op jit(solution)/shard_map/ppermute | solution.py:32
  38.0 2.8 %all-to-all-done = bf16[8,128,128]{2,1,0:T(8,128)(2,1)S(1)} async-done(((bf16[8,128,128]{2,1,0:T(8,128)(2,1)}), bf16[8,128,128]{2,1,0:T(8,128)(2,1)S(1)}, u32[]{:S(2)}, u32[]{:S(2)}) %all-to-all-start) | async-done | bytes 262176 | tf_op jit(solution)/shard_map/all_to_all | solution.py:78
  40.8 1.5 collective-permute-start.8
  42.3 1.6 collective-permute-start.13
  43.9 1.5 collective-permute-start.14
  46.4 2.2 %collective-permute-start.3 = (bf16[1024,128]{1,0:T(8,128)(2,1)S(1)}, bf16[1024,128]{1,0:T(8,128)(2,1)S(1)}, u32[]{:S(2)}, u32[]{:S(2)}) collective-permute-start(bf16[1024,128]{1,0:T(8,128)(2,1)S(1)} %collective-permute-done.1.refs_1_), channel_id=1, source_target_pairs={{0,8},{8,16},{16,24},{24,32},{32,40},{40,48},{48,56},{56,0},{64,12... | collective-permute-start | bytes 786440 | tf_op jit(solution)/shard_map/ppermute | solution.py:32
  49.2 2.0 %collective-permute-start.9 = (bf16[2048,128]{1,0:T(8,128)(2,1)S(1)}, bf16[2048,128]{1,0:T(8,128)(2,1)S(1)}, u32[]{:S(2)}, u32[]{:S(2)}) collective-permute-start(bf16[2048,128]{1,0:T(8,128)(2,1)S(1)} %pad_maximum_fusion.2.refs_8_), channel_id=1, source_target_pairs={{0,1},{1,2},{2,3},{3,0},{64,67},{65,64},{66,65},{67,66},{4,5},{5,6... | collective-permute-start | bytes 1572872 | tf_op jit(solution)/shard_map/ppermute | solution.py:32
  51.6 1.0 pad_maximum_fusion.1.refs_12_
  52.7 1.7 %collective-permute-start.15 = (bf16[4096,128]{1,0:T(8,128)(2,1)S(1)}, bf16[4096,128]{1,0:T(8,128)(2,1)S(1)}, u32[]{:S(2)}, u32[]{:S(2)}) collective-permute-start(bf16[4096,128]{1,0:T(8,128)(2,1)S(1)} %pad_maximum_fusion.1.refs_12_), channel_id=1, source_target_pairs={{0,4},{4,128},{128,132},{132,0},{64,196},{68,64},{192,68},{196,192... | collective-permute-start | bytes 3145736 | tf_op jit(solution)/shard_map/ppermute | solution.py:43
  54.4 1.0 collective-permute-start.4
  55.4 1.7 %collective-permute-start.5 = (bf16[1024,128]{1,0:T(8,128)(2,1)S(1)}, bf16[1024,128]{1,0:T(8,128)(2,1)S(1)}, u32[]{:S(2)}, u32[]{:S(2)}) collective-permute-start(bf16[1024,128]{1,0:T(8,128)(2,1)S(1)} %collective-permute-done.3.refs_3_), channel_id=1, source_target_pairs={{0,8},{8,16},{16,24},{24,32},{32,40},{40,48},{48,56},{56,0},{64,12... | collective-permute-start | bytes 786440 | tf_op jit(solution)/shard_map/ppermute | solution.py:32
  57.1 4.0 %collective-permute-done.4.refs_4_ = bf16[1024,128]{1,0:T(8,128)(2,1)S(1)} collective-permute-done((bf16[1024,128]{1,0:T(8,128)(2,1)S(1)}, bf16[1024,128]{1,0:T(8,128)(2,1)S(1)}, u32[]{:S(2)}, u32[]{:S(2)}) %collective-permute-start.4) | collective-permute-done | bytes 262176 | tf_op jit(solution)/shard_map/ppermute | solution.py:32
  61.8 2.1 %collective-permute-start.10 = (bf16[2048,128]{1,0:T(8,128)(2,1)S(1)}, bf16[2048,128]{1,0:T(8,128)(2,1)S(1)}, u32[]{:S(2)}, u32[]{:S(2)}) collective-permute-start(bf16[2048,128]{1,0:T(8,128)(2,1)S(1)} %pad_maximum_fusion.2.refs_8_), channel_id=1, source_target_pairs={{0,3},{1,0},{2,1},{3,2},{64,65},{65,66},{66,67},{67,64},{4,7},{5,4... | collective-permute-start | bytes 1572872 | tf_op jit(solution)/shard_map/ppermute | solution.py:32
  63.9 1.4 collective-permute-start.11
  65.3 4.1 %collective-permute-done.6.refs_6_ = bf16[1024,128]{1,0:T(8,128)(2,1)S(1)} collective-permute-done((bf16[1024,128]{1,0:T(8,128)(2,1)S(1)}, bf16[1024,128]{1,0:T(8,128)(2,1)S(1)}, u32[]{:S(2)}, u32[]{:S(2)}) %collective-permute-start.6) | collective-permute-done | bytes 262176 | tf_op jit(solution)/shard_map/ppermute | solution.py:32
  69.7 5.2 %collective-permute-done.7.refs_7_ = bf16[1024,128]{1,0:T(8,128)(2,1)S(1)} collective-permute-done((bf16[1024,128]{1,0:T(8,128)(2,1)S(1)}, bf16[1024,128]{1,0:T(8,128)(2,1)S(1)}, u32[]{:S(2)}, u32[]{:S(2)}) %collective-permute-start.7) | collective-permute-done | bytes 262176 | tf_op jit(solution)/shard_map/ppermute | solution.py:32
  75.0 1.3 copy-done.2
  76.3 1.0 copy-done.3
  77.3 6.4 %shard_map.28.refs_0_.refs_8_ = bf16[128,768]{1,0:T(8,128)(2,1)S(1)} custom-call(bf16[128,8192]{1,0:T(8,128)(2,1)} %bitcast.54, bf16[128,8192]{1,0:T(8,128)(2,1)} %copy-done.2, bf16[1024,128]{1,0:T(8,128)(2,1)S(1)} %bitcast.47, bf16[1024,128]{1,0:T(8,128)(2,1)S(1)} %collective-permute-done.1.refs_1_, bf16[1024,128]{1,0:T(8,128)(2,1)S(1)} %collective-permute-done.2.refs_2_, ...), custom_call_target="tpu_custom_call" | custom-call | tf_op jit(solution)/shard_map/pallas_call | solution.py:118
  83.6 1.1 collective-permute-start.23
  84.7 1.8 %collective-permute-start.16 = (bf16[128,768]{1,0:T(8,128)(2,1)S(1)}, bf16[128,768]{1,0:T(8,128)(2,1)S(1)}, u32[]{:S(2)}, u32[]{:S(2)}) collective-permute-start(bf16[128,768]{1,0:T(8,128)(2,1)S(1)} %shard_map.28.refs_0_.refs_8_), channel_id=1, source_target_pairs={{0,8},{8,16},{16,24},{24,32},{32,40},{40,48},{48,56},{56,0},{64,12... | collective-permute-start | bytes 589832 | tf_op jit(solution)/shard_map/ppermute | solution.py:32
  86.5 1.7 %collective-permute-done.23.refs_12_ = bf16[128,768]{1,0:T(8,128)(2,1)S(1)} collective-permute-done((bf16[128,768]{1,0:T(8,128)(2,1)S(1)}, bf16[128,768]{1,0:T(8,128)(2,1)S(1)}, u32[]{:S(2)}, u32[]{:S(2)}) %collective-permute-start.23) | collective-permute-done | bytes 196640 | tf_op jit(solution)/shard_map/ppermute | solution.py:54
  89.3 3.0 %collective-permute-start.18 = (bf16[128,768]{1,0:T(8,128)(2,1)S(1)}, bf16[128,768]{1,0:T(8,128)(2,1)S(1)}, u32[]{:S(2)}, u32[]{:S(2)}) collective-permute-start(bf16[128,768]{1,0:T(8,128)(2,1)S(1)} %collective-permute-done.16.refs_1_), channel_id=1, source_target_pairs={{0,8},{8,16},{16,24},{24,32},{32,40},{40,48},{48,56},{56,0},{64,12... | collective-permute-start | bytes 589832 | tf_op jit(solution)/shard_map/ppermute | solution.py:32
  92.3 2.8 %collective-permute-start.25 = (bf16[2,128,768]{2,1,0:T(8,128)(2,1)S(1)}, bf16[2,128,768]{2,1,0:T(8,128)(2,1)S(1)}, u32[]{:S(2)}, u32[]{:S(2)}) collective-permute-start(bf16[2,128,768]{2,1,0:T(8,128)(2,1)S(1)} %pad_maximum_fusion.3), channel_id=1, source_target_pairs={{0,2},{1,3},{2,0},{3,1},{4,6},{5,7},{6,4},{7,5},{8,10},{9,11},{10,... | collective-permute-start | bytes 1179656 | tf_op jit(solution)/shard_map/ppermute | solution.py:207
  96.3 3.4 %collective-permute-start.20 = (bf16[128,768]{1,0:T(8,128)(2,1)S(1)}, bf16[128,768]{1,0:T(8,128)(2,1)S(1)}, u32[]{:S(2)}, u32[]{:S(2)}) collective-permute-start(bf16[128,768]{1,0:T(8,128)(2,1)S(1)} %collective-permute-done.18.refs_3_), channel_id=1, source_target_pairs={{0,8},{8,16},{16,24},{24,32},{32,40},{40,48},{48,56},{56,0},{64,12... | collective-permute-start | bytes 589832 | tf_op jit(solution)/shard_map/ppermute | solution.py:32
  99.8 1.3 collective-permute-done.25
  101.2 1.7 %collective-permute-done.20.refs_5_ = bf16[128,768]{1,0:T(8,128)(2,1)S(1)} collective-permute-done((bf16[128,768]{1,0:T(8,128)(2,1)S(1)}, bf16[128,768]{1,0:T(8,128)(2,1)S(1)}, u32[]{:S(2)}, u32[]{:S(2)}) %collective-permute-start.20) | collective-permute-done | bytes 196640 | tf_op jit(solution)/shard_map/ppermute | solution.py:32
  102.9 3.4 %collective-permute-start.22 = (bf16[128,768]{1,0:T(8,128)(2,1)S(1)}, bf16[128,768]{1,0:T(8,128)(2,1)S(1)}, u32[]{:S(2)}, u32[]{:S(2)}) collective-permute-start(bf16[128,768]{1,0:T(8,128)(2,1)S(1)} %collective-permute-done.20.refs_5_), channel_id=1, source_target_pairs={{0,8},{8,16},{16,24},{24,32},{32,40},{40,48},{48,56},{56,0},{64,12... | collective-permute-start | bytes 589832 | tf_op jit(solution)/shard_map/ppermute | solution.py:32
  106.4 2.6 %collective-permute-done.22.refs_7_ = bf16[128,768]{1,0:T(8,128)(2,1)S(1)} collective-permute-done((bf16[128,768]{1,0:T(8,128)(2,1)S(1)}, bf16[128,768]{1,0:T(8,128)(2,1)S(1)}, u32[]{:S(2)}, u32[]{:S(2)}) %collective-permute-start.22) | collective-permute-done | bytes 196640 | tf_op jit(solution)/shard_map/ppermute | solution.py:32
  108.9 6.5 %shard_map.29 = (bf16[2,8,128,256]{3,2,1,0:T(8,128)(2,1)S(1)}, f32[2,8,128,256]{3,2,1,0:T(8,128)S(1)}) custom-call(bf16[128,768]{1,0:T(8,128)(2,1)S(1)} %shard_map.28.refs_0_.refs_8_, bf16[128,768]{1,0:T(8,128)(2,1)S(1)} %collective-permute-done.16.refs_1_, bf16[128,768]{1,0:T(8,128)(2,1)S(1)} %collective-permute-done.17.refs_2_, ...), custom_call_target="tpu_custom_call" | custom-call | tf_op jit(solution)/shard_map/pallas_call | solution.py:157
  115.4 11.8 %collective-permute-start.27 = (bf16[2,8,128,256]{3,2,1,0:T(8,128)(2,1)S(1)}, bf16[2,8,128,256]{3,2,1,0:T(8,128)(2,1)}, u32[]{:S(2)}, u32[]{:S(2)}) collective-permute-start(bf16[2,8,128,256]{3,2,1,0:T(8,128)(2,1)S(1)} %get-tuple-element.8), channel_id=1, source_target_pairs={{0,64},{64,0},{1,65},{65,1},{2,66},{66,2},{3,67},{67,3},{4,68},{68... | collective-permute-start | bytes 3145736 | tf_op jit(solution)/shard_map/ppermute | solution.py:54
  127.2 2.4 %collective-permute-done.27 = bf16[2,8,128,256]{3,2,1,0:T(8,128)(2,1)} collective-permute-done((bf16[2,8,128,256]{3,2,1,0:T(8,128)(2,1)S(1)}, bf16[2,8,128,256]{3,2,1,0:T(8,128)(2,1)}, u32[]{:S(2)}, u32[]{:S(2)}) %collective-permute-start.27) | collective-permute-done | bytes 1048608 | tf_op jit(solution)/shard_map/ppermute | solution.py:54
  129.6 1.5 convert_add_fusion
  131.1 1.3 copy-done.1
  132.6 1.2 collective-permute-start.28
  133.7 2.8 %collective-permute-start.30 = (bf16[4,128,256]{2,1,0:T(8,128)(2,1)S(1)}, bf16[4,128,256]{2,1,0:T(8,128)(2,1)S(1)}, u32[]{:S(2)}, u32[]{:S(2)}) collective-permute-start(bf16[4,128,256]{2,1,0:T(8,128)(2,1)S(1)} %get-tuple-element.12), channel_id=1, source_target_pairs={{0,132},{4,128},{128,4},{132,0},{1,133},{5,129},{129,5},{133,1},{2... | collective-permute-start | bytes 786440 | tf_op jit(solution)/shard_map/ppermute | solution.py:54
  136.5 1.1 fusion.3
  137.7 4.0 %collective-permute-done.28 = bf16[4,128,256]{2,1,0:T(8,128)(2,1)S(1)} collective-permute-done((bf16[4,128,256]{2,1,0:T(8,128)(2,1)S(1)}, bf16[4,128,256]{2,1,0:T(8,128)(2,1)S(1)}, u32[]{:S(2)}, u32[]{:S(2)}) %collective-permute-start.28) | collective-permute-done | bytes 262176 | tf_op jit(solution)/shard_map/ppermute | solution.py:54
  141.7 1.1 fusion.2
  142.8 5.2 %collective-permute-done.30 = bf16[4,128,256]{2,1,0:T(8,128)(2,1)S(1)} collective-permute-done((bf16[4,128,256]{2,1,0:T(8,128)(2,1)S(1)}, bf16[4,128,256]{2,1,0:T(8,128)(2,1)S(1)}, u32[]{:S(2)}, u32[]{:S(2)}) %collective-permute-start.30) | collective-permute-done | bytes 262176 | tf_op jit(solution)/shard_map/ppermute | solution.py:54
  148.2 1.8 %collective-permute-start.31 = (bf16[2,128,256]{2,1,0:T(8,128)(2,1)S(1)}, bf16[2,128,256]{2,1,0:T(8,128)(2,1)S(1)}, u32[]{:S(2)}, u32[]{:S(2)}) collective-permute-start(bf16[2,128,256]{2,1,0:T(8,128)(2,1)S(1)} %get-tuple-element.11), channel_id=1, source_target_pairs={{0,1},{1,2},{2,3},{3,0},{4,5},{5,6},{6,7},{7,4},{8,9},{9,10},{10,1... | collective-permute-start | bytes 393224 | tf_op jit(solution)/shard_map/ppermute | solution.py:223
  150.0 3.0 %collective-permute-start.32 = (bf16[2,128,256]{2,1,0:T(8,128)(2,1)S(1)}, bf16[2,128,256]{2,1,0:T(8,128)(2,1)S(1)}, u32[]{:S(2)}, u32[]{:S(2)}) collective-permute-start(bf16[2,128,256]{2,1,0:T(8,128)(2,1)S(1)} %get-tuple-element.10), channel_id=1, source_target_pairs={{0,2},{1,3},{2,0},{3,1},{4,6},{5,7},{6,4},{7,5},{8,10},{9,11},{10,... | collective-permute-start | bytes 393224 | tf_op jit(solution)/shard_map/ppermute | solution.py:223
  152.9 2.0 %collective-permute-start.33 = (bf16[2,128,256]{2,1,0:T(8,128)(2,1)S(1)}, bf16[2,128,256]{2,1,0:T(8,128)(2,1)S(1)}, u32[]{:S(2)}, u32[]{:S(2)}) collective-permute-start(bf16[2,128,256]{2,1,0:T(8,128)(2,1)S(1)} %get-tuple-element.9), channel_id=1, source_target_pairs={{0,3},{1,0},{2,1},{3,2},{4,7},{5,4},{6,5},{7,6},{8,11},{9,8},{10,9... | collective-permute-start | bytes 393224 | tf_op jit(solution)/shard_map/ppermute | solution.py:223
  155.6 3.4 %collective-permute-done.32.refs_1_ = bf16[2,128,256]{2,1,0:T(8,128)(2,1)S(1)} collective-permute-done((bf16[2,128,256]{2,1,0:T(8,128)(2,1)S(1)}, bf16[2,128,256]{2,1,0:T(8,128)(2,1)S(1)}, u32[]{:S(2)}, u32[]{:S(2)}) %collective-permute-start.32) | collective-permute-done | bytes 131104 | tf_op jit(solution)/shard_map/ppermute | solution.py:223
  160.3 2.2 %shard_map.30 = f32[128,2048]{1,0:T(8,128)} custom-call(f32[2,128,256]{2,1,0:T(8,128)} %fusion.5.own_ref, bf16[2,128,256]{2,1,0:T(8,128)(2,1)} %copy-done.4, bf16[2,128,256]{2,1,0:T(8,128)(2,1)} %copy-done.5, bf16[2,128,256]{2,1,0:T(8,128)(2,1)} %copy-done.6), custom_call_target="tpu_custom_call" | custom-call | tf_op jit(solution)/shard_map/pallas_call | solution.py:188
  (61 shorter events, 12.0 us)
Async XLA Ops:
  0.0 0.9 copy-start
  1.8 27.0 %all-to-all-start.1 = ((bf16[8,128,256]{2,1,0:T(8,128)(2,1)}), bf16[8,128,256]{2,1,0:T(8,128)(2,1)S(1)}, u32[]{:S(2)}, u32[]{:S(2)}) async-start(bf16[8,128,256]{2,1,0:T(8,128)(2,1)} %broadcast_in_dim.7), calls=%async_computation.1 | async-start | bytes 1048576 | tf_op jit(solution)/shard_map/all_to_all | solution.py:78
  10.8 64.2 %collective-permute-start = (bf16[128,8192]{1,0:T(8,128)(2,1)}, bf16[128,8192]{1,0:T(8,128)(2,1)S(1)}, u32[]{:S(2)}, u32[]{:S(2)}) collective-permute-start(bf16[128,8192]{1,0:T(8,128)(2,1)} %bitcast.53), channel_id=1, source_target_pairs={{0,64},{64,0},{1,65},{65,1},{2,66},{66,2},{3,67},{67,3},{4,68},{68... | collective-permute-start | bytes 6291464 | tf_op jit(solution)/shard_map/ppermute | solution.py:54
  29.5 11.3 %all-to-all-start = ((bf16[8,128,128]{2,1,0:T(8,128)(2,1)}), bf16[8,128,128]{2,1,0:T(8,128)(2,1)S(1)}, u32[]{:S(2)}, u32[]{:S(2)}) async-start(bf16[8,128,128]{2,1,0:T(8,128)(2,1)} %broadcast_in_dim.6), calls=%async_computation | async-start | bytes 524288 | tf_op jit(solution)/shard_map/all_to_all | solution.py:78
  35.3 8.5 %collective-permute-start.12 = (bf16[1024,128]{1,0:T(8,128)(2,1)}, bf16[1024,128]{1,0:T(8,128)(2,1)S(1)}, u32[]{:S(2)}, u32[]{:S(2)}) collective-permute-start(bf16[1024,128]{1,0:T(8,128)(2,1)} %get-tuple-element.14), channel_id=1, source_target_pairs={{0,1},{1,2},{2,3},{3,0},{64,67},{65,64},{66,65},{67,66},{4,5},{5,6... | collective-permute-start | bytes 786440 | tf_op jit(solution)/shard_map/ppermute | solution.py:32
  40.8 5.2 %collective-permute-start.1 = (bf16[1024,128]{1,0:T(8,128)(2,1)S(1)}, bf16[1024,128]{1,0:T(8,128)(2,1)S(1)}, u32[]{:S(2)}, u32[]{:S(2)}) collective-permute-start(bf16[1024,128]{1,0:T(8,128)(2,1)S(1)} %bitcast.45), channel_id=1, source_target_pairs={{0,8},{8,16},{16,24},{24,32},{32,40},{40,48},{48,56},{56,0},{64,12... | collective-permute-start | bytes 786440 | tf_op jit(solution)/shard_map/ppermute | solution.py:32
  40.8 5.7 %collective-permute-start.8 = (bf16[1024,128]{1,0:T(8,128)(2,1)S(1)}, bf16[1024,128]{1,0:T(8,128)(2,1)S(1)}, u32[]{:S(2)}, u32[]{:S(2)}) collective-permute-start(bf16[1024,128]{1,0:T(8,128)(2,1)S(1)} %get-tuple-element.15), channel_id=1, source_target_pairs={{0,4},{4,128},{128,132},{132,0},{64,196},{68,64},{192,68},{196,192... | collective-permute-start | bytes 786440 | tf_op jit(solution)/shard_map/ppermute | solution.py:43
  42.3 6.9 %collective-permute-start.13 = (bf16[1024,128]{1,0:T(8,128)(2,1)}, bf16[1024,128]{1,0:T(8,128)(2,1)S(1)}, u32[]{:S(2)}, u32[]{:S(2)}) collective-permute-start(bf16[1024,128]{1,0:T(8,128)(2,1)} %get-tuple-element.14), channel_id=1, source_target_pairs={{0,3},{1,0},{2,1},{3,2},{64,65},{65,66},{66,67},{67,64},{4,7},{5,4... | collective-permute-start | bytes 786440 | tf_op jit(solution)/shard_map/ppermute | solution.py:32
  43.9 7.8 %collective-permute-start.14 = (bf16[1024,128]{1,0:T(8,128)(2,1)S(1)}, bf16[1024,128]{1,0:T(8,128)(2,1)S(1)}, u32[]{:S(2)}, u32[]{:S(2)}) collective-permute-start(bf16[1024,128]{1,0:T(8,128)(2,1)S(1)} %collective-permute-done.12), channel_id=1, source_target_pairs={{0,1},{1,2},{2,3},{3,0},{64,67},{65,64},{66,65},{67,66},{4,5},{5,6... | collective-permute-start | bytes 786440 | tf_op jit(solution)/shard_map/ppermute | solution.py:32
  46.0 8.4 %collective-permute-start.2 = (bf16[1024,128]{1,0:T(8,128)(2,1)S(1)}, bf16[1024,128]{1,0:T(8,128)(2,1)S(1)}, u32[]{:S(2)}, u32[]{:S(2)}) collective-permute-start(bf16[1024,128]{1,0:T(8,128)(2,1)S(1)} %bitcast.46), channel_id=1, source_target_pairs={{0,56},{8,0},{16,8},{24,16},{32,24},{40,32},{48,40},{56,48},{64,72... | collective-permute-start | bytes 786440 | tf_op jit(solution)/shard_map/ppermute | solution.py:32
  46.4 8.9 %collective-permute-start.3 = (bf16[1024,128]{1,0:T(8,128)(2,1)S(1)}, bf16[1024,128]{1,0:T(8,128)(2,1)S(1)}, u32[]{:S(2)}, u32[]{:S(2)}) collective-permute-start(bf16[1024,128]{1,0:T(8,128)(2,1)S(1)} %collective-permute-done.1.refs_1_), channel_id=1, source_target_pairs={{0,8},{8,16},{16,24},{24,32},{32,40},{40,48},{48,56},{56,0},{64,12... | collective-permute-start | bytes 786440 | tf_op jit(solution)/shard_map/ppermute | solution.py:32
  49.2 14.6 %collective-permute-start.9 = (bf16[2048,128]{1,0:T(8,128)(2,1)S(1)}, bf16[2048,128]{1,0:T(8,128)(2,1)S(1)}, u32[]{:S(2)}, u32[]{:S(2)}) collective-permute-start(bf16[2048,128]{1,0:T(8,128)(2,1)S(1)} %pad_maximum_fusion.2.refs_8_), channel_id=1, source_target_pairs={{0,1},{1,2},{2,3},{3,0},{64,67},{65,64},{66,65},{67,66},{4,5},{5,6... | collective-permute-start | bytes 1572872 | tf_op jit(solution)/shard_map/ppermute | solution.py:32
  52.7 22.3 %collective-permute-start.15 = (bf16[4096,128]{1,0:T(8,128)(2,1)S(1)}, bf16[4096,128]{1,0:T(8,128)(2,1)S(1)}, u32[]{:S(2)}, u32[]{:S(2)}) collective-permute-start(bf16[4096,128]{1,0:T(8,128)(2,1)S(1)} %pad_maximum_fusion.1.refs_12_), channel_id=1, source_target_pairs={{0,4},{4,128},{128,132},{132,0},{64,196},{68,64},{192,68},{196,192... | collective-permute-start | bytes 3145736 | tf_op jit(solution)/shard_map/ppermute | solution.py:43
  54.4 6.7 %collective-permute-start.4 = (bf16[1024,128]{1,0:T(8,128)(2,1)S(1)}, bf16[1024,128]{1,0:T(8,128)(2,1)S(1)}, u32[]{:S(2)}, u32[]{:S(2)}) collective-permute-start(bf16[1024,128]{1,0:T(8,128)(2,1)S(1)} %collective-permute-done.2.refs_2_), channel_id=1, source_target_pairs={{0,56},{8,0},{16,8},{24,16},{32,24},{40,32},{48,40},{56,48},{64,72... | collective-permute-start | bytes 786440 | tf_op jit(solution)/shard_map/ppermute | solution.py:32
  55.4 6.4 %collective-permute-start.5 = (bf16[1024,128]{1,0:T(8,128)(2,1)S(1)}, bf16[1024,128]{1,0:T(8,128)(2,1)S(1)}, u32[]{:S(2)}, u32[]{:S(2)}) collective-permute-start(bf16[1024,128]{1,0:T(8,128)(2,1)S(1)} %collective-permute-done.3.refs_3_), channel_id=1, source_target_pairs={{0,8},{8,16},{16,24},{24,32},{32,40},{40,48},{48,56},{56,0},{64,12... | collective-permute-start | bytes 786440 | tf_op jit(solution)/shard_map/ppermute | solution.py:32
  61.1 8.3 %collective-permute-start.6 = (bf16[1024,128]{1,0:T(8,128)(2,1)S(1)}, bf16[1024,128]{1,0:T(8,128)(2,1)S(1)}, u32[]{:S(2)}, u32[]{:S(2)}) collective-permute-start(bf16[1024,128]{1,0:T(8,128)(2,1)S(1)} %collective-permute-done.4.refs_4_), channel_id=1, source_target_pairs={{0,56},{8,0},{16,8},{24,16},{32,24},{40,32},{48,40},{56,48},{64,72... | collective-permute-start | bytes 786440 | tf_op jit(solution)/shard_map/ppermute | solution.py:32
  61.8 13.2 %collective-permute-start.10 = (bf16[2048,128]{1,0:T(8,128)(2,1)S(1)}, bf16[2048,128]{1,0:T(8,128)(2,1)S(1)}, u32[]{:S(2)}, u32[]{:S(2)}) collective-permute-start(bf16[2048,128]{1,0:T(8,128)(2,1)S(1)} %pad_maximum_fusion.2.refs_8_), channel_id=1, source_target_pairs={{0,3},{1,0},{2,1},{3,2},{64,65},{65,66},{66,67},{67,64},{4,7},{5,4... | collective-permute-start | bytes 1572872 | tf_op jit(solution)/shard_map/ppermute | solution.py:32
  63.9 11.1 %collective-permute-start.11 = (bf16[2048,128]{1,0:T(8,128)(2,1)S(1)}, bf16[2048,128]{1,0:T(8,128)(2,1)S(1)}, u32[]{:S(2)}, u32[]{:S(2)}) collective-permute-start(bf16[2048,128]{1,0:T(8,128)(2,1)S(1)} %collective-permute-done.9.refs_9_), channel_id=1, source_target_pairs={{0,1},{1,2},{2,3},{3,0},{64,67},{65,64},{66,65},{67,66},{4,5},{5,6... | collective-permute-start | bytes 1572872 | tf_op jit(solution)/shard_map/ppermute | solution.py:32
  69.4 5.5 %collective-permute-start.7 = (bf16[1024,128]{1,0:T(8,128)(2,1)S(1)}, bf16[1024,128]{1,0:T(8,128)(2,1)S(1)}, u32[]{:S(2)}, u32[]{:S(2)}) collective-permute-start(bf16[1024,128]{1,0:T(8,128)(2,1)S(1)} %collective-permute-done.5.refs_5_), channel_id=1, source_target_pairs={{0,8},{8,16},{16,24},{24,32},{32,40},{40,48},{48,56},{56,0},{64,12... | collective-permute-start | bytes 786440 | tf_op jit(solution)/shard_map/ppermute | solution.py:32
  74.9 1.3 copy-start.2
  76.3 1.0 copy-start.3
  83.6 4.6 %collective-permute-start.23 = (bf16[128,768]{1,0:T(8,128)(2,1)S(1)}, bf16[128,768]{1,0:T(8,128)(2,1)S(1)}, u32[]{:S(2)}, u32[]{:S(2)}) collective-permute-start(bf16[128,768]{1,0:T(8,128)(2,1)S(1)} %shard_map.28.refs_0_.refs_8_), channel_id=1, source_target_pairs={{0,4},{4,0},{1,5},{5,1},{2,6},{6,2},{3,7},{7,3},{8,12},{12,8},{9,1... | collective-permute-start | bytes 589832 | tf_op jit(solution)/shard_map/ppermute | solution.py:54
  84.7 4.5 %collective-permute-start.16 = (bf16[128,768]{1,0:T(8,128)(2,1)S(1)}, bf16[128,768]{1,0:T(8,128)(2,1)S(1)}, u32[]{:S(2)}, u32[]{:S(2)}) collective-permute-start(bf16[128,768]{1,0:T(8,128)(2,1)S(1)} %shard_map.28.refs_0_.refs_8_), channel_id=1, source_target_pairs={{0,8},{8,16},{16,24},{24,32},{32,40},{40,48},{48,56},{56,0},{64,12... | collective-permute-start | bytes 589832 | tf_op jit(solution)/shard_map/ppermute | solution.py:32
  86.5 5.7 %collective-permute-start.17 = (bf16[128,768]{1,0:T(8,128)(2,1)S(1)}, bf16[128,768]{1,0:T(8,128)(2,1)S(1)}, u32[]{:S(2)}, u32[]{:S(2)}) collective-permute-start(bf16[128,768]{1,0:T(8,128)(2,1)S(1)} %shard_map.28.refs_0_.refs_8_), channel_id=1, source_target_pairs={{0,56},{8,0},{16,8},{24,16},{32,24},{40,32},{48,40},{56,48},{64,72... | collective-permute-start | bytes 589832 | tf_op jit(solution)/shard_map/ppermute | solution.py:32
  88.3 11.5 %collective-permute-start.26 = (bf16[2,128,768]{2,1,0:T(8,128)(2,1)S(1)}, bf16[2,128,768]{2,1,0:T(8,128)(2,1)S(1)}, u32[]{:S(2)}, u32[]{:S(2)}) collective-permute-start(bf16[2,128,768]{2,1,0:T(8,128)(2,1)S(1)} %pad_maximum_fusion.3), channel_id=1, source_target_pairs={{0,1},{1,2},{2,3},{3,0},{4,5},{5,6},{6,7},{7,4},{8,9},{9,10},{10,1... | collective-permute-start | bytes 1179656 | tf_op jit(solution)/shard_map/ppermute | solution.py:207
  89.3 7.1 %collective-permute-start.18 = (bf16[128,768]{1,0:T(8,128)(2,1)S(1)}, bf16[128,768]{1,0:T(8,128)(2,1)S(1)}, u32[]{:S(2)}, u32[]{:S(2)}) collective-permute-start(bf16[128,768]{1,0:T(8,128)(2,1)S(1)} %collective-permute-done.16.refs_1_), channel_id=1, source_target_pairs={{0,8},{8,16},{16,24},{24,32},{32,40},{40,48},{48,56},{56,0},{64,12... | collective-permute-start | bytes 589832 | tf_op jit(solution)/shard_map/ppermute | solution.py:32
  92.3 7.5 %collective-permute-start.19 = (bf16[128,768]{1,0:T(8,128)(2,1)S(1)}, bf16[128,768]{1,0:T(8,128)(2,1)S(1)}, u32[]{:S(2)}, u32[]{:S(2)}) collective-permute-start(bf16[128,768]{1,0:T(8,128)(2,1)S(1)} %collective-permute-done.17.refs_2_), channel_id=1, source_target_pairs={{0,56},{8,0},{16,8},{24,16},{32,24},{40,32},{48,40},{56,48},{64,72... | collective-permute-start | bytes 589832 | tf_op jit(solution)/shard_map/ppermute | solution.py:32
  92.3 8.9 %collective-permute-start.25 = (bf16[2,128,768]{2,1,0:T(8,128)(2,1)S(1)}, bf16[2,128,768]{2,1,0:T(8,128)(2,1)S(1)}, u32[]{:S(2)}, u32[]{:S(2)}) collective-permute-start(bf16[2,128,768]{2,1,0:T(8,128)(2,1)S(1)} %pad_maximum_fusion.3), channel_id=1, source_target_pairs={{0,2},{1,3},{2,0},{3,1},{4,6},{5,7},{6,4},{7,5},{8,10},{9,11},{10,... | collective-permute-start | bytes 1179656 | tf_op jit(solution)/shard_map/ppermute | solution.py:207
  95.0 11.3 %collective-permute-start.24 = (bf16[2,128,768]{2,1,0:T(8,128)(2,1)S(1)}, bf16[2,128,768]{2,1,0:T(8,128)(2,1)S(1)}, u32[]{:S(2)}, u32[]{:S(2)}) collective-permute-start(bf16[2,128,768]{2,1,0:T(8,128)(2,1)S(1)} %pad_maximum_fusion.3), channel_id=1, source_target_pairs={{0,3},{1,0},{2,1},{3,2},{4,7},{5,4},{6,5},{7,6},{8,11},{9,8},{10,9... | collective-permute-start | bytes 1179656 | tf_op jit(solution)/shard_map/ppermute | solution.py:207
  96.3 6.6 %collective-permute-start.20 = (bf16[128,768]{1,0:T(8,128)(2,1)S(1)}, bf16[128,768]{1,0:T(8,128)(2,1)S(1)}, u32[]{:S(2)}, u32[]{:S(2)}) collective-permute-start(bf16[128,768]{1,0:T(8,128)(2,1)S(1)} %collective-permute-done.18.refs_3_), channel_id=1, source_target_pairs={{0,8},{8,16},{16,24},{24,32},{32,40},{40,48},{48,56},{56,0},{64,12... | collective-permute-start | bytes 589832 | tf_op jit(solution)/shard_map/ppermute | solution.py:32
  99.8 6.6 %collective-permute-start.21 = (bf16[128,768]{1,0:T(8,128)(2,1)S(1)}, bf16[128,768]{1,0:T(8,128)(2,1)S(1)}, u32[]{:S(2)}, u32[]{:S(2)}) collective-permute-start(bf16[128,768]{1,0:T(8,128)(2,1)S(1)} %collective-permute-done.19.refs_4_), channel_id=1, source_target_pairs={{0,56},{8,0},{16,8},{24,16},{32,24},{40,32},{48,40},{56,48},{64,72... | collective-permute-start | bytes 589832 | tf_op jit(solution)/shard_map/ppermute | solution.py:32
  102.9 6.0 %collective-permute-start.22 = (bf16[128,768]{1,0:T(8,128)(2,1)S(1)}, bf16[128,768]{1,0:T(8,128)(2,1)S(1)}, u32[]{:S(2)}, u32[]{:S(2)}) collective-permute-start(bf16[128,768]{1,0:T(8,128)(2,1)S(1)} %collective-permute-done.20.refs_5_), channel_id=1, source_target_pairs={{0,8},{8,16},{16,24},{24,32},{32,40},{40,48},{48,56},{56,0},{64,12... | collective-permute-start | bytes 589832 | tf_op jit(solution)/shard_map/ppermute | solution.py:32
  115.4 14.2 %collective-permute-start.27 = (bf16[2,8,128,256]{3,2,1,0:T(8,128)(2,1)S(1)}, bf16[2,8,128,256]{3,2,1,0:T(8,128)(2,1)}, u32[]{:S(2)}, u32[]{:S(2)}) collective-permute-start(bf16[2,8,128,256]{3,2,1,0:T(8,128)(2,1)S(1)} %get-tuple-element.8), channel_id=1, source_target_pairs={{0,64},{64,0},{1,65},{65,1},{2,66},{66,2},{3,67},{67,3},{4,68},{68... | collective-permute-start | bytes 3145736 | tf_op jit(solution)/shard_map/ppermute | solution.py:54
  131.1 1.3 copy-start.1
  132.6 9.2 %collective-permute-start.28 = (bf16[4,128,256]{2,1,0:T(8,128)(2,1)S(1)}, bf16[4,128,256]{2,1,0:T(8,128)(2,1)S(1)}, u32[]{:S(2)}, u32[]{:S(2)}) collective-permute-start(bf16[4,128,256]{2,1,0:T(8,128)(2,1)S(1)} %get-tuple-element.13), channel_id=1, source_target_pairs={{0,128},{4,132},{128,0},{132,4},{1,129},{5,133},{129,1},{133,5},{2... | collective-permute-start | bytes 786440 | tf_op jit(solution)/shard_map/ppermute | solution.py:54
  133.7 14.2 %collective-permute-start.30 = (bf16[4,128,256]{2,1,0:T(8,128)(2,1)S(1)}, bf16[4,128,256]{2,1,0:T(8,128)(2,1)S(1)}, u32[]{:S(2)}, u32[]{:S(2)}) collective-permute-start(bf16[4,128,256]{2,1,0:T(8,128)(2,1)S(1)} %get-tuple-element.12), channel_id=1, source_target_pairs={{0,132},{4,128},{128,4},{132,0},{1,133},{5,129},{129,5},{133,1},{2... | collective-permute-start | bytes 786440 | tf_op jit(solution)/shard_map/ppermute | solution.py:54
  137.6 10.4 %collective-permute-start.29 = (bf16[4,128,256]{2,1,0:T(8,128)(2,1)S(1)}, bf16[4,128,256]{2,1,0:T(8,128)(2,1)S(1)}, u32[]{:S(2)}, u32[]{:S(2)}) collective-permute-start(bf16[4,128,256]{2,1,0:T(8,128)(2,1)S(1)} %fusion.3), channel_id=1, source_target_pairs={{0,4},{4,0},{128,132},{132,128},{1,5},{5,1},{129,133},{133,129},{2... | collective-permute-start | bytes 786440 | tf_op jit(solution)/shard_map/ppermute | solution.py:54
  148.2 7.5 %collective-permute-start.31 = (bf16[2,128,256]{2,1,0:T(8,128)(2,1)S(1)}, bf16[2,128,256]{2,1,0:T(8,128)(2,1)S(1)}, u32[]{:S(2)}, u32[]{:S(2)}) collective-permute-start(bf16[2,128,256]{2,1,0:T(8,128)(2,1)S(1)} %get-tuple-element.11), channel_id=1, source_target_pairs={{0,1},{1,2},{2,3},{3,0},{4,5},{5,6},{6,7},{7,4},{8,9},{9,10},{10,1... | collective-permute-start | bytes 393224 | tf_op jit(solution)/shard_map/ppermute | solution.py:223
  150.0 9.1 %collective-permute-start.32 = (bf16[2,128,256]{2,1,0:T(8,128)(2,1)S(1)}, bf16[2,128,256]{2,1,0:T(8,128)(2,1)S(1)}, u32[]{:S(2)}, u32[]{:S(2)}) collective-permute-start(bf16[2,128,256]{2,1,0:T(8,128)(2,1)S(1)} %get-tuple-element.10), channel_id=1, source_target_pairs={{0,2},{1,3},{2,0},{3,1},{4,6},{5,7},{6,4},{7,5},{8,10},{9,11},{10,... | collective-permute-start | bytes 393224 | tf_op jit(solution)/shard_map/ppermute | solution.py:223
  152.9 6.1 %collective-permute-start.33 = (bf16[2,128,256]{2,1,0:T(8,128)(2,1)S(1)}, bf16[2,128,256]{2,1,0:T(8,128)(2,1)S(1)}, u32[]{:S(2)}, u32[]{:S(2)}) collective-permute-start(bf16[2,128,256]{2,1,0:T(8,128)(2,1)S(1)} %get-tuple-element.9), channel_id=1, source_target_pairs={{0,3},{1,0},{2,1},{3,2},{4,7},{5,4},{6,5},{7,6},{8,11},{9,8},{10,9... | collective-permute-start | bytes 393224 | tf_op jit(solution)/shard_map/ppermute | solution.py:223
  155.6 3.4 %copy-start.4 = (bf16[2,128,256]{2,1,0:T(8,128)(2,1)}, bf16[2,128,256]{2,1,0:T(8,128)(2,1)S(1)}, u32[]{:S(2)}) copy-start(bf16[2,128,256]{2,1,0:T(8,128)(2,1)S(1)} %collective-permute-done.31.refs_0_) | copy-start | bytes 393220
  159.0 0.6 copy-start.5
  159.7 0.7 copy-start.6
where the time goes:
time: 163 us
  starting transfers between devices  74.5 us (46%)
  waiting for transfers between devices  58.9 us (36%)
  Pallas kernels  15.1 us (9%)
  local copies, waits for them, and re-layouts  9.4 us (6%)
  other arithmetic  4.52 us (3%)
    ppermute x20, starting transfers between devices, ring_send(): return lax.ppermute(x, ('core', axis), ring_pairs(size, step))  28.5 us
    ppermute x20, waiting for transfers between devices, ring_send(): return lax.ppermute(x, ('core', axis), ring_pairs(size, step))  21 us
    all_to_all x2, waiting for transfers between devices, gathered_by_exchange(): lax.all_to_all(jnp.broadcast_to(x, (size, *x.shape)), axes, 0, 0, tiled=T...  19.8 us
    ppermute x6, starting transfers between devices, swap(): return lax.ppermute(x, axes, [(i, i ^ mask) for i in range(total)])  17.9 us
    all_to_all x2, starting transfers between devices, gathered_by_exchange(): lax.all_to_all(jnp.broadcast_to(x, (size, *x.shape)), axes, 0, 0, tiled=T...  14.1 us
    ppermute x6, waiting for transfers between devices, swap(): return lax.ppermute(x, axes, [(i, i ^ mask) for i in range(total)])  13.3 us
    ppermute x3, starting transfers between devices, body(): lax.ppermute(outgoing[:, s - 1], 'y', [(i, (i + s) % NY) for i in range(N...  6.74 us
    pallas_call x1, Pallas kernels, tile_product(): pl.pallas_call(tile_kernel, in_specs=[anyspace] * 16, out_shape=[jax.Shap...  6.46 us
  transfers between devices with their start and end apart: 36, of which 19 were waited for; matrix products, arithmetic and copies ran while one was open for 3% of the time, Pallas kernels for 0%

commit v1 on v0

v1 whole, which is shorter than its diff:
```python
import jax
import jax.numpy as jnp
from jax import lax
from jax.experimental import pallas as pl
from jax.experimental.pallas import tpu as pltpu
from jax.sharding import Mesh
from jax.sharding import PartitionSpec as P

AXES = ("x_hi", "core", "z", "x_lo", "y")
SIZES = (2, 2, 8, 2, 4)
NZ, NX, NY = 8, 2, 4
ROWS = 128
N = 8192
OCC = 768
COLS = OCC // 2
WIDTH = 128
F32 = jnp.float32
BF16 = jnp.bfloat16


def ring_pairs(size, step):
    pairs = []
    for core in range(2):
        sign = 1 - 2 * core
        for i in range(size):
            pairs.append((core * size + i, core * size + (i + sign * step) % size))
    return pairs


def ring_send(x, axis, step):
    size = SIZES[AXES.index(axis)]
    return lax.ppermute(x, ("core", axis), ring_pairs(size, step))


def x_send(x):
    pairs = []
    for core in range(2):
        for i in range(4):
            j = (i + 1 - 2 * core) % 4
            src = ((i // 2) * 2 + core) * 2 + i % 2
            dst = ((j // 2) * 2 + core) * 2 + j % 2
            pairs.append((src, dst))
    return lax.ppermute(x, ("x_hi", "core", "x_lo"), pairs)


def swap(x, axes, flips):
    sizes = [SIZES[AXES.index(a)] for a in axes]
    total = 1
    for s in sizes:
        total *= s
    mask = 0
    for f in flips:
        mask = mask * 2 + f
    return lax.ppermute(x, axes, [(i, i ^ mask) for i in range(total)])


RING = {"z": (0, -1, 1, -2, 2, -3, 3, -4), "y": (0, -1, 1, -2), "x": (0, 1)}


class Ring:
    def __init__(self, x, axis):
        self.axis, self.size = axis, SIZES[AXES.index(axis)]
        self.fwd, self.bwd, self.blocks, self.k = x, x, [x], 0

    def step(self, count=1):
        for _ in range(count):
            self.k += 1
            self.fwd = ring_send(self.fwd, self.axis, 1)
            self.blocks.append(self.fwd)
            if 2 * self.k < self.size:
                self.bwd = ring_send(self.bwd, self.axis, -1)
                self.blocks.append(self.bwd)
        return self

    def finish(self):
        return self.step(self.size // 2 - self.k).blocks

    def wait_for(self, *others):
        self.fwd, self.bwd, *others = lax.optimization_barrier((self.fwd, self.bwd, *others))
        return others


def ring_gather(x, axis):
    if axis == "x":
        return [x, x_send(x)]
    return Ring(x, axis).finish()


def gathered_by_exchange(x, axes):
    size = 1
    for axis in axes:
        size *= SIZES[AXES.index(axis)]
    return lax.all_to_all(jnp.broadcast_to(x, (size, *x.shape)), axes, 0, 0, tiled=True)


def dot(lhs, rhs):
    return jnp.dot(lhs, rhs, preferred_element_type=F32)


def half_kernel(own_ref, sib_ref, *refs):
    by_z, by_y, by_x, out = refs[:8], refs[8:12], refs[12:14], refs[14]
    sign = 1 - 2 * lax.axis_index("core")
    x, y = lax.axis_index("x_lo"), lax.axis_index("y")
    z_line = [(lax.axis_index("z") + sign * off) % NZ for off in RING["z"]]
    depth = NZ * ROWS

    def plane(ref, z):
        return ref[:, pl.ds(pl.multiple_of(z * NX * NY * ROWS, ROWS), NX * NY * ROWS)]

    def line(ref, dx, off):
        start = (((x + dx) % NX) * NY + (y + sign * off) % NY) * ROWS
        cols = [pl.multiple_of(z * NX * NY * ROWS + start, ROWS) for z in z_line]
        return jnp.concatenate([ref[:, pl.ds(c, ROWS)] for c in cols], axis=1)

    for p, ref in enumerate((own_ref, sib_ref)):
        totals = [jnp.zeros((ROWS, WIDTH), F32) for _ in range(3)]
        for k, z in enumerate(z_line):
            totals[0] += dot(plane(ref, z), by_z[k][...])
        for k, off in enumerate(RING["y"]):
            for dx in range(NX):
                lhs = line(ref, dx, off)
                totals[1] += dot(lhs, by_y[k][dx * depth : (dx + 1) * depth])
                totals[2] += dot(lhs, by_x[dx][k * depth : (k + 1) * depth])
        for k, total in enumerate(totals):
            out[:, (3 * p + k) * WIDTH : (3 * p + k + 1) * WIDTH] = total.astype(BF16)


def half_blocks(own, sib, by_z, by_y, by_x):
    return pl.pallas_call(
        half_kernel,
        out_shape=jax.ShapeDtypeStruct((ROWS, OCC), BF16),
        compiler_params=pltpu.CompilerParams(vmem_limit_bytes=48 << 20),
    )(own, sib, *by_z, *by_y, *by_x)


def tile_kernel(keep, *refs):
    z_blocks, xy_blocks, refs = refs[:8], refs[8:16], refs[16:]
    added = refs[0] if keep else None
    out, z_buf, xy_buf, z_sem, xy_sem = refs[-5:]
    core = lax.axis_index("core")
    low = core if keep else 1 - core
    sign = 1 - 2 * core
    z, x, y = lax.axis_index("z"), lax.axis_index("x_lo"), lax.axis_index("y")
    copies = [
        pltpu.make_async_copy(z_blocks[k], z_buf.at[(z + sign * off) % NZ], z_sem.at[k])
        for k, off in enumerate(RING["z"])
    ]
    for k in range(8):
        slot = ((x + k // 4) % NX) * NY + (y + k % 4) % NY
        copies.append(pltpu.make_async_copy(xy_blocks[k], xy_buf.at[slot], xy_sem.at[k]))
    for c in copies:
        c.start()
    for c in copies:
        c.wait()
    for high in range(2):
        rhs = z_buf[pl.ds(4 * high + 2 * low, 2)].reshape(2 * ROWS, OCC)
        for k in range(0, 8, 4):
            prod = lax.dot_general(
                xy_buf[k : k + 4].reshape(4 * ROWS, OCC),
                rhs,
                (((1,), (1,)), ((), ())),
                preferred_element_type=F32,
            ).reshape(4, ROWS, 2 * ROWS)
            rows = slice(8 * high + k, 8 * high + k + 4)
            if keep:
                prod = prod + added[rows].astype(F32)
            out[rows] = prod.astype(BF16)


def tile_product(z_blocks, xy_blocks, *added):
    anyspace = pl.BlockSpec(memory_space=pl.ANY)
    keep = bool(added)
    return pl.pallas_call(
        lambda *refs: tile_kernel(keep, *refs),
        in_specs=[anyspace] * 16 + [pl.BlockSpec(memory_space=pltpu.VMEM)] * len(added),
        out_shape=jax.ShapeDtypeStruct((16, ROWS, 2 * ROWS), BF16),
        scratch_shapes=[
            pltpu.VMEM((8, ROWS, OCC), BF16),
            pltpu.VMEM((8, ROWS, OCC), BF16),
            pltpu.SemaphoreType.DMA((8,)),
            pltpu.SemaphoreType.DMA((8,)),
        ],
        compiler_params=pltpu.CompilerParams(vmem_limit_bytes=48 << 20),
    )(*z_blocks, *xy_blocks, *added)


def final_kernel(pieces, out):
    for src in range(NX * NY):
        total = pieces[src].astype(F32) + pieces[NX * NY + src].astype(F32)
        for zl in range(2):
            start = (zl * NX * NY + src) * ROWS
            out[:, start : start + ROWS] = total[:, zl * ROWS : (zl + 1) * ROWS]


def assemble(pieces):
    return pl.pallas_call(
        final_kernel, out_shape=jax.ShapeDtypeStruct((ROWS, 16 * ROWS), F32)
    )(pieces)


def body(integrals, orbitals):
    own = integrals[0]
    sib = swap(own, ("core",), (1,))
    core = lax.axis_index("core")
    mine = lax.dynamic_slice(orbitals, (0, core * COLS), (ROWS, COLS))
    plane = gathered_by_exchange(mine[:, :WIDTH], ("x_lo", "y")).reshape(NX * NY * ROWS, WIDTH)
    line_ring = Ring(mine[:, WIDTH:], "z").step()
    (plane,) = line_ring.wait_for(plane)
    line_ring.step(2)
    plane_ring = Ring(plane, "z").step()
    plane_ring.fwd, plane_ring.bwd = line_ring.wait_for(plane_ring.fwd, plane_ring.bwd)
    lines = jnp.concatenate(line_ring.finish(), axis=0)
    by_z = plane_ring.finish()
    by_y = ring_gather(jnp.concatenate(ring_gather(lines[:, :WIDTH], "x"), axis=0), "y")
    by_x = ring_gather(jnp.concatenate(ring_gather(lines[:, WIDTH:], "y"), axis=0), "x")
    half = half_blocks(own, sib, by_z, by_y, by_x)

    z_blocks = ring_gather(half, "z")
    pair = jnp.stack([half, swap(half, ("x_lo",), (1,))])
    lines = [pair] + [lax.ppermute(pair, "y", [(i, (i - s) % NY) for i in range(NY)]) for s in (1, 2, 3)]
    xy_blocks = [lines[s][dx] for dx in range(2) for s in range(4)]

    other = tile_product(z_blocks, xy_blocks)
    mine = tile_product(z_blocks, xy_blocks, swap(other, ("core",), (1,)))
    pieces = lax.all_to_all(mine, ("x_hi", "x_lo", "y"), 0, 0, tiled=True)
    return assemble(pieces)


def solution(mesh):
    split = Mesh(mesh.devices.reshape(SIZES), AXES)
    row = ("z", "x_lo", "y")
    aux = ("x_hi", "core")
    return jax.shard_map(
        body,
        mesh=split,
        in_specs=(P(aux, row, None), P(row, None)),
        out_specs=P(row, aux),
        check_vma=False,
    )
```

time: 163 us -> 159 us (0.975)
  blocking collectives: 0 us -> 20.6 us
  waiting for transfers between devices: 58.9 us -> 45.7 us
  starting transfers between devices: 74.5 us -> 67 us
  Pallas kernels: 15.1 us -> 20 us
  local copies, waits for them, and re-layouts: 9.4 us -> 4.81 us
  other arithmetic: 4.52 us -> 0.14 us
    all_to_all x0 -> x1, blocking collectives: none -> 20.6 us  [body(): pieces = lax.all_to_all(mine, ('x_hi', 'x_lo', 'y'), 0, 0, tiled=True)]
    all_to_all x2 -> x1, waiting for transfers between devices: 19.8 us -> 0.01 us  [gathered_by_exchange(): lax.all_to_all(jnp.broadcast_to(x, (size, *x.shape)), axes, 0, 0, tiled=T...]
    ppermute x20 -> x27, waiting for transfers between devices: 21 us -> 35.8 us  [ring_send(): return lax.ppermute(x, ('core', axis), ring_pairs(size, step))]
    ppermute x20 -> x27, starting transfers between devices: 28.5 us -> 37.9 us  [ring_send(): return lax.ppermute(x, ('core', axis), ring_pairs(size, step))]
    ppermute x6 -> x3, waiting for transfers between devices: 13.3 us -> 4.01 us  [swap(): return lax.ppermute(x, axes, [(i, i ^ mask) for i in range(total)])]
    all_to_all x2 -> x1, starting transfers between devices: 14.1 us -> 5.95 us  [gathered_by_exchange(): lax.all_to_all(jnp.broadcast_to(x, (size, *x.shape)), axes, 0, 0, tiled=T...]
    ppermute x3 -> x0, starting transfers between devices: 6.74 us -> none  [body(): lax.ppermute(outgoing[:, s - 1], 'y', [(i, (i + s) % NY) for i in range(N...]
    pallas_call x1 -> x2, Pallas kernels: 6.46 us -> 11.6 us  [tile_product(): pl.pallas_call(lambda *refs: tile_kernel(keep, *refs), in_specs=[anyspace...]
  transfers between devices with their start and end apart: 36 -> 36, of which waited for: 19 -> 19; matrix products, arithmetic and copies ran while one was open for 3% -> 1% of each run, Pallas kernels for 0% -> 0%
where the time goes in v1:
time: 159 us; the launch traced here: 158 us
  starting transfers between devices  67 us (42%)
  waiting for transfers between devices  45.7 us (29%)
  blocking collectives  20.6 us (13%)
  Pallas kernels  20 us (13%)
  local copies, waits for them, and re-layouts  4.81 us (3%)
    ppermute x27, starting transfers between devices, ring_send(): return lax.ppermute(x, ('core', axis), ring_pairs(size, step))  37.9 us
    ppermute x27, waiting for transfers between devices, ring_send(): return lax.ppermute(x, ('core', axis), ring_pairs(size, step))  35.8 us
    all_to_all x1, blocking collectives, body(): pieces = lax.all_to_all(mine, ('x_hi', 'x_lo', 'y'), 0, 0, tiled=True)  20.6 us
    ppermute x3, starting transfers between devices, swap(): return lax.ppermute(x, axes, [(i, i ^ mask) for i in range(total)])  14.7 us
    pallas_call x2, Pallas kernels, tile_product(): pl.pallas_call(lambda *refs: tile_kernel(keep, *refs), in_specs=[anyspace...  11.6 us
    pallas_call x1, Pallas kernels, half_blocks(): pl.pallas_call(half_kernel, out_shape=jax.ShapeDtypeStruct((ROWS, OCC), B...  6.1 us
    all_to_all x1, starting transfers between devices, gathered_by_exchange(): lax.all_to_all(jnp.broadcast_to(x, (size, *x.shape)), axes, 0, 0, tiled=T...  5.95 us
    ppermute x3, waiting for transfers between devices, body(): lax.ppermute(pair, 'y', [(i, (i - s) % NY) for i in range(NY)])  5.9 us
  transfers between devices with their start and end apart: 36, of which 19 were waited for; matrix products, arithmetic and copies ran while one was open for 1% of the time, Pallas kernels for 0%

profile of v1, /device:TPU:1, one launch (start us, length us, event | category | flops | bytes accessed | tf_op | source)
XLA Modules:
  0.0 158.4 jit_solution(3855748216713594431)
XLA Ops:
  0.0 0.8 constant_dynamic-slice_fusion.1
  0.8 0.7 broadcast_in_dim.3
  1.5 5.9 %all-to-all-start = ((bf16[8,128,128]{2,1,0:T(8,128)(2,1)}), bf16[8,128,128]{2,1,0:T(8,128)(2,1)S(1)}, u32[]{:S(2)}, u32[]{:S(2)}) async-start(bf16[8,128,128]{2,1,0:T(8,128)(2,1)} %broadcast_in_dim.3), calls=%async_computation | async-start | bytes 524288 | tf_op jit(solution)/shard_map/all_to_all | solution.py:93
  7.4 0.8 constant_dynamic-update-slice_fusion.7
  8.3 5.7 %collective-permute-start.1 = (bf16[128,256]{1,0:T(8,128)(2,1)S(1)}, bf16[128,256]{1,0:T(8,128)(2,1)S(1)}, u32[]{:S(2)}, u32[]{:S(2)}) collective-permute-start(bf16[128,256]{1,0:T(8,128)(2,1)S(1)} %get-tuple-element.18), channel_id=1, source_target_pairs={{0,8},{8,16},{16,24},{24,32},{32,40},{40,48},{48,56},{56,0},{64,12... | collective-permute-start | bytes 196616 | tf_op jit(solution)/shard_map/ppermute | solution.py:32
  14.0 1.3 collective-permute-start
  15.3 3.0 %collective-permute-done.2 = bf16[128,256]{1,0:T(8,128)(2,1)S(1)} collective-permute-done((bf16[128,256]{1,0:T(8,128)(2,1)S(1)}, bf16[128,256]{1,0:T(8,128)(2,1)S(1)}, u32[]{:S(2)}, u32[]{:S(2)}) %collective-permute-start.2) | collective-permute-done | bytes 65568 | tf_op jit(solution)/shard_map/ppermute | solution.py:32
  18.3 0.8 collective-permute-start.5
  19.1 0.6 collective-permute-start.4
  19.8 2.1 %collective-permute-start.3 = (bf16[1024,128]{1,0:T(8,128)(2,1)S(1)}, bf16[1024,128]{1,0:T(8,128)(2,1)S(1)}, u32[]{:S(2)}, u32[]{:S(2)}) collective-permute-start(bf16[1024,128]{1,0:T(8,128)(2,1)S(1)} %bitcast.19), channel_id=1, source_target_pairs={{0,8},{8,16},{16,24},{24,32},{32,40},{40,48},{48,56},{56,0},{64,12... | collective-permute-start | bytes 786440 | tf_op jit(solution)/shard_map/ppermute | solution.py:32
  21.8 2.7 %collective-permute-start.6 = (bf16[128,256]{1,0:T(8,128)(2,1)S(1)}, bf16[128,256]{1,0:T(8,128)(2,1)S(1)}, u32[]{:S(2)}, u32[]{:S(2)}) collective-permute-start(bf16[128,256]{1,0:T(8,128)(2,1)S(1)} %collective-permute-done.5), channel_id=1, source_target_pairs={{0,8},{8,16},{16,24},{24,32},{32,40},{40,48},{48,56},{56,0},{64,12... | collective-permute-start | bytes 196616 | tf_op jit(solution)/shard_map/ppermute | solution.py:32
  24.5 3.2 %collective-permute-done.7 = bf16[128,256]{1,0:T(8,128)(2,1)S(1)} collective-permute-done((bf16[128,256]{1,0:T(8,128)(2,1)S(1)}, bf16[128,256]{1,0:T(8,128)(2,1)S(1)}, u32[]{:S(2)}, u32[]{:S(2)}) %collective-permute-start.7) | collective-permute-done | bytes 65568 | tf_op jit(solution)/shard_map/ppermute | solution.py:32
  27.7 1.7 %collective-permute-done.6 = bf16[128,256]{1,0:T(8,128)(2,1)S(1)} collective-permute-done((bf16[128,256]{1,0:T(8,128)(2,1)S(1)}, bf16[128,256]{1,0:T(8,128)(2,1)S(1)}, u32[]{:S(2)}, u32[]{:S(2)}) %collective-permute-start.6) | collective-permute-done | bytes 65568 | tf_op jit(solution)/shard_map/ppermute | solution.py:32
  29.4 2.6 %collective-permute-done.8 = bf16[128,256]{1,0:T(8,128)(2,1)S(1)} collective-permute-done((bf16[128,256]{1,0:T(8,128)(2,1)S(1)}, bf16[128,256]{1,0:T(8,128)(2,1)S(1)}, u32[]{:S(2)}, u32[]{:S(2)}) %collective-permute-start.8) | collective-permute-done | bytes 65568 | tf_op jit(solution)/shard_map/ppermute | solution.py:32
  32.0 0.7 collective-permute-start.14
  32.7 2.4 %collective-permute-done.14 = bf16[128,256]{1,0:T(8,128)(2,1)S(1)} collective-permute-done((bf16[128,256]{1,0:T(8,128)(2,1)S(1)}, bf16[128,256]{1,0:T(8,128)(2,1)S(1)}, u32[]{:S(2)}, u32[]{:S(2)}) %collective-permute-start.14) | collective-permute-done | bytes 65568 | tf_op jit(solution)/shard_map/ppermute | solution.py:32
  35.2 2.3 %collective-permute-start.19 = (bf16[1024,128]{1,0:T(8,128)(2,1)S(1)}, bf16[1024,128]{1,0:T(8,128)(2,1)S(1)}, u32[]{:S(2)}, u32[]{:S(2)}) collective-permute-start(bf16[1024,128]{1,0:T(8,128)(2,1)S(1)} %get-tuple-element.19), channel_id=1, source_target_pairs={{0,1},{1,2},{2,3},{3,0},{64,67},{65,64},{66,65},{67,66},{4,5},{5,6... | collective-permute-start | bytes 786440 | tf_op jit(solution)/shard_map/ppermute | solution.py:32
  37.5 2.5 %collective-permute-start.15 = (bf16[1024,128]{1,0:T(8,128)(2,1)S(1)}, bf16[1024,128]{1,0:T(8,128)(2,1)S(1)}, u32[]{:S(2)}, u32[]{:S(2)}) collective-permute-start(bf16[1024,128]{1,0:T(8,128)(2,1)S(1)} %get-tuple-element.20), channel_id=1, source_target_pairs={{0,4},{4,128},{128,132},{132,0},{64,196},{68,64},{192,68},{196,192... | collective-permute-start | bytes 786440 | tf_op jit(solution)/shard_map/ppermute | solution.py:43
  39.9 0.9 collective-permute-done.19
  40.8 3.1 %collective-permute-start.21 = (bf16[1024,128]{1,0:T(8,128)(2,1)S(1)}, bf16[1024,128]{1,0:T(8,128)(2,1)S(1)}, u32[]{:S(2)}, u32[]{:S(2)}) collective-permute-start(bf16[1024,128]{1,0:T(8,128)(2,1)S(1)} %collective-permute-done.19), channel_id=1, source_target_pairs={{0,1},{1,2},{2,3},{3,0},{64,67},{65,64},{66,65},{67,66},{4,5},{5,6... | collective-permute-start | bytes 786440 | tf_op jit(solution)/shard_map/ppermute | solution.py:32
  43.9 1.9 %collective-permute-start.9 = (bf16[1024,128]{1,0:T(8,128)(2,1)S(1)}, bf16[1024,128]{1,0:T(8,128)(2,1)S(1)}, u32[]{:S(2)}, u32[]{:S(2)}) collective-permute-start(bf16[1024,128]{1,0:T(8,128)(2,1)S(1)} %collective-permute-done.3.refs_1_), channel_id=1, source_target_pairs={{0,8},{8,16},{16,24},{24,32},{32,40},{40,48},{48,56},{56,0},{64,12... | collective-permute-start | bytes 786440 | tf_op jit(solution)/shard_map/ppermute | solution.py:32
  46.2 1.6 collective-permute-done.20
  48.1 3.4 %collective-permute-start.22 = (bf16[4096,128]{1,0:T(8,128)(2,1)S(1)}, bf16[4096,128]{1,0:T(8,128)(2,1)S(1)}, u32[]{:S(2)}, u32[]{:S(2)}) collective-permute-start(bf16[4096,128]{1,0:T(8,128)(2,1)S(1)} %pad_maximum_fusion.refs_12_), channel_id=1, source_target_pairs={{0,4},{4,128},{128,132},{132,0},{64,196},{68,64},{192,68},{196,192... | collective-permute-start | bytes 3145736 | tf_op jit(solution)/shard_map/ppermute | solution.py:43
  51.5 0.5 collective-permute-start.10
  52.0 2.2 %collective-permute-start.11 = (bf16[1024,128]{1,0:T(8,128)(2,1)S(1)}, bf16[1024,128]{1,0:T(8,128)(2,1)S(1)}, u32[]{:S(2)}, u32[]{:S(2)}) collective-permute-start(bf16[1024,128]{1,0:T(8,128)(2,1)S(1)} %collective-permute-done.9.refs_3_), channel_id=1, source_target_pairs={{0,8},{8,16},{16,24},{24,32},{32,40},{40,48},{48,56},{56,0},{64,12... | collective-permute-start | bytes 786440 | tf_op jit(solution)/shard_map/ppermute | solution.py:32
  54.1 5.7 %collective-permute-done.10.refs_4_ = bf16[1024,128]{1,0:T(8,128)(2,1)S(1)} collective-permute-done((bf16[1024,128]{1,0:T(8,128)(2,1)S(1)}, bf16[1024,128]{1,0:T(8,128)(2,1)S(1)}, u32[]{:S(2)}, u32[]{:S(2)}) %collective-permute-start.10) | collective-permute-done | bytes 262176 | tf_op jit(solution)/shard_map/ppermute | solution.py:32
  59.9 3.0 %collective-permute-start.18 = (bf16[2048,128]{1,0:T(8,128)(2,1)S(1)}, bf16[2048,128]{1,0:T(8,128)(2,1)S(1)}, u32[]{:S(2)}, u32[]{:S(2)}) collective-permute-start(bf16[2048,128]{1,0:T(8,128)(2,1)S(1)} %collective-permute-done.16.refs_9_), channel_id=1, source_target_pairs={{0,1},{1,2},{2,3},{3,0},{64,67},{65,64},{66,65},{67,66},{4,5},{5,6... | collective-permute-start | bytes 1572872 | tf_op jit(solution)/shard_map/ppermute | solution.py:32
  62.9 6.1 %collective-permute-done.12.refs_6_ = bf16[1024,128]{1,0:T(8,128)(2,1)S(1)} collective-permute-done((bf16[1024,128]{1,0:T(8,128)(2,1)S(1)}, bf16[1024,128]{1,0:T(8,128)(2,1)S(1)}, u32[]{:S(2)}, u32[]{:S(2)}) %collective-permute-start.12) | collective-permute-done | bytes 262176 | tf_op jit(solution)/shard_map/ppermute | solution.py:32
  69.0 5.5 %collective-permute-done.13.refs_7_ = bf16[1024,128]{1,0:T(8,128)(2,1)S(1)} collective-permute-done((bf16[1024,128]{1,0:T(8,128)(2,1)S(1)}, bf16[1024,128]{1,0:T(8,128)(2,1)S(1)}, u32[]{:S(2)}, u32[]{:S(2)}) %collective-permute-start.13) | collective-permute-done | bytes 262176 | tf_op jit(solution)/shard_map/ppermute | solution.py:32
  74.6 1.3 copy-done
  75.9 1.0 copy-done.1
  76.9 6.1 %shard_map.28.refs_0_.refs_8_ = bf16[128,768]{1,0:T(8,128)(2,1)S(1)} custom-call(bf16[128,8192]{1,0:T(8,128)(2,1)} %bitcast.22, bf16[128,8192]{1,0:T(8,128)(2,1)} %copy-done, bf16[1024,128]{1,0:T(8,128)(2,1)S(1)} %bitcast.20, bf16[1024,128]{1,0:T(8,128)(2,1)S(1)} %collective-permute-done.3.refs_1_, bf16[1024,128]{1,0:T(8,128)(2,1)S(1)} %collective-permute-done.4.refs_2_, ...), custom_call_target="tpu_custom_call" | custom-call | tf_op jit(solution)/shard_map/pallas_call | solution.py:129
  83.2 2.7 %collective-permute-start.23 = (bf16[128,768]{1,0:T(8,128)(2,1)S(1)}, bf16[128,768]{1,0:T(8,128)(2,1)S(1)}, u32[]{:S(2)}, u32[]{:S(2)}) collective-permute-start(bf16[128,768]{1,0:T(8,128)(2,1)S(1)} %shard_map.28.refs_0_.refs_8_), channel_id=1, source_target_pairs={{0,8},{8,16},{16,24},{24,32},{32,40},{40,48},{48,56},{56,0},{64,12... | collective-permute-start | bytes 589832 | tf_op jit(solution)/shard_map/ppermute | solution.py:32
  85.9 1.7 %collective-permute-done.30.refs_12_ = bf16[128,768]{1,0:T(8,128)(2,1)S(1)} collective-permute-done((bf16[128,768]{1,0:T(8,128)(2,1)S(1)}, bf16[128,768]{1,0:T(8,128)(2,1)S(1)}, u32[]{:S(2)}, u32[]{:S(2)}) %collective-permute-start.30) | collective-permute-done | bytes 196640 | tf_op jit(solution)/shard_map/ppermute | solution.py:54
  87.7 1.2 collective-permute-done.24.refs_2_
  88.9 2.7 %collective-permute-start.25 = (bf16[128,768]{1,0:T(8,128)(2,1)S(1)}, bf16[128,768]{1,0:T(8,128)(2,1)S(1)}, u32[]{:S(2)}, u32[]{:S(2)}) collective-permute-start(bf16[128,768]{1,0:T(8,128)(2,1)S(1)} %collective-permute-done.23.refs_1_), channel_id=1, source_target_pairs={{0,8},{8,16},{16,24},{24,32},{32,40},{40,48},{48,56},{56,0},{64,12... | collective-permute-start | bytes 589832 | tf_op jit(solution)/shard_map/ppermute | solution.py:32
  91.6 2.5 %collective-permute-start.32 = (bf16[2,128,768]{2,1,0:T(8,128)(2,1)S(1)}, bf16[2,128,768]{2,1,0:T(8,128)(2,1)S(1)}, u32[]{:S(2)}, u32[]{:S(2)}) collective-permute-start(bf16[2,128,768]{2,1,0:T(8,128)(2,1)S(1)} %pad_maximum_fusion.2), channel_id=1, source_target_pairs={{0,2},{1,3},{2,0},{3,1},{4,6},{5,7},{6,4},{7,5},{8,10},{9,11},{10,... | collective-permute-start | bytes 1179656 | tf_op jit(solution)/shard_map/ppermute | solution.py:220
  94.6 0.9 collective-permute-done.25.refs_3_
  95.5 3.4 %collective-permute-start.27 = (bf16[128,768]{1,0:T(8,128)(2,1)S(1)}, bf16[128,768]{1,0:T(8,128)(2,1)S(1)}, u32[]{:S(2)}, u32[]{:S(2)}) collective-permute-start(bf16[128,768]{1,0:T(8,128)(2,1)S(1)} %collective-permute-done.25.refs_3_), channel_id=1, source_target_pairs={{0,8},{8,16},{16,24},{24,32},{32,40},{40,48},{48,56},{56,0},{64,12... | collective-permute-start | bytes 589832 | tf_op jit(solution)/shard_map/ppermute | solution.py:32
  99.0 3.6 %collective-permute-done.32 = bf16[2,128,768]{2,1,0:T(8,128)(2,1)S(1)} collective-permute-done((bf16[2,128,768]{2,1,0:T(8,128)(2,1)S(1)}, bf16[2,128,768]{2,1,0:T(8,128)(2,1)S(1)}, u32[]{:S(2)}, u32[]{:S(2)}) %collective-permute-start.32) | collective-permute-done | bytes 393248 | tf_op jit(solution)/shard_map/ppermute | solution.py:220
  102.7 3.1 %collective-permute-start.29 = (bf16[128,768]{1,0:T(8,128)(2,1)S(1)}, bf16[128,768]{1,0:T(8,128)(2,1)S(1)}, u32[]{:S(2)}, u32[]{:S(2)}) collective-permute-start(bf16[128,768]{1,0:T(8,128)(2,1)S(1)} %collective-permute-done.27.refs_5_), channel_id=1, source_target_pairs={{0,8},{8,16},{16,24},{24,32},{32,40},{40,48},{48,56},{56,0},{64,12... | collective-permute-start | bytes 589832 | tf_op jit(solution)/shard_map/ppermute | solution.py:32
  105.7 2.3 %collective-permute-done.31 = bf16[2,128,768]{2,1,0:T(8,128)(2,1)S(1)} collective-permute-done((bf16[2,128,768]{2,1,0:T(8,128)(2,1)S(1)}, bf16[2,128,768]{2,1,0:T(8,128)(2,1)S(1)}, u32[]{:S(2)}, u32[]{:S(2)}) %collective-permute-start.31) | collective-permute-done | bytes 393248 | tf_op jit(solution)/shard_map/ppermute | solution.py:220
  108.4 5.8 %shard_map.29 = bf16[16,128,256]{2,1,0:T(8,128)(2,1)S(1)} custom-call(bf16[128,768]{1,0:T(8,128)(2,1)S(1)} %shard_map.28.refs_0_.refs_8_, bf16[128,768]{1,0:T(8,128)(2,1)S(1)} %collective-permute-done.23.refs_1_, bf16[128,768]{1,0:T(8,128)(2,1)S(1)} %collective-permute-done.24.refs_2_, bf16[128,768]{1,0:T(8,128)(2,1)S(1)} %collective-permute-done.25.refs_3_, ...), custom_call_target="tpu_custom_call" | custom-call | tf_op jit(solution)/shard_map/pallas_call | solution.py:173
  114.1 13.3 %collective-permute-start.34 = (bf16[16,128,256]{2,1,0:T(8,128)(2,1)S(1)}, bf16[16,128,256]{2,1,0:T(8,128)(2,1)S(1)}, u32[]{:S(2)}, u32[]{:S(2)}) collective-permute-start(bf16[16,128,256]{2,1,0:T(8,128)(2,1)S(1)} %shard_map.29), channel_id=1, source_target_pairs={{0,64},{64,0},{1,65},{65,1},{2,66},{66,2},{3,67},{67,3},{4,68},{68... | collective-permute-start | bytes 3145736 | tf_op jit(solution)/shard_map/ppermute | solution.py:54
  127.4 2.3 %collective-permute-done.34.refs_16_ = bf16[16,128,256]{2,1,0:T(8,128)(2,1)S(1)} collective-permute-done((bf16[16,128,256]{2,1,0:T(8,128)(2,1)S(1)}, bf16[16,128,256]{2,1,0:T(8,128)(2,1)S(1)}, u32[]{:S(2)}, u32[]{:S(2)}) %collective-permute-start.34) | collective-permute-done | bytes 1048608 | tf_op jit(solution)/shard_map/ppermute | solution.py:54
  129.7 5.8 %shard_map.30 = bf16[16,128,256]{2,1,0:T(8,128)(2,1)S(1)} custom-call(bf16[128,768]{1,0:T(8,128)(2,1)S(1)} %shard_map.28.refs_0_.refs_8_, bf16[128,768]{1,0:T(8,128)(2,1)S(1)} %collective-permute-done.23.refs_1_, bf16[128,768]{1,0:T(8,128)(2,1)S(1)} %collective-permute-done.24.refs_2_, bf16[128,768]{1,0:T(8,128)(2,1)S(1)} %collective-permute-done.25.refs_3_, ...), custom_call_target="tpu_custom_call" | custom-call | tf_op jit(solution)/shard_map/pallas_call | solution.py:173
  135.5 20.6 %all_to_all.10.pieces = bf16[16,128,256]{2,1,0:T(8,128)(2,1)} all-to-all(bf16[16,128,256]{2,1,0:T(8,128)(2,1)S(1)} %shard_map.30), channel_id=1, replica_groups=mesh['x_hi'=2,'core'=2,'z'=8,'x_lo'=2,'y'=4] {'x_hi','x_lo','y'}, dimensions={0} | all-to-all | bytes 2097152 | tf_op jit(solution)/shard_map/all_to_all | solution.py:225
  156.1 2.3 %shard_map.31 = f32[128,2048]{1,0:T(8,128)} custom-call(bf16[16,128,256]{2,1,0:T(8,128)(2,1)} %all_to_all.10.pieces), custom_call_target="tpu_custom_call" | custom-call | tf_op jit(solution)/shard_map/pallas_call | solution.py:196
  (50 shorter events, 2.0 us)
Async XLA Ops:
  1.5 16.8 %all-to-all-start = ((bf16[8,128,128]{2,1,0:T(8,128)(2,1)}), bf16[8,128,128]{2,1,0:T(8,128)(2,1)S(1)}, u32[]{:S(2)}, u32[]{:S(2)}) async-start(bf16[8,128,128]{2,1,0:T(8,128)(2,1)} %broadcast_in_dim.3), calls=%async_computation | async-start | bytes 524288 | tf_op jit(solution)/shard_map/all_to_all | solution.py:93
  8.3 7.0 %collective-permute-start.1 = (bf16[128,256]{1,0:T(8,128)(2,1)S(1)}, bf16[128,256]{1,0:T(8,128)(2,1)S(1)}, u32[]{:S(2)}, u32[]{:S(2)}) collective-permute-start(bf16[128,256]{1,0:T(8,128)(2,1)S(1)} %get-tuple-element.18), channel_id=1, source_target_pairs={{0,8},{8,16},{16,24},{24,32},{32,40},{40,48},{48,56},{56,0},{64,12... | collective-permute-start | bytes 196616 | tf_op jit(solution)/shard_map/ppermute | solution.py:32
  14.0 4.3 %collective-permute-start.2 = (bf16[128,256]{1,0:T(8,128)(2,1)S(1)}, bf16[128,256]{1,0:T(8,128)(2,1)S(1)}, u32[]{:S(2)}, u32[]{:S(2)}) collective-permute-start(bf16[128,256]{1,0:T(8,128)(2,1)S(1)} %get-tuple-element.18), channel_id=1, source_target_pairs={{0,56},{8,0},{16,8},{24,16},{32,24},{40,32},{48,40},{56,48},{64,72... | collective-permute-start | bytes 196616 | tf_op jit(solution)/shard_map/ppermute | solution.py:32
  14.0 60.6 %collective-permute-start = (bf16[128,8192]{1,0:T(8,128)(2,1)}, bf16[128,8192]{1,0:T(8,128)(2,1)S(1)}, u32[]{:S(2)}, u32[]{:S(2)}) collective-permute-start(bf16[128,8192]{1,0:T(8,128)(2,1)} %bitcast.21), channel_id=1, source_target_pairs={{0,64},{64,0},{1,65},{65,1},{2,66},{66,2},{3,67},{67,3},{4,68},{68... | collective-permute-start | bytes 6291464 | tf_op jit(solution)/shard_map/ppermute | solution.py:54
  18.3 3.5 %collective-permute-start.5 = (bf16[128,256]{1,0:T(8,128)(2,1)S(1)}, bf16[128,256]{1,0:T(8,128)(2,1)S(1)}, u32[]{:S(2)}, u32[]{:S(2)}) collective-permute-start(bf16[128,256]{1,0:T(8,128)(2,1)S(1)} %collective-permute-done.1), channel_id=1, source_target_pairs={{0,8},{8,16},{16,24},{24,32},{32,40},{40,48},{48,56},{56,0},{64,12... | collective-permute-start | bytes 196616 | tf_op jit(solution)/shard_map/ppermute | solution.py:32
  19.1 12.9 %collective-permute-start.4 = (bf16[1024,128]{1,0:T(8,128)(2,1)S(1)}, bf16[1024,128]{1,0:T(8,128)(2,1)S(1)}, u32[]{:S(2)}, u32[]{:S(2)}) collective-permute-start(bf16[1024,128]{1,0:T(8,128)(2,1)S(1)} %bitcast.18), channel_id=1, source_target_pairs={{0,56},{8,0},{16,8},{24,16},{32,24},{40,32},{48,40},{56,48},{64,72... | collective-permute-start | bytes 786440 | tf_op jit(solution)/shard_map/ppermute | solution.py:32
  19.8 12.2 %collective-permute-start.3 = (bf16[1024,128]{1,0:T(8,128)(2,1)S(1)}, bf16[1024,128]{1,0:T(8,128)(2,1)S(1)}, u32[]{:S(2)}, u32[]{:S(2)}) collective-permute-start(bf16[1024,128]{1,0:T(8,128)(2,1)S(1)} %bitcast.19), channel_id=1, source_target_pairs={{0,8},{8,16},{16,24},{24,32},{32,40},{40,48},{48,56},{56,0},{64,12... | collective-permute-start | bytes 786440 | tf_op jit(solution)/shard_map/ppermute | solution.py:32
  21.8 5.9 %collective-permute-start.7 = (bf16[128,256]{1,0:T(8,128)(2,1)S(1)}, bf16[128,256]{1,0:T(8,128)(2,1)S(1)}, u32[]{:S(2)}, u32[]{:S(2)}) collective-permute-start(bf16[128,256]{1,0:T(8,128)(2,1)S(1)} %collective-permute-done.2), channel_id=1, source_target_pairs={{0,56},{8,0},{16,8},{24,16},{32,24},{40,32},{48,40},{56,48},{64,72... | collective-permute-start | bytes 196616 | tf_op jit(solution)/shard_map/ppermute | solution.py:32
  21.8 7.5 %collective-permute-start.6 = (bf16[128,256]{1,0:T(8,128)(2,1)S(1)}, bf16[128,256]{1,0:T(8,128)(2,1)S(1)}, u32[]{:S(2)}, u32[]{:S(2)}) collective-permute-start(bf16[128,256]{1,0:T(8,128)(2,1)S(1)} %collective-permute-done.5), channel_id=1, source_target_pairs={{0,8},{8,16},{16,24},{24,32},{32,40},{40,48},{48,56},{56,0},{64,12... | collective-permute-start | bytes 196616 | tf_op jit(solution)/shard_map/ppermute | solution.py:32
  27.7 4.3 %collective-permute-start.8 = (bf16[128,256]{1,0:T(8,128)(2,1)S(1)}, bf16[128,256]{1,0:T(8,128)(2,1)S(1)}, u32[]{:S(2)}, u32[]{:S(2)}) collective-permute-start(bf16[128,256]{1,0:T(8,128)(2,1)S(1)} %collective-permute-done.7), channel_id=1, source_target_pairs={{0,56},{8,0},{16,8},{24,16},{32,24},{40,32},{48,40},{56,48},{64,72... | collective-permute-start | bytes 196616 | tf_op jit(solution)/shard_map/ppermute | solution.py:32
  32.0 3.1 %collective-permute-start.14 = (bf16[128,256]{1,0:T(8,128)(2,1)S(1)}, bf16[128,256]{1,0:T(8,128)(2,1)S(1)}, u32[]{:S(2)}, u32[]{:S(2)}) collective-permute-start(bf16[128,256]{1,0:T(8,128)(2,1)S(1)} %collective-permute-done.6), channel_id=1, source_target_pairs={{0,8},{8,16},{16,24},{24,32},{32,40},{40,48},{48,56},{56,0},{64,12... | collective-permute-start | bytes 196616 | tf_op jit(solution)/shard_map/ppermute | solution.py:32
  35.2 5.6 %collective-permute-start.19 = (bf16[1024,128]{1,0:T(8,128)(2,1)S(1)}, bf16[1024,128]{1,0:T(8,128)(2,1)S(1)}, u32[]{:S(2)}, u32[]{:S(2)}) collective-permute-start(bf16[1024,128]{1,0:T(8,128)(2,1)S(1)} %get-tuple-element.19), channel_id=1, source_target_pairs={{0,1},{1,2},{2,3},{3,0},{64,67},{65,64},{66,65},{67,66},{4,5},{5,6... | collective-permute-start | bytes 786440 | tf_op jit(solution)/shard_map/ppermute | solution.py:32
  37.5 8.4 %collective-permute-start.15 = (bf16[1024,128]{1,0:T(8,128)(2,1)S(1)}, bf16[1024,128]{1,0:T(8,128)(2,1)S(1)}, u32[]{:S(2)}, u32[]{:S(2)}) collective-permute-start(bf16[1024,128]{1,0:T(8,128)(2,1)S(1)} %get-tuple-element.20), channel_id=1, source_target_pairs={{0,4},{4,128},{128,132},{132,0},{64,196},{68,64},{192,68},{196,192... | collective-permute-start | bytes 786440 | tf_op jit(solution)/shard_map/ppermute | solution.py:43
  39.9 7.8 %collective-permute-start.20 = (bf16[1024,128]{1,0:T(8,128)(2,1)S(1)}, bf16[1024,128]{1,0:T(8,128)(2,1)S(1)}, u32[]{:S(2)}, u32[]{:S(2)}) collective-permute-start(bf16[1024,128]{1,0:T(8,128)(2,1)S(1)} %get-tuple-element.19), channel_id=1, source_target_pairs={{0,3},{1,0},{2,1},{3,2},{64,65},{65,66},{66,67},{67,64},{4,7},{5,4... | collective-permute-start | bytes 786440 | tf_op jit(solution)/shard_map/ppermute | solution.py:32
  40.8 7.2 %collective-permute-start.21 = (bf16[1024,128]{1,0:T(8,128)(2,1)S(1)}, bf16[1024,128]{1,0:T(8,128)(2,1)S(1)}, u32[]{:S(2)}, u32[]{:S(2)}) collective-permute-start(bf16[1024,128]{1,0:T(8,128)(2,1)S(1)} %collective-permute-done.19), channel_id=1, source_target_pairs={{0,1},{1,2},{2,3},{3,0},{64,67},{65,64},{66,65},{67,66},{4,5},{5,6... | collective-permute-start | bytes 786440 | tf_op jit(solution)/shard_map/ppermute | solution.py:32
  43.9 8.1 %collective-permute-start.9 = (bf16[1024,128]{1,0:T(8,128)(2,1)S(1)}, bf16[1024,128]{1,0:T(8,128)(2,1)S(1)}, u32[]{:S(2)}, u32[]{:S(2)}) collective-permute-start(bf16[1024,128]{1,0:T(8,128)(2,1)S(1)} %collective-permute-done.3.refs_1_), channel_id=1, source_target_pairs={{0,8},{8,16},{16,24},{24,32},{32,40},{40,48},{48,56},{56,0},{64,12... | collective-permute-start | bytes 786440 | tf_op jit(solution)/shard_map/ppermute | solution.py:32
  45.9 14.0 %collective-permute-start.16 = (bf16[2048,128]{1,0:T(8,128)(2,1)S(1)}, bf16[2048,128]{1,0:T(8,128)(2,1)S(1)}, u32[]{:S(2)}, u32[]{:S(2)}) collective-permute-start(bf16[2048,128]{1,0:T(8,128)(2,1)S(1)} %pad_maximum_fusion.1.refs_8_), channel_id=1, source_target_pairs={{0,1},{1,2},{2,3},{3,0},{64,67},{65,64},{66,65},{67,66},{4,5},{5,6... | collective-permute-start | bytes 1572872 | tf_op jit(solution)/shard_map/ppermute | solution.py:32
  48.1 26.5 %collective-permute-start.22 = (bf16[4096,128]{1,0:T(8,128)(2,1)S(1)}, bf16[4096,128]{1,0:T(8,128)(2,1)S(1)}, u32[]{:S(2)}, u32[]{:S(2)}) collective-permute-start(bf16[4096,128]{1,0:T(8,128)(2,1)S(1)} %pad_maximum_fusion.refs_12_), channel_id=1, source_target_pairs={{0,4},{4,128},{128,132},{132,0},{64,196},{68,64},{192,68},{196,192... | collective-permute-start | bytes 3145736 | tf_op jit(solution)/shard_map/ppermute | solution.py:43
  51.5 8.4 %collective-permute-start.10 = (bf16[1024,128]{1,0:T(8,128)(2,1)S(1)}, bf16[1024,128]{1,0:T(8,128)(2,1)S(1)}, u32[]{:S(2)}, u32[]{:S(2)}) collective-permute-start(bf16[1024,128]{1,0:T(8,128)(2,1)S(1)} %collective-permute-done.4.refs_2_), channel_id=1, source_target_pairs={{0,56},{8,0},{16,8},{24,16},{32,24},{40,32},{48,40},{56,48},{64,72... | collective-permute-start | bytes 786440 | tf_op jit(solution)/shard_map/ppermute | solution.py:32
  52.0 7.9 %collective-permute-start.11 = (bf16[1024,128]{1,0:T(8,128)(2,1)S(1)}, bf16[1024,128]{1,0:T(8,128)(2,1)S(1)}, u32[]{:S(2)}, u32[]{:S(2)}) collective-permute-start(bf16[1024,128]{1,0:T(8,128)(2,1)S(1)} %collective-permute-done.9.refs_3_), channel_id=1, source_target_pairs={{0,8},{8,16},{16,24},{24,32},{32,40},{40,48},{48,56},{56,0},{64,12... | collective-permute-start | bytes 786440 | tf_op jit(solution)/shard_map/ppermute | solution.py:32
  59.9 9.2 %collective-permute-start.12 = (bf16[1024,128]{1,0:T(8,128)(2,1)S(1)}, bf16[1024,128]{1,0:T(8,128)(2,1)S(1)}, u32[]{:S(2)}, u32[]{:S(2)}) collective-permute-start(bf16[1024,128]{1,0:T(8,128)(2,1)S(1)} %collective-permute-done.10.refs_4_), channel_id=1, source_target_pairs={{0,56},{8,0},{16,8},{24,16},{32,24},{40,32},{48,40},{56,48},{64,72... | collective-permute-start | bytes 786440 | tf_op jit(solution)/shard_map/ppermute | solution.py:32
  59.9 14.7 %collective-permute-start.17 = (bf16[2048,128]{1,0:T(8,128)(2,1)S(1)}, bf16[2048,128]{1,0:T(8,128)(2,1)S(1)}, u32[]{:S(2)}, u32[]{:S(2)}) collective-permute-start(bf16[2048,128]{1,0:T(8,128)(2,1)S(1)} %pad_maximum_fusion.1.refs_8_), channel_id=1, source_target_pairs={{0,3},{1,0},{2,1},{3,2},{64,65},{65,66},{66,67},{67,64},{4,7},{5,4... | collective-permute-start | bytes 1572872 | tf_op jit(solution)/shard_map/ppermute | solution.py:32
  59.9 14.7 %collective-permute-start.18 = (bf16[2048,128]{1,0:T(8,128)(2,1)S(1)}, bf16[2048,128]{1,0:T(8,128)(2,1)S(1)}, u32[]{:S(2)}, u32[]{:S(2)}) collective-permute-start(bf16[2048,128]{1,0:T(8,128)(2,1)S(1)} %collective-permute-done.16.refs_9_), channel_id=1, source_target_pairs={{0,1},{1,2},{2,3},{3,0},{64,67},{65,64},{66,65},{67,66},{4,5},{5,6... | collective-permute-start | bytes 1572872 | tf_op jit(solution)/shard_map/ppermute | solution.py:32
  69.0 5.5 %collective-permute-start.13 = (bf16[1024,128]{1,0:T(8,128)(2,1)S(1)}, bf16[1024,128]{1,0:T(8,128)(2,1)S(1)}, u32[]{:S(2)}, u32[]{:S(2)}) collective-permute-start(bf16[1024,128]{1,0:T(8,128)(2,1)S(1)} %collective-permute-done.11.refs_5_), channel_id=1, source_target_pairs={{0,8},{8,16},{16,24},{24,32},{32,40},{40,48},{48,56},{56,0},{64,12... | collective-permute-start | bytes 786440 | tf_op jit(solution)/shard_map/ppermute | solution.py:32
  74.6 1.4 copy-start
  75.9 1.0 copy-start.1
  83.0 4.6 %collective-permute-start.30 = (bf16[128,768]{1,0:T(8,128)(2,1)S(1)}, bf16[128,768]{1,0:T(8,128)(2,1)S(1)}, u32[]{:S(2)}, u32[]{:S(2)}) collective-permute-start(bf16[128,768]{1,0:T(8,128)(2,1)S(1)} %shard_map.28.refs_0_.refs_8_), channel_id=1, source_target_pairs={{0,4},{4,0},{1,5},{5,1},{2,6},{6,2},{3,7},{7,3},{8,12},{12,8},{9,1... | collective-permute-start | bytes 589832 | tf_op jit(solution)/shard_map/ppermute | solution.py:54
  83.1 5.8 %collective-permute-start.24 = (bf16[128,768]{1,0:T(8,128)(2,1)S(1)}, bf16[128,768]{1,0:T(8,128)(2,1)S(1)}, u32[]{:S(2)}, u32[]{:S(2)}) collective-permute-start(bf16[128,768]{1,0:T(8,128)(2,1)S(1)} %shard_map.28.refs_0_.refs_8_), channel_id=1, source_target_pairs={{0,56},{8,0},{16,8},{24,16},{32,24},{40,32},{48,40},{56,48},{64,72... | collective-permute-start | bytes 589832 | tf_op jit(solution)/shard_map/ppermute | solution.py:32
  83.2 5.7 %collective-permute-start.23 = (bf16[128,768]{1,0:T(8,128)(2,1)S(1)}, bf16[128,768]{1,0:T(8,128)(2,1)S(1)}, u32[]{:S(2)}, u32[]{:S(2)}) collective-permute-start(bf16[128,768]{1,0:T(8,128)(2,1)S(1)} %shard_map.28.refs_0_.refs_8_), channel_id=1, source_target_pairs={{0,8},{8,16},{16,24},{24,32},{32,40},{40,48},{48,56},{56,0},{64,12... | collective-permute-start | bytes 589832 | tf_op jit(solution)/shard_map/ppermute | solution.py:32
  87.6 11.3 %collective-permute-start.33 = (bf16[2,128,768]{2,1,0:T(8,128)(2,1)S(1)}, bf16[2,128,768]{2,1,0:T(8,128)(2,1)S(1)}, u32[]{:S(2)}, u32[]{:S(2)}) collective-permute-start(bf16[2,128,768]{2,1,0:T(8,128)(2,1)S(1)} %pad_maximum_fusion.2), channel_id=1, source_target_pairs={{0,1},{1,2},{2,3},{3,0},{4,5},{5,6},{6,7},{7,4},{8,9},{9,10},{10,1... | collective-permute-start | bytes 1179656 | tf_op jit(solution)/shard_map/ppermute | solution.py:220
  88.9 5.7 %collective-permute-start.26 = (bf16[128,768]{1,0:T(8,128)(2,1)S(1)}, bf16[128,768]{1,0:T(8,128)(2,1)S(1)}, u32[]{:S(2)}, u32[]{:S(2)}) collective-permute-start(bf16[128,768]{1,0:T(8,128)(2,1)S(1)} %collective-permute-done.24.refs_2_), channel_id=1, source_target_pairs={{0,56},{8,0},{16,8},{24,16},{32,24},{40,32},{48,40},{56,48},{64,72... | collective-permute-start | bytes 589832 | tf_op jit(solution)/shard_map/ppermute | solution.py:32
  88.9 6.6 %collective-permute-start.25 = (bf16[128,768]{1,0:T(8,128)(2,1)S(1)}, bf16[128,768]{1,0:T(8,128)(2,1)S(1)}, u32[]{:S(2)}, u32[]{:S(2)}) collective-permute-start(bf16[128,768]{1,0:T(8,128)(2,1)S(1)} %collective-permute-done.23.refs_1_), channel_id=1, source_target_pairs={{0,8},{8,16},{16,24},{24,32},{32,40},{40,48},{48,56},{56,0},{64,12... | collective-permute-start | bytes 589832 | tf_op jit(solution)/shard_map/ppermute | solution.py:32
  91.6 11.0 %collective-permute-start.32 = (bf16[2,128,768]{2,1,0:T(8,128)(2,1)S(1)}, bf16[2,128,768]{2,1,0:T(8,128)(2,1)S(1)}, u32[]{:S(2)}, u32[]{:S(2)}) collective-permute-start(bf16[2,128,768]{2,1,0:T(8,128)(2,1)S(1)} %pad_maximum_fusion.2), channel_id=1, source_target_pairs={{0,2},{1,3},{2,0},{3,1},{4,6},{5,7},{6,4},{7,5},{8,10},{9,11},{10,... | collective-permute-start | bytes 1179656 | tf_op jit(solution)/shard_map/ppermute | solution.py:220
  94.1 13.9 %collective-permute-start.31 = (bf16[2,128,768]{2,1,0:T(8,128)(2,1)S(1)}, bf16[2,128,768]{2,1,0:T(8,128)(2,1)S(1)}, u32[]{:S(2)}, u32[]{:S(2)}) collective-permute-start(bf16[2,128,768]{2,1,0:T(8,128)(2,1)S(1)} %pad_maximum_fusion.2), channel_id=1, source_target_pairs={{0,3},{1,0},{2,1},{3,2},{4,7},{5,4},{6,5},{7,6},{8,11},{9,8},{10,9... | collective-permute-start | bytes 1179656 | tf_op jit(solution)/shard_map/ppermute | solution.py:220
  94.6 13.4 %collective-permute-start.28 = (bf16[128,768]{1,0:T(8,128)(2,1)S(1)}, bf16[128,768]{1,0:T(8,128)(2,1)S(1)}, u32[]{:S(2)}, u32[]{:S(2)}) collective-permute-start(bf16[128,768]{1,0:T(8,128)(2,1)S(1)} %collective-permute-done.26.refs_4_), channel_id=1, source_target_pairs={{0,56},{8,0},{16,8},{24,16},{32,24},{40,32},{48,40},{56,48},{64,72... | collective-permute-start | bytes 589832 | tf_op jit(solution)/shard_map/ppermute | solution.py:32
  95.5 7.1 %collective-permute-start.27 = (bf16[128,768]{1,0:T(8,128)(2,1)S(1)}, bf16[128,768]{1,0:T(8,128)(2,1)S(1)}, u32[]{:S(2)}, u32[]{:S(2)}) collective-permute-start(bf16[128,768]{1,0:T(8,128)(2,1)S(1)} %collective-permute-done.25.refs_3_), channel_id=1, source_target_pairs={{0,8},{8,16},{16,24},{24,32},{32,40},{40,48},{48,56},{56,0},{64,12... | collective-permute-start | bytes 589832 | tf_op jit(solution)/shard_map/ppermute | solution.py:32
  102.7 5.7 %collective-permute-start.29 = (bf16[128,768]{1,0:T(8,128)(2,1)S(1)}, bf16[128,768]{1,0:T(8,128)(2,1)S(1)}, u32[]{:S(2)}, u32[]{:S(2)}) collective-permute-start(bf16[128,768]{1,0:T(8,128)(2,1)S(1)} %collective-permute-done.27.refs_5_), channel_id=1, source_target_pairs={{0,8},{8,16},{16,24},{24,32},{32,40},{40,48},{48,56},{56,0},{64,12... | collective-permute-start | bytes 589832 | tf_op jit(solution)/shard_map/ppermute | solution.py:32
  114.1 15.6 %collective-permute-start.34 = (bf16[16,128,256]{2,1,0:T(8,128)(2,1)S(1)}, bf16[16,128,256]{2,1,0:T(8,128)(2,1)S(1)}, u32[]{:S(2)}, u32[]{:S(2)}) collective-permute-start(bf16[16,128,256]{2,1,0:T(8,128)(2,1)S(1)} %shard_map.29), channel_id=1, source_target_pairs={{0,64},{64,0},{1,65},{65,1},{2,66},{66,2},{3,67},{67,3},{4,68},{68... | collective-permute-start | bytes 3145736 | tf_op jit(solution)/shard_map/ppermute | solution.py:54

commit v2 on v1

--- a/solution.py
+++ b/solution.py
@@ -13,7 +13,6 @@
 N = 8192
 OCC = 768
 COLS = OCC // 2
-WIDTH = 128
 F32 = jnp.float32
 BF16 = jnp.bfloat16
 
@@ -72,12 +71,12 @@
                 self.blocks.append(self.bwd)
         return self
 
-    def finish(self):
-        return self.step(self.size // 2 - self.k).blocks
-
     def wait_for(self, *others):
         self.fwd, self.bwd, *others = lax.optimization_barrier((self.fwd, self.bwd, *others))
         return others
+
+    def finish(self):
+        return self.step(self.size // 2 - self.k).blocks
 
 
 def ring_gather(x, axis):
@@ -86,51 +85,47 @@
     return Ring(x, axis).finish()
 
 
-def gathered_by_exchange(x, axes):
-    size = 1
-    for axis in axes:
-        size *= SIZES[AXES.index(axis)]
-    return lax.all_to_all(jnp.broadcast_to(x, (size, *x.shape)), axes, 0, 0, tiled=True)
-
-
-def dot(lhs, rhs):
-    return jnp.dot(lhs, rhs, preferred_element_type=F32)
-
-
-def half_kernel(own_ref, sib_ref, *refs):
-    by_z, by_y, by_x, out = refs[:8], refs[8:12], refs[12:14], refs[14]
+def by_y_kernel(x_ref, out_ref):
+    for y in range(NY):
+        for k in range(NZ * NX):
+            out_ref[y, :, k * ROWS : (k + 1) * ROWS] = x_ref[:, (k * NY + y) * ROWS : (k * NY + y + 1) * ROWS]
+
+
+def columns_by_y(x):
+    return pl.pallas_call(
+        by_y_kernel, out_shape=jax.ShapeDtypeStruct((NY, ROWS, N // NY), BF16)
+    )(x)
+
+
+def partial_kernel(own_ref, sib_ref, *refs):
+    chunks, out, rhs, sems = refs[:8], refs[8], refs[9], refs[10]
     sign = 1 - 2 * lax.axis_index("core")
-    x, y = lax.axis_index("x_lo"), lax.axis_index("y")
-    z_line = [(lax.axis_index("z") + sign * off) % NZ for off in RING["z"]]
-    depth = NZ * ROWS
-
-    def plane(ref, z):
-        return ref[:, pl.ds(pl.multiple_of(z * NX * NY * ROWS, ROWS), NX * NY * ROWS)]
-
-    def line(ref, dx, off):
-        start = (((x + dx) % NX) * NY + (y + sign * off) % NY) * ROWS
-        cols = [pl.multiple_of(z * NX * NY * ROWS + start, ROWS) for z in z_line]
-        return jnp.concatenate([ref[:, pl.ds(c, ROWS)] for c in cols], axis=1)
-
+    z, x = lax.axis_index("z"), lax.axis_index("x_lo")
+    copies = []
+    for k, off in enumerate(RING["z"]):
+        for dx in range(NX):
+            slot = ((z + sign * off) % NZ) * NX + (x + dx) % NX
+            dst = rhs.at[pl.ds(pl.multiple_of(slot * ROWS, ROWS), ROWS)]
+            copies.append(pltpu.make_async_copy(chunks[k].at[pl.ds(dx * ROWS, ROWS)], dst, sems.at[2 * k + dx]))
+    for c in copies:
+        c.start()
+    for c in copies:
+        c.wait()
     for p, ref in enumerate((own_ref, sib_ref)):
-        totals = [jnp.zeros((ROWS, WIDTH), F32) for _ in range(3)]
-        for k, z in enumerate(z_line):
-            totals[0] += dot(plane(ref, z), by_z[k][...])
-        for k, off in enumerate(RING["y"]):
-            for dx in range(NX):
-                lhs = line(ref, dx, off)
-                totals[1] += dot(lhs, by_y[k][dx * depth : (dx + 1) * depth])
-                totals[2] += dot(lhs, by_x[dx][k * depth : (k + 1) * depth])
-        for k, total in enumerate(totals):
-            out[:, (3 * p + k) * WIDTH : (3 * p + k + 1) * WIDTH] = total.astype(BF16)
-
-
-def half_blocks(own, sib, by_z, by_y, by_x):
-    return pl.pallas_call(
-        half_kernel,
-        out_shape=jax.ShapeDtypeStruct((ROWS, OCC), BF16),
+        prod = jnp.dot(ref[...].reshape(NY * ROWS, N // NY), rhs[...], preferred_element_type=F32)
+        out[:, :, p * COLS : (p + 1) * COLS] = prod.reshape(NY, ROWS, COLS)
+
+
+def partial_half(own, sib, chunks):
+    anyspace = pl.BlockSpec(memory_space=pl.ANY)
+    vmem = pl.BlockSpec(memory_space=pltpu.VMEM)
+    return pl.pallas_call(
+        partial_kernel,
+        in_specs=[vmem, vmem] + [anyspace] * 8,
+        out_shape=jax.ShapeDtypeStruct((NY, ROWS, OCC), F32),
+        scratch_shapes=[pltpu.VMEM((N // NY, COLS), BF16), pltpu.SemaphoreType.DMA((16,))],
         compiler_params=pltpu.CompilerParams(vmem_limit_bytes=48 << 20),
-    )(own, sib, *by_z, *by_y, *by_x)
+    )(own, sib, *chunks)
 
 
 def tile_kernel(keep, *refs):
@@ -199,21 +194,15 @@
 
 
 def body(integrals, orbitals):
-    own = integrals[0]
-    sib = swap(own, ("core",), (1,))
+    own = lax.all_to_all(columns_by_y(integrals[0]), "y", 0, 0, tiled=True)
     core = lax.axis_index("core")
     mine = lax.dynamic_slice(orbitals, (0, core * COLS), (ROWS, COLS))
-    plane = gathered_by_exchange(mine[:, :WIDTH], ("x_lo", "y")).reshape(NX * NY * ROWS, WIDTH)
-    line_ring = Ring(mine[:, WIDTH:], "z").step()
-    (plane,) = line_ring.wait_for(plane)
-    line_ring.step(2)
-    plane_ring = Ring(plane, "z").step()
-    plane_ring.fwd, plane_ring.bwd = line_ring.wait_for(plane_ring.fwd, plane_ring.bwd)
-    lines = jnp.concatenate(line_ring.finish(), axis=0)
-    by_z = plane_ring.finish()
-    by_y = ring_gather(jnp.concatenate(ring_gather(lines[:, :WIDTH], "x"), axis=0), "y")
-    by_x = ring_gather(jnp.concatenate(ring_gather(lines[:, WIDTH:], "y"), axis=0), "x")
-    half = half_blocks(own, sib, by_z, by_y, by_x)
+    ring = Ring(jnp.concatenate(ring_gather(mine, "x"), axis=0), "z").step(3)
+    (own,) = ring.wait_for(own)
+    sib = swap(own, ("core",), (1,))
+    chunks = ring.finish()
+    parts = lax.all_to_all(partial_half(own, sib, chunks), "y", 0, 0, tiled=True)
+    half = parts.sum(axis=0).astype(BF16)
 
     z_blocks = ring_gather(half, "z")
     pair = jnp.stack([half, swap(half, ("x_lo",), (1,))])

time: 159 us -> 154 us (0.969)
  blocking collectives: 20.6 us -> 43.3 us
  starting transfers between devices: 67 us -> 45.3 us
  waiting for transfers between devices: 45.7 us -> 39.5 us
  Pallas kernels: 20 us -> 23.7 us
  local copies, waits for them, and re-layouts: 4.81 us -> 1.43 us
    all_to_all x0 -> x1, blocking collectives: none -> 21.9 us  [body(): lax.all_to_all(partial_half(own, sib, chunks), 'y', 0, 0, tiled=True)]
    ppermute x27 -> x14, starting transfers between devices: 37.9 us -> 23.2 us  [ring_send(): return lax.ppermute(x, ('core', axis), ring_pairs(size, step))]
    ppermute x27 -> x14, waiting for transfers between devices: 35.8 us -> 25.1 us  [ring_send(): return lax.ppermute(x, ('core', axis), ring_pairs(size, step))]
    ppermute x3, waiting for transfers between devices: 5.9 us -> 10.5 us  [body(): lax.ppermute(pair, 'y', [(i, (i - s) % NY) for i in range(NY)])]
    pallas_call x1 -> x2, Pallas kernels: 6.1 us -> 9.7 us  [the longest x1 6.36 us: partial_half(): pl.pallas_call(partial_kernel, in_specs=[vmem, vmem] + [anyspace] * 8, ou...]
    ppermute x3, starting transfers between devices: 14.7 us -> 11.3 us  [swap(): return lax.ppermute(x, axes, [(i, i ^ mask) for i in range(total)])]
    ppermute x2 -> x1, starting transfers between devices: 5.83 us -> 2.56 us  [x_send(): return lax.ppermute(x, ('x_hi', 'core', 'x_lo'), pairs)]
    unnamed x11 -> x4, local copies, waits for them, and re-layouts: 3.19 us -> 1.34 us
  transfers between devices with their start and end apart: 36 -> 22, of which waited for: 19 -> 12; matrix products, arithmetic and copies ran while one was open for 1% -> 0% of each run, Pallas kernels for 0% -> 0%
where the time goes in v2:
time: 154 us
  starting transfers between devices  45.3 us (29%)
  blocking collectives  43.3 us (28%)
  waiting for transfers between devices  39.5 us (26%)
  Pallas kernels  23.7 us (15%)
    ppermute x14, waiting for transfers between devices, ring_send(): return lax.ppermute(x, ('core', axis), ring_pairs(size, step))  25.1 us
    ppermute x14, starting transfers between devices, ring_send(): return lax.ppermute(x, ('core', axis), ring_pairs(size, step))  23.2 us
    all_to_all x1, blocking collectives, body(): lax.all_to_all(partial_half(own, sib, chunks), 'y', 0, 0, tiled=True)  21.9 us
    all_to_all x1, blocking collectives, body(): pieces = lax.all_to_all(mine, ('x_hi', 'x_lo', 'y'), 0, 0, tiled=True)  21.5 us
    pallas_call x2, Pallas kernels, tile_product(): pl.pallas_call(lambda *refs: tile_kernel(keep, *refs), in_specs=[anyspace...  11.7 us
    ppermute x3, starting transfers between devices, swap(): return lax.ppermute(x, axes, [(i, i ^ mask) for i in range(total)])  11.3 us
    ppermute x3, waiting for transfers between devices, body(): lax.ppermute(pair, 'y', [(i, (i - s) % NY) for i in range(NY)])  10.5 us
    pallas_call x1, Pallas kernels, partial_half(): pl.pallas_call(partial_kernel, in_specs=[vmem, vmem] + [anyspace] * 8, ou...  6.36 us
  transfers between devices with their start and end apart: 22, of which 12 were waited for; matrix products, arithmetic and copies ran while one was open for 0% of the time, Pallas kernels for 0%

profile of v2, /device:TPU:1, one launch (start us, length us, event | category | flops | bytes accessed | tf_op | source)
XLA Modules:
  0.0 153.6 jit_solution(1766711895410472500)
XLA Ops:
  0.0 3.3 %shard_map.28 = bf16[4,128,2048]{2,1,0:T(8,128)(2,1)} custom-call(bf16[128,8192]{1,0:T(8,128)(2,1)} %bitcast.17), custom_call_target="tpu_custom_call" | custom-call | tf_op jit(solution)/shard_map/pallas_call | solution.py:95
  3.3 5.0 %all-to-all-start = ((bf16[4,128,2048]{2,1,0:T(8,128)(2,1)}), bf16[4,128,2048]{2,1,0:T(8,128)(2,1)S(1)}, u32[]{:S(2)}, u32[]{:S(2)}) async-start(bf16[4,128,2048]{2,1,0:T(8,128)(2,1)} %shard_map.28), calls=%async_computation | async-start | bytes 4194304 | tf_op jit(solution)/shard_map/all_to_all | solution.py:197
  8.4 2.6 %collective-permute-start = (bf16[128,384]{1,0:T(8,128)(2,1)S(1)}, bf16[128,384]{1,0:T(8,128)(2,1)S(1)}, u32[]{:S(2)}, u32[]{:S(2)}) collective-permute-start(bf16[128,384]{1,0:T(8,128)(2,1)S(1)} %constant_dynamic-slice_fusion), channel_id=1, source_target_pairs={{0,4},{4,128},{128,132},{132,0},{64,196},{68,64},{192,68},{196,192... | collective-permute-start | bytes 294920 | tf_op jit(solution)/shard_map/ppermute | solution.py:42
  10.9 1.6 %collective-permute-done = bf16[128,384]{1,0:T(8,128)(2,1)S(1)} collective-permute-done((bf16[128,384]{1,0:T(8,128)(2,1)S(1)}, bf16[128,384]{1,0:T(8,128)(2,1)S(1)}, u32[]{:S(2)}, u32[]{:S(2)}) %collective-permute-start) | collective-permute-done | bytes 98336 | tf_op jit(solution)/shard_map/ppermute | solution.py:42
  12.6 1.7 %collective-permute-start.4 = (bf16[256,384]{1,0:T(8,128)(2,1)S(1)}, bf16[256,384]{1,0:T(8,128)(2,1)S(1)}, u32[]{:S(2)}, u32[]{:S(2)}) collective-permute-start(bf16[256,384]{1,0:T(8,128)(2,1)S(1)} %pad_maximum_fusion.1.refs_0_), channel_id=1, source_target_pairs={{0,56},{8,0},{16,8},{24,16},{32,24},{40,32},{48,40},{56,48},{64,72... | collective-permute-start | bytes 589832 | tf_op jit(solution)/shard_map/ppermute | solution.py:31
  14.3 4.0 %collective-permute-start.1 = (bf16[256,384]{1,0:T(8,128)(2,1)S(1)}, bf16[256,384]{1,0:T(8,128)(2,1)S(1)}, u32[]{:S(2)}, u32[]{:S(2)}) collective-permute-start(bf16[256,384]{1,0:T(8,128)(2,1)S(1)} %pad_maximum_fusion.1.refs_0_), channel_id=1, source_target_pairs={{0,8},{8,16},{16,24},{24,32},{32,40},{40,48},{48,56},{56,0},{64,12... | collective-permute-start | bytes 589832 | tf_op jit(solution)/shard_map/ppermute | solution.py:31
  18.3 3.3 %collective-permute-done.4.refs_2_ = bf16[256,384]{1,0:T(8,128)(2,1)S(1)} collective-permute-done((bf16[256,384]{1,0:T(8,128)(2,1)S(1)}, bf16[256,384]{1,0:T(8,128)(2,1)S(1)}, u32[]{:S(2)}, u32[]{:S(2)}) %collective-permute-start.4) | collective-permute-done | bytes 196640 | tf_op jit(solution)/shard_map/ppermute | solution.py:31
  21.6 0.0 collective-permute-start.5
  21.6 0.0 collective-permute-done.1.refs_1_
  21.6 2.8 %collective-permute-start.2 = (bf16[256,384]{1,0:T(8,128)(2,1)S(1)}, bf16[256,384]{1,0:T(8,128)(2,1)S(1)}, u32[]{:S(2)}, u32[]{:S(2)}) collective-permute-start(bf16[256,384]{1,0:T(8,128)(2,1)S(1)} %collective-permute-done.1.refs_1_), channel_id=1, source_target_pairs={{0,8},{8,16},{16,24},{24,32},{32,40},{40,48},{48,56},{56,0},{64,12... | collective-permute-start | bytes 589832 | tf_op jit(solution)/shard_map/ppermute | solution.py:31
  24.4 5.3 %collective-permute-done.5.refs_4_ = bf16[256,384]{1,0:T(8,128)(2,1)S(1)} collective-permute-done((bf16[256,384]{1,0:T(8,128)(2,1)S(1)}, bf16[256,384]{1,0:T(8,128)(2,1)S(1)}, u32[]{:S(2)}, u32[]{:S(2)}) %collective-permute-start.5) | collective-permute-done | bytes 196640 | tf_op jit(solution)/shard_map/ppermute | solution.py:31
  29.7 0.0 collective-permute-start.6
  29.7 0.0 collective-permute-done.2.refs_3_
  29.7 2.7 %collective-permute-start.3 = (bf16[256,384]{1,0:T(8,128)(2,1)S(1)}, bf16[256,384]{1,0:T(8,128)(2,1)}, u32[]{:S(2)}, u32[]{:S(2)}) collective-permute-start(bf16[256,384]{1,0:T(8,128)(2,1)S(1)} %collective-permute-done.2.refs_3_), channel_id=1, source_target_pairs={{0,8},{8,16},{16,24},{24,32},{32,40},{40,48},{48,56},{56,0},{64,12... | collective-permute-start | bytes 589832 | tf_op jit(solution)/shard_map/ppermute | solution.py:31
  32.4 4.6 %collective-permute-done.6.refs_6_ = bf16[256,384]{1,0:T(8,128)(2,1)S(1)} collective-permute-done((bf16[256,384]{1,0:T(8,128)(2,1)S(1)}, bf16[256,384]{1,0:T(8,128)(2,1)S(1)}, u32[]{:S(2)}, u32[]{:S(2)}) %collective-permute-start.6) | collective-permute-done | bytes 196640 | tf_op jit(solution)/shard_map/ppermute | solution.py:31
  36.9 0.0 collective-permute-done.3.refs_5_
  36.9 8.3 %collective-permute-start.7 = (bf16[4,128,2048]{2,1,0:T(8,128)(2,1)S(1)}, bf16[4,128,2048]{2,1,0:T(8,128)(2,1)S(1)}, u32[]{:S(2)}, u32[]{:S(2)}) collective-permute-start(bf16[4,128,2048]{2,1,0:T(8,128)(2,1)S(1)} %all-to-all-done.own_ref), channel_id=1, source_target_pairs={{0,64},{64,0},{1,65},{65,1},{2,66},{66,2},{3,67},{67,3},{4,68},{68... | collective-permute-start | bytes 6291464 | tf_op jit(solution)/shard_map/ppermute | solution.py:53
  45.2 5.0 %collective-permute-done.8.refs_7_ = bf16[256,384]{1,0:T(8,128)(2,1)S(1)} collective-permute-done((bf16[256,384]{1,0:T(8,128)(2,1)}, bf16[256,384]{1,0:T(8,128)(2,1)S(1)}, u32[]{:S(2)}, u32[]{:S(2)}) %collective-permute-start.8) | collective-permute-done | bytes 196640 | tf_op jit(solution)/shard_map/ppermute | solution.py:31
  50.2 0.0 collective-permute-done.7.sib_ref
  50.2 1.3 copy-done.1
  51.6 6.4 %shard_map.29 = f32[4,128,768]{2,1,0:T(8,128)S(1)} custom-call(bf16[4,128,2048]{2,1,0:T(8,128)(2,1)S(1)} %all-to-all-done.own_ref, bf16[4,128,2048]{2,1,0:T(8,128)(2,1)} %copy-done.1, bf16[256,384]{1,0:T(8,128)(2,1)S(1)} %pad_maximum_fusion.1.refs_0_, bf16[256,384]{1,0:T(8,128)(2,1)S(1)} %collective-permute-done.1.refs_1_, ...), custom_call_target="tpu_custom_call" | custom-call | tf_op jit(solution)/shard_map/pallas_call | solution.py:122
  57.9 21.9 %all_to_all.15 = f32[4,128,768]{2,1,0:T(8,128)S(1)} all-to-all(f32[4,128,768]{2,1,0:T(8,128)S(1)} %shard_map.29), channel_id=1, replica_groups=mesh['x_hi'=2,'core'=2,'z'=8,'x_lo'=2,'y'=4] {'y'}, dimensions={0} | all-to-all | bytes 3145728 | tf_op jit(solution)/shard_map/all_to_all | solution.py:204
  79.8 0.1 reduce_sum.9.refs_0_.refs_8_
  79.9 2.4 %collective-permute-start.9 = (bf16[128,768]{1,0:T(8,128)(2,1)S(1)}, bf16[128,768]{1,0:T(8,128)(2,1)S(1)}, u32[]{:S(2)}, u32[]{:S(2)}) collective-permute-start(bf16[128,768]{1,0:T(8,128)(2,1)S(1)} %reduce_sum.9.refs_0_.refs_8_), channel_id=1, source_target_pairs={{0,8},{8,16},{16,24},{24,32},{32,40},{40,48},{48,56},{56,0},{64,12... | collective-permute-start | bytes 589832 | tf_op jit(solution)/shard_map/ppermute | solution.py:31
  82.2 0.8 collective-permute-start.16
  83.0 0.0 collective-permute-start.10
  83.0 1.8 %collective-permute-done.9.refs_1_ = bf16[128,768]{1,0:T(8,128)(2,1)S(1)} collective-permute-done((bf16[128,768]{1,0:T(8,128)(2,1)S(1)}, bf16[128,768]{1,0:T(8,128)(2,1)S(1)}, u32[]{:S(2)}, u32[]{:S(2)}) %collective-permute-start.9) | collective-permute-done | bytes 196640 | tf_op jit(solution)/shard_map/ppermute | solution.py:31
  84.9 3.1 %collective-permute-start.11 = (bf16[128,768]{1,0:T(8,128)(2,1)S(1)}, bf16[128,768]{1,0:T(8,128)(2,1)S(1)}, u32[]{:S(2)}, u32[]{:S(2)}) collective-permute-start(bf16[128,768]{1,0:T(8,128)(2,1)S(1)} %collective-permute-done.9.refs_1_), channel_id=1, source_target_pairs={{0,8},{8,16},{16,24},{24,32},{32,40},{40,48},{48,56},{56,0},{64,12... | collective-permute-start | bytes 589832 | tf_op jit(solution)/shard_map/ppermute | solution.py:31
  88.0 0.5 collective-permute-start.19
  88.6 2.0 %collective-permute-done.10.refs_2_ = bf16[128,768]{1,0:T(8,128)(2,1)S(1)} collective-permute-done((bf16[128,768]{1,0:T(8,128)(2,1)S(1)}, bf16[128,768]{1,0:T(8,128)(2,1)S(1)}, u32[]{:S(2)}, u32[]{:S(2)}) %collective-permute-start.10) | collective-permute-done | bytes 196640 | tf_op jit(solution)/shard_map/ppermute | solution.py:31
  90.6 0.0 collective-permute-start.12
  90.6 1.9 %collective-permute-done.11.refs_3_ = bf16[128,768]{1,0:T(8,128)(2,1)S(1)} collective-permute-done((bf16[128,768]{1,0:T(8,128)(2,1)S(1)}, bf16[128,768]{1,0:T(8,128)(2,1)S(1)}, u32[]{:S(2)}, u32[]{:S(2)}) %collective-permute-start.11) | collective-permute-done | bytes 196640 | tf_op jit(solution)/shard_map/ppermute | solution.py:31
  92.5 3.2 %collective-permute-start.13 = (bf16[128,768]{1,0:T(8,128)(2,1)S(1)}, bf16[128,768]{1,0:T(8,128)(2,1)S(1)}, u32[]{:S(2)}, u32[]{:S(2)}) collective-permute-start(bf16[128,768]{1,0:T(8,128)(2,1)S(1)} %collective-permute-done.11.refs_3_), channel_id=1, source_target_pairs={{0,8},{8,16},{16,24},{24,32},{32,40},{40,48},{48,56},{56,0},{64,12... | collective-permute-start | bytes 589832 | tf_op jit(solution)/shard_map/ppermute | solution.py:31
  95.6 0.5 collective-permute-start.18
  96.1 2.1 %collective-permute-start.17 = (bf16[2,128,768]{2,1,0:T(8,128)(2,1)S(1)}, bf16[2,128,768]{2,1,0:T(8,128)(2,1)S(1)}, u32[]{:S(2)}, u32[]{:S(2)}) collective-permute-start(bf16[2,128,768]{2,1,0:T(8,128)(2,1)S(1)} %pad_maximum_fusion), channel_id=1, source_target_pairs={{0,3},{1,0},{2,1},{3,2},{4,7},{5,4},{6,5},{7,6},{8,11},{9,8},{10,9... | collective-permute-start | bytes 1179656 | tf_op jit(solution)/shard_map/ppermute | solution.py:209
  98.3 0.0 collective-permute-done.12.refs_4_
  98.3 0.0 collective-permute-start.14
  98.3 1.2 collective-permute-done.13.refs_5_
  99.5 3.4 %collective-permute-start.15 = (bf16[128,768]{1,0:T(8,128)(2,1)S(1)}, bf16[128,768]{1,0:T(8,128)(2,1)S(1)}, u32[]{:S(2)}, u32[]{:S(2)}) collective-permute-start(bf16[128,768]{1,0:T(8,128)(2,1)S(1)} %collective-permute-done.13.refs_5_), channel_id=1, source_target_pairs={{0,8},{8,16},{16,24},{24,32},{32,40},{40,48},{48,56},{56,0},{64,12... | collective-permute-start | bytes 589832 | tf_op jit(solution)/shard_map/ppermute | solution.py:31
  102.9 1.8 %collective-permute-done.18 = bf16[2,128,768]{2,1,0:T(8,128)(2,1)S(1)} collective-permute-done((bf16[2,128,768]{2,1,0:T(8,128)(2,1)S(1)}, bf16[2,128,768]{2,1,0:T(8,128)(2,1)S(1)}, u32[]{:S(2)}, u32[]{:S(2)}) %collective-permute-start.18) | collective-permute-done | bytes 393248 | tf_op jit(solution)/shard_map/ppermute | solution.py:209
  104.7 8.7 %collective-permute-done.17 = bf16[2,128,768]{2,1,0:T(8,128)(2,1)S(1)} collective-permute-done((bf16[2,128,768]{2,1,0:T(8,128)(2,1)S(1)}, bf16[2,128,768]{2,1,0:T(8,128)(2,1)S(1)}, u32[]{:S(2)}, u32[]{:S(2)}) %collective-permute-start.17) | collective-permute-done | bytes 393248 | tf_op jit(solution)/shard_map/ppermute | solution.py:209
  113.5 0.0 collective-permute-done.15.refs_7_
  113.5 5.9 %shard_map.30 = bf16[16,128,256]{2,1,0:T(8,128)(2,1)S(1)} custom-call(bf16[128,768]{1,0:T(8,128)(2,1)S(1)} %reduce_sum.9.refs_0_.refs_8_, bf16[128,768]{1,0:T(8,128)(2,1)S(1)} %collective-permute-done.9.refs_1_, bf16[128,768]{1,0:T(8,128)(2,1)S(1)} %collective-permute-done.10.refs_2_, bf16[128,768]{1,0:T(8,128)(2,1)S(1)} %collective-permute-done.11.refs_3_, ...), custom_call_target="tpu_custom_call" | custom-call | tf_op jit(solution)/shard_map/pallas_call | solution.py:168
  119.4 2.2 %collective-permute-start.20 = (bf16[16,128,256]{2,1,0:T(8,128)(2,1)S(1)}, bf16[16,128,256]{2,1,0:T(8,128)(2,1)S(1)}, u32[]{:S(2)}, u32[]{:S(2)}) collective-permute-start(bf16[16,128,256]{2,1,0:T(8,128)(2,1)S(1)} %shard_map.30), channel_id=1, source_target_pairs={{0,64},{64,0},{1,65},{65,1},{2,66},{66,2},{3,67},{67,3},{4,68},{68... | collective-permute-start | bytes 3145736 | tf_op jit(solution)/shard_map/ppermute | solution.py:53
  121.6 2.3 %collective-permute-done.20.refs_16_ = bf16[16,128,256]{2,1,0:T(8,128)(2,1)S(1)} collective-permute-done((bf16[16,128,256]{2,1,0:T(8,128)(2,1)S(1)}, bf16[16,128,256]{2,1,0:T(8,128)(2,1)S(1)}, u32[]{:S(2)}, u32[]{:S(2)}) %collective-permute-start.20) | collective-permute-done | bytes 1048608 | tf_op jit(solution)/shard_map/ppermute | solution.py:53
  123.9 5.8 %shard_map.31 = bf16[16,128,256]{2,1,0:T(8,128)(2,1)S(1)} custom-call(bf16[128,768]{1,0:T(8,128)(2,1)S(1)} %reduce_sum.9.refs_0_.refs_8_, bf16[128,768]{1,0:T(8,128)(2,1)S(1)} %collective-permute-done.9.refs_1_, bf16[128,768]{1,0:T(8,128)(2,1)S(1)} %collective-permute-done.10.refs_2_, bf16[128,768]{1,0:T(8,128)(2,1)S(1)} %collective-permute-done.11.refs_3_, ...), custom_call_target="tpu_custom_call" | custom-call | tf_op jit(solution)/shard_map/pallas_call | solution.py:168
  129.7 21.5 %all_to_all.16.pieces = bf16[16,128,256]{2,1,0:T(8,128)(2,1)} all-to-all(bf16[16,128,256]{2,1,0:T(8,128)(2,1)S(1)} %shard_map.31), channel_id=1, replica_groups=mesh['x_hi'=2,'core'=2,'z'=8,'x_lo'=2,'y'=4] {'x_hi','x_lo','y'}, dimensions={0} | all-to-all | bytes 2097152 | tf_op jit(solution)/shard_map/all_to_all | solution.py:214
  151.2 2.3 %shard_map.32 = f32[128,2048]{1,0:T(8,128)} custom-call(bf16[16,128,256]{2,1,0:T(8,128)(2,1)} %all_to_all.16.pieces), custom_call_target="tpu_custom_call" | custom-call | tf_op jit(solution)/shard_map/pallas_call | solution.py:191
  (14 shorter events, 0.2 us)
Async XLA Ops:
  0.0 8.4 %copy-start = (bf16[128,768]{1,0:T(8,128)(2,1)S(1)}, bf16[128,768]{1,0:T(8,128)(2,1)}, u32[]{:S(2)}) copy-start(bf16[128,768]{1,0:T(8,128)(2,1)} %param.3) | copy-start | bytes 589828
  3.3 33.6 %all-to-all-start = ((bf16[4,128,2048]{2,1,0:T(8,128)(2,1)}), bf16[4,128,2048]{2,1,0:T(8,128)(2,1)S(1)}, u32[]{:S(2)}, u32[]{:S(2)}) async-start(bf16[4,128,2048]{2,1,0:T(8,128)(2,1)} %shard_map.28), calls=%async_computation | async-start | bytes 4194304 | tf_op jit(solution)/shard_map/all_to_all | solution.py:197
  8.4 4.2 %collective-permute-start = (bf16[128,384]{1,0:T(8,128)(2,1)S(1)}, bf16[128,384]{1,0:T(8,128)(2,1)S(1)}, u32[]{:S(2)}, u32[]{:S(2)}) collective-permute-start(bf16[128,384]{1,0:T(8,128)(2,1)S(1)} %constant_dynamic-slice_fusion), channel_id=1, source_target_pairs={{0,4},{4,128},{128,132},{132,0},{64,196},{68,64},{192,68},{196,192... | collective-permute-start | bytes 294920 | tf_op jit(solution)/shard_map/ppermute | solution.py:42
  12.6 9.0 %collective-permute-start.4 = (bf16[256,384]{1,0:T(8,128)(2,1)S(1)}, bf16[256,384]{1,0:T(8,128)(2,1)S(1)}, u32[]{:S(2)}, u32[]{:S(2)}) collective-permute-start(bf16[256,384]{1,0:T(8,128)(2,1)S(1)} %pad_maximum_fusion.1.refs_0_), channel_id=1, source_target_pairs={{0,56},{8,0},{16,8},{24,16},{32,24},{40,32},{48,40},{56,48},{64,72... | collective-permute-start | bytes 589832 | tf_op jit(solution)/shard_map/ppermute | solution.py:31
  14.3 7.3 %collective-permute-start.1 = (bf16[256,384]{1,0:T(8,128)(2,1)S(1)}, bf16[256,384]{1,0:T(8,128)(2,1)S(1)}, u32[]{:S(2)}, u32[]{:S(2)}) collective-permute-start(bf16[256,384]{1,0:T(8,128)(2,1)S(1)} %pad_maximum_fusion.1.refs_0_), channel_id=1, source_target_pairs={{0,8},{8,16},{16,24},{24,32},{32,40},{40,48},{48,56},{56,0},{64,12... | collective-permute-start | bytes 589832 | tf_op jit(solution)/shard_map/ppermute | solution.py:31
  21.6 8.1 %collective-permute-start.5 = (bf16[256,384]{1,0:T(8,128)(2,1)S(1)}, bf16[256,384]{1,0:T(8,128)(2,1)S(1)}, u32[]{:S(2)}, u32[]{:S(2)}) collective-permute-start(bf16[256,384]{1,0:T(8,128)(2,1)S(1)} %collective-permute-done.4.refs_2_), channel_id=1, source_target_pairs={{0,56},{8,0},{16,8},{24,16},{32,24},{40,32},{48,40},{56,48},{64,72... | collective-permute-start | bytes 589832 | tf_op jit(solution)/shard_map/ppermute | solution.py:31
  21.6 8.1 %collective-permute-start.2 = (bf16[256,384]{1,0:T(8,128)(2,1)S(1)}, bf16[256,384]{1,0:T(8,128)(2,1)S(1)}, u32[]{:S(2)}, u32[]{:S(2)}) collective-permute-start(bf16[256,384]{1,0:T(8,128)(2,1)S(1)} %collective-permute-done.1.refs_1_), channel_id=1, source_target_pairs={{0,8},{8,16},{16,24},{24,32},{32,40},{40,48},{48,56},{56,0},{64,12... | collective-permute-start | bytes 589832 | tf_op jit(solution)/shard_map/ppermute | solution.py:31
  29.7 7.2 %collective-permute-start.6 = (bf16[256,384]{1,0:T(8,128)(2,1)S(1)}, bf16[256,384]{1,0:T(8,128)(2,1)S(1)}, u32[]{:S(2)}, u32[]{:S(2)}) collective-permute-start(bf16[256,384]{1,0:T(8,128)(2,1)S(1)} %collective-permute-done.5.refs_4_), channel_id=1, source_target_pairs={{0,56},{8,0},{16,8},{24,16},{32,24},{40,32},{48,40},{56,48},{64,72... | collective-permute-start | bytes 589832 | tf_op jit(solution)/shard_map/ppermute | solution.py:31
  29.7 7.2 %collective-permute-start.3 = (bf16[256,384]{1,0:T(8,128)(2,1)S(1)}, bf16[256,384]{1,0:T(8,128)(2,1)}, u32[]{:S(2)}, u32[]{:S(2)}) collective-permute-start(bf16[256,384]{1,0:T(8,128)(2,1)S(1)} %collective-permute-done.2.refs_3_), channel_id=1, source_target_pairs={{0,8},{8,16},{16,24},{24,32},{32,40},{40,48},{48,56},{56,0},{64,12... | collective-permute-start | bytes 589832 | tf_op jit(solution)/shard_map/ppermute | solution.py:31
  36.9 13.3 %collective-permute-start.7 = (bf16[4,128,2048]{2,1,0:T(8,128)(2,1)S(1)}, bf16[4,128,2048]{2,1,0:T(8,128)(2,1)S(1)}, u32[]{:S(2)}, u32[]{:S(2)}) collective-permute-start(bf16[4,128,2048]{2,1,0:T(8,128)(2,1)S(1)} %all-to-all-done.own_ref), channel_id=1, source_target_pairs={{0,64},{64,0},{1,65},{65,1},{2,66},{66,2},{3,67},{67,3},{4,68},{68... | collective-permute-start | bytes 6291464 | tf_op jit(solution)/shard_map/ppermute | solution.py:53
  45.2 5.0 %collective-permute-start.8 = (bf16[256,384]{1,0:T(8,128)(2,1)}, bf16[256,384]{1,0:T(8,128)(2,1)S(1)}, u32[]{:S(2)}, u32[]{:S(2)}) collective-permute-start(bf16[256,384]{1,0:T(8,128)(2,1)} %collective-permute-done.3.refs_5_), channel_id=1, source_target_pairs={{0,8},{8,16},{16,24},{24,32},{32,40},{40,48},{48,56},{56,0},{64,12... | collective-permute-start | bytes 589832 | tf_op jit(solution)/shard_map/ppermute | solution.py:31
  50.2 1.3 copy-start.1
  79.9 5.0 %collective-permute-start.9 = (bf16[128,768]{1,0:T(8,128)(2,1)S(1)}, bf16[128,768]{1,0:T(8,128)(2,1)S(1)}, u32[]{:S(2)}, u32[]{:S(2)}) collective-permute-start(bf16[128,768]{1,0:T(8,128)(2,1)S(1)} %reduce_sum.9.refs_0_.refs_8_), channel_id=1, source_target_pairs={{0,8},{8,16},{16,24},{24,32},{32,40},{40,48},{48,56},{56,0},{64,12... | collective-permute-start | bytes 589832 | tf_op jit(solution)/shard_map/ppermute | solution.py:31
  82.2 5.7 %collective-permute-start.16 = (bf16[128,768]{1,0:T(8,128)(2,1)S(1)}, bf16[128,768]{1,0:T(8,128)(2,1)S(1)}, u32[]{:S(2)}, u32[]{:S(2)}) collective-permute-start(bf16[128,768]{1,0:T(8,128)(2,1)S(1)} %reduce_sum.9.refs_0_.refs_8_), channel_id=1, source_target_pairs={{0,4},{4,0},{1,5},{5,1},{2,6},{6,2},{3,7},{7,3},{8,12},{12,8},{9,1... | collective-permute-start | bytes 589832 | tf_op jit(solution)/shard_map/ppermute | solution.py:53
  83.0 7.5 %collective-permute-start.10 = (bf16[128,768]{1,0:T(8,128)(2,1)S(1)}, bf16[128,768]{1,0:T(8,128)(2,1)S(1)}, u32[]{:S(2)}, u32[]{:S(2)}) collective-permute-start(bf16[128,768]{1,0:T(8,128)(2,1)S(1)} %reduce_sum.9.refs_0_.refs_8_), channel_id=1, source_target_pairs={{0,56},{8,0},{16,8},{24,16},{32,24},{40,32},{48,40},{56,48},{64,72... | collective-permute-start | bytes 589832 | tf_op jit(solution)/shard_map/ppermute | solution.py:31
  84.9 7.6 %collective-permute-start.11 = (bf16[128,768]{1,0:T(8,128)(2,1)S(1)}, bf16[128,768]{1,0:T(8,128)(2,1)S(1)}, u32[]{:S(2)}, u32[]{:S(2)}) collective-permute-start(bf16[128,768]{1,0:T(8,128)(2,1)S(1)} %collective-permute-done.9.refs_1_), channel_id=1, source_target_pairs={{0,8},{8,16},{16,24},{24,32},{32,40},{40,48},{48,56},{56,0},{64,12... | collective-permute-start | bytes 589832 | tf_op jit(solution)/shard_map/ppermute | solution.py:31
  88.0 14.9 %collective-permute-start.19 = (bf16[2,128,768]{2,1,0:T(8,128)(2,1)S(1)}, bf16[2,128,768]{2,1,0:T(8,128)(2,1)S(1)}, u32[]{:S(2)}, u32[]{:S(2)}) collective-permute-start(bf16[2,128,768]{2,1,0:T(8,128)(2,1)S(1)} %pad_maximum_fusion), channel_id=1, source_target_pairs={{0,1},{1,2},{2,3},{3,0},{4,5},{5,6},{6,7},{7,4},{8,9},{9,10},{10,1... | collective-permute-start | bytes 1179656 | tf_op jit(solution)/shard_map/ppermute | solution.py:209
  90.6 7.7 %collective-permute-start.12 = (bf16[128,768]{1,0:T(8,128)(2,1)S(1)}, bf16[128,768]{1,0:T(8,128)(2,1)S(1)}, u32[]{:S(2)}, u32[]{:S(2)}) collective-permute-start(bf16[128,768]{1,0:T(8,128)(2,1)S(1)} %collective-permute-done.10.refs_2_), channel_id=1, source_target_pairs={{0,56},{8,0},{16,8},{24,16},{32,24},{40,32},{48,40},{56,48},{64,72... | collective-permute-start | bytes 589832 | tf_op jit(solution)/shard_map/ppermute | solution.py:31
  92.5 7.1 %collective-permute-start.13 = (bf16[128,768]{1,0:T(8,128)(2,1)S(1)}, bf16[128,768]{1,0:T(8,128)(2,1)S(1)}, u32[]{:S(2)}, u32[]{:S(2)}) collective-permute-start(bf16[128,768]{1,0:T(8,128)(2,1)S(1)} %collective-permute-done.11.refs_3_), channel_id=1, source_target_pairs={{0,8},{8,16},{16,24},{24,32},{32,40},{40,48},{48,56},{56,0},{64,12... | collective-permute-start | bytes 589832 | tf_op jit(solution)/shard_map/ppermute | solution.py:31
  95.6 9.1 %collective-permute-start.18 = (bf16[2,128,768]{2,1,0:T(8,128)(2,1)S(1)}, bf16[2,128,768]{2,1,0:T(8,128)(2,1)S(1)}, u32[]{:S(2)}, u32[]{:S(2)}) collective-permute-start(bf16[2,128,768]{2,1,0:T(8,128)(2,1)S(1)} %pad_maximum_fusion), channel_id=1, source_target_pairs={{0,2},{1,3},{2,0},{3,1},{4,6},{5,7},{6,4},{7,5},{8,10},{9,11},{10,... | collective-permute-start | bytes 1179656 | tf_op jit(solution)/shard_map/ppermute | solution.py:209
  96.1 17.3 %collective-permute-start.17 = (bf16[2,128,768]{2,1,0:T(8,128)(2,1)S(1)}, bf16[2,128,768]{2,1,0:T(8,128)(2,1)S(1)}, u32[]{:S(2)}, u32[]{:S(2)}) collective-permute-start(bf16[2,128,768]{2,1,0:T(8,128)(2,1)S(1)} %pad_maximum_fusion), channel_id=1, source_target_pairs={{0,3},{1,0},{2,1},{3,2},{4,7},{5,4},{6,5},{7,6},{8,11},{9,8},{10,9... | collective-permute-start | bytes 1179656 | tf_op jit(solution)/shard_map/ppermute | solution.py:209
  98.3 15.2 %collective-permute-start.14 = (bf16[128,768]{1,0:T(8,128)(2,1)S(1)}, bf16[128,768]{1,0:T(8,128)(2,1)S(1)}, u32[]{:S(2)}, u32[]{:S(2)}) collective-permute-start(bf16[128,768]{1,0:T(8,128)(2,1)S(1)} %collective-permute-done.12.refs_4_), channel_id=1, source_target_pairs={{0,56},{8,0},{16,8},{24,16},{32,24},{40,32},{48,40},{56,48},{64,72... | collective-permute-start | bytes 589832 | tf_op jit(solution)/shard_map/ppermute | solution.py:31
  99.5 14.0 %collective-permute-start.15 = (bf16[128,768]{1,0:T(8,128)(2,1)S(1)}, bf16[128,768]{1,0:T(8,128)(2,1)S(1)}, u32[]{:S(2)}, u32[]{:S(2)}) collective-permute-start(bf16[128,768]{1,0:T(8,128)(2,1)S(1)} %collective-permute-done.13.refs_5_), channel_id=1, source_target_pairs={{0,8},{8,16},{16,24},{24,32},{32,40},{40,48},{48,56},{56,0},{64,12... | collective-permute-start | bytes 589832 | tf_op jit(solution)/shard_map/ppermute | solution.py:31
  119.4 4.5 %collective-permute-start.20 = (bf16[16,128,256]{2,1,0:T(8,128)(2,1)S(1)}, bf16[16,128,256]{2,1,0:T(8,128)(2,1)S(1)}, u32[]{:S(2)}, u32[]{:S(2)}) collective-permute-start(bf16[16,128,256]{2,1,0:T(8,128)(2,1)S(1)} %shard_map.30), channel_id=1, source_target_pairs={{0,64},{64,0},{1,65},{65,1},{2,66},{66,2},{3,67},{67,3},{4,68},{68... | collective-permute-start | bytes 3145736 | tf_op jit(solution)/shard_map/ppermute | solution.py:53

commit v3 on v2

v3 whole, which is shorter than its diff:
```python
import jax
import jax.numpy as jnp
from jax import lax
from jax.experimental import pallas as pl
from jax.experimental.pallas import tpu as pltpu
from jax.sharding import Mesh
from jax.sharding import PartitionSpec as P

AXES = ("x_hi", "core", "z", "x_lo", "y")
SIZES = (2, 2, 8, 2, 4)
NZ, NX, NY = 8, 2, 4
ROWS = 128
N = 8192
OCC = 768
COLS = OCC // 2
F32 = jnp.float32
BF16 = jnp.bfloat16


def ring_pairs(size, step):
    pairs = []
    for core in range(2):
        sign = 1 - 2 * core
        for i in range(size):
            pairs.append((core * size + i, core * size + (i + sign * step) % size))
    return pairs


def ring_send(x, axis, step):
    size = SIZES[AXES.index(axis)]
    return lax.ppermute(x, ("core", axis), ring_pairs(size, step))


def x_send(x):
    pairs = []
    for core in range(2):
        for i in range(4):
            j = (i + 1 - 2 * core) % 4
            src = ((i // 2) * 2 + core) * 2 + i % 2
            dst = ((j // 2) * 2 + core) * 2 + j % 2
            pairs.append((src, dst))
    return lax.ppermute(x, ("x_hi", "core", "x_lo"), pairs)


def swap(x, axis):
    return lax.ppermute(x, axis, [(0, 1), (1, 0)])


def y_send(x, step):
    return lax.ppermute(x, "y", [(i, (i + step) % NY) for i in range(NY)])


Z_OFFSETS = (0, -1, 1, -2, 2, -3, 3, -4)


def z_gather(x, each_round=lambda blocks: ()):
    fwd, bwd = ring_send(x, "z", 1), ring_send(x, "z", -1)
    blocks, given = [x, fwd, bwd], [each_round([x, fwd, bwd])]
    fwd2, bwd2 = ring_send(fwd, "z", 1), ring_send(bwd, "z", -1)
    fwd2, bwd2, given[0] = lax.optimization_barrier((fwd2, bwd2, given[0]))
    given.append(each_round([fwd2, bwd2]))
    last = [ring_send(fwd2, "z", 1), ring_send(bwd2, "z", -1), ring_send(fwd2, "z", 2)]
    last, given[1] = lax.optimization_barrier((last, given[1]))
    given.append(each_round(last))
    return blocks + [fwd2, bwd2] + last, given


def z_slots():
    sign = 1 - 2 * lax.axis_index("core")
    return [(lax.axis_index("z") + sign * off) % NZ for off in Z_OFFSETS]


PARAMS = pltpu.CompilerParams(vmem_limit_bytes=12 << 20)


def by_y_kernel(x_ref, out_ref):
    for y in range(NY):
        for k in range(NZ * NX // NY):
            block = k * NY + y
            out_ref[y, :, k * ROWS : (k + 1) * ROWS] = x_ref[:, block * ROWS : (block + 1) * ROWS]


def columns_by_y(x):
    width = N // NY
    return pl.pallas_call(
        by_y_kernel,
        grid=(NY,),
        in_specs=[pl.BlockSpec((ROWS, width), lambda j: (0, j))],
        out_specs=pl.BlockSpec((NY, ROWS, width // NY), lambda j: (0, 0, j)),
        out_shape=jax.ShapeDtypeStruct((NY, ROWS, width), BF16),
    )(x)


def collect_kernel(*refs):
    near, far, out = refs[:8], refs[8:11], refs[11]
    x = lax.axis_index("x_lo")
    slots = z_slots()
    far_blocks = [(ref, k) for ref in far for k in range(ref.shape[0] // ROWS)]
    for k, z in enumerate(slots):
        here = pl.multiple_of((z * NX + x) * ROWS, ROWS)
        there = pl.multiple_of((z * NX + 1 - x) * ROWS, ROWS)
        out[pl.ds(here, ROWS)] = near[k][...]
        ref, i = far_blocks[k]
        out[pl.ds(there, ROWS)] = ref[i * ROWS : (i + 1) * ROWS]


def collect(near, far):
    return pl.pallas_call(
        collect_kernel, out_shape=jax.ShapeDtypeStruct((N // NY, COLS), BF16), compiler_params=PARAMS
    )(*near, *far)


def partial_kernel(steps, own_ref, sib_ref, rhs_ref, *outs):
    y = lax.axis_index("y")
    for step, out in zip(steps, outs):
        row = (y + step) % NY
        lhs = jnp.concatenate([own_ref[row], sib_ref[row]], axis=0)
        prod = jnp.dot(lhs, rhs_ref[...], preferred_element_type=F32)
        out[:, :COLS] = prod[:ROWS]
        out[:, COLS:] = prod[ROWS:]


def partial_half(own, sib, rhs, *steps):
    return pl.pallas_call(
        lambda *refs: partial_kernel(steps, *refs),
        out_shape=[jax.ShapeDtypeStruct((ROWS, OCC), F32)] * len(steps),
        compiler_params=PARAMS,
    )(own, sib, rhs)


def tile_kernel(keep, *refs):
    z_blocks, lines, refs = refs[:8], refs[8:12], refs[12:]
    added = refs[0] if keep else None
    out, z_buf, xy_buf = refs[-3:]
    core, x, y = lax.axis_index("core"), lax.axis_index("x_lo"), lax.axis_index("y")
    low = core if keep else 1 - core
    for k, z in enumerate(z_slots()):
        z_buf[z] = z_blocks[k][...]
    for s in range(NY):
        for dx in range(NX):
            xy_buf[((x + dx) % NX) * NY + (y + s) % NY] = lines[s][dx]
    for high in range(2):
        rhs = z_buf[pl.ds(4 * high + 2 * low, 2)].reshape(2 * ROWS, OCC)
        for k in range(0, 8, 4):
            prod = lax.dot_general(
                xy_buf[k : k + 4].reshape(4 * ROWS, OCC),
                rhs,
                (((1,), (1,)), ((), ())),
                preferred_element_type=F32,
            ).reshape(4, ROWS, 2 * ROWS)
            rows = slice(8 * high + k, 8 * high + k + 4)
            if keep:
                prod = prod + added[rows].astype(F32)
            out[rows] = prod.astype(BF16)


def tile_product(z_blocks, lines, *added):
    keep = bool(added)
    return pl.pallas_call(
        lambda *refs: tile_kernel(keep, *refs),
        out_shape=jax.ShapeDtypeStruct((16, ROWS, 2 * ROWS), BF16),
        scratch_shapes=[pltpu.VMEM((8, ROWS, OCC), BF16)] * 2,
        compiler_params=PARAMS,
    )(*z_blocks, *lines, *added)


def final_kernel(pieces, out):
    for k in range(4):
        out[:, k * ROWS : (k + 1) * ROWS] = pieces[0, k].astype(F32) + pieces[1, k].astype(F32)


def assemble(pieces):
    return pl.pallas_call(
        final_kernel,
        grid=(4,),
        in_specs=[pl.BlockSpec((2, 4, ROWS, ROWS), lambda j: (0, j % 2, 0, j // 2))],
        out_specs=pl.BlockSpec((ROWS, 4 * ROWS), lambda j: (0, j)),
        out_shape=jax.ShapeDtypeStruct((ROWS, 16 * ROWS), F32),
    )(pieces.reshape(2, 8, ROWS, 2 * ROWS))


def body(integrals, orbitals):
    own = lax.all_to_all(columns_by_y(integrals[0]), "y", 0, 0, tiled=True)
    core = lax.axis_index("core")
    mine = lax.dynamic_slice(orbitals, (0, core * COLS), (ROWS, COLS))
    near, far = z_gather(mine, lambda blocks: x_send(jnp.concatenate(blocks, axis=0)))
    own, far[-1] = lax.optimization_barrier((own, far[-1]))
    sib = swap(own, "core")
    rhs = collect(near, far)
    (across,) = partial_half(own, sib, rhs, 2)
    across = y_send(across, 2)
    up, down = partial_half(own, sib, rhs, 1, 3)
    up, down = y_send(up, 1), y_send(down, 3)
    (here,) = partial_half(own, sib, rhs, 0)
    half = (here + up + down + across).astype(BF16)

    pair = jnp.stack([half, swap(half, "x_lo")])
    lines = [pair] + [y_send(pair, -s) for s in (1, 2, 3)]
    z_blocks, _ = z_gather(half)

    other = tile_product(z_blocks, lines)
    mine = tile_product(z_blocks, lines, swap(other, "core"))
    pieces = lax.all_to_all(mine, ("x_hi", "x_lo", "y"), 0, 0, tiled=True)
    return assemble(pieces)


def solution(mesh):
    split = Mesh(mesh.devices.reshape(SIZES), AXES)
    row = ("z", "x_lo", "y")
    aux = ("x_hi", "core")
    return jax.shard_map(
        body,
        mesh=split,
        in_specs=(P(aux, row, None), P(row, None)),
        out_specs=P(row, aux),
        check_vma=False,
    )
```

time: 154 us -> 143 us (0.929)
  blocking collectives: 43.3 us -> 19.6 us
  waiting for transfers between devices: 39.5 us -> 57.5 us
  Pallas kernels: 23.7 us -> 12.7 us
  starting transfers between devices: 45.3 us -> 49.1 us
  local copies, waits for them, and re-layouts: 1.43 us -> 3.29 us
    all_to_all x1 -> x0, blocking collectives: 21.9 us -> none  [body(): lax.all_to_all(partial_half(own, sib, chunks), 'y', 0, 0, tiled=True)]
    ppermute x6 -> x9, waiting for transfers between devices: 12.8 us -> 27.3 us  [the longest x6 21.3 us: y_send(): return lax.ppermute(x, 'y', [(i, (i + step) % NY) for i in range(NY)])]
    pallas_call x5 -> x8, Pallas kernels: 23.7 us -> 12.7 us  [the longest x1 4.05 us: columns_by_y(): pl.pallas_call(by_y_kernel, grid=(NY,), in_specs=[pl.BlockSpec((ROWS, wid...]
    ppermute x1 -> x3, waiting for transfers between devices: 1.64 us -> 5.57 us  [x_send(): return lax.ppermute(x, ('x_hi', 'core', 'x_lo'), pairs)]
    ppermute x6 -> x9, starting transfers between devices: 14.5 us -> 17.7 us  [the longest x6 9.88 us: y_send(): return lax.ppermute(x, 'y', [(i, (i + step) % NY) for i in range(NY)])]
    ppermute x1 -> x3, starting transfers between devices: 2.56 us -> 4.81 us  [x_send(): return lax.ppermute(x, ('x_hi', 'core', 'x_lo'), pairs)]
    unnamed x4 -> x10, local copies, waits for them, and re-layouts: 1.34 us -> 3.28 us
    all_to_all x1, blocking collectives: 21.5 us -> 19.6 us  [body(): pieces = lax.all_to_all(mine, ('x_hi', 'x_lo', 'y'), 0, 0, tiled=True)]
  transfers between devices with their start and end apart: 22 -> 27, of which waited for: 12 -> 20; matrix products, arithmetic and copies ran while one was open for 0% -> 0% of each run, Pallas kernels for 0% -> 1%
where the time goes in v3:
time: 143 us; the launch traced here: 142 us
  waiting for transfers between devices  57.5 us (40%)
  starting transfers between devices  49.1 us (34%)
  blocking collectives  19.6 us (14%)
  Pallas kernels  12.7 us (9%)
  local copies, waits for them, and re-layouts  3.29 us (2%)
    ppermute x14, waiting for transfers between devices, ring_send(): return lax.ppermute(x, ('core', axis), ring_pairs(size, step))  24.7 us
    ppermute x14, starting transfers between devices, ring_send(): return lax.ppermute(x, ('core', axis), ring_pairs(size, step))  21.5 us
    ppermute x6, waiting for transfers between devices, y_send(): return lax.ppermute(x, 'y', [(i, (i + step) % NY) for i in range(NY)])  21.3 us
    all_to_all x1, blocking collectives, body(): pieces = lax.all_to_all(mine, ('x_hi', 'x_lo', 'y'), 0, 0, tiled=True)  19.6 us
    ppermute x6, starting transfers between devices, y_send(): return lax.ppermute(x, 'y', [(i, (i + step) % NY) for i in range(NY)])  9.88 us
    ppermute x3, starting transfers between devices, swap(): return lax.ppermute(x, axis, [(0, 1), (1, 0)])  7.86 us
    ppermute x3, waiting for transfers between devices, swap(): return lax.ppermute(x, axis, [(0, 1), (1, 0)])  5.99 us
    ppermute x3, waiting for transfers between devices, x_send(): return lax.ppermute(x, ('x_hi', 'core', 'x_lo'), pairs)  5.57 us
  transfers between devices with their start and end apart: 27, of which 20 were waited for; matrix products, arithmetic and copies ran while one was open for 0% of the time, Pallas kernels for 1%

profile of v3, /device:TPU:1, one launch (start us, length us, event | category | flops | bytes accessed | tf_op | source)
XLA Modules:
  0.0 142.5 jit_solution(12510748081208241772)
XLA Ops:
  0.0 4.1 %shard_map.28 = bf16[4,128,2048]{2,1,0:T(8,128)(2,1)} custom-call(bf16[128,8192]{1,0:T(8,128)(2,1)} %bitcast.6), custom_call_target="tpu_custom_call" | custom-call | tf_op jit(solution)/shard_map/pallas_call | solution.py:85
  4.1 5.0 %all-to-all-start = ((bf16[4,128,2048]{2,1,0:T(8,128)(2,1)}), bf16[4,128,2048]{2,1,0:T(8,128)(2,1)S(1)}, u32[]{:S(2)}, u32[]{:S(2)}) async-start(bf16[4,128,2048]{2,1,0:T(8,128)(2,1)} %shard_map.28), calls=%async_computation | async-start | bytes 4194304 | tf_op jit(solution)/shard_map/all_to_all | solution.py:183
  9.1 1.7 %collective-permute-start.2 = (bf16[128,384]{1,0:T(8,128)(2,1)S(1)}, bf16[128,384]{1,0:T(8,128)(2,1)S(1)}, u32[]{:S(2)}, u32[]{:S(2)}) collective-permute-start(bf16[128,384]{1,0:T(8,128)(2,1)S(1)} %constant_dynamic-slice_fusion.refs_0_), channel_id=1, source_target_pairs={{0,56},{8,0},{16,8},{24,16},{32,24},{40,32},{48,40},{56,48},{64,72... | collective-permute-start | bytes 294920 | tf_op jit(solution)/shard_map/ppermute | solution.py:31
  10.8 4.0 %collective-permute-start = (bf16[128,384]{1,0:T(8,128)(2,1)S(1)}, bf16[128,384]{1,0:T(8,128)(2,1)S(1)}, u32[]{:S(2)}, u32[]{:S(2)}) collective-permute-start(bf16[128,384]{1,0:T(8,128)(2,1)S(1)} %constant_dynamic-slice_fusion.refs_0_), channel_id=1, source_target_pairs={{0,8},{8,16},{16,24},{24,32},{32,40},{40,48},{48,56},{56,0},{64,12... | collective-permute-start | bytes 294920 | tf_op jit(solution)/shard_map/ppermute | solution.py:31
  14.8 2.2 %collective-permute-done.2.refs_2_ = bf16[128,384]{1,0:T(8,128)(2,1)S(1)} collective-permute-done((bf16[128,384]{1,0:T(8,128)(2,1)S(1)}, bf16[128,384]{1,0:T(8,128)(2,1)S(1)}, u32[]{:S(2)}, u32[]{:S(2)}) %collective-permute-start.2) | collective-permute-done | bytes 98336 | tf_op jit(solution)/shard_map/ppermute | solution.py:31
  17.1 2.6 %collective-permute-start.4 = (bf16[384,384]{1,0:T(8,128)(2,1)S(1)}, bf16[384,384]{1,0:T(8,128)(2,1)S(1)}, u32[]{:S(2)}, u32[]{:S(2)}) collective-permute-start(bf16[384,384]{1,0:T(8,128)(2,1)S(1)} %pad_maximum_fusion.1), channel_id=1, source_target_pairs={{0,4},{4,128},{128,132},{132,0},{64,196},{68,64},{192,68},{196,192... | collective-permute-start | bytes 884744 | tf_op jit(solution)/shard_map/ppermute | solution.py:42
  19.6 2.7 %collective-permute-start.1 = (bf16[128,384]{1,0:T(8,128)(2,1)S(1)}, bf16[128,384]{1,0:T(8,128)(2,1)S(1)}, u32[]{:S(2)}, u32[]{:S(2)}) collective-permute-start(bf16[128,384]{1,0:T(8,128)(2,1)S(1)} %collective-permute-done.refs_1_), channel_id=1, source_target_pairs={{0,8},{8,16},{16,24},{24,32},{32,40},{40,48},{48,56},{56,0},{64,12... | collective-permute-start | bytes 294920 | tf_op jit(solution)/shard_map/ppermute | solution.py:31
  22.3 2.3 %collective-permute-done.3.refs_4_ = bf16[128,384]{1,0:T(8,128)(2,1)S(1)} collective-permute-done((bf16[128,384]{1,0:T(8,128)(2,1)S(1)}, bf16[128,384]{1,0:T(8,128)(2,1)S(1)}, u32[]{:S(2)}, u32[]{:S(2)}) %collective-permute-start.3) | collective-permute-done | bytes 98336 | tf_op jit(solution)/shard_map/ppermute | solution.py:31
  24.6 2.2 %collective-permute-start.8 = (bf16[256,384]{1,0:T(8,128)(2,1)S(1)}, bf16[256,384]{1,0:T(8,128)(2,1)S(1)}, u32[]{:S(2)}, u32[]{:S(2)}) collective-permute-start(bf16[256,384]{1,0:T(8,128)(2,1)S(1)} %pad_maximum_fusion.3), channel_id=1, source_target_pairs={{0,4},{4,128},{128,132},{132,0},{64,196},{68,64},{192,68},{196,192... | collective-permute-start | bytes 589832 | tf_op jit(solution)/shard_map/ppermute | solution.py:42
  26.8 1.4 collective-permute-start.6
  28.2 2.2 %collective-permute-start.7 = (bf16[128,384]{1,0:T(8,128)(2,1)S(1)}, bf16[128,384]{1,0:T(8,128)(2,1)S(1)}, u32[]{:S(2)}, u32[]{:S(2)}) collective-permute-start(bf16[128,384]{1,0:T(8,128)(2,1)S(1)} %collective-permute-done.1.refs_3_), channel_id=1, source_target_pairs={{0,16},{8,24},{16,32},{24,40},{32,48},{40,56},{48,0},{56,8},{64,11... | collective-permute-start | bytes 294920 | tf_op jit(solution)/shard_map/ppermute | solution.py:31
  30.5 0.9 collective-permute-start.5
  31.8 2.7 %collective-permute-done.7.refs_7_ = bf16[128,384]{1,0:T(8,128)(2,1)S(1)} collective-permute-done((bf16[128,384]{1,0:T(8,128)(2,1)S(1)}, bf16[128,384]{1,0:T(8,128)(2,1)S(1)}, u32[]{:S(2)}, u32[]{:S(2)}) %collective-permute-start.7) | collective-permute-done | bytes 98336 | tf_op jit(solution)/shard_map/ppermute | solution.py:31
  34.5 1.4 collective-permute-done.5.refs_5_
  35.9 0.7 copy-done.3
  36.7 5.6 %collective-permute-done.9.refs_10_ = bf16[384,384]{1,0:T(8,128)(2,1)S(1)} collective-permute-done((bf16[384,384]{1,0:T(8,128)(2,1)S(1)}, bf16[384,384]{1,0:T(8,128)(2,1)S(1)}, u32[]{:S(2)}, u32[]{:S(2)}) %collective-permute-start.9) | collective-permute-done | bytes 294944 | tf_op jit(solution)/shard_map/ppermute | solution.py:42
  42.3 0.7 copy-done.1
  43.0 6.2 %collective-permute-start.10 = (bf16[4,128,2048]{2,1,0:T(8,128)(2,1)S(1)}, bf16[4,128,2048]{2,1,0:T(8,128)(2,1)S(1)}, u32[]{:S(2)}, u32[]{:S(2)}) collective-permute-start(bf16[4,128,2048]{2,1,0:T(8,128)(2,1)S(1)} %all-to-all-done.refs_0_), channel_id=1, source_target_pairs={{0,64},{64,0},{1,65},{65,1},{2,66},{66,2},{3,67},{67,3},{4,68},{68... | collective-permute-start | bytes 6291464 | tf_op jit(solution)/shard_map/ppermute | solution.py:46
  49.2 1.0 copy-done.2
  50.2 0.9 copy-done.4
  51.3 1.7 %collective-permute-done.10.refs_1_ = bf16[4,128,2048]{2,1,0:T(8,128)(2,1)S(1)} collective-permute-done((bf16[4,128,2048]{2,1,0:T(8,128)(2,1)S(1)}, bf16[4,128,2048]{2,1,0:T(8,128)(2,1)S(1)}, u32[]{:S(2)}, u32[]{:S(2)}) %collective-permute-start.10) | collective-permute-done | bytes 2097184 | tf_op jit(solution)/shard_map/ppermute | solution.py:46
  53.0 1.3 shard_map.31
  54.3 3.4 %collective-permute-start.11 = (f32[128,768]{1,0:T(8,128)S(1)}, f32[128,768]{1,0:T(8,128)S(1)}, u32[]{:S(2)}, u32[]{:S(2)}) collective-permute-start(f32[128,768]{1,0:T(8,128)S(1)} %get-tuple-element.30), channel_id=1, source_target_pairs={{0,1},{1,2},{2,3},{3,0},{4,5},{5,6},{6,7},{7,4},{8,9},{9,10},{10,1... | collective-permute-start | bytes 1179656 | tf_op jit(solution)/shard_map/ppermute | solution.py:50
  57.6 0.7 collective-permute-start.12
  58.4 0.7 shard_map.32
  59.1 2.3 %collective-permute-start.13 = (f32[128,768]{1,0:T(8,128)S(1)}, f32[128,768]{1,0:T(8,128)S(1)}, u32[]{:S(2)}, u32[]{:S(2)}) collective-permute-start(f32[128,768]{1,0:T(8,128)S(1)} %shard_map.32), channel_id=1, source_target_pairs={{0,2},{1,3},{2,0},{3,1},{4,6},{5,7},{6,4},{7,5},{8,10},{9,11},{10,... | collective-permute-start | bytes 1179656 | tf_op jit(solution)/shard_map/ppermute | solution.py:50
  61.4 0.7 shard_map.30
  62.1 5.2 %collective-permute-done.11 = f32[128,768]{1,0:T(8,128)S(1)} collective-permute-done((f32[128,768]{1,0:T(8,128)S(1)}, f32[128,768]{1,0:T(8,128)S(1)}, u32[]{:S(2)}, u32[]{:S(2)}) %collective-permute-start.11) | collective-permute-done | bytes 393248 | tf_op jit(solution)/shard_map/ppermute | solution.py:50
  67.6 8.9 %collective-permute-done.13 = f32[128,768]{1,0:T(8,128)S(1)} collective-permute-done((f32[128,768]{1,0:T(8,128)S(1)}, f32[128,768]{1,0:T(8,128)S(1)}, u32[]{:S(2)}, u32[]{:S(2)}) %collective-permute-start.13) | collective-permute-done | bytes 393248 | tf_op jit(solution)/shard_map/ppermute | solution.py:50
  76.9 2.5 %collective-permute-start.14 = (bf16[128,768]{1,0:T(8,128)(2,1)S(1)}, bf16[128,768]{1,0:T(8,128)(2,1)S(1)}, u32[]{:S(2)}, u32[]{:S(2)}) collective-permute-start(bf16[128,768]{1,0:T(8,128)(2,1)S(1)} %add_convert_fusion.refs_0_), channel_id=1, source_target_pairs={{0,8},{8,16},{16,24},{24,32},{32,40},{40,48},{48,56},{56,0},{64,12... | collective-permute-start | bytes 589832 | tf_op jit(solution)/shard_map/ppermute | solution.py:31
  79.4 3.4 %collective-permute-done.15.refs_2_ = bf16[128,768]{1,0:T(8,128)(2,1)S(1)} collective-permute-done((bf16[128,768]{1,0:T(8,128)(2,1)S(1)}, bf16[128,768]{1,0:T(8,128)(2,1)S(1)}, u32[]{:S(2)}, u32[]{:S(2)}) %collective-permute-start.15) | collective-permute-done | bytes 196640 | tf_op jit(solution)/shard_map/ppermute | solution.py:31
  83.2 3.1 %collective-permute-start.16 = (bf16[128,768]{1,0:T(8,128)(2,1)S(1)}, bf16[128,768]{1,0:T(8,128)(2,1)S(1)}, u32[]{:S(2)}, u32[]{:S(2)}) collective-permute-start(bf16[128,768]{1,0:T(8,128)(2,1)S(1)} %collective-permute-done.14.refs_1_), channel_id=1, source_target_pairs={{0,8},{8,16},{16,24},{24,32},{32,40},{40,48},{48,56},{56,0},{64,12... | collective-permute-start | bytes 589832 | tf_op jit(solution)/shard_map/ppermute | solution.py:31
  86.3 2.2 %collective-permute-done.17.refs_4_ = bf16[128,768]{1,0:T(8,128)(2,1)S(1)} collective-permute-done((bf16[128,768]{1,0:T(8,128)(2,1)S(1)}, bf16[128,768]{1,0:T(8,128)(2,1)S(1)}, u32[]{:S(2)}, u32[]{:S(2)}) %collective-permute-start.17) | collective-permute-done | bytes 196640 | tf_op jit(solution)/shard_map/ppermute | solution.py:31
  88.5 2.3 %collective-permute-done.16.refs_3_ = bf16[128,768]{1,0:T(8,128)(2,1)S(1)} collective-permute-done((bf16[128,768]{1,0:T(8,128)(2,1)S(1)}, bf16[128,768]{1,0:T(8,128)(2,1)S(1)}, u32[]{:S(2)}, u32[]{:S(2)}) %collective-permute-start.16) | collective-permute-done | bytes 196640 | tf_op jit(solution)/shard_map/ppermute | solution.py:31
  90.8 2.0 %collective-permute-done.21 = bf16[128,768]{1,0:T(8,128)(2,1)S(1)} collective-permute-done((bf16[128,768]{1,0:T(8,128)(2,1)S(1)}, bf16[128,768]{1,0:T(8,128)(2,1)S(1)}, u32[]{:S(2)}, u32[]{:S(2)}) %collective-permute-start.21) | collective-permute-done | bytes 196640 | tf_op jit(solution)/shard_map/ppermute | solution.py:46
  92.9 0.7 collective-permute-start.24
  93.6 2.3 %collective-permute-start.23 = (bf16[2,128,768]{2,1,0:T(8,128)(2,1)S(1)}, bf16[2,128,768]{2,1,0:T(8,128)(2,1)S(1)}, u32[]{:S(2)}, u32[]{:S(2)}) collective-permute-start(bf16[2,128,768]{2,1,0:T(8,128)(2,1)S(1)} %pad_maximum_fusion.refs_8_), channel_id=1, source_target_pairs={{0,2},{1,3},{2,0},{3,1},{4,6},{5,7},{6,4},{7,5},{8,10},{9,11},{10,... | collective-permute-start | bytes 1179656 | tf_op jit(solution)/shard_map/ppermute | solution.py:50
  96.3 2.7 %collective-permute-start.20 = (bf16[128,768]{1,0:T(8,128)(2,1)S(1)}, bf16[128,768]{1,0:T(8,128)(2,1)S(1)}, u32[]{:S(2)}, u32[]{:S(2)}) collective-permute-start(bf16[128,768]{1,0:T(8,128)(2,1)S(1)} %collective-permute-done.16.refs_3_), channel_id=1, source_target_pairs={{0,16},{8,24},{16,32},{24,40},{32,48},{40,56},{48,0},{56,8},{64,11... | collective-permute-start | bytes 589832 | tf_op jit(solution)/shard_map/ppermute | solution.py:31
  99.0 4.7 %collective-permute-done.20.refs_7_ = bf16[128,768]{1,0:T(8,128)(2,1)S(1)} collective-permute-done((bf16[128,768]{1,0:T(8,128)(2,1)S(1)}, bf16[128,768]{1,0:T(8,128)(2,1)S(1)}, u32[]{:S(2)}, u32[]{:S(2)}) %collective-permute-start.20) | collective-permute-done | bytes 196640 | tf_op jit(solution)/shard_map/ppermute | solution.py:31
  103.7 2.6 %collective-permute-done.18.refs_5_ = bf16[128,768]{1,0:T(8,128)(2,1)S(1)} collective-permute-done((bf16[128,768]{1,0:T(8,128)(2,1)S(1)}, bf16[128,768]{1,0:T(8,128)(2,1)S(1)}, u32[]{:S(2)}, u32[]{:S(2)}) %collective-permute-start.18) | collective-permute-done | bytes 196640 | tf_op jit(solution)/shard_map/ppermute | solution.py:31
  106.3 4.2 %collective-permute-done.23.refs_10_ = bf16[2,128,768]{2,1,0:T(8,128)(2,1)S(1)} collective-permute-done((bf16[2,128,768]{2,1,0:T(8,128)(2,1)S(1)}, bf16[2,128,768]{2,1,0:T(8,128)(2,1)S(1)}, u32[]{:S(2)}, u32[]{:S(2)}) %collective-permute-start.23) | collective-permute-done | bytes 393248 | tf_op jit(solution)/shard_map/ppermute | solution.py:50
  110.5 2.6 %collective-permute-done.22.refs_9_ = bf16[2,128,768]{2,1,0:T(8,128)(2,1)S(1)} collective-permute-done((bf16[2,128,768]{2,1,0:T(8,128)(2,1)S(1)}, bf16[2,128,768]{2,1,0:T(8,128)(2,1)S(1)}, u32[]{:S(2)}, u32[]{:S(2)}) %collective-permute-start.22) | collective-permute-done | bytes 393248 | tf_op jit(solution)/shard_map/ppermute | solution.py:50
  113.2 1.2 shard_map.33
  114.4 1.6 %collective-permute-start.25 = (bf16[16,128,256]{2,1,0:T(8,128)(2,1)S(1)}, bf16[16,128,256]{2,1,0:T(8,128)(2,1)S(1)}, u32[]{:S(2)}, u32[]{:S(2)}) collective-permute-start(bf16[16,128,256]{2,1,0:T(8,128)(2,1)S(1)} %shard_map.33), channel_id=1, source_target_pairs={{0,64},{64,0},{1,65},{65,1},{2,66},{66,2},{3,67},{67,3},{4,68},{68... | collective-permute-start | bytes 3145736 | tf_op jit(solution)/shard_map/ppermute | solution.py:46
  116.0 2.3 %collective-permute-done.25.refs_12_ = bf16[16,128,256]{2,1,0:T(8,128)(2,1)S(1)} collective-permute-done((bf16[16,128,256]{2,1,0:T(8,128)(2,1)S(1)}, bf16[16,128,256]{2,1,0:T(8,128)(2,1)S(1)}, u32[]{:S(2)}, u32[]{:S(2)}) %collective-permute-start.25) | collective-permute-done | bytes 1048608 | tf_op jit(solution)/shard_map/ppermute | solution.py:46
  118.3 1.2 shard_map.34
  119.5 19.6 %all_to_all.10 = bf16[16,128,256]{2,1,0:T(8,128)(2,1)} all-to-all(bf16[16,128,256]{2,1,0:T(8,128)(2,1)S(1)} %shard_map.34), channel_id=1, replica_groups=mesh['x_hi'=2,'core'=2,'z'=8,'x_lo'=2,'y'=4] {'x_hi','x_lo','y'}, dimensions={0} | all-to-all | bytes 2097152 | tf_op jit(solution)/shard_map/all_to_all | solution.py:203
  139.1 3.4 %shard_map.35 = f32[128,2048]{1,0:T(8,128)} custom-call(bf16[2,8,128,256]{3,2,1,0:T(8,128)(2,1)} %bitcast.5), custom_call_target="tpu_custom_call" | custom-call | tf_op jit(solution)/shard_map/pallas_call | solution.py:173
  (31 shorter events, 2.4 us)
Async XLA Ops:
  0.0 9.1 %copy-start = (bf16[128,768]{1,0:T(8,128)(2,1)S(1)}, bf16[128,768]{1,0:T(8,128)(2,1)}, u32[]{:S(2)}) copy-start(bf16[128,768]{1,0:T(8,128)(2,1)} %param.3) | copy-start | bytes 589828
  4.1 38.9 %all-to-all-start = ((bf16[4,128,2048]{2,1,0:T(8,128)(2,1)}), bf16[4,128,2048]{2,1,0:T(8,128)(2,1)S(1)}, u32[]{:S(2)}, u32[]{:S(2)}) async-start(bf16[4,128,2048]{2,1,0:T(8,128)(2,1)} %shard_map.28), calls=%async_computation | async-start | bytes 4194304 | tf_op jit(solution)/shard_map/all_to_all | solution.py:183
  9.1 8.0 %collective-permute-start.2 = (bf16[128,384]{1,0:T(8,128)(2,1)S(1)}, bf16[128,384]{1,0:T(8,128)(2,1)S(1)}, u32[]{:S(2)}, u32[]{:S(2)}) collective-permute-start(bf16[128,384]{1,0:T(8,128)(2,1)S(1)} %constant_dynamic-slice_fusion.refs_0_), channel_id=1, source_target_pairs={{0,56},{8,0},{16,8},{24,16},{32,24},{40,32},{48,40},{56,48},{64,72... | collective-permute-start | bytes 294920 | tf_op jit(solution)/shard_map/ppermute | solution.py:31
  10.8 6.2 %collective-permute-start = (bf16[128,384]{1,0:T(8,128)(2,1)S(1)}, bf16[128,384]{1,0:T(8,128)(2,1)S(1)}, u32[]{:S(2)}, u32[]{:S(2)}) collective-permute-start(bf16[128,384]{1,0:T(8,128)(2,1)S(1)} %constant_dynamic-slice_fusion.refs_0_), channel_id=1, source_target_pairs={{0,8},{8,16},{16,24},{24,32},{32,40},{40,48},{48,56},{56,0},{64,12... | collective-permute-start | bytes 294920 | tf_op jit(solution)/shard_map/ppermute | solution.py:31
  17.1 7.5 %collective-permute-start.4 = (bf16[384,384]{1,0:T(8,128)(2,1)S(1)}, bf16[384,384]{1,0:T(8,128)(2,1)S(1)}, u32[]{:S(2)}, u32[]{:S(2)}) collective-permute-start(bf16[384,384]{1,0:T(8,128)(2,1)S(1)} %pad_maximum_fusion.1), channel_id=1, source_target_pairs={{0,4},{4,128},{128,132},{132,0},{64,196},{68,64},{192,68},{196,192... | collective-permute-start | bytes 884744 | tf_op jit(solution)/shard_map/ppermute | solution.py:42
  19.6 5.0 %collective-permute-start.3 = (bf16[128,384]{1,0:T(8,128)(2,1)S(1)}, bf16[128,384]{1,0:T(8,128)(2,1)S(1)}, u32[]{:S(2)}, u32[]{:S(2)}) collective-permute-start(bf16[128,384]{1,0:T(8,128)(2,1)S(1)} %collective-permute-done.2.refs_2_), channel_id=1, source_target_pairs={{0,56},{8,0},{16,8},{24,16},{32,24},{40,32},{48,40},{56,48},{64,72... | collective-permute-start | bytes 294920 | tf_op jit(solution)/shard_map/ppermute | solution.py:31
  19.6 5.0 %collective-permute-start.1 = (bf16[128,384]{1,0:T(8,128)(2,1)S(1)}, bf16[128,384]{1,0:T(8,128)(2,1)S(1)}, u32[]{:S(2)}, u32[]{:S(2)}) collective-permute-start(bf16[128,384]{1,0:T(8,128)(2,1)S(1)} %collective-permute-done.refs_1_), channel_id=1, source_target_pairs={{0,8},{8,16},{16,24},{24,32},{32,40},{40,48},{48,56},{56,0},{64,12... | collective-permute-start | bytes 294920 | tf_op jit(solution)/shard_map/ppermute | solution.py:31
  24.6 11.3 %collective-permute-start.8 = (bf16[256,384]{1,0:T(8,128)(2,1)S(1)}, bf16[256,384]{1,0:T(8,128)(2,1)S(1)}, u32[]{:S(2)}, u32[]{:S(2)}) collective-permute-start(bf16[256,384]{1,0:T(8,128)(2,1)S(1)} %pad_maximum_fusion.3), channel_id=1, source_target_pairs={{0,4},{4,128},{128,132},{132,0},{64,196},{68,64},{192,68},{196,192... | collective-permute-start | bytes 589832 | tf_op jit(solution)/shard_map/ppermute | solution.py:42
  26.8 5.0 %collective-permute-start.6 = (bf16[128,384]{1,0:T(8,128)(2,1)S(1)}, bf16[128,384]{1,0:T(8,128)(2,1)S(1)}, u32[]{:S(2)}, u32[]{:S(2)}) collective-permute-start(bf16[128,384]{1,0:T(8,128)(2,1)S(1)} %collective-permute-done.3.refs_4_), channel_id=1, source_target_pairs={{0,56},{8,0},{16,8},{24,16},{32,24},{40,32},{48,40},{56,48},{64,72... | collective-permute-start | bytes 294920 | tf_op jit(solution)/shard_map/ppermute | solution.py:31
  28.2 6.3 %collective-permute-start.7 = (bf16[128,384]{1,0:T(8,128)(2,1)S(1)}, bf16[128,384]{1,0:T(8,128)(2,1)S(1)}, u32[]{:S(2)}, u32[]{:S(2)}) collective-permute-start(bf16[128,384]{1,0:T(8,128)(2,1)S(1)} %collective-permute-done.1.refs_3_), channel_id=1, source_target_pairs={{0,16},{8,24},{16,32},{24,40},{32,48},{40,56},{48,0},{56,8},{64,11... | collective-permute-start | bytes 294920 | tf_op jit(solution)/shard_map/ppermute | solution.py:31
  30.5 5.4 %collective-permute-start.5 = (bf16[128,384]{1,0:T(8,128)(2,1)S(1)}, bf16[128,384]{1,0:T(8,128)(2,1)S(1)}, u32[]{:S(2)}, u32[]{:S(2)}) collective-permute-start(bf16[128,384]{1,0:T(8,128)(2,1)S(1)} %collective-permute-done.1.refs_3_), channel_id=1, source_target_pairs={{0,8},{8,16},{16,24},{24,32},{32,40},{40,48},{48,56},{56,0},{64,12... | collective-permute-start | bytes 294920 | tf_op jit(solution)/shard_map/ppermute | solution.py:31
  35.9 0.7 copy-start.3
  36.6 5.7 %collective-permute-start.9 = (bf16[384,384]{1,0:T(8,128)(2,1)S(1)}, bf16[384,384]{1,0:T(8,128)(2,1)S(1)}, u32[]{:S(2)}, u32[]{:S(2)}) collective-permute-start(bf16[384,384]{1,0:T(8,128)(2,1)S(1)} %pad_maximum_fusion.2), channel_id=1, source_target_pairs={{0,4},{4,128},{128,132},{132,0},{64,196},{68,64},{192,68},{196,192... | collective-permute-start | bytes 884744 | tf_op jit(solution)/shard_map/ppermute | solution.py:42
  42.3 0.7 copy-start.1
  43.0 10.0 %collective-permute-start.10 = (bf16[4,128,2048]{2,1,0:T(8,128)(2,1)S(1)}, bf16[4,128,2048]{2,1,0:T(8,128)(2,1)S(1)}, u32[]{:S(2)}, u32[]{:S(2)}) collective-permute-start(bf16[4,128,2048]{2,1,0:T(8,128)(2,1)S(1)} %all-to-all-done.refs_0_), channel_id=1, source_target_pairs={{0,64},{64,0},{1,65},{65,1},{2,66},{66,2},{3,67},{67,3},{4,68},{68... | collective-permute-start | bytes 6291464 | tf_op jit(solution)/shard_map/ppermute | solution.py:46
  49.2 1.0 copy-start.2
  50.2 0.9 copy-start.4
  54.3 13.0 %collective-permute-start.11 = (f32[128,768]{1,0:T(8,128)S(1)}, f32[128,768]{1,0:T(8,128)S(1)}, u32[]{:S(2)}, u32[]{:S(2)}) collective-permute-start(f32[128,768]{1,0:T(8,128)S(1)} %get-tuple-element.30), channel_id=1, source_target_pairs={{0,1},{1,2},{2,3},{3,0},{4,5},{5,6},{6,7},{7,4},{8,9},{9,10},{10,1... | collective-permute-start | bytes 1179656 | tf_op jit(solution)/shard_map/ppermute | solution.py:50
  57.6 10.0 %collective-permute-start.12 = (f32[128,768]{1,0:T(8,128)S(1)}, f32[128,768]{1,0:T(8,128)S(1)}, u32[]{:S(2)}, u32[]{:S(2)}) collective-permute-start(f32[128,768]{1,0:T(8,128)S(1)} %get-tuple-element.31), channel_id=1, source_target_pairs={{0,3},{1,0},{2,1},{3,2},{4,7},{5,4},{6,5},{7,6},{8,11},{9,8},{10,9... | collective-permute-start | bytes 1179656 | tf_op jit(solution)/shard_map/ppermute | solution.py:50
  59.1 17.5 %collective-permute-start.13 = (f32[128,768]{1,0:T(8,128)S(1)}, f32[128,768]{1,0:T(8,128)S(1)}, u32[]{:S(2)}, u32[]{:S(2)}) collective-permute-start(f32[128,768]{1,0:T(8,128)S(1)} %shard_map.32), channel_id=1, source_target_pairs={{0,2},{1,3},{2,0},{3,1},{4,6},{5,7},{6,4},{7,5},{8,10},{9,11},{10,... | collective-permute-start | bytes 1179656 | tf_op jit(solution)/shard_map/ppermute | solution.py:50
  76.7 6.1 %collective-permute-start.15 = (bf16[128,768]{1,0:T(8,128)(2,1)S(1)}, bf16[128,768]{1,0:T(8,128)(2,1)S(1)}, u32[]{:S(2)}, u32[]{:S(2)}) collective-permute-start(bf16[128,768]{1,0:T(8,128)(2,1)S(1)} %add_convert_fusion.refs_0_), channel_id=1, source_target_pairs={{0,56},{8,0},{16,8},{24,16},{32,24},{40,32},{48,40},{56,48},{64,72... | collective-permute-start | bytes 589832 | tf_op jit(solution)/shard_map/ppermute | solution.py:31
  76.9 6.3 %collective-permute-start.14 = (bf16[128,768]{1,0:T(8,128)(2,1)S(1)}, bf16[128,768]{1,0:T(8,128)(2,1)S(1)}, u32[]{:S(2)}, u32[]{:S(2)}) collective-permute-start(bf16[128,768]{1,0:T(8,128)(2,1)S(1)} %add_convert_fusion.refs_0_), channel_id=1, source_target_pairs={{0,8},{8,16},{16,24},{24,32},{32,40},{40,48},{48,56},{56,0},{64,12... | collective-permute-start | bytes 589832 | tf_op jit(solution)/shard_map/ppermute | solution.py:31
  82.8 5.7 %collective-permute-start.17 = (bf16[128,768]{1,0:T(8,128)(2,1)S(1)}, bf16[128,768]{1,0:T(8,128)(2,1)S(1)}, u32[]{:S(2)}, u32[]{:S(2)}) collective-permute-start(bf16[128,768]{1,0:T(8,128)(2,1)S(1)} %collective-permute-done.15.refs_2_), channel_id=1, source_target_pairs={{0,56},{8,0},{16,8},{24,16},{32,24},{40,32},{48,40},{56,48},{64,72... | collective-permute-start | bytes 589832 | tf_op jit(solution)/shard_map/ppermute | solution.py:31
  83.2 7.6 %collective-permute-start.16 = (bf16[128,768]{1,0:T(8,128)(2,1)S(1)}, bf16[128,768]{1,0:T(8,128)(2,1)S(1)}, u32[]{:S(2)}, u32[]{:S(2)}) collective-permute-start(bf16[128,768]{1,0:T(8,128)(2,1)S(1)} %collective-permute-done.14.refs_1_), channel_id=1, source_target_pairs={{0,8},{8,16},{16,24},{24,32},{32,40},{40,48},{48,56},{56,0},{64,12... | collective-permute-start | bytes 589832 | tf_op jit(solution)/shard_map/ppermute | solution.py:31
  86.3 6.5 %collective-permute-start.21 = (bf16[128,768]{1,0:T(8,128)(2,1)S(1)}, bf16[128,768]{1,0:T(8,128)(2,1)S(1)}, u32[]{:S(2)}, u32[]{:S(2)}) collective-permute-start(bf16[128,768]{1,0:T(8,128)(2,1)S(1)} %add_convert_fusion.refs_0_), channel_id=1, source_target_pairs={{0,4},{4,0},{1,5},{5,1},{2,6},{6,2},{3,7},{7,3},{8,12},{12,8},{9,1... | collective-permute-start | bytes 589832 | tf_op jit(solution)/shard_map/ppermute | solution.py:46
  90.8 8.2 %collective-permute-start.19 = (bf16[128,768]{1,0:T(8,128)(2,1)S(1)}, bf16[128,768]{1,0:T(8,128)(2,1)S(1)}, u32[]{:S(2)}, u32[]{:S(2)}) collective-permute-start(bf16[128,768]{1,0:T(8,128)(2,1)S(1)} %collective-permute-done.17.refs_4_), channel_id=1, source_target_pairs={{0,56},{8,0},{16,8},{24,16},{32,24},{40,32},{48,40},{56,48},{64,72... | collective-permute-start | bytes 589832 | tf_op jit(solution)/shard_map/ppermute | solution.py:31
  92.9 13.5 %collective-permute-start.24 = (bf16[2,128,768]{2,1,0:T(8,128)(2,1)S(1)}, bf16[2,128,768]{2,1,0:T(8,128)(2,1)S(1)}, u32[]{:S(2)}, u32[]{:S(2)}) collective-permute-start(bf16[2,128,768]{2,1,0:T(8,128)(2,1)S(1)} %pad_maximum_fusion.refs_8_), channel_id=1, source_target_pairs={{0,1},{1,2},{2,3},{3,0},{4,5},{5,6},{6,7},{7,4},{8,9},{9,10},{10,1... | collective-permute-start | bytes 1179656 | tf_op jit(solution)/shard_map/ppermute | solution.py:50
  93.6 16.9 %collective-permute-start.23 = (bf16[2,128,768]{2,1,0:T(8,128)(2,1)S(1)}, bf16[2,128,768]{2,1,0:T(8,128)(2,1)S(1)}, u32[]{:S(2)}, u32[]{:S(2)}) collective-permute-start(bf16[2,128,768]{2,1,0:T(8,128)(2,1)S(1)} %pad_maximum_fusion.refs_8_), channel_id=1, source_target_pairs={{0,2},{1,3},{2,0},{3,1},{4,6},{5,7},{6,4},{7,5},{8,10},{9,11},{10,... | collective-permute-start | bytes 1179656 | tf_op jit(solution)/shard_map/ppermute | solution.py:50
  95.9 17.3 %collective-permute-start.22 = (bf16[2,128,768]{2,1,0:T(8,128)(2,1)S(1)}, bf16[2,128,768]{2,1,0:T(8,128)(2,1)S(1)}, u32[]{:S(2)}, u32[]{:S(2)}) collective-permute-start(bf16[2,128,768]{2,1,0:T(8,128)(2,1)S(1)} %pad_maximum_fusion.refs_8_), channel_id=1, source_target_pairs={{0,3},{1,0},{2,1},{3,2},{4,7},{5,4},{6,5},{7,6},{8,11},{9,8},{10,9... | collective-permute-start | bytes 1179656 | tf_op jit(solution)/shard_map/ppermute | solution.py:50
  96.3 7.4 %collective-permute-start.20 = (bf16[128,768]{1,0:T(8,128)(2,1)S(1)}, bf16[128,768]{1,0:T(8,128)(2,1)S(1)}, u32[]{:S(2)}, u32[]{:S(2)}) collective-permute-start(bf16[128,768]{1,0:T(8,128)(2,1)S(1)} %collective-permute-done.16.refs_3_), channel_id=1, source_target_pairs={{0,16},{8,24},{16,32},{24,40},{32,48},{40,56},{48,0},{56,8},{64,11... | collective-permute-start | bytes 589832 | tf_op jit(solution)/shard_map/ppermute | solution.py:31
  99.0 7.3 %collective-permute-start.18 = (bf16[128,768]{1,0:T(8,128)(2,1)S(1)}, bf16[128,768]{1,0:T(8,128)(2,1)S(1)}, u32[]{:S(2)}, u32[]{:S(2)}) collective-permute-start(bf16[128,768]{1,0:T(8,128)(2,1)S(1)} %collective-permute-done.16.refs_3_), channel_id=1, source_target_pairs={{0,8},{8,16},{16,24},{24,32},{32,40},{40,48},{48,56},{56,0},{64,12... | collective-permute-start | bytes 589832 | tf_op jit(solution)/shard_map/ppermute | solution.py:31
  114.4 3.9 %collective-permute-start.25 = (bf16[16,128,256]{2,1,0:T(8,128)(2,1)S(1)}, bf16[16,128,256]{2,1,0:T(8,128)(2,1)S(1)}, u32[]{:S(2)}, u32[]{:S(2)}) collective-permute-start(bf16[16,128,256]{2,1,0:T(8,128)(2,1)S(1)} %shard_map.33), channel_id=1, source_target_pairs={{0,64},{64,0},{1,65},{65,1},{2,66},{66,2},{3,67},{67,3},{4,68},{68... | collective-permute-start | bytes 3145736 | tf_op jit(solution)/shard_map/ppermute | solution.py:46

commit v4 on v3

--- a/solution.py
+++ b/solution.py
@@ -53,16 +53,15 @@
 Z_OFFSETS = (0, -1, 1, -2, 2, -3, 3, -4)
 
 
-def z_gather(x, each_round=lambda blocks: ()):
-    fwd, bwd = ring_send(x, "z", 1), ring_send(x, "z", -1)
-    blocks, given = [x, fwd, bwd], [each_round([x, fwd, bwd])]
-    fwd2, bwd2 = ring_send(fwd, "z", 1), ring_send(bwd, "z", -1)
-    fwd2, bwd2, given[0] = lax.optimization_barrier((fwd2, bwd2, given[0]))
-    given.append(each_round([fwd2, bwd2]))
-    last = [ring_send(fwd2, "z", 1), ring_send(bwd2, "z", -1), ring_send(fwd2, "z", 2)]
-    last, given[1] = lax.optimization_barrier((last, given[1]))
-    given.append(each_round(last))
-    return blocks + [fwd2, bwd2] + last, given
+def z_gather(x, hops=1, in_step=False):
+    blocks, fwd, bwd = [x], [x], [x]
+    for k in range(3):
+        if in_step and k:
+            fwd[-1], bwd[-1] = lax.optimization_barrier((fwd[-1], bwd[-1]))
+        fwd.append(ring_send(fwd[-1], "z", 1))
+        bwd.append(ring_send(bwd[-1], "z", -1))
+        blocks += [fwd[-1], bwd[-1]]
+    return blocks + [ring_send(fwd[4 - hops], "z", hops)]
 
 
 def z_slots():
@@ -75,39 +74,30 @@
 
 def by_y_kernel(x_ref, out_ref):
     for y in range(NY):
-        for k in range(NZ * NX // NY):
+        for k in range(NZ * NX):
             block = k * NY + y
             out_ref[y, :, k * ROWS : (k + 1) * ROWS] = x_ref[:, block * ROWS : (block + 1) * ROWS]
 
 
 def columns_by_y(x):
-    width = N // NY
-    return pl.pallas_call(
-        by_y_kernel,
-        grid=(NY,),
-        in_specs=[pl.BlockSpec((ROWS, width), lambda j: (0, j))],
-        out_specs=pl.BlockSpec((NY, ROWS, width // NY), lambda j: (0, 0, j)),
-        out_shape=jax.ShapeDtypeStruct((NY, ROWS, width), BF16),
+    return pl.pallas_call(
+        by_y_kernel, out_shape=jax.ShapeDtypeStruct((NY, ROWS, N // NY), BF16), compiler_params=PARAMS
     )(x)
 
 
 def collect_kernel(*refs):
-    near, far, out = refs[:8], refs[8:11], refs[11]
+    blocks, out = refs[:8], refs[8]
     x = lax.axis_index("x_lo")
-    slots = z_slots()
-    far_blocks = [(ref, k) for ref in far for k in range(ref.shape[0] // ROWS)]
-    for k, z in enumerate(slots):
-        here = pl.multiple_of((z * NX + x) * ROWS, ROWS)
-        there = pl.multiple_of((z * NX + 1 - x) * ROWS, ROWS)
-        out[pl.ds(here, ROWS)] = near[k][...]
-        ref, i = far_blocks[k]
-        out[pl.ds(there, ROWS)] = ref[i * ROWS : (i + 1) * ROWS]
-
-
-def collect(near, far):
+    for k, z in enumerate(z_slots()):
+        for dx in range(NX):
+            slot = z * NX + (x + dx) % NX
+            out[pl.ds(pl.multiple_of(slot * ROWS, ROWS), ROWS)] = blocks[k][dx * ROWS : (dx + 1) * ROWS]
+
+
+def collect(blocks):
     return pl.pallas_call(
         collect_kernel, out_shape=jax.ShapeDtypeStruct((N // NY, COLS), BF16), compiler_params=PARAMS
-    )(*near, *far)
+    )(*blocks)
 
 
 def partial_kernel(steps, own_ref, sib_ref, rhs_ref, *outs):
@@ -165,28 +155,28 @@
 
 
 def final_kernel(pieces, out):
-    for k in range(4):
-        out[:, k * ROWS : (k + 1) * ROWS] = pieces[0, k].astype(F32) + pieces[1, k].astype(F32)
+    for src in range(NX * NY):
+        total = pieces[src].astype(F32) + pieces[NX * NY + src].astype(F32)
+        for zl in range(2):
+            start = (zl * NX * NY + src) * ROWS
+            out[:, start : start + ROWS] = total[:, zl * ROWS : (zl + 1) * ROWS]
 
 
 def assemble(pieces):
     return pl.pallas_call(
-        final_kernel,
-        grid=(4,),
-        in_specs=[pl.BlockSpec((2, 4, ROWS, ROWS), lambda j: (0, j % 2, 0, j // 2))],
-        out_specs=pl.BlockSpec((ROWS, 4 * ROWS), lambda j: (0, j)),
-        out_shape=jax.ShapeDtypeStruct((ROWS, 16 * ROWS), F32),
-    )(pieces.reshape(2, 8, ROWS, 2 * ROWS))
+        final_kernel, out_shape=jax.ShapeDtypeStruct((ROWS, 16 * ROWS), F32), compiler_params=PARAMS
+    )(pieces)
 
 
 def body(integrals, orbitals):
-    own = lax.all_to_all(columns_by_y(integrals[0]), "y", 0, 0, tiled=True)
     core = lax.axis_index("core")
     mine = lax.dynamic_slice(orbitals, (0, core * COLS), (ROWS, COLS))
-    near, far = z_gather(mine, lambda blocks: x_send(jnp.concatenate(blocks, axis=0)))
-    own, far[-1] = lax.optimization_barrier((own, far[-1]))
+    theirs, columns = lax.optimization_barrier((x_send(mine), columns_by_y(integrals[0])))
+    own = lax.all_to_all(columns, "y", 0, 0, tiled=True)
+    blocks = z_gather(jnp.concatenate([mine, theirs], axis=0), 2, True)
+    own, blocks[5], blocks[6] = lax.optimization_barrier((own, blocks[5], blocks[6]))
     sib = swap(own, "core")
-    rhs = collect(near, far)
+    rhs = collect(blocks)
     (across,) = partial_half(own, sib, rhs, 2)
     across = y_send(across, 2)
     up, down = partial_half(own, sib, rhs, 1, 3)
@@ -196,7 +186,7 @@
 
     pair = jnp.stack([half, swap(half, "x_lo")])
     lines = [pair] + [y_send(pair, -s) for s in (1, 2, 3)]
-    z_blocks, _ = z_gather(half)
+    z_blocks = z_gather(half)
 
     other = tile_product(z_blocks, lines)
     mine = tile_product(z_blocks, lines, swap(other, "core"))

time: 143 us -> 132 us (0.923)
  waiting for transfers between devices: 57.5 us -> 44.5 us
  starting transfers between devices: 49.1 us -> 56.2 us
  Pallas kernels: 12.7 us -> 6.73 us
  local copies, waits for them, and re-layouts: 3.29 us -> 5.47 us
    ppermute x14, starting transfers between devices: 21.5 us -> 28.1 us  [ring_send(): return lax.ppermute(x, ('core', axis), ring_pairs(size, step))]
    pallas_call x2, Pallas kernels: 7.45 us -> 1.49 us  [the longest x1 1.12 us: assemble(): pl.pallas_call(final_kernel, out_shape=jax.ShapeDtypeStruct((ROWS, 16 * R...]
    ppermute x3 -> x1, waiting for transfers between devices: 5.57 us -> 0.01 us  [x_send(): return lax.ppermute(x, ('x_hi', 'core', 'x_lo'), pairs)]
    ppermute x6, waiting for transfers between devices: 21.3 us -> 17.2 us  [y_send(): return lax.ppermute(x, 'y', [(i, (i + step) % NY) for i in range(NY)])]
    ppermute x3, waiting for transfers between devices: 5.99 us -> 2.29 us  [swap(): return lax.ppermute(x, axis, [(0, 1), (1, 0)])]
    unnamed x10, local copies, waits for them, and re-layouts: 3.28 us -> 5.46 us
    ppermute x3 -> x1, starting transfers between devices: 4.81 us -> 3.39 us  [x_send(): return lax.ppermute(x, ('x_hi', 'core', 'x_lo'), pairs)]
  transfers between devices with their start and end apart: 27 -> 25, of which waited for: 20 -> 16; matrix products, arithmetic and copies ran while one was open for 0% -> 0% of each run, Pallas kernels for 1% -> 1%
where the time goes in v4:
time: 132 us
  starting transfers between devices  56.2 us (43%)
  waiting for transfers between devices  44.5 us (34%)
  blocking collectives  19 us (14%)
  Pallas kernels  6.73 us (5%)
  local copies, waits for them, and re-layouts  5.47 us (4%)
    ppermute x14, starting transfers between devices, ring_send(): return lax.ppermute(x, ('core', axis), ring_pairs(size, step))  28.1 us
    ppermute x14, waiting for transfers between devices, ring_send(): return lax.ppermute(x, ('core', axis), ring_pairs(size, step))  24.9 us
    all_to_all x1, blocking collectives, body(): pieces = lax.all_to_all(mine, ('x_hi', 'x_lo', 'y'), 0, 0, tiled=True)  19 us
    ppermute x6, waiting for transfers between devices, y_send(): return lax.ppermute(x, 'y', [(i, (i + step) % NY) for i in range(NY)])  17.2 us
    ppermute x6, starting transfers between devices, y_send(): return lax.ppermute(x, 'y', [(i, (i + step) % NY) for i in range(NY)])  11.2 us
    ppermute x3, starting transfers between devices, swap(): return lax.ppermute(x, axis, [(0, 1), (1, 0)])  9.2 us
    unnamed x10, local copies, waits for them, and re-layouts  5.46 us
    all_to_all x1, starting transfers between devices, body(): own = lax.all_to_all(columns, 'y', 0, 0, tiled=True)  4.18 us
  transfers between devices with their start and end apart: 25, of which 16 were waited for; matrix products, arithmetic and copies ran while one was open for 0% of the time, Pallas kernels for 1%

profile of v4, /device:TPU:1, one launch (start us, length us, event | category | flops | bytes accessed | tf_op | source)
XLA Modules:
  0.0 132.1 jit_solution(13459801926612314360)
XLA Ops:
  0.0 0.9 copy-done
  0.9 3.4 %collective-permute-start = (bf16[128,384]{1,0:T(8,128)(2,1)S(1)}, bf16[128,384]{1,0:T(8,128)(2,1)S(1)}, u32[]{:S(2)}, u32[]{:S(2)}) collective-permute-start(bf16[128,384]{1,0:T(8,128)(2,1)S(1)} %constant_dynamic-slice_fusion), channel_id=1, source_target_pairs={{0,4},{4,128},{128,132},{132,0},{64,196},{68,64},{192,68},{196,192... | collective-permute-start | bytes 294920 | tf_op jit(solution)/shard_map/ppermute | solution.py:42
  4.3 1.6 %copy-done.2 = bf16[1,128,8192]{2,1,0:T(8,128)(2,1)S(1)} copy-done((bf16[1,128,8192]{2,1,0:T(8,128)(2,1)S(1)}, bf16[1,128,8192]{2,1,0:T(8,128)(2,1)}, u32[]{:S(2)}) %copy-start.2) | copy-done | bytes 2097176
  5.9 0.4 shard_map.28
  6.3 1.3 %copy-done.1 = bf16[4,128,2048]{2,1,0:T(8,128)(2,1)} copy-done((bf16[4,128,2048]{2,1,0:T(8,128)(2,1)}, bf16[4,128,2048]{2,1,0:T(8,128)(2,1)S(1)}, u32[]{:S(2)}) %copy-start.1) | copy-done | bytes 2097176
  7.7 4.2 %all-to-all-start = ((bf16[4,128,2048]{2,1,0:T(8,128)(2,1)}), bf16[4,128,2048]{2,1,0:T(8,128)(2,1)S(1)}, u32[]{:S(2)}, u32[]{:S(2)}) async-start(bf16[4,128,2048]{2,1,0:T(8,128)(2,1)} %copy-done.1), calls=%async_computation | async-start | bytes 4194304 | tf_op jit(solution)/shard_map/all_to_all | solution.py:175
  11.9 1.7 %collective-permute-start.2 = (bf16[256,384]{1,0:T(8,128)(2,1)S(1)}, bf16[256,384]{1,0:T(8,128)(2,1)S(1)}, u32[]{:S(2)}, u32[]{:S(2)}) collective-permute-start(bf16[256,384]{1,0:T(8,128)(2,1)S(1)} %pad_maximum_fusion.1.refs_0_), channel_id=1, source_target_pairs={{0,56},{8,0},{16,8},{24,16},{32,24},{40,32},{48,40},{56,48},{64,72... | collective-permute-start | bytes 589832 | tf_op jit(solution)/shard_map/ppermute | solution.py:31
  13.6 4.0 %collective-permute-start.1 = (bf16[256,384]{1,0:T(8,128)(2,1)S(1)}, bf16[256,384]{1,0:T(8,128)(2,1)S(1)}, u32[]{:S(2)}, u32[]{:S(2)}) collective-permute-start(bf16[256,384]{1,0:T(8,128)(2,1)S(1)} %pad_maximum_fusion.1.refs_0_), channel_id=1, source_target_pairs={{0,8},{8,16},{16,24},{24,32},{32,40},{40,48},{48,56},{56,0},{64,12... | collective-permute-start | bytes 589832 | tf_op jit(solution)/shard_map/ppermute | solution.py:31
  17.6 3.3 %collective-permute-done.2.refs_2_ = bf16[256,384]{1,0:T(8,128)(2,1)S(1)} collective-permute-done((bf16[256,384]{1,0:T(8,128)(2,1)S(1)}, bf16[256,384]{1,0:T(8,128)(2,1)S(1)}, u32[]{:S(2)}, u32[]{:S(2)}) %collective-permute-start.2) | collective-permute-done | bytes 196640 | tf_op jit(solution)/shard_map/ppermute | solution.py:31
  20.9 3.4 %collective-permute-start.3 = (bf16[256,384]{1,0:T(8,128)(2,1)S(1)}, bf16[256,384]{1,0:T(8,128)(2,1)S(1)}, u32[]{:S(2)}, u32[]{:S(2)}) collective-permute-start(bf16[256,384]{1,0:T(8,128)(2,1)S(1)} %collective-permute-done.1.refs_1_), channel_id=1, source_target_pairs={{0,8},{8,16},{16,24},{24,32},{32,40},{40,48},{48,56},{56,0},{64,12... | collective-permute-start | bytes 589832 | tf_op jit(solution)/shard_map/ppermute | solution.py:31
  24.3 2.6 %collective-permute-done.3.refs_3_ = bf16[256,384]{1,0:T(8,128)(2,1)S(1)} collective-permute-done((bf16[256,384]{1,0:T(8,128)(2,1)S(1)}, bf16[256,384]{1,0:T(8,128)(2,1)S(1)}, u32[]{:S(2)}, u32[]{:S(2)}) %collective-permute-start.3) | collective-permute-done | bytes 196640 | tf_op jit(solution)/shard_map/ppermute | solution.py:31
  27.0 3.7 %collective-permute-done.4.refs_4_ = bf16[256,384]{1,0:T(8,128)(2,1)S(1)} collective-permute-done((bf16[256,384]{1,0:T(8,128)(2,1)S(1)}, bf16[256,384]{1,0:T(8,128)(2,1)S(1)}, u32[]{:S(2)}, u32[]{:S(2)}) %collective-permute-start.4) | collective-permute-done | bytes 196640 | tf_op jit(solution)/shard_map/ppermute | solution.py:31
  30.6 2.7 %collective-permute-start.5 = (bf16[256,384]{1,0:T(8,128)(2,1)S(1)}, bf16[256,384]{1,0:T(8,128)(2,1)S(1)}, u32[]{:S(2)}, u32[]{:S(2)}) collective-permute-start(bf16[256,384]{1,0:T(8,128)(2,1)S(1)} %collective-permute-done.3.refs_3_), channel_id=1, source_target_pairs={{0,8},{8,16},{16,24},{24,32},{32,40},{40,48},{48,56},{56,0},{64,12... | collective-permute-start | bytes 589832 | tf_op jit(solution)/shard_map/ppermute | solution.py:31
  33.3 3.3 %collective-permute-done.6.refs_6_ = bf16[256,384]{1,0:T(8,128)(2,1)S(1)} collective-permute-done((bf16[256,384]{1,0:T(8,128)(2,1)S(1)}, bf16[256,384]{1,0:T(8,128)(2,1)S(1)}, u32[]{:S(2)}, u32[]{:S(2)}) %collective-permute-start.6) | collective-permute-done | bytes 196640 | tf_op jit(solution)/shard_map/ppermute | solution.py:31
  36.7 0.7 copy-done.3
  37.3 6.0 %collective-permute-start.7 = (bf16[4,128,2048]{2,1,0:T(8,128)(2,1)S(1)}, bf16[4,128,2048]{2,1,0:T(8,128)(2,1)S(1)}, u32[]{:S(2)}, u32[]{:S(2)}) collective-permute-start(bf16[4,128,2048]{2,1,0:T(8,128)(2,1)S(1)} %all-to-all-done.refs_0_), channel_id=1, source_target_pairs={{0,64},{64,0},{1,65},{65,1},{2,66},{66,2},{3,67},{67,3},{4,68},{68... | collective-permute-start | bytes 6291464 | tf_op jit(solution)/shard_map/ppermute | solution.py:46
  43.3 1.8 %collective-permute-start.8 = (bf16[256,384]{1,0:T(8,128)(2,1)S(1)}, bf16[256,384]{1,0:T(8,128)(2,1)S(1)}, u32[]{:S(2)}, u32[]{:S(2)}) collective-permute-start(bf16[256,384]{1,0:T(8,128)(2,1)S(1)} %collective-permute-done.3.refs_3_), channel_id=1, source_target_pairs={{0,16},{8,24},{16,32},{24,40},{32,48},{40,56},{48,0},{56,8},{64,11... | collective-permute-start | bytes 589832 | tf_op jit(solution)/shard_map/ppermute | solution.py:31
  45.1 4.3 %collective-permute-done.8.refs_7_ = bf16[256,384]{1,0:T(8,128)(2,1)S(1)} collective-permute-done((bf16[256,384]{1,0:T(8,128)(2,1)S(1)}, bf16[256,384]{1,0:T(8,128)(2,1)S(1)}, u32[]{:S(2)}, u32[]{:S(2)}) %collective-permute-start.8) | collective-permute-done | bytes 196640 | tf_op jit(solution)/shard_map/ppermute | solution.py:31
  49.4 0.9 copy-done.4
  50.4 0.2 shard_map.29.refs_2_
  50.6 1.3 shard_map.31
  51.8 2.6 %collective-permute-start.9 = (f32[128,768]{1,0:T(8,128)S(1)}, f32[128,768]{1,0:T(8,128)S(1)}, u32[]{:S(2)}, u32[]{:S(2)}) collective-permute-start(f32[128,768]{1,0:T(8,128)S(1)} %get-tuple-element.25), channel_id=1, source_target_pairs={{0,1},{1,2},{2,3},{3,0},{4,5},{5,6},{6,7},{7,4},{8,9},{9,10},{10,1... | collective-permute-start | bytes 1179656 | tf_op jit(solution)/shard_map/ppermute | solution.py:50
  54.5 1.2 collective-permute-start.10
  55.6 0.7 shard_map.32
  56.3 2.1 %collective-permute-start.11 = (f32[128,768]{1,0:T(8,128)S(1)}, f32[128,768]{1,0:T(8,128)S(1)}, u32[]{:S(2)}, u32[]{:S(2)}) collective-permute-start(f32[128,768]{1,0:T(8,128)S(1)} %shard_map.32), channel_id=1, source_target_pairs={{0,2},{1,3},{2,0},{3,1},{4,6},{5,7},{6,4},{7,5},{8,10},{9,11},{10,... | collective-permute-start | bytes 1179656 | tf_op jit(solution)/shard_map/ppermute | solution.py:50
  58.4 0.7 shard_map.30
  59.1 2.9 %collective-permute-done.9 = f32[128,768]{1,0:T(8,128)S(1)} collective-permute-done((f32[128,768]{1,0:T(8,128)S(1)}, f32[128,768]{1,0:T(8,128)S(1)}, u32[]{:S(2)}, u32[]{:S(2)}) %collective-permute-start.9) | collective-permute-done | bytes 393248 | tf_op jit(solution)/shard_map/ppermute | solution.py:50
  62.0 0.4 collective-permute-done.10
  62.4 9.0 %collective-permute-done.11 = f32[128,768]{1,0:T(8,128)S(1)} collective-permute-done((f32[128,768]{1,0:T(8,128)S(1)}, f32[128,768]{1,0:T(8,128)S(1)}, u32[]{:S(2)}, u32[]{:S(2)}) %collective-permute-start.11) | collective-permute-done | bytes 393248 | tf_op jit(solution)/shard_map/ppermute | solution.py:50
  71.4 5.3 %collective-permute-start.12 = (bf16[128,768]{1,0:T(8,128)(2,1)S(1)}, bf16[128,768]{1,0:T(8,128)(2,1)S(1)}, u32[]{:S(2)}, u32[]{:S(2)}) collective-permute-start(bf16[128,768]{1,0:T(8,128)(2,1)S(1)} %add_convert_fusion.refs_0_), channel_id=1, source_target_pairs={{0,8},{8,16},{16,24},{24,32},{32,40},{40,48},{48,56},{56,0},{64,12... | collective-permute-start | bytes 589832 | tf_op jit(solution)/shard_map/ppermute | solution.py:31
  76.7 2.6 %collective-permute-done.12.refs_1_ = bf16[128,768]{1,0:T(8,128)(2,1)S(1)} collective-permute-done((bf16[128,768]{1,0:T(8,128)(2,1)S(1)}, bf16[128,768]{1,0:T(8,128)(2,1)S(1)}, u32[]{:S(2)}, u32[]{:S(2)}) %collective-permute-start.12) | collective-permute-done | bytes 196640 | tf_op jit(solution)/shard_map/ppermute | solution.py:31
  79.3 3.1 %collective-permute-start.14 = (bf16[128,768]{1,0:T(8,128)(2,1)S(1)}, bf16[128,768]{1,0:T(8,128)(2,1)S(1)}, u32[]{:S(2)}, u32[]{:S(2)}) collective-permute-start(bf16[128,768]{1,0:T(8,128)(2,1)S(1)} %collective-permute-done.12.refs_1_), channel_id=1, source_target_pairs={{0,8},{8,16},{16,24},{24,32},{32,40},{40,48},{48,56},{56,0},{64,12... | collective-permute-start | bytes 589832 | tf_op jit(solution)/shard_map/ppermute | solution.py:31
  82.5 1.2 collective-permute-done.13.refs_2_
  83.7 1.0 collective-permute-start.22
  84.7 2.7 %collective-permute-start.21 = (bf16[2,128,768]{2,1,0:T(8,128)(2,1)S(1)}, bf16[2,128,768]{2,1,0:T(8,128)(2,1)S(1)}, u32[]{:S(2)}, u32[]{:S(2)}) collective-permute-start(bf16[2,128,768]{2,1,0:T(8,128)(2,1)S(1)} %pad_maximum_fusion.refs_8_), channel_id=1, source_target_pairs={{0,2},{1,3},{2,0},{3,1},{4,6},{5,7},{6,4},{7,5},{8,10},{9,11},{10,... | collective-permute-start | bytes 1179656 | tf_op jit(solution)/shard_map/ppermute | solution.py:50
  87.4 2.7 %collective-permute-start.16 = (bf16[128,768]{1,0:T(8,128)(2,1)S(1)}, bf16[128,768]{1,0:T(8,128)(2,1)S(1)}, u32[]{:S(2)}, u32[]{:S(2)}) collective-permute-start(bf16[128,768]{1,0:T(8,128)(2,1)S(1)} %collective-permute-done.14.refs_3_), channel_id=1, source_target_pairs={{0,8},{8,16},{16,24},{24,32},{32,40},{40,48},{48,56},{56,0},{64,12... | collective-permute-start | bytes 589832 | tf_op jit(solution)/shard_map/ppermute | solution.py:31
  90.0 1.7 %collective-permute-start.20 = (bf16[2,128,768]{2,1,0:T(8,128)(2,1)S(1)}, bf16[2,128,768]{2,1,0:T(8,128)(2,1)S(1)}, u32[]{:S(2)}, u32[]{:S(2)}) collective-permute-start(bf16[2,128,768]{2,1,0:T(8,128)(2,1)S(1)} %pad_maximum_fusion.refs_8_), channel_id=1, source_target_pairs={{0,3},{1,0},{2,1},{3,2},{4,7},{5,4},{6,5},{7,6},{8,11},{9,8},{10,9... | collective-permute-start | bytes 1179656 | tf_op jit(solution)/shard_map/ppermute | solution.py:50
  91.8 0.9 collective-permute-done.16.refs_5_
  92.7 3.4 %collective-permute-start.18 = (bf16[128,768]{1,0:T(8,128)(2,1)S(1)}, bf16[128,768]{1,0:T(8,128)(2,1)S(1)}, u32[]{:S(2)}, u32[]{:S(2)}) collective-permute-start(bf16[128,768]{1,0:T(8,128)(2,1)S(1)} %collective-permute-done.16.refs_5_), channel_id=1, source_target_pairs={{0,8},{8,16},{16,24},{24,32},{32,40},{40,48},{48,56},{56,0},{64,12... | collective-permute-start | bytes 589832 | tf_op jit(solution)/shard_map/ppermute | solution.py:31
  96.1 3.0 %collective-permute-done.17.refs_6_ = bf16[128,768]{1,0:T(8,128)(2,1)S(1)} collective-permute-done((bf16[128,768]{1,0:T(8,128)(2,1)S(1)}, bf16[128,768]{1,0:T(8,128)(2,1)S(1)}, u32[]{:S(2)}, u32[]{:S(2)}) %collective-permute-start.17) | collective-permute-done | bytes 196640 | tf_op jit(solution)/shard_map/ppermute | solution.py:31
  99.0 3.9 %collective-permute-done.21.refs_10_ = bf16[2,128,768]{2,1,0:T(8,128)(2,1)S(1)} collective-permute-done((bf16[2,128,768]{2,1,0:T(8,128)(2,1)S(1)}, bf16[2,128,768]{2,1,0:T(8,128)(2,1)S(1)}, u32[]{:S(2)}, u32[]{:S(2)}) %collective-permute-start.21) | collective-permute-done | bytes 393248 | tf_op jit(solution)/shard_map/ppermute | solution.py:50
  103.0 1.1 collective-permute-done.20.refs_9_
  104.1 1.2 shard_map.33
  105.3 3.2 %collective-permute-start.23 = (bf16[16,128,256]{2,1,0:T(8,128)(2,1)S(1)}, bf16[16,128,256]{2,1,0:T(8,128)(2,1)S(1)}, u32[]{:S(2)}, u32[]{:S(2)}) collective-permute-start(bf16[16,128,256]{2,1,0:T(8,128)(2,1)S(1)} %shard_map.33), channel_id=1, source_target_pairs={{0,64},{64,0},{1,65},{65,1},{2,66},{66,2},{3,67},{67,3},{4,68},{68... | collective-permute-start | bytes 3145736 | tf_op jit(solution)/shard_map/ppermute | solution.py:46
  108.5 2.3 %collective-permute-done.23.refs_12_ = bf16[16,128,256]{2,1,0:T(8,128)(2,1)S(1)} collective-permute-done((bf16[16,128,256]{2,1,0:T(8,128)(2,1)S(1)}, bf16[16,128,256]{2,1,0:T(8,128)(2,1)S(1)}, u32[]{:S(2)}, u32[]{:S(2)}) %collective-permute-start.23) | collective-permute-done | bytes 1048608 | tf_op jit(solution)/shard_map/ppermute | solution.py:46
  110.8 1.2 shard_map.34
  112.0 19.0 %all_to_all.10.pieces = bf16[16,128,256]{2,1,0:T(8,128)(2,1)S(1)} all-to-all(bf16[16,128,256]{2,1,0:T(8,128)(2,1)S(1)} %shard_map.34), channel_id=1, replica_groups=mesh['x_hi'=2,'core'=2,'z'=8,'x_lo'=2,'y'=4] {'x_hi','x_lo','y'}, dimensions={0} | all-to-all | bytes 2097152 | tf_op jit(solution)/shard_map/all_to_all | solution.py:193
  131.0 1.1 shard_map.35
  (25 shorter events, 0.3 us)
Async XLA Ops:
  0.0 0.9 copy-start
  0.9 6.7 %collective-permute-start = (bf16[128,384]{1,0:T(8,128)(2,1)S(1)}, bf16[128,384]{1,0:T(8,128)(2,1)S(1)}, u32[]{:S(2)}, u32[]{:S(2)}) collective-permute-start(bf16[128,384]{1,0:T(8,128)(2,1)S(1)} %constant_dynamic-slice_fusion), channel_id=1, source_target_pairs={{0,4},{4,128},{128,132},{132,0},{64,196},{68,64},{192,68},{196,192... | collective-permute-start | bytes 294920 | tf_op jit(solution)/shard_map/ppermute | solution.py:42
  4.3 1.6 %copy-start.2 = (bf16[1,128,8192]{2,1,0:T(8,128)(2,1)S(1)}, bf16[1,128,8192]{2,1,0:T(8,128)(2,1)}, u32[]{:S(2)}) copy-start(bf16[1,128,8192]{2,1,0:T(8,128)(2,1)} %param.2) | copy-start | bytes 6291460
  6.3 1.3 %copy-start.1 = (bf16[4,128,2048]{2,1,0:T(8,128)(2,1)}, bf16[4,128,2048]{2,1,0:T(8,128)(2,1)S(1)}, u32[]{:S(2)}) copy-start(bf16[4,128,2048]{2,1,0:T(8,128)(2,1)S(1)} %shard_map.28) | copy-start | bytes 6291460
  7.7 29.7 %all-to-all-start = ((bf16[4,128,2048]{2,1,0:T(8,128)(2,1)}), bf16[4,128,2048]{2,1,0:T(8,128)(2,1)S(1)}, u32[]{:S(2)}, u32[]{:S(2)}) async-start(bf16[4,128,2048]{2,1,0:T(8,128)(2,1)} %copy-done.1), calls=%async_computation | async-start | bytes 4194304 | tf_op jit(solution)/shard_map/all_to_all | solution.py:175
  11.9 9.0 %collective-permute-start.2 = (bf16[256,384]{1,0:T(8,128)(2,1)S(1)}, bf16[256,384]{1,0:T(8,128)(2,1)S(1)}, u32[]{:S(2)}, u32[]{:S(2)}) collective-permute-start(bf16[256,384]{1,0:T(8,128)(2,1)S(1)} %pad_maximum_fusion.1.refs_0_), channel_id=1, source_target_pairs={{0,56},{8,0},{16,8},{24,16},{32,24},{40,32},{48,40},{56,48},{64,72... | collective-permute-start | bytes 589832 | tf_op jit(solution)/shard_map/ppermute | solution.py:31
  13.6 7.4 %collective-permute-start.1 = (bf16[256,384]{1,0:T(8,128)(2,1)S(1)}, bf16[256,384]{1,0:T(8,128)(2,1)S(1)}, u32[]{:S(2)}, u32[]{:S(2)}) collective-permute-start(bf16[256,384]{1,0:T(8,128)(2,1)S(1)} %pad_maximum_fusion.1.refs_0_), channel_id=1, source_target_pairs={{0,8},{8,16},{16,24},{24,32},{32,40},{40,48},{48,56},{56,0},{64,12... | collective-permute-start | bytes 589832 | tf_op jit(solution)/shard_map/ppermute | solution.py:31
  20.9 6.0 %collective-permute-start.3 = (bf16[256,384]{1,0:T(8,128)(2,1)S(1)}, bf16[256,384]{1,0:T(8,128)(2,1)S(1)}, u32[]{:S(2)}, u32[]{:S(2)}) collective-permute-start(bf16[256,384]{1,0:T(8,128)(2,1)S(1)} %collective-permute-done.1.refs_1_), channel_id=1, source_target_pairs={{0,8},{8,16},{16,24},{24,32},{32,40},{40,48},{48,56},{56,0},{64,12... | collective-permute-start | bytes 589832 | tf_op jit(solution)/shard_map/ppermute | solution.py:31
  24.3 6.3 %collective-permute-start.4 = (bf16[256,384]{1,0:T(8,128)(2,1)S(1)}, bf16[256,384]{1,0:T(8,128)(2,1)S(1)}, u32[]{:S(2)}, u32[]{:S(2)}) collective-permute-start(bf16[256,384]{1,0:T(8,128)(2,1)S(1)} %collective-permute-done.2.refs_2_), channel_id=1, source_target_pairs={{0,56},{8,0},{16,8},{24,16},{32,24},{40,32},{48,40},{56,48},{64,72... | collective-permute-start | bytes 589832 | tf_op jit(solution)/shard_map/ppermute | solution.py:31
  30.6 6.0 %collective-permute-start.6 = (bf16[256,384]{1,0:T(8,128)(2,1)S(1)}, bf16[256,384]{1,0:T(8,128)(2,1)S(1)}, u32[]{:S(2)}, u32[]{:S(2)}) collective-permute-start(bf16[256,384]{1,0:T(8,128)(2,1)S(1)} %collective-permute-done.4.refs_4_), channel_id=1, source_target_pairs={{0,56},{8,0},{16,8},{24,16},{32,24},{40,32},{48,40},{56,48},{64,72... | collective-permute-start | bytes 589832 | tf_op jit(solution)/shard_map/ppermute | solution.py:31
  30.6 6.0 %collective-permute-start.5 = (bf16[256,384]{1,0:T(8,128)(2,1)S(1)}, bf16[256,384]{1,0:T(8,128)(2,1)S(1)}, u32[]{:S(2)}, u32[]{:S(2)}) collective-permute-start(bf16[256,384]{1,0:T(8,128)(2,1)S(1)} %collective-permute-done.3.refs_3_), channel_id=1, source_target_pairs={{0,8},{8,16},{16,24},{24,32},{32,40},{40,48},{48,56},{56,0},{64,12... | collective-permute-start | bytes 589832 | tf_op jit(solution)/shard_map/ppermute | solution.py:31
  36.7 0.7 copy-start.3
  37.3 13.2 %collective-permute-start.7 = (bf16[4,128,2048]{2,1,0:T(8,128)(2,1)S(1)}, bf16[4,128,2048]{2,1,0:T(8,128)(2,1)S(1)}, u32[]{:S(2)}, u32[]{:S(2)}) collective-permute-start(bf16[4,128,2048]{2,1,0:T(8,128)(2,1)S(1)} %all-to-all-done.refs_0_), channel_id=1, source_target_pairs={{0,64},{64,0},{1,65},{65,1},{2,66},{66,2},{3,67},{67,3},{4,68},{68... | collective-permute-start | bytes 6291464 | tf_op jit(solution)/shard_map/ppermute | solution.py:46
  43.3 6.1 %collective-permute-start.8 = (bf16[256,384]{1,0:T(8,128)(2,1)S(1)}, bf16[256,384]{1,0:T(8,128)(2,1)S(1)}, u32[]{:S(2)}, u32[]{:S(2)}) collective-permute-start(bf16[256,384]{1,0:T(8,128)(2,1)S(1)} %collective-permute-done.3.refs_3_), channel_id=1, source_target_pairs={{0,16},{8,24},{16,32},{24,40},{32,48},{40,56},{48,0},{56,8},{64,11... | collective-permute-start | bytes 589832 | tf_op jit(solution)/shard_map/ppermute | solution.py:31
  49.4 0.9 copy-start.4
  51.8 10.2 %collective-permute-start.9 = (f32[128,768]{1,0:T(8,128)S(1)}, f32[128,768]{1,0:T(8,128)S(1)}, u32[]{:S(2)}, u32[]{:S(2)}) collective-permute-start(f32[128,768]{1,0:T(8,128)S(1)} %get-tuple-element.25), channel_id=1, source_target_pairs={{0,1},{1,2},{2,3},{3,0},{4,5},{5,6},{6,7},{7,4},{8,9},{9,10},{10,1... | collective-permute-start | bytes 1179656 | tf_op jit(solution)/shard_map/ppermute | solution.py:50
  54.5 7.9 %collective-permute-start.10 = (f32[128,768]{1,0:T(8,128)S(1)}, f32[128,768]{1,0:T(8,128)S(1)}, u32[]{:S(2)}, u32[]{:S(2)}) collective-permute-start(f32[128,768]{1,0:T(8,128)S(1)} %get-tuple-element.26), channel_id=1, source_target_pairs={{0,3},{1,0},{2,1},{3,2},{4,7},{5,4},{6,5},{7,6},{8,11},{9,8},{10,9... | collective-permute-start | bytes 1179656 | tf_op jit(solution)/shard_map/ppermute | solution.py:50
  56.3 15.0 %collective-permute-start.11 = (f32[128,768]{1,0:T(8,128)S(1)}, f32[128,768]{1,0:T(8,128)S(1)}, u32[]{:S(2)}, u32[]{:S(2)}) collective-permute-start(f32[128,768]{1,0:T(8,128)S(1)} %shard_map.32), channel_id=1, source_target_pairs={{0,2},{1,3},{2,0},{3,1},{4,6},{5,7},{6,4},{7,5},{8,10},{9,11},{10,... | collective-permute-start | bytes 1179656 | tf_op jit(solution)/shard_map/ppermute | solution.py:50
  71.4 7.9 %collective-permute-start.12 = (bf16[128,768]{1,0:T(8,128)(2,1)S(1)}, bf16[128,768]{1,0:T(8,128)(2,1)S(1)}, u32[]{:S(2)}, u32[]{:S(2)}) collective-permute-start(bf16[128,768]{1,0:T(8,128)(2,1)S(1)} %add_convert_fusion.refs_0_), channel_id=1, source_target_pairs={{0,8},{8,16},{16,24},{24,32},{32,40},{40,48},{48,56},{56,0},{64,12... | collective-permute-start | bytes 589832 | tf_op jit(solution)/shard_map/ppermute | solution.py:31
  76.7 7.0 %collective-permute-start.13 = (bf16[128,768]{1,0:T(8,128)(2,1)S(1)}, bf16[128,768]{1,0:T(8,128)(2,1)S(1)}, u32[]{:S(2)}, u32[]{:S(2)}) collective-permute-start(bf16[128,768]{1,0:T(8,128)(2,1)S(1)} %add_convert_fusion.refs_0_), channel_id=1, source_target_pairs={{0,56},{8,0},{16,8},{24,16},{32,24},{40,32},{48,40},{56,48},{64,72... | collective-permute-start | bytes 589832 | tf_op jit(solution)/shard_map/ppermute | solution.py:31
  76.7 7.0 %collective-permute-start.19 = (bf16[128,768]{1,0:T(8,128)(2,1)S(1)}, bf16[128,768]{1,0:T(8,128)(2,1)S(1)}, u32[]{:S(2)}, u32[]{:S(2)}) collective-permute-start(bf16[128,768]{1,0:T(8,128)(2,1)S(1)} %add_convert_fusion.refs_0_), channel_id=1, source_target_pairs={{0,4},{4,0},{1,5},{5,1},{2,6},{6,2},{3,7},{7,3},{8,12},{12,8},{9,1... | collective-permute-start | bytes 589832 | tf_op jit(solution)/shard_map/ppermute | solution.py:46
  79.3 8.0 %collective-permute-start.14 = (bf16[128,768]{1,0:T(8,128)(2,1)S(1)}, bf16[128,768]{1,0:T(8,128)(2,1)S(1)}, u32[]{:S(2)}, u32[]{:S(2)}) collective-permute-start(bf16[128,768]{1,0:T(8,128)(2,1)S(1)} %collective-permute-done.12.refs_1_), channel_id=1, source_target_pairs={{0,8},{8,16},{16,24},{24,32},{32,40},{40,48},{48,56},{56,0},{64,12... | collective-permute-start | bytes 589832 | tf_op jit(solution)/shard_map/ppermute | solution.py:31
  83.7 8.1 %collective-permute-start.15 = (bf16[128,768]{1,0:T(8,128)(2,1)S(1)}, bf16[128,768]{1,0:T(8,128)(2,1)S(1)}, u32[]{:S(2)}, u32[]{:S(2)}) collective-permute-start(bf16[128,768]{1,0:T(8,128)(2,1)S(1)} %collective-permute-done.13.refs_2_), channel_id=1, source_target_pairs={{0,56},{8,0},{16,8},{24,16},{32,24},{40,32},{48,40},{56,48},{64,72... | collective-permute-start | bytes 589832 | tf_op jit(solution)/shard_map/ppermute | solution.py:31
  83.7 15.3 %collective-permute-start.22 = (bf16[2,128,768]{2,1,0:T(8,128)(2,1)S(1)}, bf16[2,128,768]{2,1,0:T(8,128)(2,1)S(1)}, u32[]{:S(2)}, u32[]{:S(2)}) collective-permute-start(bf16[2,128,768]{2,1,0:T(8,128)(2,1)S(1)} %pad_maximum_fusion.refs_8_), channel_id=1, source_target_pairs={{0,1},{1,2},{2,3},{3,0},{4,5},{5,6},{6,7},{7,4},{8,9},{9,10},{10,1... | collective-permute-start | bytes 1179656 | tf_op jit(solution)/shard_map/ppermute | solution.py:50
  84.7 18.3 %collective-permute-start.21 = (bf16[2,128,768]{2,1,0:T(8,128)(2,1)S(1)}, bf16[2,128,768]{2,1,0:T(8,128)(2,1)S(1)}, u32[]{:S(2)}, u32[]{:S(2)}) collective-permute-start(bf16[2,128,768]{2,1,0:T(8,128)(2,1)S(1)} %pad_maximum_fusion.refs_8_), channel_id=1, source_target_pairs={{0,2},{1,3},{2,0},{3,1},{4,6},{5,7},{6,4},{7,5},{8,10},{9,11},{10,... | collective-permute-start | bytes 1179656 | tf_op jit(solution)/shard_map/ppermute | solution.py:50
  87.4 5.3 %collective-permute-start.16 = (bf16[128,768]{1,0:T(8,128)(2,1)S(1)}, bf16[128,768]{1,0:T(8,128)(2,1)S(1)}, u32[]{:S(2)}, u32[]{:S(2)}) collective-permute-start(bf16[128,768]{1,0:T(8,128)(2,1)S(1)} %collective-permute-done.14.refs_3_), channel_id=1, source_target_pairs={{0,8},{8,16},{16,24},{24,32},{32,40},{40,48},{48,56},{56,0},{64,12... | collective-permute-start | bytes 589832 | tf_op jit(solution)/shard_map/ppermute | solution.py:31
  90.0 14.0 %collective-permute-start.20 = (bf16[2,128,768]{2,1,0:T(8,128)(2,1)S(1)}, bf16[2,128,768]{2,1,0:T(8,128)(2,1)S(1)}, u32[]{:S(2)}, u32[]{:S(2)}) collective-permute-start(bf16[2,128,768]{2,1,0:T(8,128)(2,1)S(1)} %pad_maximum_fusion.refs_8_), channel_id=1, source_target_pairs={{0,3},{1,0},{2,1},{3,2},{4,7},{5,4},{6,5},{7,6},{8,11},{9,8},{10,9... | collective-permute-start | bytes 1179656 | tf_op jit(solution)/shard_map/ppermute | solution.py:50
  91.8 7.3 %collective-permute-start.17 = (bf16[128,768]{1,0:T(8,128)(2,1)S(1)}, bf16[128,768]{1,0:T(8,128)(2,1)S(1)}, u32[]{:S(2)}, u32[]{:S(2)}) collective-permute-start(bf16[128,768]{1,0:T(8,128)(2,1)S(1)} %collective-permute-done.15.refs_4_), channel_id=1, source_target_pairs={{0,56},{8,0},{16,8},{24,16},{32,24},{40,32},{48,40},{56,48},{64,72... | collective-permute-start | bytes 589832 | tf_op jit(solution)/shard_map/ppermute | solution.py:31
  92.7 11.4 %collective-permute-start.18 = (bf16[128,768]{1,0:T(8,128)(2,1)S(1)}, bf16[128,768]{1,0:T(8,128)(2,1)S(1)}, u32[]{:S(2)}, u32[]{:S(2)}) collective-permute-start(bf16[128,768]{1,0:T(8,128)(2,1)S(1)} %collective-permute-done.16.refs_5_), channel_id=1, source_target_pairs={{0,8},{8,16},{16,24},{24,32},{32,40},{40,48},{48,56},{56,0},{64,12... | collective-permute-start | bytes 589832 | tf_op jit(solution)/shard_map/ppermute | solution.py:31
  105.3 5.5 %collective-permute-start.23 = (bf16[16,128,256]{2,1,0:T(8,128)(2,1)S(1)}, bf16[16,128,256]{2,1,0:T(8,128)(2,1)S(1)}, u32[]{:S(2)}, u32[]{:S(2)}) collective-permute-start(bf16[16,128,256]{2,1,0:T(8,128)(2,1)S(1)} %shard_map.33), channel_id=1, source_target_pairs={{0,64},{64,0},{1,65},{65,1},{2,66},{66,2},{3,67},{67,3},{4,68},{68... | collective-permute-start | bytes 3145736 | tf_op jit(solution)/shard_map/ppermute | solution.py:46

commit v5 on v4

--- a/solution.py
+++ b/solution.py
@@ -53,15 +53,16 @@
 Z_OFFSETS = (0, -1, 1, -2, 2, -3, 3, -4)
 
 
-def z_gather(x, hops=1, in_step=False):
-    blocks, fwd, bwd = [x], [x], [x]
-    for k in range(3):
-        if in_step and k:
-            fwd[-1], bwd[-1] = lax.optimization_barrier((fwd[-1], bwd[-1]))
-        fwd.append(ring_send(fwd[-1], "z", 1))
-        bwd.append(ring_send(bwd[-1], "z", -1))
-        blocks += [fwd[-1], bwd[-1]]
-    return blocks + [ring_send(fwd[4 - hops], "z", hops)]
+def z_step(fwd, bwd):
+    return ring_send(fwd, "z", 1), ring_send(bwd, "z", -1)
+
+
+def z_gather(x):
+    blocks, fwd, bwd = [x], x, x
+    for _ in range(3):
+        fwd, bwd = z_step(fwd, bwd)
+        blocks += [fwd, bwd]
+    return blocks + [ring_send(fwd, "z", 1)]
 
 
 def z_slots():
@@ -72,17 +73,17 @@
 PARAMS = pltpu.CompilerParams(vmem_limit_bytes=12 << 20)
 
 
-def by_y_kernel(x_ref, out_ref):
-    for y in range(NY):
+def by_y_kernel(x_ref, *outs):
+    y = lax.axis_index("y")
+    for s, out in enumerate(outs):
         for k in range(NZ * NX):
-            block = k * NY + y
-            out_ref[y, :, k * ROWS : (k + 1) * ROWS] = x_ref[:, block * ROWS : (block + 1) * ROWS]
+            start = pl.multiple_of((k * NY + (y + s) % NY) * ROWS, ROWS)
+            out[:, k * ROWS : (k + 1) * ROWS] = x_ref[:, pl.ds(start, ROWS)]
 
 
 def columns_by_y(x):
-    return pl.pallas_call(
-        by_y_kernel, out_shape=jax.ShapeDtypeStruct((NY, ROWS, N // NY), BF16), compiler_params=PARAMS
-    )(x)
+    shape = jax.ShapeDtypeStruct((ROWS, N // NY), BF16)
+    return pl.pallas_call(by_y_kernel, out_shape=[shape] * NY, compiler_params=PARAMS)(x)
 
 
 def collect_kernel(*refs):
@@ -100,22 +101,21 @@
     )(*blocks)
 
 
-def partial_kernel(steps, own_ref, sib_ref, rhs_ref, *outs):
-    y = lax.axis_index("y")
-    for step, out in zip(steps, outs):
-        row = (y + step) % NY
-        lhs = jnp.concatenate([own_ref[row], sib_ref[row]], axis=0)
+def partial_kernel(rhs_ref, *refs):
+    count = len(refs) // 3
+    for own, sib, out in zip(refs[:count], refs[count : 2 * count], refs[2 * count :]):
+        lhs = jnp.concatenate([own[...], sib[...]], axis=0)
         prod = jnp.dot(lhs, rhs_ref[...], preferred_element_type=F32)
         out[:, :COLS] = prod[:ROWS]
         out[:, COLS:] = prod[ROWS:]
 
 
-def partial_half(own, sib, rhs, *steps):
-    return pl.pallas_call(
-        lambda *refs: partial_kernel(steps, *refs),
-        out_shape=[jax.ShapeDtypeStruct((ROWS, OCC), F32)] * len(steps),
+def partial_half(rhs, own, sib):
+    return pl.pallas_call(
+        partial_kernel,
+        out_shape=[jax.ShapeDtypeStruct((ROWS, OCC), F32)] * len(own),
         compiler_params=PARAMS,
-    )(own, sib, rhs)
+    )(rhs, *own, *sib)
 
 
 def tile_kernel(keep, *refs):
@@ -172,16 +172,24 @@
     core = lax.axis_index("core")
     mine = lax.dynamic_slice(orbitals, (0, core * COLS), (ROWS, COLS))
     theirs, columns = lax.optimization_barrier((x_send(mine), columns_by_y(integrals[0])))
-    own = lax.all_to_all(columns, "y", 0, 0, tiled=True)
-    blocks = z_gather(jnp.concatenate([mine, theirs], axis=0), 2, True)
-    own, blocks[5], blocks[6] = lax.optimization_barrier((own, blocks[5], blocks[6]))
-    sib = swap(own, "core")
-    rhs = collect(blocks)
-    (across,) = partial_half(own, sib, rhs, 2)
+    rows = [columns[0]] + [y_send(columns[s], s) for s in (1, 2, 3)]
+    sib = [swap(rows[0], "core"), None, None, None]
+    pair = jnp.concatenate([mine, theirs], axis=0)
+    first = z_step(pair, pair)
+    first, sib[0] = lax.optimization_barrier((first, sib[0]))
+    second = z_step(*first)
+    second, rows[1], rows[3] = lax.optimization_barrier((second, rows[1], rows[3]))
+    third = z_step(*second)
+    far = ring_send(second[0], "z", 2)
+    sib[1], sib[3] = swap(rows[1], "core"), swap(rows[3], "core")
+    third, far, rows[2] = lax.optimization_barrier((third, far, rows[2]))
+    sib[2] = swap(rows[2], "core")
+    rhs = collect([pair, *first, *second, *third, far])
+    down, up = partial_half(rhs, [rows[1], rows[3]], [sib[1], sib[3]])
+    down, up = y_send(down, -1), y_send(up, 1)
+    (across,) = partial_half(rhs, [rows[2]], [sib[2]])
     across = y_send(across, 2)
-    up, down = partial_half(own, sib, rhs, 1, 3)
-    up, down = y_send(up, 1), y_send(down, 3)
-    (here,) = partial_half(own, sib, rhs, 0)
+    (here,) = partial_half(rhs, [rows[0]], [sib[0]])
     half = (here + up + down + across).astype(BF16)
 
     pair = jnp.stack([half, swap(half, "x_lo")])

time: 132 us -> 131 us (level)
  starting transfers between devices: 56.2 us -> 43.7 us
  waiting for transfers between devices: 44.5 us -> 56.9 us
  local copies, waits for them, and re-layouts: 5.47 us -> 2.53 us
  blocking collectives: 19 us -> 20.4 us
    ppermute x6 -> x9, waiting for transfers between devices: 17.2 us -> 36 us  [y_send(): return lax.ppermute(x, 'y', [(i, (i + step) % NY) for i in range(NY)])]
    ppermute x14, starting transfers between devices: 28.1 us -> 20.7 us  [ring_send(): return lax.ppermute(x, ('core', axis), ring_pairs(size, step))]
    ppermute x14, waiting for transfers between devices: 24.9 us -> 18.3 us  [ring_send(): return lax.ppermute(x, ('core', axis), ring_pairs(size, step))]
    all_to_all x1 -> x0, starting transfers between devices: 4.18 us -> none  [body(): own = lax.all_to_all(columns, 'y', 0, 0, tiled=True)]
    unnamed x10 -> x4, local copies, waits for them, and re-layouts: 5.46 us -> 2.52 us
    ppermute x3 -> x6, starting transfers between devices: 9.2 us -> 6.66 us  [swap(): return lax.ppermute(x, axis, [(0, 1), (1, 0)])]
    ppermute x6 -> x9, starting transfers between devices: 11.2 us -> 12.9 us  [y_send(): return lax.ppermute(x, 'y', [(i, (i + step) % NY) for i in range(NY)])]
    all_to_all x1, blocking collectives: 19 us -> 20.4 us  [body(): pieces = lax.all_to_all(mine, ('x_hi', 'x_lo', 'y'), 0, 0, tiled=True)]
  transfers between devices with their start and end apart: 25 -> 30, of which waited for: 16 -> 14; matrix products, arithmetic and copies ran while one was open for 0% -> 0% of each run, Pallas kernels for 1% -> 3%
where the time goes in v5:
time: 131 us
  waiting for transfers between devices  56.9 us (43%)
  starting transfers between devices  43.7 us (33%)
  blocking collectives  20.4 us (16%)
  Pallas kernels  6.9 us (5%)
  local copies, waits for them, and re-layouts  2.53 us (2%)
    ppermute x9, waiting for transfers between devices, y_send(): return lax.ppermute(x, 'y', [(i, (i + step) % NY) for i in range(NY)])  36 us
    ppermute x14, starting transfers between devices, ring_send(): return lax.ppermute(x, ('core', axis), ring_pairs(size, step))  20.7 us
    all_to_all x1, blocking collectives, body(): pieces = lax.all_to_all(mine, ('x_hi', 'x_lo', 'y'), 0, 0, tiled=True)  20.4 us
    ppermute x14, waiting for transfers between devices, ring_send(): return lax.ppermute(x, ('core', axis), ring_pairs(size, step))  18.3 us
    ppermute x9, starting transfers between devices, y_send(): return lax.ppermute(x, 'y', [(i, (i + step) % NY) for i in range(NY)])  12.9 us
    ppermute x6, starting transfers between devices, swap(): return lax.ppermute(x, axis, [(0, 1), (1, 0)])  6.66 us
    ppermute x1, starting transfers between devices, x_send(): return lax.ppermute(x, ('x_hi', 'core', 'x_lo'), pairs)  3.39 us
    pallas_call x3, Pallas kernels, partial_half(): pl.pallas_call(partial_kernel, out_shape=[jax.ShapeDtypeStruct((ROWS, OCC...  2.66 us
  transfers between devices with their start and end apart: 30, of which 14 were waited for; matrix products, arithmetic and copies ran while one was open for 0% of the time, Pallas kernels for 3%

profile of v5, /device:TPU:1, one launch (start us, length us, event | category | flops | bytes accessed | tf_op | source)
XLA Modules:
  0.0 130.7 jit_solution(1832103950806115984)
XLA Ops:
  0.0 0.9 copy-done
  0.9 3.4 %collective-permute-start = (bf16[128,384]{1,0:T(8,128)(2,1)S(1)}, bf16[128,384]{1,0:T(8,128)(2,1)S(1)}, u32[]{:S(2)}, u32[]{:S(2)}) collective-permute-start(bf16[128,384]{1,0:T(8,128)(2,1)S(1)} %constant_dynamic-slice_fusion), channel_id=1, source_target_pairs={{0,4},{4,128},{128,132},{132,0},{64,196},{68,64},{192,68},{196,192... | collective-permute-start | bytes 294920 | tf_op jit(solution)/shard_map/ppermute | solution.py:42
  4.3 1.6 %copy-done.1 = bf16[1,128,8192]{2,1,0:T(8,128)(2,1)S(1)} copy-done((bf16[1,128,8192]{2,1,0:T(8,128)(2,1)S(1)}, bf16[1,128,8192]{2,1,0:T(8,128)(2,1)}, u32[]{:S(2)}) %copy-start.1) | copy-done | bytes 2097176
  5.9 0.5 shard_map.28
  6.5 3.6 %collective-permute-start.3 = (bf16[128,2048]{1,0:T(8,128)(2,1)S(1)}, bf16[128,2048]{1,0:T(8,128)(2,1)S(1)}, u32[]{:S(2)}, u32[]{:S(2)}) collective-permute-start(bf16[128,2048]{1,0:T(8,128)(2,1)S(1)} %get-tuple-element.32.refs_0_), channel_id=1, source_target_pairs={{0,64},{64,0},{1,65},{65,1},{2,66},{66,2},{3,67},{67,3},{4,68},{68... | collective-permute-start | bytes 1572872 | tf_op jit(solution)/shard_map/ppermute | solution.py:46
  10.1 2.7 %collective-permute-start.7 = (bf16[128,2048]{1,0:T(8,128)(2,1)S(1)}, bf16[128,2048]{1,0:T(8,128)(2,1)S(1)}, u32[]{:S(2)}, u32[]{:S(2)}) collective-permute-start(bf16[128,2048]{1,0:T(8,128)(2,1)S(1)} %get-tuple-element.36), channel_id=1, source_target_pairs={{0,3},{1,0},{2,1},{3,2},{4,7},{5,4},{6,5},{7,6},{8,11},{9,8},{10,9... | collective-permute-start | bytes 1572872 | tf_op jit(solution)/shard_map/ppermute | solution.py:50
  12.8 0.1 collective-permute-start.2
  12.9 4.0 %collective-permute-start.1 = (bf16[256,384]{1,0:T(8,128)(2,1)S(1)}, bf16[256,384]{1,0:T(8,128)(2,1)S(1)}, u32[]{:S(2)}, u32[]{:S(2)}) collective-permute-start(bf16[256,384]{1,0:T(8,128)(2,1)S(1)} %pad_maximum_fusion.1.refs_0_), channel_id=1, source_target_pairs={{0,8},{8,16},{16,24},{24,32},{32,40},{40,48},{48,56},{56,0},{64,12... | collective-permute-start | bytes 589832 | tf_op jit(solution)/shard_map/ppermute | solution.py:31
  16.9 3.3 %collective-permute-done.2.refs_2_ = bf16[256,384]{1,0:T(8,128)(2,1)S(1)} collective-permute-done((bf16[256,384]{1,0:T(8,128)(2,1)S(1)}, bf16[256,384]{1,0:T(8,128)(2,1)S(1)}, u32[]{:S(2)}, u32[]{:S(2)}) %collective-permute-start.2) | collective-permute-done | bytes 196640 | tf_op jit(solution)/shard_map/ppermute | solution.py:31
  20.1 1.3 %collective-permute-start.11 = (bf16[128,2048]{1,0:T(8,128)(2,1)S(1)}, bf16[128,2048]{1,0:T(8,128)(2,1)S(1)}, u32[]{:S(2)}, u32[]{:S(2)}) collective-permute-start(bf16[128,2048]{1,0:T(8,128)(2,1)S(1)} %get-tuple-element.39), channel_id=1, source_target_pairs={{0,2},{1,3},{2,0},{3,1},{4,6},{5,7},{6,4},{7,5},{8,10},{9,11},{10,... | collective-permute-start | bytes 1572872 | tf_op jit(solution)/shard_map/ppermute | solution.py:50
  21.5 2.7 %collective-permute-start.4 = (bf16[256,384]{1,0:T(8,128)(2,1)S(1)}, bf16[256,384]{1,0:T(8,128)(2,1)S(1)}, u32[]{:S(2)}, u32[]{:S(2)}) collective-permute-start(bf16[256,384]{1,0:T(8,128)(2,1)S(1)} %collective-permute-done.1.refs_1_), channel_id=1, source_target_pairs={{0,8},{8,16},{16,24},{24,32},{32,40},{40,48},{48,56},{56,0},{64,12... | collective-permute-start | bytes 589832 | tf_op jit(solution)/shard_map/ppermute | solution.py:31
  24.1 11.9 %collective-permute-done.6.refs_0_ = bf16[128,2048]{1,0:T(8,128)(2,1)S(1)} collective-permute-done((bf16[128,2048]{1,0:T(8,128)(2,1)S(1)}, bf16[128,2048]{1,0:T(8,128)(2,1)S(1)}, u32[]{:S(2)}, u32[]{:S(2)}) %collective-permute-start.6) | collective-permute-done | bytes 524320 | tf_op jit(solution)/shard_map/ppermute | solution.py:50
  36.2 0.1 collective-permute-start.10
  36.3 2.6 %collective-permute-start.8 = (bf16[256,384]{1,0:T(8,128)(2,1)S(1)}, bf16[256,384]{1,0:T(8,128)(2,1)S(1)}, u32[]{:S(2)}, u32[]{:S(2)}) collective-permute-start(bf16[256,384]{1,0:T(8,128)(2,1)S(1)} %collective-permute-done.4.refs_3_), channel_id=1, source_target_pairs={{0,8},{8,16},{16,24},{24,32},{32,40},{40,48},{48,56},{56,0},{64,12... | collective-permute-start | bytes 589832 | tf_op jit(solution)/shard_map/ppermute | solution.py:31
  38.9 0.1 collective-permute-start.12
  39.0 0.4 collective-permute-start.13
  39.4 2.5 %collective-permute-done.9.refs_6_ = bf16[256,384]{1,0:T(8,128)(2,1)S(1)} collective-permute-done((bf16[256,384]{1,0:T(8,128)(2,1)S(1)}, bf16[256,384]{1,0:T(8,128)(2,1)S(1)}, u32[]{:S(2)}, u32[]{:S(2)}) %collective-permute-start.9) | collective-permute-done | bytes 196640 | tf_op jit(solution)/shard_map/ppermute | solution.py:31
  41.9 0.6 collective-permute-done.10.refs_7_
  42.5 5.9 %collective-permute-done.8.refs_5_ = bf16[256,384]{1,0:T(8,128)(2,1)S(1)} collective-permute-done((bf16[256,384]{1,0:T(8,128)(2,1)S(1)}, bf16[256,384]{1,0:T(8,128)(2,1)S(1)}, u32[]{:S(2)}, u32[]{:S(2)}) %collective-permute-start.8) | collective-permute-done | bytes 196640 | tf_op jit(solution)/shard_map/ppermute | solution.py:31
  48.4 0.7 collective-permute-start.16
  49.2 0.2 shard_map.29.rhs_ref
  49.4 1.2 shard_map.31
  50.7 4.0 %collective-permute-start.15 = (f32[128,768]{1,0:T(8,128)S(1)}, f32[128,768]{1,0:T(8,128)S(1)}, u32[]{:S(2)}, u32[]{:S(2)}) collective-permute-start(f32[128,768]{1,0:T(8,128)S(1)} %get-tuple-element.47), channel_id=1, source_target_pairs={{0,3},{1,0},{2,1},{3,2},{4,7},{5,4},{6,5},{7,6},{8,11},{9,8},{10,9... | collective-permute-start | bytes 1179656 | tf_op jit(solution)/shard_map/ppermute | solution.py:50
  54.8 0.7 shard_map.32
  55.5 1.2 collective-permute-start.17
  56.7 0.7 shard_map.30
  57.4 6.8 %collective-permute-done.14 = f32[128,768]{1,0:T(8,128)S(1)} collective-permute-done((f32[128,768]{1,0:T(8,128)S(1)}, f32[128,768]{1,0:T(8,128)S(1)}, u32[]{:S(2)}, u32[]{:S(2)}) %collective-permute-start.14) | collective-permute-done | bytes 393248 | tf_op jit(solution)/shard_map/ppermute | solution.py:50
  64.2 7.4 %collective-permute-done.15 = f32[128,768]{1,0:T(8,128)S(1)} collective-permute-done((f32[128,768]{1,0:T(8,128)S(1)}, f32[128,768]{1,0:T(8,128)S(1)}, u32[]{:S(2)}, u32[]{:S(2)}) %collective-permute-start.15) | collective-permute-done | bytes 393248 | tf_op jit(solution)/shard_map/ppermute | solution.py:50
  71.6 2.0 %collective-permute-done.17 = f32[128,768]{1,0:T(8,128)S(1)} collective-permute-done((f32[128,768]{1,0:T(8,128)S(1)}, f32[128,768]{1,0:T(8,128)S(1)}, u32[]{:S(2)}, u32[]{:S(2)}) %collective-permute-start.17) | collective-permute-done | bytes 393248 | tf_op jit(solution)/shard_map/ppermute | solution.py:50
  73.6 0.1 add_convert_fusion.refs_0_
  73.7 2.5 %collective-permute-start.18 = (bf16[128,768]{1,0:T(8,128)(2,1)S(1)}, bf16[128,768]{1,0:T(8,128)(2,1)S(1)}, u32[]{:S(2)}, u32[]{:S(2)}) collective-permute-start(bf16[128,768]{1,0:T(8,128)(2,1)S(1)} %add_convert_fusion.refs_0_), channel_id=1, source_target_pairs={{0,8},{8,16},{16,24},{24,32},{32,40},{40,48},{48,56},{56,0},{64,12... | collective-permute-start | bytes 589832 | tf_op jit(solution)/shard_map/ppermute | solution.py:31
  76.1 2.6 %collective-permute-done.18.refs_1_ = bf16[128,768]{1,0:T(8,128)(2,1)S(1)} collective-permute-done((bf16[128,768]{1,0:T(8,128)(2,1)S(1)}, bf16[128,768]{1,0:T(8,128)(2,1)S(1)}, u32[]{:S(2)}, u32[]{:S(2)}) %collective-permute-start.18) | collective-permute-done | bytes 196640 | tf_op jit(solution)/shard_map/ppermute | solution.py:31
  78.7 3.1 %collective-permute-start.20 = (bf16[128,768]{1,0:T(8,128)(2,1)S(1)}, bf16[128,768]{1,0:T(8,128)(2,1)S(1)}, u32[]{:S(2)}, u32[]{:S(2)}) collective-permute-start(bf16[128,768]{1,0:T(8,128)(2,1)S(1)} %collective-permute-done.18.refs_1_), channel_id=1, source_target_pairs={{0,8},{8,16},{16,24},{24,32},{32,40},{40,48},{48,56},{56,0},{64,12... | collective-permute-start | bytes 589832 | tf_op jit(solution)/shard_map/ppermute | solution.py:31
  81.9 0.3 collective-permute-done.25
  82.2 1.1 collective-permute-start.28
  83.3 1.7 %collective-permute-start.27 = (bf16[2,128,768]{2,1,0:T(8,128)(2,1)S(1)}, bf16[2,128,768]{2,1,0:T(8,128)(2,1)S(1)}, u32[]{:S(2)}, u32[]{:S(2)}) collective-permute-start(bf16[2,128,768]{2,1,0:T(8,128)(2,1)S(1)} %pad_maximum_fusion.refs_8_), channel_id=1, source_target_pairs={{0,2},{1,3},{2,0},{3,1},{4,6},{5,7},{6,4},{7,5},{8,10},{9,11},{10,... | collective-permute-start | bytes 1179656 | tf_op jit(solution)/shard_map/ppermute | solution.py:50
  85.0 0.8 collective-permute-start.26
  85.8 2.7 %collective-permute-start.22 = (bf16[128,768]{1,0:T(8,128)(2,1)S(1)}, bf16[128,768]{1,0:T(8,128)(2,1)S(1)}, u32[]{:S(2)}, u32[]{:S(2)}) collective-permute-start(bf16[128,768]{1,0:T(8,128)(2,1)S(1)} %collective-permute-done.20.refs_3_), channel_id=1, source_target_pairs={{0,8},{8,16},{16,24},{24,32},{32,40},{40,48},{48,56},{56,0},{64,12... | collective-permute-start | bytes 589832 | tf_op jit(solution)/shard_map/ppermute | solution.py:31
  88.5 3.3 %collective-permute-done.21.refs_4_ = bf16[128,768]{1,0:T(8,128)(2,1)S(1)} collective-permute-done((bf16[128,768]{1,0:T(8,128)(2,1)S(1)}, bf16[128,768]{1,0:T(8,128)(2,1)S(1)}, u32[]{:S(2)}, u32[]{:S(2)}) %collective-permute-start.21) | collective-permute-done | bytes 196640 | tf_op jit(solution)/shard_map/ppermute | solution.py:31
  91.8 3.0 %collective-permute-start.24 = (bf16[128,768]{1,0:T(8,128)(2,1)S(1)}, bf16[128,768]{1,0:T(8,128)(2,1)S(1)}, u32[]{:S(2)}, u32[]{:S(2)}) collective-permute-start(bf16[128,768]{1,0:T(8,128)(2,1)S(1)} %collective-permute-done.22.refs_5_), channel_id=1, source_target_pairs={{0,8},{8,16},{16,24},{24,32},{32,40},{40,48},{48,56},{56,0},{64,12... | collective-permute-start | bytes 589832 | tf_op jit(solution)/shard_map/ppermute | solution.py:31
  94.9 7.7 %collective-permute-done.27.refs_10_ = bf16[2,128,768]{2,1,0:T(8,128)(2,1)S(1)} collective-permute-done((bf16[2,128,768]{2,1,0:T(8,128)(2,1)S(1)}, bf16[2,128,768]{2,1,0:T(8,128)(2,1)S(1)}, u32[]{:S(2)}, u32[]{:S(2)}) %collective-permute-start.27) | collective-permute-done | bytes 393248 | tf_op jit(solution)/shard_map/ppermute | solution.py:50
  102.5 0.2 collective-permute-done.26.refs_9_
  102.7 1.2 shard_map.33
  103.9 1.8 %collective-permute-start.29 = (bf16[16,128,256]{2,1,0:T(8,128)(2,1)S(1)}, bf16[16,128,256]{2,1,0:T(8,128)(2,1)S(1)}, u32[]{:S(2)}, u32[]{:S(2)}) collective-permute-start(bf16[16,128,256]{2,1,0:T(8,128)(2,1)S(1)} %shard_map.33), channel_id=1, source_target_pairs={{0,64},{64,0},{1,65},{65,1},{2,66},{66,2},{3,67},{67,3},{4,68},{68... | collective-permute-start | bytes 3145736 | tf_op jit(solution)/shard_map/ppermute | solution.py:46
  105.7 2.3 %collective-permute-done.29.refs_12_ = bf16[16,128,256]{2,1,0:T(8,128)(2,1)S(1)} collective-permute-done((bf16[16,128,256]{2,1,0:T(8,128)(2,1)S(1)}, bf16[16,128,256]{2,1,0:T(8,128)(2,1)S(1)}, u32[]{:S(2)}, u32[]{:S(2)}) %collective-permute-start.29) | collective-permute-done | bytes 1048608 | tf_op jit(solution)/shard_map/ppermute | solution.py:46
  108.0 1.2 shard_map.34
  109.2 20.4 %all_to_all.5.pieces = bf16[16,128,256]{2,1,0:T(8,128)(2,1)S(1)} all-to-all(bf16[16,128,256]{2,1,0:T(8,128)(2,1)S(1)} %shard_map.34), channel_id=1, replica_groups=mesh['x_hi'=2,'core'=2,'z'=8,'x_lo'=2,'y'=4] {'x_hi','x_lo','y'}, dimensions={0} | all-to-all | bytes 2097152 | tf_op jit(solution)/shard_map/all_to_all | solution.py:201
  129.6 1.1 shard_map.35
  (29 shorter events, 0.3 us)
Async XLA Ops:
  0.0 0.9 copy-start
  0.9 5.5 %collective-permute-start = (bf16[128,384]{1,0:T(8,128)(2,1)S(1)}, bf16[128,384]{1,0:T(8,128)(2,1)S(1)}, u32[]{:S(2)}, u32[]{:S(2)}) collective-permute-start(bf16[128,384]{1,0:T(8,128)(2,1)S(1)} %constant_dynamic-slice_fusion), channel_id=1, source_target_pairs={{0,4},{4,128},{128,132},{132,0},{64,196},{68,64},{192,68},{196,192... | collective-permute-start | bytes 294920 | tf_op jit(solution)/shard_map/ppermute | solution.py:42
  4.3 1.6 %copy-start.1 = (bf16[1,128,8192]{2,1,0:T(8,128)(2,1)S(1)}, bf16[1,128,8192]{2,1,0:T(8,128)(2,1)}, u32[]{:S(2)}) copy-start(bf16[1,128,8192]{2,1,0:T(8,128)(2,1)} %param.2) | copy-start | bytes 6291460
  6.5 15.0 %collective-permute-start.3 = (bf16[128,2048]{1,0:T(8,128)(2,1)S(1)}, bf16[128,2048]{1,0:T(8,128)(2,1)S(1)}, u32[]{:S(2)}, u32[]{:S(2)}) collective-permute-start(bf16[128,2048]{1,0:T(8,128)(2,1)S(1)} %get-tuple-element.32.refs_0_), channel_id=1, source_target_pairs={{0,64},{64,0},{1,65},{65,1},{2,66},{66,2},{3,67},{67,3},{4,68},{68... | collective-permute-start | bytes 1572872 | tf_op jit(solution)/shard_map/ppermute | solution.py:46
  10.1 26.0 %collective-permute-start.6 = (bf16[128,2048]{1,0:T(8,128)(2,1)S(1)}, bf16[128,2048]{1,0:T(8,128)(2,1)S(1)}, u32[]{:S(2)}, u32[]{:S(2)}) collective-permute-start(bf16[128,2048]{1,0:T(8,128)(2,1)S(1)} %get-tuple-element.35), channel_id=1, source_target_pairs={{0,1},{1,2},{2,3},{3,0},{4,5},{5,6},{6,7},{7,4},{8,9},{9,10},{10,1... | collective-permute-start | bytes 1572872 | tf_op jit(solution)/shard_map/ppermute | solution.py:50
  10.1 26.0 %collective-permute-start.7 = (bf16[128,2048]{1,0:T(8,128)(2,1)S(1)}, bf16[128,2048]{1,0:T(8,128)(2,1)S(1)}, u32[]{:S(2)}, u32[]{:S(2)}) collective-permute-start(bf16[128,2048]{1,0:T(8,128)(2,1)S(1)} %get-tuple-element.36), channel_id=1, source_target_pairs={{0,3},{1,0},{2,1},{3,2},{4,7},{5,4},{6,5},{7,6},{8,11},{9,8},{10,9... | collective-permute-start | bytes 1572872 | tf_op jit(solution)/shard_map/ppermute | solution.py:50
  12.8 7.3 %collective-permute-start.2 = (bf16[256,384]{1,0:T(8,128)(2,1)S(1)}, bf16[256,384]{1,0:T(8,128)(2,1)S(1)}, u32[]{:S(2)}, u32[]{:S(2)}) collective-permute-start(bf16[256,384]{1,0:T(8,128)(2,1)S(1)} %pad_maximum_fusion.1.refs_0_), channel_id=1, source_target_pairs={{0,56},{8,0},{16,8},{24,16},{32,24},{40,32},{48,40},{56,48},{64,72... | collective-permute-start | bytes 589832 | tf_op jit(solution)/shard_map/ppermute | solution.py:31
  12.9 8.6 %collective-permute-start.1 = (bf16[256,384]{1,0:T(8,128)(2,1)S(1)}, bf16[256,384]{1,0:T(8,128)(2,1)S(1)}, u32[]{:S(2)}, u32[]{:S(2)}) collective-permute-start(bf16[256,384]{1,0:T(8,128)(2,1)S(1)} %pad_maximum_fusion.1.refs_0_), channel_id=1, source_target_pairs={{0,8},{8,16},{16,24},{24,32},{32,40},{40,48},{48,56},{56,0},{64,12... | collective-permute-start | bytes 589832 | tf_op jit(solution)/shard_map/ppermute | solution.py:31
  20.1 18.9 %collective-permute-start.11 = (bf16[128,2048]{1,0:T(8,128)(2,1)S(1)}, bf16[128,2048]{1,0:T(8,128)(2,1)S(1)}, u32[]{:S(2)}, u32[]{:S(2)}) collective-permute-start(bf16[128,2048]{1,0:T(8,128)(2,1)S(1)} %get-tuple-element.39), channel_id=1, source_target_pairs={{0,2},{1,3},{2,0},{3,1},{4,6},{5,7},{6,4},{7,5},{8,10},{9,11},{10,... | collective-permute-start | bytes 1572872 | tf_op jit(solution)/shard_map/ppermute | solution.py:50
  21.5 14.6 %collective-permute-start.4 = (bf16[256,384]{1,0:T(8,128)(2,1)S(1)}, bf16[256,384]{1,0:T(8,128)(2,1)S(1)}, u32[]{:S(2)}, u32[]{:S(2)}) collective-permute-start(bf16[256,384]{1,0:T(8,128)(2,1)S(1)} %collective-permute-done.1.refs_1_), channel_id=1, source_target_pairs={{0,8},{8,16},{16,24},{24,32},{32,40},{40,48},{48,56},{56,0},{64,12... | collective-permute-start | bytes 589832 | tf_op jit(solution)/shard_map/ppermute | solution.py:31
  24.1 12.0 %collective-permute-start.5 = (bf16[256,384]{1,0:T(8,128)(2,1)S(1)}, bf16[256,384]{1,0:T(8,128)(2,1)S(1)}, u32[]{:S(2)}, u32[]{:S(2)}) collective-permute-start(bf16[256,384]{1,0:T(8,128)(2,1)S(1)} %collective-permute-done.2.refs_2_), channel_id=1, source_target_pairs={{0,56},{8,0},{16,8},{24,16},{32,24},{40,32},{48,40},{56,48},{64,72... | collective-permute-start | bytes 589832 | tf_op jit(solution)/shard_map/ppermute | solution.py:31
  36.1 5.8 %collective-permute-start.9 = (bf16[256,384]{1,0:T(8,128)(2,1)S(1)}, bf16[256,384]{1,0:T(8,128)(2,1)S(1)}, u32[]{:S(2)}, u32[]{:S(2)}) collective-permute-start(bf16[256,384]{1,0:T(8,128)(2,1)S(1)} %collective-permute-done.5.refs_4_), channel_id=1, source_target_pairs={{0,56},{8,0},{16,8},{24,16},{32,24},{40,32},{48,40},{56,48},{64,72... | collective-permute-start | bytes 589832 | tf_op jit(solution)/shard_map/ppermute | solution.py:31
  36.2 6.3 %collective-permute-start.10 = (bf16[256,384]{1,0:T(8,128)(2,1)S(1)}, bf16[256,384]{1,0:T(8,128)(2,1)S(1)}, u32[]{:S(2)}, u32[]{:S(2)}) collective-permute-start(bf16[256,384]{1,0:T(8,128)(2,1)S(1)} %collective-permute-done.4.refs_3_), channel_id=1, source_target_pairs={{0,16},{8,24},{16,32},{24,40},{32,48},{40,56},{48,0},{56,8},{64,11... | collective-permute-start | bytes 589832 | tf_op jit(solution)/shard_map/ppermute | solution.py:31
  36.3 12.2 %collective-permute-start.8 = (bf16[256,384]{1,0:T(8,128)(2,1)S(1)}, bf16[256,384]{1,0:T(8,128)(2,1)S(1)}, u32[]{:S(2)}, u32[]{:S(2)}) collective-permute-start(bf16[256,384]{1,0:T(8,128)(2,1)S(1)} %collective-permute-done.4.refs_3_), channel_id=1, source_target_pairs={{0,8},{8,16},{16,24},{24,32},{32,40},{40,48},{48,56},{56,0},{64,12... | collective-permute-start | bytes 589832 | tf_op jit(solution)/shard_map/ppermute | solution.py:31
  38.9 10.5 %collective-permute-start.12 = (bf16[128,2048]{1,0:T(8,128)(2,1)S(1)}, bf16[128,2048]{1,0:T(8,128)(2,1)S(1)}, u32[]{:S(2)}, u32[]{:S(2)}) collective-permute-start(bf16[128,2048]{1,0:T(8,128)(2,1)S(1)} %collective-permute-done.6.refs_0_), channel_id=1, source_target_pairs={{0,64},{64,0},{1,65},{65,1},{2,66},{66,2},{3,67},{67,3},{4,68},{68... | collective-permute-start | bytes 1572872 | tf_op jit(solution)/shard_map/ppermute | solution.py:46
  39.0 10.4 %collective-permute-start.13 = (bf16[128,2048]{1,0:T(8,128)(2,1)S(1)}, bf16[128,2048]{1,0:T(8,128)(2,1)S(1)}, u32[]{:S(2)}, u32[]{:S(2)}) collective-permute-start(bf16[128,2048]{1,0:T(8,128)(2,1)S(1)} %collective-permute-done.7.refs_1_), channel_id=1, source_target_pairs={{0,64},{64,0},{1,65},{65,1},{2,66},{66,2},{3,67},{67,3},{4,68},{68... | collective-permute-start | bytes 1572872 | tf_op jit(solution)/shard_map/ppermute | solution.py:46
  48.4 6.4 %collective-permute-start.16 = (bf16[128,2048]{1,0:T(8,128)(2,1)S(1)}, bf16[128,2048]{1,0:T(8,128)(2,1)S(1)}, u32[]{:S(2)}, u32[]{:S(2)}) collective-permute-start(bf16[128,2048]{1,0:T(8,128)(2,1)S(1)} %collective-permute-done.11.refs_0_), channel_id=1, source_target_pairs={{0,64},{64,0},{1,65},{65,1},{2,66},{66,2},{3,67},{67,3},{4,68},{68... | collective-permute-start | bytes 1572872 | tf_op jit(solution)/shard_map/ppermute | solution.py:46
  50.7 13.5 %collective-permute-start.14 = (f32[128,768]{1,0:T(8,128)S(1)}, f32[128,768]{1,0:T(8,128)S(1)}, u32[]{:S(2)}, u32[]{:S(2)}) collective-permute-start(f32[128,768]{1,0:T(8,128)S(1)} %get-tuple-element.46), channel_id=1, source_target_pairs={{0,1},{1,2},{2,3},{3,0},{4,5},{5,6},{6,7},{7,4},{8,9},{9,10},{10,1... | collective-permute-start | bytes 1179656 | tf_op jit(solution)/shard_map/ppermute | solution.py:50
  50.7 20.9 %collective-permute-start.15 = (f32[128,768]{1,0:T(8,128)S(1)}, f32[128,768]{1,0:T(8,128)S(1)}, u32[]{:S(2)}, u32[]{:S(2)}) collective-permute-start(f32[128,768]{1,0:T(8,128)S(1)} %get-tuple-element.47), channel_id=1, source_target_pairs={{0,3},{1,0},{2,1},{3,2},{4,7},{5,4},{6,5},{7,6},{8,11},{9,8},{10,9... | collective-permute-start | bytes 1179656 | tf_op jit(solution)/shard_map/ppermute | solution.py:50
  55.5 18.1 %collective-permute-start.17 = (f32[128,768]{1,0:T(8,128)S(1)}, f32[128,768]{1,0:T(8,128)S(1)}, u32[]{:S(2)}, u32[]{:S(2)}) collective-permute-start(f32[128,768]{1,0:T(8,128)S(1)} %shard_map.32), channel_id=1, source_target_pairs={{0,2},{1,3},{2,0},{3,1},{4,6},{5,7},{6,4},{7,5},{8,10},{9,11},{10,... | collective-permute-start | bytes 1179656 | tf_op jit(solution)/shard_map/ppermute | solution.py:50
  73.7 5.1 %collective-permute-start.18 = (bf16[128,768]{1,0:T(8,128)(2,1)S(1)}, bf16[128,768]{1,0:T(8,128)(2,1)S(1)}, u32[]{:S(2)}, u32[]{:S(2)}) collective-permute-start(bf16[128,768]{1,0:T(8,128)(2,1)S(1)} %add_convert_fusion.refs_0_), channel_id=1, source_target_pairs={{0,8},{8,16},{16,24},{24,32},{32,40},{40,48},{48,56},{56,0},{64,12... | collective-permute-start | bytes 589832 | tf_op jit(solution)/shard_map/ppermute | solution.py:31
  76.1 6.0 %collective-permute-start.25 = (bf16[128,768]{1,0:T(8,128)(2,1)S(1)}, bf16[128,768]{1,0:T(8,128)(2,1)S(1)}, u32[]{:S(2)}, u32[]{:S(2)}) collective-permute-start(bf16[128,768]{1,0:T(8,128)(2,1)S(1)} %add_convert_fusion.refs_0_), channel_id=1, source_target_pairs={{0,4},{4,0},{1,5},{5,1},{2,6},{6,2},{3,7},{7,3},{8,12},{12,8},{9,1... | collective-permute-start | bytes 589832 | tf_op jit(solution)/shard_map/ppermute | solution.py:46
  76.1 9.7 %collective-permute-start.19 = (bf16[128,768]{1,0:T(8,128)(2,1)S(1)}, bf16[128,768]{1,0:T(8,128)(2,1)S(1)}, u32[]{:S(2)}, u32[]{:S(2)}) collective-permute-start(bf16[128,768]{1,0:T(8,128)(2,1)S(1)} %add_convert_fusion.refs_0_), channel_id=1, source_target_pairs={{0,56},{8,0},{16,8},{24,16},{32,24},{40,32},{48,40},{56,48},{64,72... | collective-permute-start | bytes 589832 | tf_op jit(solution)/shard_map/ppermute | solution.py:31
  78.7 7.1 %collective-permute-start.20 = (bf16[128,768]{1,0:T(8,128)(2,1)S(1)}, bf16[128,768]{1,0:T(8,128)(2,1)S(1)}, u32[]{:S(2)}, u32[]{:S(2)}) collective-permute-start(bf16[128,768]{1,0:T(8,128)(2,1)S(1)} %collective-permute-done.18.refs_1_), channel_id=1, source_target_pairs={{0,8},{8,16},{16,24},{24,32},{32,40},{40,48},{48,56},{56,0},{64,12... | collective-permute-start | bytes 589832 | tf_op jit(solution)/shard_map/ppermute | solution.py:31
  82.2 12.7 %collective-permute-start.28 = (bf16[2,128,768]{2,1,0:T(8,128)(2,1)S(1)}, bf16[2,128,768]{2,1,0:T(8,128)(2,1)S(1)}, u32[]{:S(2)}, u32[]{:S(2)}) collective-permute-start(bf16[2,128,768]{2,1,0:T(8,128)(2,1)S(1)} %pad_maximum_fusion.refs_8_), channel_id=1, source_target_pairs={{0,1},{1,2},{2,3},{3,0},{4,5},{5,6},{6,7},{7,4},{8,9},{9,10},{10,1... | collective-permute-start | bytes 1179656 | tf_op jit(solution)/shard_map/ppermute | solution.py:50
  83.3 19.2 %collective-permute-start.27 = (bf16[2,128,768]{2,1,0:T(8,128)(2,1)S(1)}, bf16[2,128,768]{2,1,0:T(8,128)(2,1)S(1)}, u32[]{:S(2)}, u32[]{:S(2)}) collective-permute-start(bf16[2,128,768]{2,1,0:T(8,128)(2,1)S(1)} %pad_maximum_fusion.refs_8_), channel_id=1, source_target_pairs={{0,2},{1,3},{2,0},{3,1},{4,6},{5,7},{6,4},{7,5},{8,10},{9,11},{10,... | collective-permute-start | bytes 1179656 | tf_op jit(solution)/shard_map/ppermute | solution.py:50
  85.0 17.7 %collective-permute-start.26 = (bf16[2,128,768]{2,1,0:T(8,128)(2,1)S(1)}, bf16[2,128,768]{2,1,0:T(8,128)(2,1)S(1)}, u32[]{:S(2)}, u32[]{:S(2)}) collective-permute-start(bf16[2,128,768]{2,1,0:T(8,128)(2,1)S(1)} %pad_maximum_fusion.refs_8_), channel_id=1, source_target_pairs={{0,3},{1,0},{2,1},{3,2},{4,7},{5,4},{6,5},{7,6},{8,11},{9,8},{10,9... | collective-permute-start | bytes 1179656 | tf_op jit(solution)/shard_map/ppermute | solution.py:50
  85.8 6.0 %collective-permute-start.21 = (bf16[128,768]{1,0:T(8,128)(2,1)S(1)}, bf16[128,768]{1,0:T(8,128)(2,1)S(1)}, u32[]{:S(2)}, u32[]{:S(2)}) collective-permute-start(bf16[128,768]{1,0:T(8,128)(2,1)S(1)} %collective-permute-done.19.refs_2_), channel_id=1, source_target_pairs={{0,56},{8,0},{16,8},{24,16},{32,24},{40,32},{48,40},{56,48},{64,72... | collective-permute-start | bytes 589832 | tf_op jit(solution)/shard_map/ppermute | solution.py:31
  85.8 6.0 %collective-permute-start.22 = (bf16[128,768]{1,0:T(8,128)(2,1)S(1)}, bf16[128,768]{1,0:T(8,128)(2,1)S(1)}, u32[]{:S(2)}, u32[]{:S(2)}) collective-permute-start(bf16[128,768]{1,0:T(8,128)(2,1)S(1)} %collective-permute-done.20.refs_3_), channel_id=1, source_target_pairs={{0,8},{8,16},{16,24},{24,32},{32,40},{40,48},{48,56},{56,0},{64,12... | collective-permute-start | bytes 589832 | tf_op jit(solution)/shard_map/ppermute | solution.py:31
  91.8 10.9 %collective-permute-start.23 = (bf16[128,768]{1,0:T(8,128)(2,1)S(1)}, bf16[128,768]{1,0:T(8,128)(2,1)S(1)}, u32[]{:S(2)}, u32[]{:S(2)}) collective-permute-start(bf16[128,768]{1,0:T(8,128)(2,1)S(1)} %collective-permute-done.21.refs_4_), channel_id=1, source_target_pairs={{0,56},{8,0},{16,8},{24,16},{32,24},{40,32},{48,40},{56,48},{64,72... | collective-permute-start | bytes 589832 | tf_op jit(solution)/shard_map/ppermute | solution.py:31
  91.8 10.9 %collective-permute-start.24 = (bf16[128,768]{1,0:T(8,128)(2,1)S(1)}, bf16[128,768]{1,0:T(8,128)(2,1)S(1)}, u32[]{:S(2)}, u32[]{:S(2)}) collective-permute-start(bf16[128,768]{1,0:T(8,128)(2,1)S(1)} %collective-permute-done.22.refs_5_), channel_id=1, source_target_pairs={{0,8},{8,16},{16,24},{24,32},{32,40},{40,48},{48,56},{56,0},{64,12... | collective-permute-start | bytes 589832 | tf_op jit(solution)/shard_map/ppermute | solution.py:31
  103.9 4.1 %collective-permute-start.29 = (bf16[16,128,256]{2,1,0:T(8,128)(2,1)S(1)}, bf16[16,128,256]{2,1,0:T(8,128)(2,1)S(1)}, u32[]{:S(2)}, u32[]{:S(2)}) collective-permute-start(bf16[16,128,256]{2,1,0:T(8,128)(2,1)S(1)} %shard_map.33), channel_id=1, source_target_pairs={{0,64},{64,0},{1,65},{65,1},{2,66},{66,2},{3,67},{67,3},{4,68},{68... | collective-permute-start | bytes 3145736 | tf_op jit(solution)/shard_map/ppermute | solution.py:46

commit v6 on v5

--- a/solution.py
+++ b/solution.py
@@ -58,11 +58,9 @@
 
 
 def z_gather(x):
-    blocks, fwd, bwd = [x], x, x
-    for _ in range(3):
-        fwd, bwd = z_step(fwd, bwd)
-        blocks += [fwd, bwd]
-    return blocks + [ring_send(fwd, "z", 1)]
+    first = z_step(x, x)
+    second = z_step(*first)
+    return [x, *first, *second, *z_step(*second), ring_send(second[0], "z", 2)]
 
 
 def z_slots():
@@ -177,23 +175,26 @@
     pair = jnp.concatenate([mine, theirs], axis=0)
     first = z_step(pair, pair)
     first, sib[0] = lax.optimization_barrier((first, sib[0]))
-    second = z_step(*first)
-    second, rows[1], rows[3] = lax.optimization_barrier((second, rows[1], rows[3]))
+    fwd, bwd = z_step(*first)
+    bwd, rows[1], rows[3] = lax.optimization_barrier((bwd, rows[1], rows[3]))
+    second = [fwd, bwd]
     third = z_step(*second)
-    far = ring_send(second[0], "z", 2)
+    far = ring_send(fwd, "z", 2)
     sib[1], sib[3] = swap(rows[1], "core"), swap(rows[3], "core")
     third, far, rows[2] = lax.optimization_barrier((third, far, rows[2]))
     sib[2] = swap(rows[2], "core")
     rhs = collect([pair, *first, *second, *third, far])
+    (across,) = partial_half(rhs, [rows[2]], [sib[2]])
+    rhs, across = lax.optimization_barrier((rhs, across))
+    across = y_send(across, 2)
     down, up = partial_half(rhs, [rows[1], rows[3]], [sib[1], sib[3]])
     down, up = y_send(down, -1), y_send(up, 1)
-    (across,) = partial_half(rhs, [rows[2]], [sib[2]])
-    across = y_send(across, 2)
     (here,) = partial_half(rhs, [rows[0]], [sib[0]])
     half = (here + up + down + across).astype(BF16)
 
     pair = jnp.stack([half, swap(half, "x_lo")])
-    lines = [pair] + [y_send(pair, -s) for s in (1, 2, 3)]
+    far = y_send(half, -2)
+    lines = [pair, y_send(pair, -1), jnp.stack([far, swap(far, "x_lo")]), y_send(pair, -3)]
     z_blocks = z_gather(half)
 
     other = tile_product(z_blocks, lines)

time: 131 us -> 129 us (0.985)
  waiting for transfers between devices: 56.9 us -> 53.9 us
    ppermute x9, waiting for transfers between devices: 36 us -> 26.1 us  [y_send(): return lax.ppermute(x, 'y', [(i, (i + step) % NY) for i in range(NY)])]
    ppermute x14, waiting for transfers between devices: 18.3 us -> 23.9 us  [ring_send(): return lax.ppermute(x, ('core', axis), ring_pairs(size, step))]
    ppermute x14, starting transfers between devices: 20.7 us -> 16.7 us  [ring_send(): return lax.ppermute(x, ('core', axis), ring_pairs(size, step))]
    ppermute x9, starting transfers between devices: 12.9 us -> 16.8 us  [y_send(): return lax.ppermute(x, 'y', [(i, (i + step) % NY) for i in range(NY)])]
    ppermute x6 -> x7, waiting for transfers between devices: 2.59 us -> 3.95 us  [swap(): return lax.ppermute(x, axis, [(0, 1), (1, 0)])]
    ppermute x6 -> x7, starting transfers between devices: 6.66 us -> 7.53 us  [swap(): return lax.ppermute(x, axis, [(0, 1), (1, 0)])]
  transfers between devices with their start and end apart: 30 -> 31, of which waited for: 14 -> 17; matrix products, arithmetic and copies ran while one was open for 0% -> 0% of each run, Pallas kernels for 3% -> 3%
where the time goes in v6:
time: 129 us
  waiting for transfers between devices  53.9 us (42%)
  starting transfers between devices  44.4 us (34%)
  blocking collectives  20.6 us (16%)
  Pallas kernels  6.9 us (5%)
  local copies, waits for them, and re-layouts  2.53 us (2%)
    ppermute x9, waiting for transfers between devices, y_send(): return lax.ppermute(x, 'y', [(i, (i + step) % NY) for i in range(NY)])  26.1 us
    ppermute x14, waiting for transfers between devices, ring_send(): return lax.ppermute(x, ('core', axis), ring_pairs(size, step))  23.9 us
    all_to_all x1, blocking collectives, body(): pieces = lax.all_to_all(mine, ('x_hi', 'x_lo', 'y'), 0, 0, tiled=True)  20.6 us
    ppermute x9, starting transfers between devices, y_send(): return lax.ppermute(x, 'y', [(i, (i + step) % NY) for i in range(NY)])  16.8 us
    ppermute x14, starting transfers between devices, ring_send(): return lax.ppermute(x, ('core', axis), ring_pairs(size, step))  16.7 us
    ppermute x7, starting transfers between devices, swap(): return lax.ppermute(x, axis, [(0, 1), (1, 0)])  7.53 us
    ppermute x7, waiting for transfers between devices, swap(): return lax.ppermute(x, axis, [(0, 1), (1, 0)])  3.95 us
    ppermute x1, starting transfers between devices, x_send(): return lax.ppermute(x, ('x_hi', 'core', 'x_lo'), pairs)  3.39 us
  transfers between devices with their start and end apart: 31, of which 17 were waited for; matrix products, arithmetic and copies ran while one was open for 0% of the time, Pallas kernels for 3%

profile of v6, /device:TPU:1, one launch (start us, length us, event | category | flops | bytes accessed | tf_op | source)
XLA Modules:
  0.0 128.7 jit_solution(3269378623817116330)
XLA Ops:
  0.0 0.9 copy-done
  0.9 3.4 %collective-permute-start = (bf16[128,384]{1,0:T(8,128)(2,1)S(1)}, bf16[128,384]{1,0:T(8,128)(2,1)S(1)}, u32[]{:S(2)}, u32[]{:S(2)}) collective-permute-start(bf16[128,384]{1,0:T(8,128)(2,1)S(1)} %constant_dynamic-slice_fusion), channel_id=1, source_target_pairs={{0,4},{4,128},{128,132},{132,0},{64,196},{68,64},{192,68},{196,192... | collective-permute-start | bytes 294920 | tf_op jit(solution)/shard_map/ppermute | solution.py:42
  4.3 1.6 %copy-done.1 = bf16[1,128,8192]{2,1,0:T(8,128)(2,1)S(1)} copy-done((bf16[1,128,8192]{2,1,0:T(8,128)(2,1)S(1)}, bf16[1,128,8192]{2,1,0:T(8,128)(2,1)}, u32[]{:S(2)}) %copy-start.1) | copy-done | bytes 2097176
  5.9 0.5 shard_map.28
  6.5 3.6 %collective-permute-start.3 = (bf16[128,2048]{1,0:T(8,128)(2,1)S(1)}, bf16[128,2048]{1,0:T(8,128)(2,1)S(1)}, u32[]{:S(2)}, u32[]{:S(2)}) collective-permute-start(bf16[128,2048]{1,0:T(8,128)(2,1)S(1)} %get-tuple-element.33.refs_0_), channel_id=1, source_target_pairs={{0,64},{64,0},{1,65},{65,1},{2,66},{66,2},{3,67},{67,3},{4,68},{68... | collective-permute-start | bytes 1572872 | tf_op jit(solution)/shard_map/ppermute | solution.py:46
  10.1 2.7 %collective-permute-start.7 = (bf16[128,2048]{1,0:T(8,128)(2,1)S(1)}, bf16[128,2048]{1,0:T(8,128)(2,1)S(1)}, u32[]{:S(2)}, u32[]{:S(2)}) collective-permute-start(bf16[128,2048]{1,0:T(8,128)(2,1)S(1)} %get-tuple-element.37), channel_id=1, source_target_pairs={{0,3},{1,0},{2,1},{3,2},{4,7},{5,4},{6,5},{7,6},{8,11},{9,8},{10,9... | collective-permute-start | bytes 1572872 | tf_op jit(solution)/shard_map/ppermute | solution.py:50
  12.9 4.0 %collective-permute-start.1 = (bf16[256,384]{1,0:T(8,128)(2,1)S(1)}, bf16[256,384]{1,0:T(8,128)(2,1)S(1)}, u32[]{:S(2)}, u32[]{:S(2)}) collective-permute-start(bf16[256,384]{1,0:T(8,128)(2,1)S(1)} %pad_maximum_fusion.2.refs_0_), channel_id=1, source_target_pairs={{0,8},{8,16},{16,24},{24,32},{32,40},{40,48},{48,56},{56,0},{64,12... | collective-permute-start | bytes 589832 | tf_op jit(solution)/shard_map/ppermute | solution.py:31
  16.9 3.3 %collective-permute-done.2.refs_2_ = bf16[256,384]{1,0:T(8,128)(2,1)S(1)} collective-permute-done((bf16[256,384]{1,0:T(8,128)(2,1)S(1)}, bf16[256,384]{1,0:T(8,128)(2,1)S(1)}, u32[]{:S(2)}, u32[]{:S(2)}) %collective-permute-start.2) | collective-permute-done | bytes 196640 | tf_op jit(solution)/shard_map/ppermute | solution.py:31
  20.1 1.3 %collective-permute-start.11 = (bf16[128,2048]{1,0:T(8,128)(2,1)S(1)}, bf16[128,2048]{1,0:T(8,128)(2,1)S(1)}, u32[]{:S(2)}, u32[]{:S(2)}) collective-permute-start(bf16[128,2048]{1,0:T(8,128)(2,1)S(1)} %get-tuple-element.39), channel_id=1, source_target_pairs={{0,2},{1,3},{2,0},{3,1},{4,6},{5,7},{6,4},{7,5},{8,10},{9,11},{10,... | collective-permute-start | bytes 1572872 | tf_op jit(solution)/shard_map/ppermute | solution.py:50
  21.5 2.7 %collective-permute-start.4 = (bf16[256,384]{1,0:T(8,128)(2,1)S(1)}, bf16[256,384]{1,0:T(8,128)(2,1)S(1)}, u32[]{:S(2)}, u32[]{:S(2)}) collective-permute-start(bf16[256,384]{1,0:T(8,128)(2,1)S(1)} %collective-permute-done.1.refs_1_), channel_id=1, source_target_pairs={{0,8},{8,16},{16,24},{24,32},{32,40},{40,48},{48,56},{56,0},{64,12... | collective-permute-start | bytes 589832 | tf_op jit(solution)/shard_map/ppermute | solution.py:31
  24.2 11.9 %collective-permute-done.6.refs_0_ = bf16[128,2048]{1,0:T(8,128)(2,1)S(1)} collective-permute-done((bf16[128,2048]{1,0:T(8,128)(2,1)S(1)}, bf16[128,2048]{1,0:T(8,128)(2,1)S(1)}, u32[]{:S(2)}, u32[]{:S(2)}) %collective-permute-start.6) | collective-permute-done | bytes 524320 | tf_op jit(solution)/shard_map/ppermute | solution.py:50
  36.3 1.5 %collective-permute-start.9 = (bf16[256,384]{1,0:T(8,128)(2,1)S(1)}, bf16[256,384]{1,0:T(8,128)(2,1)S(1)}, u32[]{:S(2)}, u32[]{:S(2)}) collective-permute-start(bf16[256,384]{1,0:T(8,128)(2,1)S(1)} %collective-permute-done.5.refs_4_), channel_id=1, source_target_pairs={{0,56},{8,0},{16,8},{24,16},{32,24},{40,32},{48,40},{56,48},{64,72... | collective-permute-start | bytes 589832 | tf_op jit(solution)/shard_map/ppermute | solution.py:31
  37.7 5.9 %collective-permute-done.10.refs_7_ = bf16[256,384]{1,0:T(8,128)(2,1)S(1)} collective-permute-done((bf16[256,384]{1,0:T(8,128)(2,1)S(1)}, bf16[256,384]{1,0:T(8,128)(2,1)S(1)}, u32[]{:S(2)}, u32[]{:S(2)}) %collective-permute-start.10) | collective-permute-done | bytes 196640 | tf_op jit(solution)/shard_map/ppermute | solution.py:31
  43.7 0.5 collective-permute-done.8.refs_5_
  44.2 1.2 collective-permute-done.9.refs_6_
  45.4 1.6 %collective-permute-start.12 = (bf16[128,2048]{1,0:T(8,128)(2,1)S(1)}, bf16[128,2048]{1,0:T(8,128)(2,1)S(1)}, u32[]{:S(2)}, u32[]{:S(2)}) collective-permute-start(bf16[128,2048]{1,0:T(8,128)(2,1)S(1)} %collective-permute-done.11.refs_0_), channel_id=1, source_target_pairs={{0,64},{64,0},{1,65},{65,1},{2,66},{66,2},{3,67},{67,3},{4,68},{68... | collective-permute-start | bytes 1572872 | tf_op jit(solution)/shard_map/ppermute | solution.py:46
  47.0 0.5 collective-permute-start.14
  47.7 0.8 collective-permute-done.12.refs_1_
  48.5 0.7 shard_map.30
  49.2 3.9 %collective-permute-start.17 = (f32[128,768]{1,0:T(8,128)S(1)}, f32[128,768]{1,0:T(8,128)S(1)}, u32[]{:S(2)}, u32[]{:S(2)}) collective-permute-start(f32[128,768]{1,0:T(8,128)S(1)} %shard_map.30), channel_id=1, source_target_pairs={{0,2},{1,3},{2,0},{3,1},{4,6},{5,7},{6,4},{7,5},{8,10},{9,11},{10,... | collective-permute-start | bytes 1179656 | tf_op jit(solution)/shard_map/ppermute | solution.py:50
  53.2 1.3 shard_map.32
  54.4 1.6 %collective-permute-start.15 = (f32[128,768]{1,0:T(8,128)S(1)}, f32[128,768]{1,0:T(8,128)S(1)}, u32[]{:S(2)}, u32[]{:S(2)}) collective-permute-start(f32[128,768]{1,0:T(8,128)S(1)} %get-tuple-element.48), channel_id=1, source_target_pairs={{0,1},{1,2},{2,3},{3,0},{4,5},{5,6},{6,7},{7,4},{8,9},{9,10},{10,1... | collective-permute-start | bytes 1179656 | tf_op jit(solution)/shard_map/ppermute | solution.py:50
  56.0 1.1 collective-permute-start.16
  57.2 0.7 shard_map.31
  57.9 4.5 %collective-permute-done.17 = f32[128,768]{1,0:T(8,128)S(1)} collective-permute-done((f32[128,768]{1,0:T(8,128)S(1)}, f32[128,768]{1,0:T(8,128)S(1)}, u32[]{:S(2)}, u32[]{:S(2)}) %collective-permute-start.17) | collective-permute-done | bytes 393248 | tf_op jit(solution)/shard_map/ppermute | solution.py:50
  62.4 8.8 %collective-permute-done.15 = f32[128,768]{1,0:T(8,128)S(1)} collective-permute-done((f32[128,768]{1,0:T(8,128)S(1)}, f32[128,768]{1,0:T(8,128)S(1)}, u32[]{:S(2)}, u32[]{:S(2)}) %collective-permute-start.15) | collective-permute-done | bytes 393248 | tf_op jit(solution)/shard_map/ppermute | solution.py:50
  71.2 0.9 collective-permute-done.16
  72.3 2.7 %collective-permute-start.18 = (bf16[128,768]{1,0:T(8,128)(2,1)S(1)}, bf16[128,768]{1,0:T(8,128)(2,1)S(1)}, u32[]{:S(2)}, u32[]{:S(2)}) collective-permute-start(bf16[128,768]{1,0:T(8,128)(2,1)S(1)} %add_convert_fusion.refs_0_), channel_id=1, source_target_pairs={{0,8},{8,16},{16,24},{24,32},{32,40},{40,48},{48,56},{56,0},{64,12... | collective-permute-start | bytes 589832 | tf_op jit(solution)/shard_map/ppermute | solution.py:31
  75.0 2.1 %collective-permute-start.27 = (bf16[128,768]{1,0:T(8,128)(2,1)S(1)}, bf16[128,768]{1,0:T(8,128)(2,1)S(1)}, u32[]{:S(2)}, u32[]{:S(2)}) collective-permute-start(bf16[128,768]{1,0:T(8,128)(2,1)S(1)} %add_convert_fusion.refs_0_), channel_id=1, source_target_pairs={{0,2},{1,3},{2,0},{3,1},{4,6},{5,7},{6,4},{7,5},{8,10},{9,11},{10,... | collective-permute-start | bytes 589832 | tf_op jit(solution)/shard_map/ppermute | solution.py:50
  77.1 0.3 collective-permute-done.25
  77.4 1.5 %collective-permute-start.29 = (bf16[2,128,768]{2,1,0:T(8,128)(2,1)S(1)}, bf16[2,128,768]{2,1,0:T(8,128)(2,1)S(1)}, u32[]{:S(2)}, u32[]{:S(2)}) collective-permute-start(bf16[2,128,768]{2,1,0:T(8,128)(2,1)S(1)} %pad_maximum_fusion.refs_8_), channel_id=1, source_target_pairs={{0,1},{1,2},{2,3},{3,0},{4,5},{5,6},{6,7},{7,4},{8,9},{9,10},{10,1... | collective-permute-start | bytes 1179656 | tf_op jit(solution)/shard_map/ppermute | solution.py:50
  79.0 2.5 %collective-permute-start.26 = (bf16[2,128,768]{2,1,0:T(8,128)(2,1)S(1)}, bf16[2,128,768]{2,1,0:T(8,128)(2,1)S(1)}, u32[]{:S(2)}, u32[]{:S(2)}) collective-permute-start(bf16[2,128,768]{2,1,0:T(8,128)(2,1)S(1)} %pad_maximum_fusion.refs_8_), channel_id=1, source_target_pairs={{0,3},{1,0},{2,1},{3,2},{4,7},{5,4},{6,5},{7,6},{8,11},{9,8},{10,9... | collective-permute-start | bytes 1179656 | tf_op jit(solution)/shard_map/ppermute | solution.py:50
  81.5 2.7 %collective-permute-start.20 = (bf16[128,768]{1,0:T(8,128)(2,1)S(1)}, bf16[128,768]{1,0:T(8,128)(2,1)S(1)}, u32[]{:S(2)}, u32[]{:S(2)}) collective-permute-start(bf16[128,768]{1,0:T(8,128)(2,1)S(1)} %collective-permute-done.18.refs_1_), channel_id=1, source_target_pairs={{0,8},{8,16},{16,24},{24,32},{32,40},{40,48},{48,56},{56,0},{64,12... | collective-permute-start | bytes 589832 | tf_op jit(solution)/shard_map/ppermute | solution.py:31
  84.1 0.3 collective-permute-start.28
  84.4 3.0 %collective-permute-done.21.refs_4_ = bf16[128,768]{1,0:T(8,128)(2,1)S(1)} collective-permute-done((bf16[128,768]{1,0:T(8,128)(2,1)S(1)}, bf16[128,768]{1,0:T(8,128)(2,1)S(1)}, u32[]{:S(2)}, u32[]{:S(2)}) %collective-permute-start.21) | collective-permute-done | bytes 196640 | tf_op jit(solution)/shard_map/ppermute | solution.py:31
  87.5 1.2 collective-permute-done.20.refs_3_
  88.7 0.4 collective-permute-start.24
  89.0 0.5 collective-permute-done.28
  89.6 2.5 %collective-permute-start.22 = (bf16[128,768]{1,0:T(8,128)(2,1)S(1)}, bf16[128,768]{1,0:T(8,128)(2,1)S(1)}, u32[]{:S(2)}, u32[]{:S(2)}) collective-permute-start(bf16[128,768]{1,0:T(8,128)(2,1)S(1)} %collective-permute-done.20.refs_3_), channel_id=1, source_target_pairs={{0,8},{8,16},{16,24},{24,32},{32,40},{40,48},{48,56},{56,0},{64,12... | collective-permute-start | bytes 589832 | tf_op jit(solution)/shard_map/ppermute | solution.py:31
  92.2 1.0 collective-permute-done.23.refs_6_
  93.2 3.9 %collective-permute-done.24.refs_7_ = bf16[128,768]{1,0:T(8,128)(2,1)S(1)} collective-permute-done((bf16[128,768]{1,0:T(8,128)(2,1)S(1)}, bf16[128,768]{1,0:T(8,128)(2,1)S(1)}, u32[]{:S(2)}, u32[]{:S(2)}) %collective-permute-start.24) | collective-permute-done | bytes 196640 | tf_op jit(solution)/shard_map/ppermute | solution.py:31
  97.1 3.8 %collective-permute-done.22.refs_5_ = bf16[128,768]{1,0:T(8,128)(2,1)S(1)} collective-permute-done((bf16[128,768]{1,0:T(8,128)(2,1)S(1)}, bf16[128,768]{1,0:T(8,128)(2,1)S(1)}, u32[]{:S(2)}, u32[]{:S(2)}) %collective-permute-start.22) | collective-permute-done | bytes 196640 | tf_op jit(solution)/shard_map/ppermute | solution.py:31
  100.9 1.2 shard_map.33
  102.1 1.4 %collective-permute-start.30 = (bf16[16,128,256]{2,1,0:T(8,128)(2,1)S(1)}, bf16[16,128,256]{2,1,0:T(8,128)(2,1)S(1)}, u32[]{:S(2)}, u32[]{:S(2)}) collective-permute-start(bf16[16,128,256]{2,1,0:T(8,128)(2,1)S(1)} %shard_map.33), channel_id=1, source_target_pairs={{0,64},{64,0},{1,65},{65,1},{2,66},{66,2},{3,67},{67,3},{4,68},{68... | collective-permute-start | bytes 3145736 | tf_op jit(solution)/shard_map/ppermute | solution.py:46
  103.5 2.3 %collective-permute-done.30.refs_12_ = bf16[16,128,256]{2,1,0:T(8,128)(2,1)S(1)} collective-permute-done((bf16[16,128,256]{2,1,0:T(8,128)(2,1)S(1)}, bf16[16,128,256]{2,1,0:T(8,128)(2,1)S(1)}, u32[]{:S(2)}, u32[]{:S(2)}) %collective-permute-start.30) | collective-permute-done | bytes 1048608 | tf_op jit(solution)/shard_map/ppermute | solution.py:46
  105.8 1.2 shard_map.34
  107.0 20.6 %all_to_all.5.pieces = bf16[16,128,256]{2,1,0:T(8,128)(2,1)S(1)} all-to-all(bf16[16,128,256]{2,1,0:T(8,128)(2,1)S(1)} %shard_map.34), channel_id=1, replica_groups=mesh['x_hi'=2,'core'=2,'z'=8,'x_lo'=2,'y'=4] {'x_hi','x_lo','y'}, dimensions={0} | all-to-all | bytes 2097152 | tf_op jit(solution)/shard_map/all_to_all | solution.py:202
  127.6 1.1 shard_map.35
  (32 shorter events, 0.9 us)
Async XLA Ops:
  0.0 0.9 copy-start
  0.9 5.5 %collective-permute-start = (bf16[128,384]{1,0:T(8,128)(2,1)S(1)}, bf16[128,384]{1,0:T(8,128)(2,1)S(1)}, u32[]{:S(2)}, u32[]{:S(2)}) collective-permute-start(bf16[128,384]{1,0:T(8,128)(2,1)S(1)} %constant_dynamic-slice_fusion), channel_id=1, source_target_pairs={{0,4},{4,128},{128,132},{132,0},{64,196},{68,64},{192,68},{196,192... | collective-permute-start | bytes 294920 | tf_op jit(solution)/shard_map/ppermute | solution.py:42
  4.3 1.6 %copy-start.1 = (bf16[1,128,8192]{2,1,0:T(8,128)(2,1)S(1)}, bf16[1,128,8192]{2,1,0:T(8,128)(2,1)}, u32[]{:S(2)}) copy-start(bf16[1,128,8192]{2,1,0:T(8,128)(2,1)} %param.2) | copy-start | bytes 6291460
  6.5 15.0 %collective-permute-start.3 = (bf16[128,2048]{1,0:T(8,128)(2,1)S(1)}, bf16[128,2048]{1,0:T(8,128)(2,1)S(1)}, u32[]{:S(2)}, u32[]{:S(2)}) collective-permute-start(bf16[128,2048]{1,0:T(8,128)(2,1)S(1)} %get-tuple-element.33.refs_0_), channel_id=1, source_target_pairs={{0,64},{64,0},{1,65},{65,1},{2,66},{66,2},{3,67},{67,3},{4,68},{68... | collective-permute-start | bytes 1572872 | tf_op jit(solution)/shard_map/ppermute | solution.py:46
  10.1 26.0 %collective-permute-start.6 = (bf16[128,2048]{1,0:T(8,128)(2,1)S(1)}, bf16[128,2048]{1,0:T(8,128)(2,1)S(1)}, u32[]{:S(2)}, u32[]{:S(2)}) collective-permute-start(bf16[128,2048]{1,0:T(8,128)(2,1)S(1)} %get-tuple-element.36), channel_id=1, source_target_pairs={{0,1},{1,2},{2,3},{3,0},{4,5},{5,6},{6,7},{7,4},{8,9},{9,10},{10,1... | collective-permute-start | bytes 1572872 | tf_op jit(solution)/shard_map/ppermute | solution.py:50
  10.1 26.0 %collective-permute-start.7 = (bf16[128,2048]{1,0:T(8,128)(2,1)S(1)}, bf16[128,2048]{1,0:T(8,128)(2,1)S(1)}, u32[]{:S(2)}, u32[]{:S(2)}) collective-permute-start(bf16[128,2048]{1,0:T(8,128)(2,1)S(1)} %get-tuple-element.37), channel_id=1, source_target_pairs={{0,3},{1,0},{2,1},{3,2},{4,7},{5,4},{6,5},{7,6},{8,11},{9,8},{10,9... | collective-permute-start | bytes 1572872 | tf_op jit(solution)/shard_map/ppermute | solution.py:50
  12.8 7.3 %collective-permute-start.2 = (bf16[256,384]{1,0:T(8,128)(2,1)S(1)}, bf16[256,384]{1,0:T(8,128)(2,1)S(1)}, u32[]{:S(2)}, u32[]{:S(2)}) collective-permute-start(bf16[256,384]{1,0:T(8,128)(2,1)S(1)} %pad_maximum_fusion.2.refs_0_), channel_id=1, source_target_pairs={{0,56},{8,0},{16,8},{24,16},{32,24},{40,32},{48,40},{56,48},{64,72... | collective-permute-start | bytes 589832 | tf_op jit(solution)/shard_map/ppermute | solution.py:31
  12.9 8.6 %collective-permute-start.1 = (bf16[256,384]{1,0:T(8,128)(2,1)S(1)}, bf16[256,384]{1,0:T(8,128)(2,1)S(1)}, u32[]{:S(2)}, u32[]{:S(2)}) collective-permute-start(bf16[256,384]{1,0:T(8,128)(2,1)S(1)} %pad_maximum_fusion.2.refs_0_), channel_id=1, source_target_pairs={{0,8},{8,16},{16,24},{24,32},{32,40},{40,48},{48,56},{56,0},{64,12... | collective-permute-start | bytes 589832 | tf_op jit(solution)/shard_map/ppermute | solution.py:31
  20.1 17.6 %collective-permute-start.11 = (bf16[128,2048]{1,0:T(8,128)(2,1)S(1)}, bf16[128,2048]{1,0:T(8,128)(2,1)S(1)}, u32[]{:S(2)}, u32[]{:S(2)}) collective-permute-start(bf16[128,2048]{1,0:T(8,128)(2,1)S(1)} %get-tuple-element.39), channel_id=1, source_target_pairs={{0,2},{1,3},{2,0},{3,1},{4,6},{5,7},{6,4},{7,5},{8,10},{9,11},{10,... | collective-permute-start | bytes 1572872 | tf_op jit(solution)/shard_map/ppermute | solution.py:50
  21.5 14.6 %collective-permute-start.5 = (bf16[256,384]{1,0:T(8,128)(2,1)S(1)}, bf16[256,384]{1,0:T(8,128)(2,1)S(1)}, u32[]{:S(2)}, u32[]{:S(2)}) collective-permute-start(bf16[256,384]{1,0:T(8,128)(2,1)S(1)} %collective-permute-done.2.refs_2_), channel_id=1, source_target_pairs={{0,56},{8,0},{16,8},{24,16},{32,24},{40,32},{48,40},{56,48},{64,72... | collective-permute-start | bytes 589832 | tf_op jit(solution)/shard_map/ppermute | solution.py:31
  21.5 14.6 %collective-permute-start.4 = (bf16[256,384]{1,0:T(8,128)(2,1)S(1)}, bf16[256,384]{1,0:T(8,128)(2,1)S(1)}, u32[]{:S(2)}, u32[]{:S(2)}) collective-permute-start(bf16[256,384]{1,0:T(8,128)(2,1)S(1)} %collective-permute-done.1.refs_1_), channel_id=1, source_target_pairs={{0,8},{8,16},{16,24},{24,32},{32,40},{40,48},{48,56},{56,0},{64,12... | collective-permute-start | bytes 589832 | tf_op jit(solution)/shard_map/ppermute | solution.py:31
  36.1 7.6 %collective-permute-start.10 = (bf16[256,384]{1,0:T(8,128)(2,1)S(1)}, bf16[256,384]{1,0:T(8,128)(2,1)S(1)}, u32[]{:S(2)}, u32[]{:S(2)}) collective-permute-start(bf16[256,384]{1,0:T(8,128)(2,1)S(1)} %collective-permute-done.4.refs_3_), channel_id=1, source_target_pairs={{0,16},{8,24},{16,32},{24,40},{32,48},{40,56},{48,0},{56,8},{64,11... | collective-permute-start | bytes 589832 | tf_op jit(solution)/shard_map/ppermute | solution.py:31
  36.2 8.0 %collective-permute-start.8 = (bf16[256,384]{1,0:T(8,128)(2,1)S(1)}, bf16[256,384]{1,0:T(8,128)(2,1)S(1)}, u32[]{:S(2)}, u32[]{:S(2)}) collective-permute-start(bf16[256,384]{1,0:T(8,128)(2,1)S(1)} %collective-permute-done.4.refs_3_), channel_id=1, source_target_pairs={{0,8},{8,16},{16,24},{24,32},{32,40},{40,48},{48,56},{56,0},{64,12... | collective-permute-start | bytes 589832 | tf_op jit(solution)/shard_map/ppermute | solution.py:31
  36.3 9.1 %collective-permute-start.9 = (bf16[256,384]{1,0:T(8,128)(2,1)S(1)}, bf16[256,384]{1,0:T(8,128)(2,1)S(1)}, u32[]{:S(2)}, u32[]{:S(2)}) collective-permute-start(bf16[256,384]{1,0:T(8,128)(2,1)S(1)} %collective-permute-done.5.refs_4_), channel_id=1, source_target_pairs={{0,56},{8,0},{16,8},{24,16},{32,24},{40,32},{48,40},{56,48},{64,72... | collective-permute-start | bytes 589832 | tf_op jit(solution)/shard_map/ppermute | solution.py:31
  45.4 3.1 %collective-permute-start.12 = (bf16[128,2048]{1,0:T(8,128)(2,1)S(1)}, bf16[128,2048]{1,0:T(8,128)(2,1)S(1)}, u32[]{:S(2)}, u32[]{:S(2)}) collective-permute-start(bf16[128,2048]{1,0:T(8,128)(2,1)S(1)} %collective-permute-done.11.refs_0_), channel_id=1, source_target_pairs={{0,64},{64,0},{1,65},{65,1},{2,66},{66,2},{3,67},{67,3},{4,68},{68... | collective-permute-start | bytes 1572872 | tf_op jit(solution)/shard_map/ppermute | solution.py:46
  47.0 6.2 %collective-permute-start.13 = (bf16[128,2048]{1,0:T(8,128)(2,1)S(1)}, bf16[128,2048]{1,0:T(8,128)(2,1)S(1)}, u32[]{:S(2)}, u32[]{:S(2)}) collective-permute-start(bf16[128,2048]{1,0:T(8,128)(2,1)S(1)} %collective-permute-done.6.refs_0_), channel_id=1, source_target_pairs={{0,64},{64,0},{1,65},{65,1},{2,66},{66,2},{3,67},{67,3},{4,68},{68... | collective-permute-start | bytes 1572872 | tf_op jit(solution)/shard_map/ppermute | solution.py:46
  47.0 6.2 %collective-permute-start.14 = (bf16[128,2048]{1,0:T(8,128)(2,1)S(1)}, bf16[128,2048]{1,0:T(8,128)(2,1)S(1)}, u32[]{:S(2)}, u32[]{:S(2)}) collective-permute-start(bf16[128,2048]{1,0:T(8,128)(2,1)S(1)} %collective-permute-done.7.refs_1_), channel_id=1, source_target_pairs={{0,64},{64,0},{1,65},{65,1},{2,66},{66,2},{3,67},{67,3},{4,68},{68... | collective-permute-start | bytes 1572872 | tf_op jit(solution)/shard_map/ppermute | solution.py:46
  49.2 13.2 %collective-permute-start.17 = (f32[128,768]{1,0:T(8,128)S(1)}, f32[128,768]{1,0:T(8,128)S(1)}, u32[]{:S(2)}, u32[]{:S(2)}) collective-permute-start(f32[128,768]{1,0:T(8,128)S(1)} %shard_map.30), channel_id=1, source_target_pairs={{0,2},{1,3},{2,0},{3,1},{4,6},{5,7},{6,4},{7,5},{8,10},{9,11},{10,... | collective-permute-start | bytes 1179656 | tf_op jit(solution)/shard_map/ppermute | solution.py:50
  54.4 16.7 %collective-permute-start.15 = (f32[128,768]{1,0:T(8,128)S(1)}, f32[128,768]{1,0:T(8,128)S(1)}, u32[]{:S(2)}, u32[]{:S(2)}) collective-permute-start(f32[128,768]{1,0:T(8,128)S(1)} %get-tuple-element.48), channel_id=1, source_target_pairs={{0,1},{1,2},{2,3},{3,0},{4,5},{5,6},{6,7},{7,4},{8,9},{9,10},{10,1... | collective-permute-start | bytes 1179656 | tf_op jit(solution)/shard_map/ppermute | solution.py:50
  56.0 16.0 %collective-permute-start.16 = (f32[128,768]{1,0:T(8,128)S(1)}, f32[128,768]{1,0:T(8,128)S(1)}, u32[]{:S(2)}, u32[]{:S(2)}) collective-permute-start(f32[128,768]{1,0:T(8,128)S(1)} %get-tuple-element.49), channel_id=1, source_target_pairs={{0,3},{1,0},{2,1},{3,2},{4,7},{5,4},{6,5},{7,6},{8,11},{9,8},{10,9... | collective-permute-start | bytes 1179656 | tf_op jit(solution)/shard_map/ppermute | solution.py:50
  72.1 5.3 %collective-permute-start.25 = (bf16[128,768]{1,0:T(8,128)(2,1)S(1)}, bf16[128,768]{1,0:T(8,128)(2,1)S(1)}, u32[]{:S(2)}, u32[]{:S(2)}) collective-permute-start(bf16[128,768]{1,0:T(8,128)(2,1)S(1)} %add_convert_fusion.refs_0_), channel_id=1, source_target_pairs={{0,4},{4,0},{1,5},{5,1},{2,6},{6,2},{3,7},{7,3},{8,12},{12,8},{9,1... | collective-permute-start | bytes 589832 | tf_op jit(solution)/shard_map/ppermute | solution.py:46
  72.2 9.2 %collective-permute-start.19 = (bf16[128,768]{1,0:T(8,128)(2,1)S(1)}, bf16[128,768]{1,0:T(8,128)(2,1)S(1)}, u32[]{:S(2)}, u32[]{:S(2)}) collective-permute-start(bf16[128,768]{1,0:T(8,128)(2,1)S(1)} %add_convert_fusion.refs_0_), channel_id=1, source_target_pairs={{0,56},{8,0},{16,8},{24,16},{32,24},{40,32},{48,40},{56,48},{64,72... | collective-permute-start | bytes 589832 | tf_op jit(solution)/shard_map/ppermute | solution.py:31
  72.3 9.2 %collective-permute-start.18 = (bf16[128,768]{1,0:T(8,128)(2,1)S(1)}, bf16[128,768]{1,0:T(8,128)(2,1)S(1)}, u32[]{:S(2)}, u32[]{:S(2)}) collective-permute-start(bf16[128,768]{1,0:T(8,128)(2,1)S(1)} %add_convert_fusion.refs_0_), channel_id=1, source_target_pairs={{0,8},{8,16},{16,24},{24,32},{32,40},{40,48},{48,56},{56,0},{64,12... | collective-permute-start | bytes 589832 | tf_op jit(solution)/shard_map/ppermute | solution.py:31
  75.0 9.2 %collective-permute-start.27 = (bf16[128,768]{1,0:T(8,128)(2,1)S(1)}, bf16[128,768]{1,0:T(8,128)(2,1)S(1)}, u32[]{:S(2)}, u32[]{:S(2)}) collective-permute-start(bf16[128,768]{1,0:T(8,128)(2,1)S(1)} %add_convert_fusion.refs_0_), channel_id=1, source_target_pairs={{0,2},{1,3},{2,0},{3,1},{4,6},{5,7},{6,4},{7,5},{8,10},{9,11},{10,... | collective-permute-start | bytes 589832 | tf_op jit(solution)/shard_map/ppermute | solution.py:50
  77.4 14.7 %collective-permute-start.29 = (bf16[2,128,768]{2,1,0:T(8,128)(2,1)S(1)}, bf16[2,128,768]{2,1,0:T(8,128)(2,1)S(1)}, u32[]{:S(2)}, u32[]{:S(2)}) collective-permute-start(bf16[2,128,768]{2,1,0:T(8,128)(2,1)S(1)} %pad_maximum_fusion.refs_8_), channel_id=1, source_target_pairs={{0,1},{1,2},{2,3},{3,0},{4,5},{5,6},{6,7},{7,4},{8,9},{9,10},{10,1... | collective-permute-start | bytes 1179656 | tf_op jit(solution)/shard_map/ppermute | solution.py:50
  79.0 13.2 %collective-permute-start.26 = (bf16[2,128,768]{2,1,0:T(8,128)(2,1)S(1)}, bf16[2,128,768]{2,1,0:T(8,128)(2,1)S(1)}, u32[]{:S(2)}, u32[]{:S(2)}) collective-permute-start(bf16[2,128,768]{2,1,0:T(8,128)(2,1)S(1)} %pad_maximum_fusion.refs_8_), channel_id=1, source_target_pairs={{0,3},{1,0},{2,1},{3,2},{4,7},{5,4},{6,5},{7,6},{8,11},{9,8},{10,9... | collective-permute-start | bytes 1179656 | tf_op jit(solution)/shard_map/ppermute | solution.py:50
  81.5 6.0 %collective-permute-start.21 = (bf16[128,768]{1,0:T(8,128)(2,1)S(1)}, bf16[128,768]{1,0:T(8,128)(2,1)S(1)}, u32[]{:S(2)}, u32[]{:S(2)}) collective-permute-start(bf16[128,768]{1,0:T(8,128)(2,1)S(1)} %collective-permute-done.19.refs_2_), channel_id=1, source_target_pairs={{0,56},{8,0},{16,8},{24,16},{32,24},{40,32},{48,40},{56,48},{64,72... | collective-permute-start | bytes 589832 | tf_op jit(solution)/shard_map/ppermute | solution.py:31
  81.5 7.2 %collective-permute-start.20 = (bf16[128,768]{1,0:T(8,128)(2,1)S(1)}, bf16[128,768]{1,0:T(8,128)(2,1)S(1)}, u32[]{:S(2)}, u32[]{:S(2)}) collective-permute-start(bf16[128,768]{1,0:T(8,128)(2,1)S(1)} %collective-permute-done.18.refs_1_), channel_id=1, source_target_pairs={{0,8},{8,16},{16,24},{24,32},{32,40},{40,48},{48,56},{56,0},{64,12... | collective-permute-start | bytes 589832 | tf_op jit(solution)/shard_map/ppermute | solution.py:31
  84.1 5.4 %collective-permute-start.28 = (bf16[128,768]{1,0:T(8,128)(2,1)S(1)}, bf16[128,768]{1,0:T(8,128)(2,1)S(1)}, u32[]{:S(2)}, u32[]{:S(2)}) collective-permute-start(bf16[128,768]{1,0:T(8,128)(2,1)S(1)} %collective-permute-done.27), channel_id=1, source_target_pairs={{0,4},{4,0},{1,5},{5,1},{2,6},{6,2},{3,7},{7,3},{8,12},{12,8},{9,1... | collective-permute-start | bytes 589832 | tf_op jit(solution)/shard_map/ppermute | solution.py:46
  87.5 5.7 %collective-permute-start.23 = (bf16[128,768]{1,0:T(8,128)(2,1)S(1)}, bf16[128,768]{1,0:T(8,128)(2,1)S(1)}, u32[]{:S(2)}, u32[]{:S(2)}) collective-permute-start(bf16[128,768]{1,0:T(8,128)(2,1)S(1)} %collective-permute-done.21.refs_4_), channel_id=1, source_target_pairs={{0,56},{8,0},{16,8},{24,16},{32,24},{40,32},{48,40},{56,48},{64,72... | collective-permute-start | bytes 589832 | tf_op jit(solution)/shard_map/ppermute | solution.py:31
  88.7 8.4 %collective-permute-start.24 = (bf16[128,768]{1,0:T(8,128)(2,1)S(1)}, bf16[128,768]{1,0:T(8,128)(2,1)S(1)}, u32[]{:S(2)}, u32[]{:S(2)}) collective-permute-start(bf16[128,768]{1,0:T(8,128)(2,1)S(1)} %collective-permute-done.20.refs_3_), channel_id=1, source_target_pairs={{0,16},{8,24},{16,32},{24,40},{32,48},{40,56},{48,0},{56,8},{64,11... | collective-permute-start | bytes 589832 | tf_op jit(solution)/shard_map/ppermute | solution.py:31
  89.6 11.3 %collective-permute-start.22 = (bf16[128,768]{1,0:T(8,128)(2,1)S(1)}, bf16[128,768]{1,0:T(8,128)(2,1)S(1)}, u32[]{:S(2)}, u32[]{:S(2)}) collective-permute-start(bf16[128,768]{1,0:T(8,128)(2,1)S(1)} %collective-permute-done.20.refs_3_), channel_id=1, source_target_pairs={{0,8},{8,16},{16,24},{24,32},{32,40},{40,48},{48,56},{56,0},{64,12... | collective-permute-start | bytes 589832 | tf_op jit(solution)/shard_map/ppermute | solution.py:31
  102.1 3.7 %collective-permute-start.30 = (bf16[16,128,256]{2,1,0:T(8,128)(2,1)S(1)}, bf16[16,128,256]{2,1,0:T(8,128)(2,1)S(1)}, u32[]{:S(2)}, u32[]{:S(2)}) collective-permute-start(bf16[16,128,256]{2,1,0:T(8,128)(2,1)S(1)} %shard_map.33), channel_id=1, source_target_pairs={{0,64},{64,0},{1,65},{65,1},{2,66},{66,2},{3,67},{67,3},{4,68},{68... | collective-permute-start | bytes 3145736 | tf_op jit(solution)/shard_map/ppermute | solution.py:46

commit v7 on v6

--- a/solution.py
+++ b/solution.py
@@ -174,7 +174,7 @@
     sib = [swap(rows[0], "core"), None, None, None]
     pair = jnp.concatenate([mine, theirs], axis=0)
     first = z_step(pair, pair)
-    first, sib[0] = lax.optimization_barrier((first, sib[0]))
+    first = lax.optimization_barrier(first)
     fwd, bwd = z_step(*first)
     bwd, rows[1], rows[3] = lax.optimization_barrier((bwd, rows[1], rows[3]))
     second = [fwd, bwd]
@@ -184,11 +184,10 @@
     third, far, rows[2] = lax.optimization_barrier((third, far, rows[2]))
     sib[2] = swap(rows[2], "core")
     rhs = collect([pair, *first, *second, *third, far])
-    (across,) = partial_half(rhs, [rows[2]], [sib[2]])
-    rhs, across = lax.optimization_barrier((rhs, across))
-    across = y_send(across, 2)
     down, up = partial_half(rhs, [rows[1], rows[3]], [sib[1], sib[3]])
     down, up = y_send(down, -1), y_send(up, 1)
+    (across,) = partial_half(rhs, [rows[2]], [sib[2]])
+    across = y_send(across, 2)
     (here,) = partial_half(rhs, [rows[0]], [sib[0]])
     half = (here + up + down + across).astype(BF16)
 

time: 129 us -> 125 us (0.969)
  waiting for transfers between devices: 53.9 us -> 42.7 us
  starting transfers between devices: 44.4 us -> 49.8 us
  blocking collectives: 20.6 us -> 22.1 us
    ppermute x7, starting transfers between devices: 7.53 us -> 18.5 us  [swap(): return lax.ppermute(x, axis, [(0, 1), (1, 0)])]
    ppermute x9, waiting for transfers between devices: 26.1 us -> 15.2 us  [y_send(): return lax.ppermute(x, 'y', [(i, (i + step) % NY) for i in range(NY)])]
    ppermute x9, starting transfers between devices: 16.8 us -> 9.74 us  [y_send(): return lax.ppermute(x, 'y', [(i, (i + step) % NY) for i in range(NY)])]
    ppermute x14, starting transfers between devices: 16.7 us -> 18.2 us  [ring_send(): return lax.ppermute(x, ('core', axis), ring_pairs(size, step))]
    all_to_all x1, blocking collectives: 20.6 us -> 22.1 us  [body(): pieces = lax.all_to_all(mine, ('x_hi', 'x_lo', 'y'), 0, 0, tiled=True)]
  transfers between devices with their start and end apart: 31 -> 31, of which waited for: 17 -> 14; matrix products, arithmetic and copies ran while one was open for 0% -> 0% of each run, Pallas kernels for 3% -> 3%
where the time goes in v7:
time: 125 us; the launch traced here: 124 us
  starting transfers between devices  49.8 us (40%)
  waiting for transfers between devices  42.7 us (34%)
  blocking collectives  22.1 us (18%)
  Pallas kernels  6.9 us (6%)
  local copies, waits for them, and re-layouts  2.53 us (2%)
    ppermute x14, waiting for transfers between devices, ring_send(): return lax.ppermute(x, ('core', axis), ring_pairs(size, step))  23.7 us
    all_to_all x1, blocking collectives, body(): pieces = lax.all_to_all(mine, ('x_hi', 'x_lo', 'y'), 0, 0, tiled=True)  22.1 us
    ppermute x7, starting transfers between devices, swap(): return lax.ppermute(x, axis, [(0, 1), (1, 0)])  18.5 us
    ppermute x14, starting transfers between devices, ring_send(): return lax.ppermute(x, ('core', axis), ring_pairs(size, step))  18.2 us
    ppermute x9, waiting for transfers between devices, y_send(): return lax.ppermute(x, 'y', [(i, (i + step) % NY) for i in range(NY)])  15.2 us
    ppermute x9, starting transfers between devices, y_send(): return lax.ppermute(x, 'y', [(i, (i + step) % NY) for i in range(NY)])  9.74 us
    ppermute x7, waiting for transfers between devices, swap(): return lax.ppermute(x, axis, [(0, 1), (1, 0)])  3.84 us
    ppermute x1, starting transfers between devices, x_send(): return lax.ppermute(x, ('x_hi', 'core', 'x_lo'), pairs)  3.39 us
  transfers between devices with their start and end apart: 31, of which 14 were waited for; matrix products, arithmetic and copies ran while one was open for 0% of the time, Pallas kernels for 3%

profile of v7, /device:TPU:1, one launch (start us, length us, event | category | flops | bytes accessed | tf_op | source)
XLA Modules:
  0.0 124.4 jit_solution(12684896252049182060)
XLA Ops:
  0.0 0.9 copy-done
  0.9 3.4 %collective-permute-start = (bf16[128,384]{1,0:T(8,128)(2,1)S(1)}, bf16[128,384]{1,0:T(8,128)(2,1)S(1)}, u32[]{:S(2)}, u32[]{:S(2)}) collective-permute-start(bf16[128,384]{1,0:T(8,128)(2,1)S(1)} %constant_dynamic-slice_fusion), channel_id=1, source_target_pairs={{0,4},{4,128},{128,132},{132,0},{64,196},{68,64},{192,68},{196,192... | collective-permute-start | bytes 294920 | tf_op jit(solution)/shard_map/ppermute | solution.py:42
  4.3 1.6 %copy-done.1 = bf16[1,128,8192]{2,1,0:T(8,128)(2,1)S(1)} copy-done((bf16[1,128,8192]{2,1,0:T(8,128)(2,1)S(1)}, bf16[1,128,8192]{2,1,0:T(8,128)(2,1)}, u32[]{:S(2)}) %copy-start.1) | copy-done | bytes 2097176
  5.9 0.5 shard_map.28
  6.5 1.4 %collective-permute-start.5 = (bf16[128,2048]{1,0:T(8,128)(2,1)S(1)}, bf16[128,2048]{1,0:T(8,128)(2,1)S(1)}, u32[]{:S(2)}, u32[]{:S(2)}) collective-permute-start(bf16[128,2048]{1,0:T(8,128)(2,1)S(1)} %get-tuple-element.32), channel_id=1, source_target_pairs={{0,1},{1,2},{2,3},{3,0},{4,5},{5,6},{6,7},{7,4},{8,9},{9,10},{10,1... | collective-permute-start | bytes 1572872 | tf_op jit(solution)/shard_map/ppermute | solution.py:50
  7.9 1.5 %collective-permute-start.6 = (bf16[128,2048]{1,0:T(8,128)(2,1)S(1)}, bf16[128,2048]{1,0:T(8,128)(2,1)S(1)}, u32[]{:S(2)}, u32[]{:S(2)}) collective-permute-start(bf16[128,2048]{1,0:T(8,128)(2,1)S(1)} %get-tuple-element.33), channel_id=1, source_target_pairs={{0,3},{1,0},{2,1},{3,2},{4,7},{5,4},{6,5},{7,6},{8,11},{9,8},{10,9... | collective-permute-start | bytes 1572872 | tf_op jit(solution)/shard_map/ppermute | solution.py:50
  9.4 5.6 %collective-permute-start.1 = (bf16[256,384]{1,0:T(8,128)(2,1)S(1)}, bf16[256,384]{1,0:T(8,128)(2,1)S(1)}, u32[]{:S(2)}, u32[]{:S(2)}) collective-permute-start(bf16[256,384]{1,0:T(8,128)(2,1)S(1)} %pad_maximum_fusion.2.refs_0_), channel_id=1, source_target_pairs={{0,8},{8,16},{16,24},{24,32},{32,40},{40,48},{48,56},{56,0},{64,12... | collective-permute-start | bytes 589832 | tf_op jit(solution)/shard_map/ppermute | solution.py:31
  15.1 1.6 %collective-permute-start.10 = (bf16[128,2048]{1,0:T(8,128)(2,1)S(1)}, bf16[128,2048]{1,0:T(8,128)(2,1)S(1)}, u32[]{:S(2)}, u32[]{:S(2)}) collective-permute-start(bf16[128,2048]{1,0:T(8,128)(2,1)S(1)} %get-tuple-element.35), channel_id=1, source_target_pairs={{0,2},{1,3},{2,0},{3,1},{4,6},{5,7},{6,4},{7,5},{8,10},{9,11},{10,... | collective-permute-start | bytes 1572872 | tf_op jit(solution)/shard_map/ppermute | solution.py:50
  16.6 1.1 collective-permute-done.1.refs_1_
  17.7 5.2 %collective-permute-done.2.refs_2_ = bf16[256,384]{1,0:T(8,128)(2,1)S(1)} collective-permute-done((bf16[256,384]{1,0:T(8,128)(2,1)S(1)}, bf16[256,384]{1,0:T(8,128)(2,1)S(1)}, u32[]{:S(2)}, u32[]{:S(2)}) %collective-permute-start.2) | collective-permute-done | bytes 196640 | tf_op jit(solution)/shard_map/ppermute | solution.py:31
  22.9 1.5 %collective-permute-start.4 = (bf16[256,384]{1,0:T(8,128)(2,1)S(1)}, bf16[256,384]{1,0:T(8,128)(2,1)S(1)}, u32[]{:S(2)}, u32[]{:S(2)}) collective-permute-start(bf16[256,384]{1,0:T(8,128)(2,1)S(1)} %collective-permute-done.2.refs_2_), channel_id=1, source_target_pairs={{0,56},{8,0},{16,8},{24,16},{32,24},{40,32},{48,40},{56,48},{64,72... | collective-permute-start | bytes 589832 | tf_op jit(solution)/shard_map/ppermute | solution.py:31
  24.4 4.3 %collective-permute-done.3.refs_3_ = bf16[256,384]{1,0:T(8,128)(2,1)S(1)} collective-permute-done((bf16[256,384]{1,0:T(8,128)(2,1)S(1)}, bf16[256,384]{1,0:T(8,128)(2,1)S(1)}, u32[]{:S(2)}, u32[]{:S(2)}) %collective-permute-start.3) | collective-permute-done | bytes 196640 | tf_op jit(solution)/shard_map/ppermute | solution.py:31
  28.7 1.9 %collective-permute-done.4.refs_4_ = bf16[256,384]{1,0:T(8,128)(2,1)S(1)} collective-permute-done((bf16[256,384]{1,0:T(8,128)(2,1)S(1)}, bf16[256,384]{1,0:T(8,128)(2,1)S(1)}, u32[]{:S(2)}, u32[]{:S(2)}) %collective-permute-start.4) | collective-permute-done | bytes 196640 | tf_op jit(solution)/shard_map/ppermute | solution.py:31
  30.6 0.4 collective-permute-start.8
  31.0 7.6 %collective-permute-start.12 = (bf16[128,2048]{1,0:T(8,128)(2,1)S(1)}, bf16[128,2048]{1,0:T(8,128)(2,1)S(1)}, u32[]{:S(2)}, u32[]{:S(2)}) collective-permute-start(bf16[128,2048]{1,0:T(8,128)(2,1)S(1)} %collective-permute-done.5.refs_0_), channel_id=1, source_target_pairs={{0,64},{64,0},{1,65},{65,1},{2,66},{66,2},{3,67},{67,3},{4,68},{68... | collective-permute-start | bytes 1572872 | tf_op jit(solution)/shard_map/ppermute | solution.py:46
  38.7 0.0 collective-permute-start.13
  38.7 0.4 collective-permute-done.8.refs_6_
  39.0 4.2 %collective-permute-start.16 = (bf16[128,2048]{1,0:T(8,128)(2,1)S(1)}, bf16[128,2048]{1,0:T(8,128)(2,1)S(1)}, u32[]{:S(2)}, u32[]{:S(2)}) collective-permute-start(bf16[128,2048]{1,0:T(8,128)(2,1)S(1)} %collective-permute-done.10.refs_0_), channel_id=1, source_target_pairs={{0,64},{64,0},{1,65},{65,1},{2,66},{66,2},{3,67},{67,3},{4,68},{68... | collective-permute-start | bytes 1572872 | tf_op jit(solution)/shard_map/ppermute | solution.py:46
  43.3 0.2 shard_map.29.rhs_ref
  43.5 1.2 %shard_map.31 = (f32[128,768]{1,0:T(8,128)S(1)}, f32[128,768]{1,0:T(8,128)S(1)}) custom-call(bf16[2048,384]{1,0:T(8,128)(2,1)S(1)} %shard_map.29.rhs_ref, bf16[128,2048]{1,0:T(8,128)(2,1)S(1)} %collective-permute-done.5.refs_0_, bf16[128,2048]{1,0:T(8,128)(2,1)S(1)} %collective-permute-done.6.refs_1_, bf16[128,2048]{1,0:T(8,128)(2,1)S(1)} %collective-permute-done.12.refs_2_, ...), custom_call_target="tpu_custom_call" | custom-call | tf_op jit(solution)/shard_map/pallas_call | solution.py:112
  44.7 0.6 collective-permute-start.14
  45.3 2.2 %collective-permute-start.15 = (f32[128,768]{1,0:T(8,128)S(1)}, f32[128,768]{1,0:T(8,128)S(1)}, u32[]{:S(2)}, u32[]{:S(2)}) collective-permute-start(f32[128,768]{1,0:T(8,128)S(1)} %get-tuple-element.43), channel_id=1, source_target_pairs={{0,3},{1,0},{2,1},{3,2},{4,7},{5,4},{6,5},{7,6},{8,11},{9,8},{10,9... | collective-permute-start | bytes 1179656 | tf_op jit(solution)/shard_map/ppermute | solution.py:50
  47.5 0.7 shard_map.32
  48.2 1.0 collective-permute-start.17
  49.2 0.7 shard_map.30
  49.9 6.3 %collective-permute-done.14 = f32[128,768]{1,0:T(8,128)S(1)} collective-permute-done((f32[128,768]{1,0:T(8,128)S(1)}, f32[128,768]{1,0:T(8,128)S(1)}, u32[]{:S(2)}, u32[]{:S(2)}) %collective-permute-start.14) | collective-permute-done | bytes 393248 | tf_op jit(solution)/shard_map/ppermute | solution.py:50
  56.2 8.9 %collective-permute-done.17 = f32[128,768]{1,0:T(8,128)S(1)} collective-permute-done((f32[128,768]{1,0:T(8,128)S(1)}, f32[128,768]{1,0:T(8,128)S(1)}, u32[]{:S(2)}, u32[]{:S(2)}) %collective-permute-start.17) | collective-permute-done | bytes 393248 | tf_op jit(solution)/shard_map/ppermute | solution.py:50
  65.1 0.1 add_convert_fusion.refs_0_
  65.2 0.1 collective-permute-start.25
  65.3 3.5 %collective-permute-start.18 = (bf16[128,768]{1,0:T(8,128)(2,1)S(1)}, bf16[128,768]{1,0:T(8,128)(2,1)S(1)}, u32[]{:S(2)}, u32[]{:S(2)}) collective-permute-start(bf16[128,768]{1,0:T(8,128)(2,1)S(1)} %add_convert_fusion.refs_0_), channel_id=1, source_target_pairs={{0,8},{8,16},{16,24},{24,32},{32,40},{40,48},{48,56},{56,0},{64,12... | collective-permute-start | bytes 589832 | tf_op jit(solution)/shard_map/ppermute | solution.py:31
  68.8 1.5 %collective-permute-done.25 = bf16[128,768]{1,0:T(8,128)(2,1)S(1)} collective-permute-done((bf16[128,768]{1,0:T(8,128)(2,1)S(1)}, bf16[128,768]{1,0:T(8,128)(2,1)S(1)}, u32[]{:S(2)}, u32[]{:S(2)}) %collective-permute-start.25) | collective-permute-done | bytes 196640 | tf_op jit(solution)/shard_map/ppermute | solution.py:46
  70.4 1.5 %collective-permute-start.26 = (bf16[2,128,768]{2,1,0:T(8,128)(2,1)S(1)}, bf16[2,128,768]{2,1,0:T(8,128)(2,1)S(1)}, u32[]{:S(2)}, u32[]{:S(2)}) collective-permute-start(bf16[2,128,768]{2,1,0:T(8,128)(2,1)S(1)} %pad_maximum_fusion.refs_8_), channel_id=1, source_target_pairs={{0,3},{1,0},{2,1},{3,2},{4,7},{5,4},{6,5},{7,6},{8,11},{9,8},{10,9... | collective-permute-start | bytes 1179656 | tf_op jit(solution)/shard_map/ppermute | solution.py:50
  71.8 0.1 collective-permute-start.29
  71.9 3.5 %collective-permute-start.20 = (bf16[128,768]{1,0:T(8,128)(2,1)S(1)}, bf16[128,768]{1,0:T(8,128)(2,1)S(1)}, u32[]{:S(2)}, u32[]{:S(2)}) collective-permute-start(bf16[128,768]{1,0:T(8,128)(2,1)S(1)} %collective-permute-done.18.refs_1_), channel_id=1, source_target_pairs={{0,8},{8,16},{16,24},{24,32},{32,40},{40,48},{48,56},{56,0},{64,12... | collective-permute-start | bytes 589832 | tf_op jit(solution)/shard_map/ppermute | solution.py:31
  75.4 0.4 collective-permute-done.19.refs_2_
  75.8 1.6 %collective-permute-start.28 = (bf16[128,768]{1,0:T(8,128)(2,1)S(1)}, bf16[128,768]{1,0:T(8,128)(2,1)S(1)}, u32[]{:S(2)}, u32[]{:S(2)}) collective-permute-start(bf16[128,768]{1,0:T(8,128)(2,1)S(1)} %collective-permute-done.27), channel_id=1, source_target_pairs={{0,4},{4,0},{1,5},{5,1},{2,6},{6,2},{3,7},{7,3},{8,12},{12,8},{9,1... | collective-permute-start | bytes 589832 | tf_op jit(solution)/shard_map/ppermute | solution.py:46
  77.4 0.6 collective-permute-done.20.refs_3_
  78.0 3.1 %collective-permute-start.22 = (bf16[128,768]{1,0:T(8,128)(2,1)S(1)}, bf16[128,768]{1,0:T(8,128)(2,1)S(1)}, u32[]{:S(2)}, u32[]{:S(2)}) collective-permute-start(bf16[128,768]{1,0:T(8,128)(2,1)S(1)} %collective-permute-done.20.refs_3_), channel_id=1, source_target_pairs={{0,8},{8,16},{16,24},{24,32},{32,40},{40,48},{48,56},{56,0},{64,12... | collective-permute-start | bytes 589832 | tf_op jit(solution)/shard_map/ppermute | solution.py:31
  81.2 2.6 %collective-permute-done.21.refs_4_ = bf16[128,768]{1,0:T(8,128)(2,1)S(1)} collective-permute-done((bf16[128,768]{1,0:T(8,128)(2,1)S(1)}, bf16[128,768]{1,0:T(8,128)(2,1)S(1)}, u32[]{:S(2)}, u32[]{:S(2)}) %collective-permute-start.21) | collective-permute-done | bytes 196640 | tf_op jit(solution)/shard_map/ppermute | solution.py:31
  83.8 0.5 collective-permute-start.24
  84.3 6.9 %collective-permute-done.23.refs_6_ = bf16[128,768]{1,0:T(8,128)(2,1)S(1)} collective-permute-done((bf16[128,768]{1,0:T(8,128)(2,1)S(1)}, bf16[128,768]{1,0:T(8,128)(2,1)S(1)}, u32[]{:S(2)}, u32[]{:S(2)}) %collective-permute-start.23) | collective-permute-done | bytes 196640 | tf_op jit(solution)/shard_map/ppermute | solution.py:31
  91.3 0.3 collective-permute-done.24.refs_7_
  91.5 1.2 shard_map.33
  92.7 4.9 %collective-permute-start.30 = (bf16[16,128,256]{2,1,0:T(8,128)(2,1)S(1)}, bf16[16,128,256]{2,1,0:T(8,128)(2,1)S(1)}, u32[]{:S(2)}, u32[]{:S(2)}) collective-permute-start(bf16[16,128,256]{2,1,0:T(8,128)(2,1)S(1)} %shard_map.33), channel_id=1, source_target_pairs={{0,64},{64,0},{1,65},{65,1},{2,66},{66,2},{3,67},{67,3},{4,68},{68... | collective-permute-start | bytes 3145736 | tf_op jit(solution)/shard_map/ppermute | solution.py:46
  97.7 2.3 %collective-permute-done.30.refs_12_ = bf16[16,128,256]{2,1,0:T(8,128)(2,1)S(1)} collective-permute-done((bf16[16,128,256]{2,1,0:T(8,128)(2,1)S(1)}, bf16[16,128,256]{2,1,0:T(8,128)(2,1)S(1)}, u32[]{:S(2)}, u32[]{:S(2)}) %collective-permute-start.30) | collective-permute-done | bytes 1048608 | tf_op jit(solution)/shard_map/ppermute | solution.py:46
  100.0 1.2 shard_map.34
  101.2 22.1 %all_to_all.5.pieces = bf16[16,128,256]{2,1,0:T(8,128)(2,1)S(1)} all-to-all(bf16[16,128,256]{2,1,0:T(8,128)(2,1)S(1)} %shard_map.34), channel_id=1, replica_groups=mesh['x_hi'=2,'core'=2,'z'=8,'x_lo'=2,'y'=4] {'x_hi','x_lo','y'}, dimensions={0} | all-to-all | bytes 2097152 | tf_op jit(solution)/shard_map/all_to_all | solution.py:201
  123.2 1.1 shard_map.35
  (32 shorter events, 0.2 us)
Async XLA Ops:
  0.0 0.9 copy-start
  0.9 5.5 %collective-permute-start = (bf16[128,384]{1,0:T(8,128)(2,1)S(1)}, bf16[128,384]{1,0:T(8,128)(2,1)S(1)}, u32[]{:S(2)}, u32[]{:S(2)}) collective-permute-start(bf16[128,384]{1,0:T(8,128)(2,1)S(1)} %constant_dynamic-slice_fusion), channel_id=1, source_target_pairs={{0,4},{4,128},{128,132},{132,0},{64,196},{68,64},{192,68},{196,192... | collective-permute-start | bytes 294920 | tf_op jit(solution)/shard_map/ppermute | solution.py:42
  4.3 1.6 %copy-start.1 = (bf16[1,128,8192]{2,1,0:T(8,128)(2,1)S(1)}, bf16[1,128,8192]{2,1,0:T(8,128)(2,1)}, u32[]{:S(2)}) copy-start(bf16[1,128,8192]{2,1,0:T(8,128)(2,1)} %param.2) | copy-start | bytes 6291460
  6.5 24.1 %collective-permute-start.5 = (bf16[128,2048]{1,0:T(8,128)(2,1)S(1)}, bf16[128,2048]{1,0:T(8,128)(2,1)S(1)}, u32[]{:S(2)}, u32[]{:S(2)}) collective-permute-start(bf16[128,2048]{1,0:T(8,128)(2,1)S(1)} %get-tuple-element.32), channel_id=1, source_target_pairs={{0,1},{1,2},{2,3},{3,0},{4,5},{5,6},{6,7},{7,4},{8,9},{9,10},{10,1... | collective-permute-start | bytes 1572872 | tf_op jit(solution)/shard_map/ppermute | solution.py:50
  7.9 22.7 %collective-permute-start.6 = (bf16[128,2048]{1,0:T(8,128)(2,1)S(1)}, bf16[128,2048]{1,0:T(8,128)(2,1)S(1)}, u32[]{:S(2)}, u32[]{:S(2)}) collective-permute-start(bf16[128,2048]{1,0:T(8,128)(2,1)S(1)} %get-tuple-element.33), channel_id=1, source_target_pairs={{0,3},{1,0},{2,1},{3,2},{4,7},{5,4},{6,5},{7,6},{8,11},{9,8},{10,9... | collective-permute-start | bytes 1572872 | tf_op jit(solution)/shard_map/ppermute | solution.py:50
  9.4 8.3 %collective-permute-start.1 = (bf16[256,384]{1,0:T(8,128)(2,1)S(1)}, bf16[256,384]{1,0:T(8,128)(2,1)S(1)}, u32[]{:S(2)}, u32[]{:S(2)}) collective-permute-start(bf16[256,384]{1,0:T(8,128)(2,1)S(1)} %pad_maximum_fusion.2.refs_0_), channel_id=1, source_target_pairs={{0,8},{8,16},{16,24},{24,32},{32,40},{40,48},{48,56},{56,0},{64,12... | collective-permute-start | bytes 589832 | tf_op jit(solution)/shard_map/ppermute | solution.py:31
  15.1 7.8 %collective-permute-start.2 = (bf16[256,384]{1,0:T(8,128)(2,1)S(1)}, bf16[256,384]{1,0:T(8,128)(2,1)S(1)}, u32[]{:S(2)}, u32[]{:S(2)}) collective-permute-start(bf16[256,384]{1,0:T(8,128)(2,1)S(1)} %pad_maximum_fusion.2.refs_0_), channel_id=1, source_target_pairs={{0,56},{8,0},{16,8},{24,16},{32,24},{40,32},{48,40},{56,48},{64,72... | collective-permute-start | bytes 589832 | tf_op jit(solution)/shard_map/ppermute | solution.py:31
  15.1 23.6 %collective-permute-start.10 = (bf16[128,2048]{1,0:T(8,128)(2,1)S(1)}, bf16[128,2048]{1,0:T(8,128)(2,1)S(1)}, u32[]{:S(2)}, u32[]{:S(2)}) collective-permute-start(bf16[128,2048]{1,0:T(8,128)(2,1)S(1)} %get-tuple-element.35), channel_id=1, source_target_pairs={{0,2},{1,3},{2,0},{3,1},{4,6},{5,7},{6,4},{7,5},{8,10},{9,11},{10,... | collective-permute-start | bytes 1572872 | tf_op jit(solution)/shard_map/ppermute | solution.py:50
  22.9 5.8 %collective-permute-start.3 = (bf16[256,384]{1,0:T(8,128)(2,1)S(1)}, bf16[256,384]{1,0:T(8,128)(2,1)S(1)}, u32[]{:S(2)}, u32[]{:S(2)}) collective-permute-start(bf16[256,384]{1,0:T(8,128)(2,1)S(1)} %collective-permute-done.1.refs_1_), channel_id=1, source_target_pairs={{0,8},{8,16},{16,24},{24,32},{32,40},{40,48},{48,56},{56,0},{64,12... | collective-permute-start | bytes 589832 | tf_op jit(solution)/shard_map/ppermute | solution.py:31
  22.9 7.7 %collective-permute-start.4 = (bf16[256,384]{1,0:T(8,128)(2,1)S(1)}, bf16[256,384]{1,0:T(8,128)(2,1)S(1)}, u32[]{:S(2)}, u32[]{:S(2)}) collective-permute-start(bf16[256,384]{1,0:T(8,128)(2,1)S(1)} %collective-permute-done.2.refs_2_), channel_id=1, source_target_pairs={{0,56},{8,0},{16,8},{24,16},{32,24},{40,32},{48,40},{56,48},{64,72... | collective-permute-start | bytes 589832 | tf_op jit(solution)/shard_map/ppermute | solution.py:31
  28.7 10.0 %collective-permute-start.7 = (bf16[256,384]{1,0:T(8,128)(2,1)S(1)}, bf16[256,384]{1,0:T(8,128)(2,1)S(1)}, u32[]{:S(2)}, u32[]{:S(2)}) collective-permute-start(bf16[256,384]{1,0:T(8,128)(2,1)S(1)} %collective-permute-done.3.refs_3_), channel_id=1, source_target_pairs={{0,8},{8,16},{16,24},{24,32},{32,40},{40,48},{48,56},{56,0},{64,12... | collective-permute-start | bytes 589832 | tf_op jit(solution)/shard_map/ppermute | solution.py:31
  30.6 8.1 %collective-permute-start.9 = (bf16[256,384]{1,0:T(8,128)(2,1)S(1)}, bf16[256,384]{1,0:T(8,128)(2,1)S(1)}, u32[]{:S(2)}, u32[]{:S(2)}) collective-permute-start(bf16[256,384]{1,0:T(8,128)(2,1)S(1)} %collective-permute-done.3.refs_3_), channel_id=1, source_target_pairs={{0,16},{8,24},{16,32},{24,40},{32,48},{40,56},{48,0},{56,8},{64,11... | collective-permute-start | bytes 589832 | tf_op jit(solution)/shard_map/ppermute | solution.py:31
  30.6 8.4 %collective-permute-start.8 = (bf16[256,384]{1,0:T(8,128)(2,1)S(1)}, bf16[256,384]{1,0:T(8,128)(2,1)S(1)}, u32[]{:S(2)}, u32[]{:S(2)}) collective-permute-start(bf16[256,384]{1,0:T(8,128)(2,1)S(1)} %collective-permute-done.4.refs_4_), channel_id=1, source_target_pairs={{0,56},{8,0},{16,8},{24,16},{32,24},{40,32},{48,40},{56,48},{64,72... | collective-permute-start | bytes 589832 | tf_op jit(solution)/shard_map/ppermute | solution.py:31
  31.0 12.4 %collective-permute-start.12 = (bf16[128,2048]{1,0:T(8,128)(2,1)S(1)}, bf16[128,2048]{1,0:T(8,128)(2,1)S(1)}, u32[]{:S(2)}, u32[]{:S(2)}) collective-permute-start(bf16[128,2048]{1,0:T(8,128)(2,1)S(1)} %collective-permute-done.5.refs_0_), channel_id=1, source_target_pairs={{0,64},{64,0},{1,65},{65,1},{2,66},{66,2},{3,67},{67,3},{4,68},{68... | collective-permute-start | bytes 1572872 | tf_op jit(solution)/shard_map/ppermute | solution.py:46
  38.7 4.8 %collective-permute-start.13 = (bf16[128,2048]{1,0:T(8,128)(2,1)S(1)}, bf16[128,2048]{1,0:T(8,128)(2,1)S(1)}, u32[]{:S(2)}, u32[]{:S(2)}) collective-permute-start(bf16[128,2048]{1,0:T(8,128)(2,1)S(1)} %collective-permute-done.6.refs_1_), channel_id=1, source_target_pairs={{0,64},{64,0},{1,65},{65,1},{2,66},{66,2},{3,67},{67,3},{4,68},{68... | collective-permute-start | bytes 1572872 | tf_op jit(solution)/shard_map/ppermute | solution.py:46
  39.0 8.5 %collective-permute-start.16 = (bf16[128,2048]{1,0:T(8,128)(2,1)S(1)}, bf16[128,2048]{1,0:T(8,128)(2,1)S(1)}, u32[]{:S(2)}, u32[]{:S(2)}) collective-permute-start(bf16[128,2048]{1,0:T(8,128)(2,1)S(1)} %collective-permute-done.10.refs_0_), channel_id=1, source_target_pairs={{0,64},{64,0},{1,65},{65,1},{2,66},{66,2},{3,67},{67,3},{4,68},{68... | collective-permute-start | bytes 1572872 | tf_op jit(solution)/shard_map/ppermute | solution.py:46
  43.3 5.9 %collective-permute-start.11 = (bf16[128,2048]{1,0:T(8,128)(2,1)S(1)}, bf16[128,2048]{1,0:T(8,128)(2,1)S(1)}, u32[]{:S(2)}, u32[]{:S(2)}) collective-permute-start(bf16[128,2048]{1,0:T(8,128)(2,1)S(1)} %get-tuple-element.39.refs_0_), channel_id=1, source_target_pairs={{0,64},{64,0},{1,65},{65,1},{2,66},{66,2},{3,67},{67,3},{4,68},{68... | collective-permute-start | bytes 1572872 | tf_op jit(solution)/shard_map/ppermute | solution.py:46
  44.7 11.5 %collective-permute-start.14 = (f32[128,768]{1,0:T(8,128)S(1)}, f32[128,768]{1,0:T(8,128)S(1)}, u32[]{:S(2)}, u32[]{:S(2)}) collective-permute-start(f32[128,768]{1,0:T(8,128)S(1)} %get-tuple-element.42), channel_id=1, source_target_pairs={{0,1},{1,2},{2,3},{3,0},{4,5},{5,6},{6,7},{7,4},{8,9},{9,10},{10,1... | collective-permute-start | bytes 1179656 | tf_op jit(solution)/shard_map/ppermute | solution.py:50
  45.3 10.9 %collective-permute-start.15 = (f32[128,768]{1,0:T(8,128)S(1)}, f32[128,768]{1,0:T(8,128)S(1)}, u32[]{:S(2)}, u32[]{:S(2)}) collective-permute-start(f32[128,768]{1,0:T(8,128)S(1)} %get-tuple-element.43), channel_id=1, source_target_pairs={{0,3},{1,0},{2,1},{3,2},{4,7},{5,4},{6,5},{7,6},{8,11},{9,8},{10,9... | collective-permute-start | bytes 1179656 | tf_op jit(solution)/shard_map/ppermute | solution.py:50
  48.2 16.9 %collective-permute-start.17 = (f32[128,768]{1,0:T(8,128)S(1)}, f32[128,768]{1,0:T(8,128)S(1)}, u32[]{:S(2)}, u32[]{:S(2)}) collective-permute-start(f32[128,768]{1,0:T(8,128)S(1)} %shard_map.32), channel_id=1, source_target_pairs={{0,2},{1,3},{2,0},{3,1},{4,6},{5,7},{6,4},{7,5},{8,10},{9,11},{10,... | collective-permute-start | bytes 1179656 | tf_op jit(solution)/shard_map/ppermute | solution.py:50
  65.2 5.1 %collective-permute-start.25 = (bf16[128,768]{1,0:T(8,128)(2,1)S(1)}, bf16[128,768]{1,0:T(8,128)(2,1)S(1)}, u32[]{:S(2)}, u32[]{:S(2)}) collective-permute-start(bf16[128,768]{1,0:T(8,128)(2,1)S(1)} %add_convert_fusion.refs_0_), channel_id=1, source_target_pairs={{0,4},{4,0},{1,5},{5,1},{2,6},{6,2},{3,7},{7,3},{8,12},{12,8},{9,1... | collective-permute-start | bytes 589832 | tf_op jit(solution)/shard_map/ppermute | solution.py:46
  65.3 6.6 %collective-permute-start.18 = (bf16[128,768]{1,0:T(8,128)(2,1)S(1)}, bf16[128,768]{1,0:T(8,128)(2,1)S(1)}, u32[]{:S(2)}, u32[]{:S(2)}) collective-permute-start(bf16[128,768]{1,0:T(8,128)(2,1)S(1)} %add_convert_fusion.refs_0_), channel_id=1, source_target_pairs={{0,8},{8,16},{16,24},{24,32},{32,40},{40,48},{48,56},{56,0},{64,12... | collective-permute-start | bytes 589832 | tf_op jit(solution)/shard_map/ppermute | solution.py:31
  68.8 7.1 %collective-permute-start.19 = (bf16[128,768]{1,0:T(8,128)(2,1)S(1)}, bf16[128,768]{1,0:T(8,128)(2,1)S(1)}, u32[]{:S(2)}, u32[]{:S(2)}) collective-permute-start(bf16[128,768]{1,0:T(8,128)(2,1)S(1)} %add_convert_fusion.refs_0_), channel_id=1, source_target_pairs={{0,56},{8,0},{16,8},{24,16},{32,24},{40,32},{48,40},{56,48},{64,72... | collective-permute-start | bytes 589832 | tf_op jit(solution)/shard_map/ppermute | solution.py:31
  68.8 7.1 %collective-permute-start.27 = (bf16[128,768]{1,0:T(8,128)(2,1)S(1)}, bf16[128,768]{1,0:T(8,128)(2,1)S(1)}, u32[]{:S(2)}, u32[]{:S(2)}) collective-permute-start(bf16[128,768]{1,0:T(8,128)(2,1)S(1)} %add_convert_fusion.refs_0_), channel_id=1, source_target_pairs={{0,2},{1,3},{2,0},{3,1},{4,6},{5,7},{6,4},{7,5},{8,10},{9,11},{10,... | collective-permute-start | bytes 589832 | tf_op jit(solution)/shard_map/ppermute | solution.py:50
  70.4 14.0 %collective-permute-start.26 = (bf16[2,128,768]{2,1,0:T(8,128)(2,1)S(1)}, bf16[2,128,768]{2,1,0:T(8,128)(2,1)S(1)}, u32[]{:S(2)}, u32[]{:S(2)}) collective-permute-start(bf16[2,128,768]{2,1,0:T(8,128)(2,1)S(1)} %pad_maximum_fusion.refs_8_), channel_id=1, source_target_pairs={{0,3},{1,0},{2,1},{3,2},{4,7},{5,4},{6,5},{7,6},{8,11},{9,8},{10,9... | collective-permute-start | bytes 1179656 | tf_op jit(solution)/shard_map/ppermute | solution.py:50
  71.8 12.5 %collective-permute-start.29 = (bf16[2,128,768]{2,1,0:T(8,128)(2,1)S(1)}, bf16[2,128,768]{2,1,0:T(8,128)(2,1)S(1)}, u32[]{:S(2)}, u32[]{:S(2)}) collective-permute-start(bf16[2,128,768]{2,1,0:T(8,128)(2,1)S(1)} %pad_maximum_fusion.refs_8_), channel_id=1, source_target_pairs={{0,1},{1,2},{2,3},{3,0},{4,5},{5,6},{6,7},{7,4},{8,9},{9,10},{10,1... | collective-permute-start | bytes 1179656 | tf_op jit(solution)/shard_map/ppermute | solution.py:50
  71.9 6.1 %collective-permute-start.20 = (bf16[128,768]{1,0:T(8,128)(2,1)S(1)}, bf16[128,768]{1,0:T(8,128)(2,1)S(1)}, u32[]{:S(2)}, u32[]{:S(2)}) collective-permute-start(bf16[128,768]{1,0:T(8,128)(2,1)S(1)} %collective-permute-done.18.refs_1_), channel_id=1, source_target_pairs={{0,8},{8,16},{16,24},{24,32},{32,40},{40,48},{48,56},{56,0},{64,12... | collective-permute-start | bytes 589832 | tf_op jit(solution)/shard_map/ppermute | solution.py:31
  75.8 7.9 %collective-permute-start.21 = (bf16[128,768]{1,0:T(8,128)(2,1)S(1)}, bf16[128,768]{1,0:T(8,128)(2,1)S(1)}, u32[]{:S(2)}, u32[]{:S(2)}) collective-permute-start(bf16[128,768]{1,0:T(8,128)(2,1)S(1)} %collective-permute-done.19.refs_2_), channel_id=1, source_target_pairs={{0,56},{8,0},{16,8},{24,16},{32,24},{40,32},{48,40},{56,48},{64,72... | collective-permute-start | bytes 589832 | tf_op jit(solution)/shard_map/ppermute | solution.py:31
  75.8 7.9 %collective-permute-start.28 = (bf16[128,768]{1,0:T(8,128)(2,1)S(1)}, bf16[128,768]{1,0:T(8,128)(2,1)S(1)}, u32[]{:S(2)}, u32[]{:S(2)}) collective-permute-start(bf16[128,768]{1,0:T(8,128)(2,1)S(1)} %collective-permute-done.27), channel_id=1, source_target_pairs={{0,4},{4,0},{1,5},{5,1},{2,6},{6,2},{3,7},{7,3},{8,12},{12,8},{9,1... | collective-permute-start | bytes 589832 | tf_op jit(solution)/shard_map/ppermute | solution.py:46
  78.0 6.3 %collective-permute-start.22 = (bf16[128,768]{1,0:T(8,128)(2,1)S(1)}, bf16[128,768]{1,0:T(8,128)(2,1)S(1)}, u32[]{:S(2)}, u32[]{:S(2)}) collective-permute-start(bf16[128,768]{1,0:T(8,128)(2,1)S(1)} %collective-permute-done.20.refs_3_), channel_id=1, source_target_pairs={{0,8},{8,16},{16,24},{24,32},{32,40},{40,48},{48,56},{56,0},{64,12... | collective-permute-start | bytes 589832 | tf_op jit(solution)/shard_map/ppermute | solution.py:31
  83.8 7.5 %collective-permute-start.23 = (bf16[128,768]{1,0:T(8,128)(2,1)S(1)}, bf16[128,768]{1,0:T(8,128)(2,1)S(1)}, u32[]{:S(2)}, u32[]{:S(2)}) collective-permute-start(bf16[128,768]{1,0:T(8,128)(2,1)S(1)} %collective-permute-done.21.refs_4_), channel_id=1, source_target_pairs={{0,56},{8,0},{16,8},{24,16},{32,24},{40,32},{48,40},{56,48},{64,72... | collective-permute-start | bytes 589832 | tf_op jit(solution)/shard_map/ppermute | solution.py:31
  83.8 7.8 %collective-permute-start.24 = (bf16[128,768]{1,0:T(8,128)(2,1)S(1)}, bf16[128,768]{1,0:T(8,128)(2,1)S(1)}, u32[]{:S(2)}, u32[]{:S(2)}) collective-permute-start(bf16[128,768]{1,0:T(8,128)(2,1)S(1)} %collective-permute-done.20.refs_3_), channel_id=1, source_target_pairs={{0,16},{8,24},{16,32},{24,40},{32,48},{40,56},{48,0},{56,8},{64,11... | collective-permute-start | bytes 589832 | tf_op jit(solution)/shard_map/ppermute | solution.py:31
  92.7 7.2 %collective-permute-start.30 = (bf16[16,128,256]{2,1,0:T(8,128)(2,1)S(1)}, bf16[16,128,256]{2,1,0:T(8,128)(2,1)S(1)}, u32[]{:S(2)}, u32[]{:S(2)}) collective-permute-start(bf16[16,128,256]{2,1,0:T(8,128)(2,1)S(1)} %shard_map.33), channel_id=1, source_target_pairs={{0,64},{64,0},{1,65},{65,1},{2,66},{66,2},{3,67},{67,3},{4,68},{68... | collective-permute-start | bytes 3145736 | tf_op jit(solution)/shard_map/ppermute | solution.py:46

commit v8 on v7

--- a/solution.py
+++ b/solution.py
@@ -118,7 +118,6 @@
 
 def tile_kernel(keep, *refs):
     z_blocks, lines, refs = refs[:8], refs[8:12], refs[12:]
-    added = refs[0] if keep else None
     out, z_buf, xy_buf = refs[-3:]
     core, x, y = lax.axis_index("core"), lax.axis_index("x_lo"), lax.axis_index("y")
     low = core if keep else 1 - core
@@ -137,19 +136,16 @@
                 preferred_element_type=F32,
             ).reshape(4, ROWS, 2 * ROWS)
             rows = slice(8 * high + k, 8 * high + k + 4)
-            if keep:
-                prod = prod + added[rows].astype(F32)
-            out[rows] = prod.astype(BF16)
-
-
-def tile_product(z_blocks, lines, *added):
-    keep = bool(added)
+            out[rows] = prod.astype(out.dtype)
+
+
+def tile_product(z_blocks, lines, keep):
     return pl.pallas_call(
         lambda *refs: tile_kernel(keep, *refs),
-        out_shape=jax.ShapeDtypeStruct((16, ROWS, 2 * ROWS), BF16),
+        out_shape=jax.ShapeDtypeStruct((16, ROWS, 2 * ROWS), F32 if keep else BF16),
         scratch_shapes=[pltpu.VMEM((8, ROWS, OCC), BF16)] * 2,
         compiler_params=PARAMS,
-    )(*z_blocks, *lines, *added)
+    )(*z_blocks, *lines)
 
 
 def final_kernel(pieces, out):
@@ -196,8 +192,9 @@
     lines = [pair, y_send(pair, -1), jnp.stack([far, swap(far, "x_lo")]), y_send(pair, -3)]
     z_blocks = z_gather(half)
 
-    other = tile_product(z_blocks, lines)
-    mine = tile_product(z_blocks, lines, swap(other, "core"))
+    arriving = swap(tile_product(z_blocks, lines, False), "core")
+    mine = tile_product(z_blocks, lines, True)
+    mine = (mine + arriving.astype(F32)).astype(BF16)
     pieces = lax.all_to_all(mine, ("x_hi", "x_lo", "y"), 0, 0, tiled=True)
     return assemble(pieces)
 

time: 125 us -> 124 us (level)
  starting transfers between devices: 49.8 us -> 57.1 us
  waiting for transfers between devices: 42.7 us -> 35.8 us
    ppermute x14, waiting for transfers between devices: 23.7 us -> 15.9 us  [ring_send(): return lax.ppermute(x, ('core', axis), ring_pairs(size, step))]
    ppermute x14, starting transfers between devices: 18.2 us -> 22.3 us  [ring_send(): return lax.ppermute(x, ('core', axis), ring_pairs(size, step))]
    ppermute x7, starting transfers between devices: 18.5 us -> 20.8 us  [swap(): return lax.ppermute(x, axis, [(0, 1), (1, 0)])]
    ppermute x9, waiting for transfers between devices: 15.2 us -> 17.3 us  [y_send(): return lax.ppermute(x, 'y', [(i, (i + step) % NY) for i in range(NY)])]
    ppermute x7, waiting for transfers between devices: 3.84 us -> 2.56 us  [swap(): return lax.ppermute(x, axis, [(0, 1), (1, 0)])]
  transfers between devices with their start and end apart: 31 -> 31, of which waited for: 14 -> 11; matrix products, arithmetic and copies ran while one was open for 0% -> 0% of each run, Pallas kernels for 3% -> 4%
where the time goes in v8:
time: 124 us
  starting transfers between devices  57.1 us (46%)
  waiting for transfers between devices  35.8 us (29%)
  blocking collectives  21.3 us (17%)
  Pallas kernels  6.9 us (6%)
  local copies, waits for them, and re-layouts  2.53 us (2%)
    ppermute x14, starting transfers between devices, ring_send(): return lax.ppermute(x, ('core', axis), ring_pairs(size, step))  22.3 us
    all_to_all x1, blocking collectives, body(): pieces = lax.all_to_all(mine, ('x_hi', 'x_lo', 'y'), 0, 0, tiled=True)  21.3 us
    ppermute x7, starting transfers between devices, swap(): return lax.ppermute(x, axis, [(0, 1), (1, 0)])  20.8 us
    ppermute x9, waiting for transfers between devices, y_send(): return lax.ppermute(x, 'y', [(i, (i + step) % NY) for i in range(NY)])  17.3 us
    ppermute x14, waiting for transfers between devices, ring_send(): return lax.ppermute(x, ('core', axis), ring_pairs(size, step))  15.9 us
    ppermute x9, starting transfers between devices, y_send(): return lax.ppermute(x, 'y', [(i, (i + step) % NY) for i in range(NY)])  10.6 us
    ppermute x1, starting transfers between devices, x_send(): return lax.ppermute(x, ('x_hi', 'core', 'x_lo'), pairs)  3.39 us
    pallas_call x3, Pallas kernels, partial_half(): pl.pallas_call(partial_kernel, out_shape=[jax.ShapeDtypeStruct((ROWS, OCC...  2.66 us
  transfers between devices with their start and end apart: 31, of which 11 were waited for; matrix products, arithmetic and copies ran while one was open for 0% of the time, Pallas kernels for 4%

profile of v8, /device:TPU:1, one launch (start us, length us, event | category | flops | bytes accessed | tf_op | source)
XLA Modules:
  0.0 124.2 jit_solution(12908853104753591664)
XLA Ops:
  0.0 0.9 copy-done
  0.9 3.4 %collective-permute-start = (bf16[128,384]{1,0:T(8,128)(2,1)S(1)}, bf16[128,384]{1,0:T(8,128)(2,1)S(1)}, u32[]{:S(2)}, u32[]{:S(2)}) collective-permute-start(bf16[128,384]{1,0:T(8,128)(2,1)S(1)} %constant_dynamic-slice_fusion), channel_id=1, source_target_pairs={{0,4},{4,128},{128,132},{132,0},{64,196},{68,64},{192,68},{196,192... | collective-permute-start | bytes 294920 | tf_op jit(solution)/shard_map/ppermute | solution.py:42
  4.3 1.6 %copy-done.1 = bf16[1,128,8192]{2,1,0:T(8,128)(2,1)S(1)} copy-done((bf16[1,128,8192]{2,1,0:T(8,128)(2,1)S(1)}, bf16[1,128,8192]{2,1,0:T(8,128)(2,1)}, u32[]{:S(2)}) %copy-start.1) | copy-done | bytes 2097176
  5.9 0.5 shard_map.28
  6.5 1.4 %collective-permute-start.5 = (bf16[128,2048]{1,0:T(8,128)(2,1)S(1)}, bf16[128,2048]{1,0:T(8,128)(2,1)S(1)}, u32[]{:S(2)}, u32[]{:S(2)}) collective-permute-start(bf16[128,2048]{1,0:T(8,128)(2,1)S(1)} %get-tuple-element.32), channel_id=1, source_target_pairs={{0,1},{1,2},{2,3},{3,0},{4,5},{5,6},{6,7},{7,4},{8,9},{9,10},{10,1... | collective-permute-start | bytes 1572872 | tf_op jit(solution)/shard_map/ppermute | solution.py:50
  7.9 1.5 %collective-permute-start.6 = (bf16[128,2048]{1,0:T(8,128)(2,1)S(1)}, bf16[128,2048]{1,0:T(8,128)(2,1)S(1)}, u32[]{:S(2)}, u32[]{:S(2)}) collective-permute-start(bf16[128,2048]{1,0:T(8,128)(2,1)S(1)} %get-tuple-element.33), channel_id=1, source_target_pairs={{0,3},{1,0},{2,1},{3,2},{4,7},{5,4},{6,5},{7,6},{8,11},{9,8},{10,9... | collective-permute-start | bytes 1572872 | tf_op jit(solution)/shard_map/ppermute | solution.py:50
  9.4 1.7 %collective-permute-start.2 = (bf16[256,384]{1,0:T(8,128)(2,1)S(1)}, bf16[256,384]{1,0:T(8,128)(2,1)S(1)}, u32[]{:S(2)}, u32[]{:S(2)}) collective-permute-start(bf16[256,384]{1,0:T(8,128)(2,1)S(1)} %pad_maximum_fusion.2.refs_0_), channel_id=1, source_target_pairs={{0,56},{8,0},{16,8},{24,16},{32,24},{40,32},{48,40},{56,48},{64,72... | collective-permute-start | bytes 589832 | tf_op jit(solution)/shard_map/ppermute | solution.py:31
  11.1 4.0 %collective-permute-start.1 = (bf16[256,384]{1,0:T(8,128)(2,1)S(1)}, bf16[256,384]{1,0:T(8,128)(2,1)S(1)}, u32[]{:S(2)}, u32[]{:S(2)}) collective-permute-start(bf16[256,384]{1,0:T(8,128)(2,1)S(1)} %pad_maximum_fusion.2.refs_0_), channel_id=1, source_target_pairs={{0,8},{8,16},{16,24},{24,32},{32,40},{40,48},{48,56},{56,0},{64,12... | collective-permute-start | bytes 589832 | tf_op jit(solution)/shard_map/ppermute | solution.py:31
  15.2 1.6 %collective-permute-start.10 = (bf16[128,2048]{1,0:T(8,128)(2,1)S(1)}, bf16[128,2048]{1,0:T(8,128)(2,1)S(1)}, u32[]{:S(2)}, u32[]{:S(2)}) collective-permute-start(bf16[128,2048]{1,0:T(8,128)(2,1)S(1)} %get-tuple-element.35), channel_id=1, source_target_pairs={{0,2},{1,3},{2,0},{3,1},{4,6},{5,7},{6,4},{7,5},{8,10},{9,11},{10,... | collective-permute-start | bytes 1572872 | tf_op jit(solution)/shard_map/ppermute | solution.py:50
  16.7 1.7 %collective-permute-done.2.refs_2_ = bf16[256,384]{1,0:T(8,128)(2,1)S(1)} collective-permute-done((bf16[256,384]{1,0:T(8,128)(2,1)S(1)}, bf16[256,384]{1,0:T(8,128)(2,1)S(1)}, u32[]{:S(2)}, u32[]{:S(2)}) %collective-permute-start.2) | collective-permute-done | bytes 196640 | tf_op jit(solution)/shard_map/ppermute | solution.py:31
  18.4 2.8 %collective-permute-start.3 = (bf16[256,384]{1,0:T(8,128)(2,1)S(1)}, bf16[256,384]{1,0:T(8,128)(2,1)S(1)}, u32[]{:S(2)}, u32[]{:S(2)}) collective-permute-start(bf16[256,384]{1,0:T(8,128)(2,1)S(1)} %collective-permute-done.1.refs_1_), channel_id=1, source_target_pairs={{0,8},{8,16},{16,24},{24,32},{32,40},{40,48},{48,56},{56,0},{64,12... | collective-permute-start | bytes 589832 | tf_op jit(solution)/shard_map/ppermute | solution.py:31
  21.2 2.6 %collective-permute-done.3.refs_3_ = bf16[256,384]{1,0:T(8,128)(2,1)S(1)} collective-permute-done((bf16[256,384]{1,0:T(8,128)(2,1)S(1)}, bf16[256,384]{1,0:T(8,128)(2,1)S(1)}, u32[]{:S(2)}, u32[]{:S(2)}) %collective-permute-start.3) | collective-permute-done | bytes 196640 | tf_op jit(solution)/shard_map/ppermute | solution.py:31
  23.8 2.2 %collective-permute-start.9 = (bf16[256,384]{1,0:T(8,128)(2,1)S(1)}, bf16[256,384]{1,0:T(8,128)(2,1)S(1)}, u32[]{:S(2)}, u32[]{:S(2)}) collective-permute-start(bf16[256,384]{1,0:T(8,128)(2,1)S(1)} %collective-permute-done.3.refs_3_), channel_id=1, source_target_pairs={{0,16},{8,24},{16,32},{24,40},{32,48},{40,56},{48,0},{56,8},{64,11... | collective-permute-start | bytes 589832 | tf_op jit(solution)/shard_map/ppermute | solution.py:31
  26.0 1.2 collective-permute-done.4.refs_4_
  27.2 1.5 %collective-permute-start.8 = (bf16[256,384]{1,0:T(8,128)(2,1)S(1)}, bf16[256,384]{1,0:T(8,128)(2,1)S(1)}, u32[]{:S(2)}, u32[]{:S(2)}) collective-permute-start(bf16[256,384]{1,0:T(8,128)(2,1)S(1)} %collective-permute-done.4.refs_4_), channel_id=1, source_target_pairs={{0,56},{8,0},{16,8},{24,16},{32,24},{40,32},{48,40},{56,48},{64,72... | collective-permute-start | bytes 589832 | tf_op jit(solution)/shard_map/ppermute | solution.py:31
  28.7 10.2 %collective-permute-start.12 = (bf16[128,2048]{1,0:T(8,128)(2,1)S(1)}, bf16[128,2048]{1,0:T(8,128)(2,1)S(1)}, u32[]{:S(2)}, u32[]{:S(2)}) collective-permute-start(bf16[128,2048]{1,0:T(8,128)(2,1)S(1)} %collective-permute-done.5.refs_0_), channel_id=1, source_target_pairs={{0,64},{64,0},{1,65},{65,1},{2,66},{66,2},{3,67},{67,3},{4,68},{68... | collective-permute-start | bytes 1572872 | tf_op jit(solution)/shard_map/ppermute | solution.py:46
  38.9 4.2 %collective-permute-start.16 = (bf16[128,2048]{1,0:T(8,128)(2,1)S(1)}, bf16[128,2048]{1,0:T(8,128)(2,1)S(1)}, u32[]{:S(2)}, u32[]{:S(2)}) collective-permute-start(bf16[128,2048]{1,0:T(8,128)(2,1)S(1)} %collective-permute-done.10.refs_0_), channel_id=1, source_target_pairs={{0,64},{64,0},{1,65},{65,1},{2,66},{66,2},{3,67},{67,3},{4,68},{68... | collective-permute-start | bytes 1572872 | tf_op jit(solution)/shard_map/ppermute | solution.py:46
  43.2 0.2 shard_map.29.rhs_ref
  43.4 1.2 %shard_map.31 = (f32[128,768]{1,0:T(8,128)S(1)}, f32[128,768]{1,0:T(8,128)S(1)}) custom-call(bf16[2048,384]{1,0:T(8,128)(2,1)S(1)} %shard_map.29.rhs_ref, bf16[128,2048]{1,0:T(8,128)(2,1)S(1)} %collective-permute-done.5.refs_0_, bf16[128,2048]{1,0:T(8,128)(2,1)S(1)} %collective-permute-done.6.refs_1_, bf16[128,2048]{1,0:T(8,128)(2,1)S(1)} %collective-permute-done.12.refs_2_, ...), custom_call_target="tpu_custom_call" | custom-call | tf_op jit(solution)/shard_map/pallas_call | solution.py:112
  44.7 0.1 collective-permute-start.14
  44.8 2.6 %collective-permute-start.15 = (f32[128,768]{1,0:T(8,128)S(1)}, f32[128,768]{1,0:T(8,128)S(1)}, u32[]{:S(2)}, u32[]{:S(2)}) collective-permute-start(f32[128,768]{1,0:T(8,128)S(1)} %get-tuple-element.43), channel_id=1, source_target_pairs={{0,3},{1,0},{2,1},{3,2},{4,7},{5,4},{6,5},{7,6},{8,11},{9,8},{10,9... | collective-permute-start | bytes 1179656 | tf_op jit(solution)/shard_map/ppermute | solution.py:50
  47.4 0.7 shard_map.32
  48.1 0.6 collective-permute-start.17
  48.8 0.7 shard_map.30
  49.5 6.6 %collective-permute-done.14 = f32[128,768]{1,0:T(8,128)S(1)} collective-permute-done((f32[128,768]{1,0:T(8,128)S(1)}, f32[128,768]{1,0:T(8,128)S(1)}, u32[]{:S(2)}, u32[]{:S(2)}) %collective-permute-start.14) | collective-permute-done | bytes 393248 | tf_op jit(solution)/shard_map/ppermute | solution.py:50
  56.1 9.0 %collective-permute-done.17 = f32[128,768]{1,0:T(8,128)S(1)} collective-permute-done((f32[128,768]{1,0:T(8,128)S(1)}, f32[128,768]{1,0:T(8,128)S(1)}, u32[]{:S(2)}, u32[]{:S(2)}) %collective-permute-start.17) | collective-permute-done | bytes 393248 | tf_op jit(solution)/shard_map/ppermute | solution.py:50
  65.1 0.1 add_convert_fusion.1.refs_0_
  65.2 0.1 collective-permute-start.25
  65.3 0.1 collective-permute-start.19
  65.4 3.5 %collective-permute-start.18 = (bf16[128,768]{1,0:T(8,128)(2,1)S(1)}, bf16[128,768]{1,0:T(8,128)(2,1)S(1)}, u32[]{:S(2)}, u32[]{:S(2)}) collective-permute-start(bf16[128,768]{1,0:T(8,128)(2,1)S(1)} %add_convert_fusion.1.refs_0_), channel_id=1, source_target_pairs={{0,8},{8,16},{16,24},{24,32},{32,40},{40,48},{48,56},{56,0},{64,12... | collective-permute-start | bytes 589832 | tf_op jit(solution)/shard_map/ppermute | solution.py:31
  68.9 1.5 %collective-permute-done.25 = bf16[128,768]{1,0:T(8,128)(2,1)S(1)} collective-permute-done((bf16[128,768]{1,0:T(8,128)(2,1)S(1)}, bf16[128,768]{1,0:T(8,128)(2,1)S(1)}, u32[]{:S(2)}, u32[]{:S(2)}) %collective-permute-start.25) | collective-permute-done | bytes 196640 | tf_op jit(solution)/shard_map/ppermute | solution.py:46
  70.4 0.8 collective-permute-start.29
  71.1 2.0 %collective-permute-start.26 = (bf16[2,128,768]{2,1,0:T(8,128)(2,1)S(1)}, bf16[2,128,768]{2,1,0:T(8,128)(2,1)S(1)}, u32[]{:S(2)}, u32[]{:S(2)}) collective-permute-start(bf16[2,128,768]{2,1,0:T(8,128)(2,1)S(1)} %pad_maximum_fusion.refs_8_), channel_id=1, source_target_pairs={{0,3},{1,0},{2,1},{3,2},{4,7},{5,4},{6,5},{7,6},{8,11},{9,8},{10,9... | collective-permute-start | bytes 1179656 | tf_op jit(solution)/shard_map/ppermute | solution.py:50
  73.1 3.5 %collective-permute-start.20 = (bf16[128,768]{1,0:T(8,128)(2,1)S(1)}, bf16[128,768]{1,0:T(8,128)(2,1)S(1)}, u32[]{:S(2)}, u32[]{:S(2)}) collective-permute-start(bf16[128,768]{1,0:T(8,128)(2,1)S(1)} %collective-permute-done.18.refs_1_), channel_id=1, source_target_pairs={{0,8},{8,16},{16,24},{24,32},{32,40},{40,48},{48,56},{56,0},{64,12... | collective-permute-start | bytes 589832 | tf_op jit(solution)/shard_map/ppermute | solution.py:31
  76.6 0.1 collective-permute-start.28
  76.7 3.1 %collective-permute-done.21.refs_4_ = bf16[128,768]{1,0:T(8,128)(2,1)S(1)} collective-permute-done((bf16[128,768]{1,0:T(8,128)(2,1)S(1)}, bf16[128,768]{1,0:T(8,128)(2,1)S(1)}, u32[]{:S(2)}, u32[]{:S(2)}) %collective-permute-start.21) | collective-permute-done | bytes 196640 | tf_op jit(solution)/shard_map/ppermute | solution.py:31
  79.9 3.1 %collective-permute-start.24 = (bf16[128,768]{1,0:T(8,128)(2,1)S(1)}, bf16[128,768]{1,0:T(8,128)(2,1)S(1)}, u32[]{:S(2)}, u32[]{:S(2)}) collective-permute-start(bf16[128,768]{1,0:T(8,128)(2,1)S(1)} %collective-permute-done.20.refs_3_), channel_id=1, source_target_pairs={{0,16},{8,24},{16,32},{24,40},{32,48},{40,56},{48,0},{56,8},{64,11... | collective-permute-start | bytes 589832 | tf_op jit(solution)/shard_map/ppermute | solution.py:31
  83.0 1.6 %collective-permute-done.29.refs_11_ = bf16[2,128,768]{2,1,0:T(8,128)(2,1)S(1)} collective-permute-done((bf16[2,128,768]{2,1,0:T(8,128)(2,1)S(1)}, bf16[2,128,768]{2,1,0:T(8,128)(2,1)S(1)}, u32[]{:S(2)}, u32[]{:S(2)}) %collective-permute-start.29) | collective-permute-done | bytes 393248 | tf_op jit(solution)/shard_map/ppermute | solution.py:50
  84.7 3.1 %collective-permute-done.23.refs_6_ = bf16[128,768]{1,0:T(8,128)(2,1)S(1)} collective-permute-done((bf16[128,768]{1,0:T(8,128)(2,1)S(1)}, bf16[128,768]{1,0:T(8,128)(2,1)S(1)}, u32[]{:S(2)}, u32[]{:S(2)}) %collective-permute-start.23) | collective-permute-done | bytes 196640 | tf_op jit(solution)/shard_map/ppermute | solution.py:31
  87.8 0.0 collective-permute-done.24.refs_7_
  87.8 4.1 %collective-permute-done.22.refs_5_ = bf16[128,768]{1,0:T(8,128)(2,1)S(1)} collective-permute-done((bf16[128,768]{1,0:T(8,128)(2,1)S(1)}, bf16[128,768]{1,0:T(8,128)(2,1)S(1)}, u32[]{:S(2)}, u32[]{:S(2)}) %collective-permute-start.22) | collective-permute-done | bytes 196640 | tf_op jit(solution)/shard_map/ppermute | solution.py:31
  91.9 1.2 shard_map.34
  93.1 6.1 %collective-permute-start.30 = (bf16[16,128,256]{2,1,0:T(8,128)(2,1)S(1)}, bf16[16,128,256]{2,1,0:T(8,128)(2,1)S(1)}, u32[]{:S(2)}, u32[]{:S(2)}) collective-permute-start(bf16[16,128,256]{2,1,0:T(8,128)(2,1)S(1)} %shard_map.34), channel_id=1, source_target_pairs={{0,64},{64,0},{1,65},{65,1},{2,66},{66,2},{3,67},{67,3},{4,68},{68... | collective-permute-start | bytes 3145736 | tf_op jit(solution)/shard_map/ppermute | solution.py:46
  99.2 1.2 shard_map.33
  100.4 1.1 collective-permute-done.30
  101.5 0.3 add_convert_fusion
  101.8 21.3 %all_to_all.5.pieces = bf16[16,128,256]{2,1,0:T(8,128)(2,1)S(1)} all-to-all(bf16[16,128,256]{2,1,0:T(8,128)(2,1)S(1)} %add_convert_fusion), channel_id=1, replica_groups=mesh['x_hi'=2,'core'=2,'z'=8,'x_lo'=2,'y'=4] {'x_hi','x_lo','y'}, dimensions={0} | all-to-all | bytes 2097152 | tf_op jit(solution)/shard_map/all_to_all | solution.py:198
  123.1 1.1 shard_map.35
  (33 shorter events, 0.2 us)
Async XLA Ops:
  0.0 0.9 copy-start
  0.9 5.5 %collective-permute-start = (bf16[128,384]{1,0:T(8,128)(2,1)S(1)}, bf16[128,384]{1,0:T(8,128)(2,1)S(1)}, u32[]{:S(2)}, u32[]{:S(2)}) collective-permute-start(bf16[128,384]{1,0:T(8,128)(2,1)S(1)} %constant_dynamic-slice_fusion), channel_id=1, source_target_pairs={{0,4},{4,128},{128,132},{132,0},{64,196},{68,64},{192,68},{196,192... | collective-permute-start | bytes 294920 | tf_op jit(solution)/shard_map/ppermute | solution.py:42
  4.3 1.6 %copy-start.1 = (bf16[1,128,8192]{2,1,0:T(8,128)(2,1)S(1)}, bf16[1,128,8192]{2,1,0:T(8,128)(2,1)}, u32[]{:S(2)}) copy-start(bf16[1,128,8192]{2,1,0:T(8,128)(2,1)} %param.2) | copy-start | bytes 6291460
  6.5 20.7 %collective-permute-start.5 = (bf16[128,2048]{1,0:T(8,128)(2,1)S(1)}, bf16[128,2048]{1,0:T(8,128)(2,1)S(1)}, u32[]{:S(2)}, u32[]{:S(2)}) collective-permute-start(bf16[128,2048]{1,0:T(8,128)(2,1)S(1)} %get-tuple-element.32), channel_id=1, source_target_pairs={{0,1},{1,2},{2,3},{3,0},{4,5},{5,6},{6,7},{7,4},{8,9},{9,10},{10,1... | collective-permute-start | bytes 1572872 | tf_op jit(solution)/shard_map/ppermute | solution.py:50
  7.9 19.4 %collective-permute-start.6 = (bf16[128,2048]{1,0:T(8,128)(2,1)S(1)}, bf16[128,2048]{1,0:T(8,128)(2,1)S(1)}, u32[]{:S(2)}, u32[]{:S(2)}) collective-permute-start(bf16[128,2048]{1,0:T(8,128)(2,1)S(1)} %get-tuple-element.33), channel_id=1, source_target_pairs={{0,3},{1,0},{2,1},{3,2},{4,7},{5,4},{6,5},{7,6},{8,11},{9,8},{10,9... | collective-permute-start | bytes 1572872 | tf_op jit(solution)/shard_map/ppermute | solution.py:50
  9.4 9.0 %collective-permute-start.2 = (bf16[256,384]{1,0:T(8,128)(2,1)S(1)}, bf16[256,384]{1,0:T(8,128)(2,1)S(1)}, u32[]{:S(2)}, u32[]{:S(2)}) collective-permute-start(bf16[256,384]{1,0:T(8,128)(2,1)S(1)} %pad_maximum_fusion.2.refs_0_), channel_id=1, source_target_pairs={{0,56},{8,0},{16,8},{24,16},{32,24},{40,32},{48,40},{56,48},{64,72... | collective-permute-start | bytes 589832 | tf_op jit(solution)/shard_map/ppermute | solution.py:31
  11.1 7.3 %collective-permute-start.1 = (bf16[256,384]{1,0:T(8,128)(2,1)S(1)}, bf16[256,384]{1,0:T(8,128)(2,1)S(1)}, u32[]{:S(2)}, u32[]{:S(2)}) collective-permute-start(bf16[256,384]{1,0:T(8,128)(2,1)S(1)} %pad_maximum_fusion.2.refs_0_), channel_id=1, source_target_pairs={{0,8},{8,16},{16,24},{24,32},{32,40},{40,48},{48,56},{56,0},{64,12... | collective-permute-start | bytes 589832 | tf_op jit(solution)/shard_map/ppermute | solution.py:31
  15.2 23.8 %collective-permute-start.10 = (bf16[128,2048]{1,0:T(8,128)(2,1)S(1)}, bf16[128,2048]{1,0:T(8,128)(2,1)S(1)}, u32[]{:S(2)}, u32[]{:S(2)}) collective-permute-start(bf16[128,2048]{1,0:T(8,128)(2,1)S(1)} %get-tuple-element.35), channel_id=1, source_target_pairs={{0,2},{1,3},{2,0},{3,1},{4,6},{5,7},{6,4},{7,5},{8,10},{9,11},{10,... | collective-permute-start | bytes 1572872 | tf_op jit(solution)/shard_map/ppermute | solution.py:50
  18.4 5.4 %collective-permute-start.3 = (bf16[256,384]{1,0:T(8,128)(2,1)S(1)}, bf16[256,384]{1,0:T(8,128)(2,1)S(1)}, u32[]{:S(2)}, u32[]{:S(2)}) collective-permute-start(bf16[256,384]{1,0:T(8,128)(2,1)S(1)} %collective-permute-done.1.refs_1_), channel_id=1, source_target_pairs={{0,8},{8,16},{16,24},{24,32},{32,40},{40,48},{48,56},{56,0},{64,12... | collective-permute-start | bytes 589832 | tf_op jit(solution)/shard_map/ppermute | solution.py:31
  21.2 6.0 %collective-permute-start.4 = (bf16[256,384]{1,0:T(8,128)(2,1)S(1)}, bf16[256,384]{1,0:T(8,128)(2,1)S(1)}, u32[]{:S(2)}, u32[]{:S(2)}) collective-permute-start(bf16[256,384]{1,0:T(8,128)(2,1)S(1)} %collective-permute-done.2.refs_2_), channel_id=1, source_target_pairs={{0,56},{8,0},{16,8},{24,16},{32,24},{40,32},{48,40},{56,48},{64,72... | collective-permute-start | bytes 589832 | tf_op jit(solution)/shard_map/ppermute | solution.py:31
  23.8 15.1 %collective-permute-start.9 = (bf16[256,384]{1,0:T(8,128)(2,1)S(1)}, bf16[256,384]{1,0:T(8,128)(2,1)S(1)}, u32[]{:S(2)}, u32[]{:S(2)}) collective-permute-start(bf16[256,384]{1,0:T(8,128)(2,1)S(1)} %collective-permute-done.3.refs_3_), channel_id=1, source_target_pairs={{0,16},{8,24},{16,32},{24,40},{32,48},{40,56},{48,0},{56,8},{64,11... | collective-permute-start | bytes 589832 | tf_op jit(solution)/shard_map/ppermute | solution.py:31
  27.2 11.7 %collective-permute-start.7 = (bf16[256,384]{1,0:T(8,128)(2,1)S(1)}, bf16[256,384]{1,0:T(8,128)(2,1)S(1)}, u32[]{:S(2)}, u32[]{:S(2)}) collective-permute-start(bf16[256,384]{1,0:T(8,128)(2,1)S(1)} %collective-permute-done.3.refs_3_), channel_id=1, source_target_pairs={{0,8},{8,16},{16,24},{24,32},{32,40},{40,48},{48,56},{56,0},{64,12... | collective-permute-start | bytes 589832 | tf_op jit(solution)/shard_map/ppermute | solution.py:31
  27.2 11.7 %collective-permute-start.8 = (bf16[256,384]{1,0:T(8,128)(2,1)S(1)}, bf16[256,384]{1,0:T(8,128)(2,1)S(1)}, u32[]{:S(2)}, u32[]{:S(2)}) collective-permute-start(bf16[256,384]{1,0:T(8,128)(2,1)S(1)} %collective-permute-done.4.refs_4_), channel_id=1, source_target_pairs={{0,56},{8,0},{16,8},{24,16},{32,24},{40,32},{48,40},{56,48},{64,72... | collective-permute-start | bytes 589832 | tf_op jit(solution)/shard_map/ppermute | solution.py:31
  28.7 14.7 %collective-permute-start.12 = (bf16[128,2048]{1,0:T(8,128)(2,1)S(1)}, bf16[128,2048]{1,0:T(8,128)(2,1)S(1)}, u32[]{:S(2)}, u32[]{:S(2)}) collective-permute-start(bf16[128,2048]{1,0:T(8,128)(2,1)S(1)} %collective-permute-done.5.refs_0_), channel_id=1, source_target_pairs={{0,64},{64,0},{1,65},{65,1},{2,66},{66,2},{3,67},{67,3},{4,68},{68... | collective-permute-start | bytes 1572872 | tf_op jit(solution)/shard_map/ppermute | solution.py:46
  38.9 4.5 %collective-permute-start.13 = (bf16[128,2048]{1,0:T(8,128)(2,1)S(1)}, bf16[128,2048]{1,0:T(8,128)(2,1)S(1)}, u32[]{:S(2)}, u32[]{:S(2)}) collective-permute-start(bf16[128,2048]{1,0:T(8,128)(2,1)S(1)} %collective-permute-done.6.refs_1_), channel_id=1, source_target_pairs={{0,64},{64,0},{1,65},{65,1},{2,66},{66,2},{3,67},{67,3},{4,68},{68... | collective-permute-start | bytes 1572872 | tf_op jit(solution)/shard_map/ppermute | solution.py:46
  38.9 8.5 %collective-permute-start.16 = (bf16[128,2048]{1,0:T(8,128)(2,1)S(1)}, bf16[128,2048]{1,0:T(8,128)(2,1)S(1)}, u32[]{:S(2)}, u32[]{:S(2)}) collective-permute-start(bf16[128,2048]{1,0:T(8,128)(2,1)S(1)} %collective-permute-done.10.refs_0_), channel_id=1, source_target_pairs={{0,64},{64,0},{1,65},{65,1},{2,66},{66,2},{3,67},{67,3},{4,68},{68... | collective-permute-start | bytes 1572872 | tf_op jit(solution)/shard_map/ppermute | solution.py:46
  43.2 5.6 %collective-permute-start.11 = (bf16[128,2048]{1,0:T(8,128)(2,1)S(1)}, bf16[128,2048]{1,0:T(8,128)(2,1)S(1)}, u32[]{:S(2)}, u32[]{:S(2)}) collective-permute-start(bf16[128,2048]{1,0:T(8,128)(2,1)S(1)} %get-tuple-element.39.refs_0_), channel_id=1, source_target_pairs={{0,64},{64,0},{1,65},{65,1},{2,66},{66,2},{3,67},{67,3},{4,68},{68... | collective-permute-start | bytes 1572872 | tf_op jit(solution)/shard_map/ppermute | solution.py:46
  44.7 11.5 %collective-permute-start.14 = (f32[128,768]{1,0:T(8,128)S(1)}, f32[128,768]{1,0:T(8,128)S(1)}, u32[]{:S(2)}, u32[]{:S(2)}) collective-permute-start(f32[128,768]{1,0:T(8,128)S(1)} %get-tuple-element.42), channel_id=1, source_target_pairs={{0,1},{1,2},{2,3},{3,0},{4,5},{5,6},{6,7},{7,4},{8,9},{9,10},{10,1... | collective-permute-start | bytes 1179656 | tf_op jit(solution)/shard_map/ppermute | solution.py:50
  44.8 11.3 %collective-permute-start.15 = (f32[128,768]{1,0:T(8,128)S(1)}, f32[128,768]{1,0:T(8,128)S(1)}, u32[]{:S(2)}, u32[]{:S(2)}) collective-permute-start(f32[128,768]{1,0:T(8,128)S(1)} %get-tuple-element.43), channel_id=1, source_target_pairs={{0,3},{1,0},{2,1},{3,2},{4,7},{5,4},{6,5},{7,6},{8,11},{9,8},{10,9... | collective-permute-start | bytes 1179656 | tf_op jit(solution)/shard_map/ppermute | solution.py:50
  48.1 17.0 %collective-permute-start.17 = (f32[128,768]{1,0:T(8,128)S(1)}, f32[128,768]{1,0:T(8,128)S(1)}, u32[]{:S(2)}, u32[]{:S(2)}) collective-permute-start(f32[128,768]{1,0:T(8,128)S(1)} %shard_map.32), channel_id=1, source_target_pairs={{0,2},{1,3},{2,0},{3,1},{4,6},{5,7},{6,4},{7,5},{8,10},{9,11},{10,... | collective-permute-start | bytes 1179656 | tf_op jit(solution)/shard_map/ppermute | solution.py:50
  65.2 5.1 %collective-permute-start.25 = (bf16[128,768]{1,0:T(8,128)(2,1)S(1)}, bf16[128,768]{1,0:T(8,128)(2,1)S(1)}, u32[]{:S(2)}, u32[]{:S(2)}) collective-permute-start(bf16[128,768]{1,0:T(8,128)(2,1)S(1)} %add_convert_fusion.1.refs_0_), channel_id=1, source_target_pairs={{0,4},{4,0},{1,5},{5,1},{2,6},{6,2},{3,7},{7,3},{8,12},{12,8},{9,1... | collective-permute-start | bytes 589832 | tf_op jit(solution)/shard_map/ppermute | solution.py:46
  65.3 7.8 %collective-permute-start.19 = (bf16[128,768]{1,0:T(8,128)(2,1)S(1)}, bf16[128,768]{1,0:T(8,128)(2,1)S(1)}, u32[]{:S(2)}, u32[]{:S(2)}) collective-permute-start(bf16[128,768]{1,0:T(8,128)(2,1)S(1)} %add_convert_fusion.1.refs_0_), channel_id=1, source_target_pairs={{0,56},{8,0},{16,8},{24,16},{32,24},{40,32},{48,40},{56,48},{64,72... | collective-permute-start | bytes 589832 | tf_op jit(solution)/shard_map/ppermute | solution.py:31
  65.4 7.7 %collective-permute-start.18 = (bf16[128,768]{1,0:T(8,128)(2,1)S(1)}, bf16[128,768]{1,0:T(8,128)(2,1)S(1)}, u32[]{:S(2)}, u32[]{:S(2)}) collective-permute-start(bf16[128,768]{1,0:T(8,128)(2,1)S(1)} %add_convert_fusion.1.refs_0_), channel_id=1, source_target_pairs={{0,8},{8,16},{16,24},{24,32},{32,40},{40,48},{48,56},{56,0},{64,12... | collective-permute-start | bytes 589832 | tf_op jit(solution)/shard_map/ppermute | solution.py:31
  68.9 7.7 %collective-permute-start.27 = (bf16[128,768]{1,0:T(8,128)(2,1)S(1)}, bf16[128,768]{1,0:T(8,128)(2,1)S(1)}, u32[]{:S(2)}, u32[]{:S(2)}) collective-permute-start(bf16[128,768]{1,0:T(8,128)(2,1)S(1)} %add_convert_fusion.1.refs_0_), channel_id=1, source_target_pairs={{0,2},{1,3},{2,0},{3,1},{4,6},{5,7},{6,4},{7,5},{8,10},{9,11},{10,... | collective-permute-start | bytes 589832 | tf_op jit(solution)/shard_map/ppermute | solution.py:50
  70.4 14.3 %collective-permute-start.29 = (bf16[2,128,768]{2,1,0:T(8,128)(2,1)S(1)}, bf16[2,128,768]{2,1,0:T(8,128)(2,1)S(1)}, u32[]{:S(2)}, u32[]{:S(2)}) collective-permute-start(bf16[2,128,768]{2,1,0:T(8,128)(2,1)S(1)} %pad_maximum_fusion.refs_8_), channel_id=1, source_target_pairs={{0,1},{1,2},{2,3},{3,0},{4,5},{5,6},{6,7},{7,4},{8,9},{9,10},{10,1... | collective-permute-start | bytes 1179656 | tf_op jit(solution)/shard_map/ppermute | solution.py:50
  71.1 13.5 %collective-permute-start.26 = (bf16[2,128,768]{2,1,0:T(8,128)(2,1)S(1)}, bf16[2,128,768]{2,1,0:T(8,128)(2,1)S(1)}, u32[]{:S(2)}, u32[]{:S(2)}) collective-permute-start(bf16[2,128,768]{2,1,0:T(8,128)(2,1)S(1)} %pad_maximum_fusion.refs_8_), channel_id=1, source_target_pairs={{0,3},{1,0},{2,1},{3,2},{4,7},{5,4},{6,5},{7,6},{8,11},{9,8},{10,9... | collective-permute-start | bytes 1179656 | tf_op jit(solution)/shard_map/ppermute | solution.py:50
  73.1 6.7 %collective-permute-start.21 = (bf16[128,768]{1,0:T(8,128)(2,1)S(1)}, bf16[128,768]{1,0:T(8,128)(2,1)S(1)}, u32[]{:S(2)}, u32[]{:S(2)}) collective-permute-start(bf16[128,768]{1,0:T(8,128)(2,1)S(1)} %collective-permute-done.19.refs_2_), channel_id=1, source_target_pairs={{0,56},{8,0},{16,8},{24,16},{32,24},{40,32},{48,40},{56,48},{64,72... | collective-permute-start | bytes 589832 | tf_op jit(solution)/shard_map/ppermute | solution.py:31
  73.1 6.7 %collective-permute-start.20 = (bf16[128,768]{1,0:T(8,128)(2,1)S(1)}, bf16[128,768]{1,0:T(8,128)(2,1)S(1)}, u32[]{:S(2)}, u32[]{:S(2)}) collective-permute-start(bf16[128,768]{1,0:T(8,128)(2,1)S(1)} %collective-permute-done.18.refs_1_), channel_id=1, source_target_pairs={{0,8},{8,16},{16,24},{24,32},{32,40},{40,48},{48,56},{56,0},{64,12... | collective-permute-start | bytes 589832 | tf_op jit(solution)/shard_map/ppermute | solution.py:31
  76.6 6.4 %collective-permute-start.28 = (bf16[128,768]{1,0:T(8,128)(2,1)S(1)}, bf16[128,768]{1,0:T(8,128)(2,1)S(1)}, u32[]{:S(2)}, u32[]{:S(2)}) collective-permute-start(bf16[128,768]{1,0:T(8,128)(2,1)S(1)} %collective-permute-done.27), channel_id=1, source_target_pairs={{0,4},{4,0},{1,5},{5,1},{2,6},{6,2},{3,7},{7,3},{8,12},{12,8},{9,1... | collective-permute-start | bytes 589832 | tf_op jit(solution)/shard_map/ppermute | solution.py:46
  79.9 7.9 %collective-permute-start.23 = (bf16[128,768]{1,0:T(8,128)(2,1)S(1)}, bf16[128,768]{1,0:T(8,128)(2,1)S(1)}, u32[]{:S(2)}, u32[]{:S(2)}) collective-permute-start(bf16[128,768]{1,0:T(8,128)(2,1)S(1)} %collective-permute-done.21.refs_4_), channel_id=1, source_target_pairs={{0,56},{8,0},{16,8},{24,16},{32,24},{40,32},{48,40},{56,48},{64,72... | collective-permute-start | bytes 589832 | tf_op jit(solution)/shard_map/ppermute | solution.py:31
  79.9 7.9 %collective-permute-start.24 = (bf16[128,768]{1,0:T(8,128)(2,1)S(1)}, bf16[128,768]{1,0:T(8,128)(2,1)S(1)}, u32[]{:S(2)}, u32[]{:S(2)}) collective-permute-start(bf16[128,768]{1,0:T(8,128)(2,1)S(1)} %collective-permute-done.20.refs_3_), channel_id=1, source_target_pairs={{0,16},{8,24},{16,32},{24,40},{32,48},{40,56},{48,0},{56,8},{64,11... | collective-permute-start | bytes 589832 | tf_op jit(solution)/shard_map/ppermute | solution.py:31
  83.0 8.9 %collective-permute-start.22 = (bf16[128,768]{1,0:T(8,128)(2,1)S(1)}, bf16[128,768]{1,0:T(8,128)(2,1)S(1)}, u32[]{:S(2)}, u32[]{:S(2)}) collective-permute-start(bf16[128,768]{1,0:T(8,128)(2,1)S(1)} %collective-permute-done.20.refs_3_), channel_id=1, source_target_pairs={{0,8},{8,16},{16,24},{24,32},{32,40},{40,48},{48,56},{56,0},{64,12... | collective-permute-start | bytes 589832 | tf_op jit(solution)/shard_map/ppermute | solution.py:31
  93.1 8.3 %collective-permute-start.30 = (bf16[16,128,256]{2,1,0:T(8,128)(2,1)S(1)}, bf16[16,128,256]{2,1,0:T(8,128)(2,1)S(1)}, u32[]{:S(2)}, u32[]{:S(2)}) collective-permute-start(bf16[16,128,256]{2,1,0:T(8,128)(2,1)S(1)} %shard_map.34), channel_id=1, source_target_pairs={{0,64},{64,0},{1,65},{65,1},{2,66},{66,2},{3,67},{67,3},{4,68},{68... | collective-permute-start | bytes 3145736 | tf_op jit(solution)/shard_map/ppermute | solution.py:46
